TPU v7x, 32 devices: a whole 2x2x4 slice. The times are simulated.
32 devices in a mesh: dp: 16 (over z, x, core), tensor: 2 (over y).
Axes of the slice: x: 2, y: 2, z: 4, core: 2. Of those that a mesh axis runs over, the one named last changes fastest.
Arguments:
- images: bfloat16 [32, 578, 1024], P('dp', 'tensor'), may hold values from -6 to 6
- cotangent: bfloat16 [32, 578, 1024], P('dp', 'tensor'), may hold values from -6 to 6
- slot_live: int32 [32], P('dp'), may hold values from 0 to 1, as said below
- first_gain: bfloat16 [1024], replicated, may hold values from 0.099609375 to 1.8984375
- first_shift: bfloat16 [1024], replicated, may hold values from -2 to 2
- query_weight: bfloat16 [1024, 1024], P('dp', 'tensor'), may hold values from -0.1875 to 0.1875
- query_bias: bfloat16 [1024], replicated, may hold values from -3 to 3
- key_weight: bfloat16 [1024, 1024], P('dp', 'tensor'), may hold values from -0.1875 to 0.1875
- value_weight: bfloat16 [1024, 1024], P('dp', 'tensor'), may hold values from -0.1875 to 0.1875
- value_bias: bfloat16 [1024], replicated, may hold values from -2 to 2
- output_weight: bfloat16 [1024, 1024], P('tensor', 'dp'), may hold values from -3 to 3
- output_bias: bfloat16 [1024], replicated, may hold values from -2 to 2
- second_gain: bfloat16 [1024], replicated, may hold values from 0.099609375 to 1.8984375
- second_shift: bfloat16 [1024], replicated, may hold values from -2 to 2
- up_weight: bfloat16 [1024, 4096], P('dp', 'tensor'), may hold values from -0.1875 to 0.1875
- up_bias: bfloat16 [4096], replicated, may hold values from -3 to 3
- down_weight: bfloat16 [4096, 1024], P('tensor', 'dp'), may hold values from -0.09375 to 0.09375
- down_bias: bfloat16 [1024], replicated, may hold values from -2 to 2
Outputs:
- layer_out: bfloat16 [32, 578, 1024], P('dp', 'tensor')
- images_grad: float32 [32, 578, 1024], P('dp', 'tensor')
- first_gain_grad: float32 [1024], replicated
- first_shift_grad: float32 [1024], replicated
- query_weight_grad: float32 [1024, 1024], P('dp', 'tensor')
- query_bias_grad: float32 [1024], replicated
- key_weight_grad: float32 [1024, 1024], P('dp', 'tensor')
- value_weight_grad: float32 [1024, 1024], P('dp', 'tensor')
- value_bias_grad: float32 [1024], replicated
- output_weight_grad: float32 [1024, 1024], P('tensor', 'dp')
- output_bias_grad: float32 [1024], replicated
- second_gain_grad: float32 [1024], replicated
- second_shift_grad: float32 [1024], replicated
- up_weight_grad: float32 [1024, 4096], P('dp', 'tensor')
- up_bias_grad: float32 [4096], replicated
- down_weight_grad: float32 [4096, 1024], P('tensor', 'dp')
- down_bias_grad: float32 [1024], replicated
Inputs may be any that keep to these rules, and one draw needn't show every extreme that they name: `slot_live`: in every group of 2 consecutive slots the first holds an image, and in some group every slot does.
All inputs are finite; a program needn't handle non-finite values.
Results may differ from a plain program's by a relative error of at most 0.017.
Values may be sent and summed in bfloat16 or wider, within the bound.
No kernel may reach another device: no remote copies, remote signals or barrier semaphores. Data moves between devices by JAX's collectives and lax.ppermute only.
A program may use at most 128 MiB of HBM per device.

v0:
```python
import jax
import jax.numpy as jnp
from jax import lax
from jax.sharding import PartitionSpec as P

HDIM = 64
VALID = 577


EPS = 1e-05
NEGATIVE = -1e30
SLOPE = 1.702


def layer_norm(values, gain, shift):
    center = values - jnp.mean(values, axis=-1, keepdims=True)
    spread = lax.rsqrt(jnp.mean(center * center, axis=-1, keepdims=True) + EPS)
    unit = center * spread
    return (unit * gain + shift, unit, spread)


def norm_back(upstream, unit, spread, gain):
    scaled = upstream * gain
    inner = (
        scaled
        - jnp.mean(scaled, axis=-1, keepdims=True)
        - unit * jnp.mean(scaled * unit, axis=-1, keepdims=True)
    )
    return (spread * inner, jnp.sum(upstream * unit, axis=(0, 1)), jnp.sum(upstream, axis=(0, 1)))


def dense(left, right):
    return jnp.einsum("spa,ab->spb", left, right, preferred_element_type=jnp.float32)


def project_back(left, right):
    return jnp.einsum("spa,ba->spb", left, right, preferred_element_type=jnp.float32)


def outer(left, right):
    return jnp.einsum("spa,spb->ab", left, right, preferred_element_type=jnp.float32)


def column_sum(values):
    return jnp.sum(values.astype(jnp.float32), axis=(0, 1))


def widen(piece, length, start):
    return lax.dynamic_update_slice_in_dim(jnp.zeros((length,), jnp.float32), piece, start, 0)


def split_heads(block):
    return block.reshape(block.shape[0], -1, HDIM)


def scores_of(query, key, key_ok):
    raw = jnp.einsum(
        "qhe,khe->hqk", split_heads(query), split_heads(key), preferred_element_type=jnp.float32
    )
    return jnp.where(key_ok[None, None, :], raw * HDIM ** (-0.5), NEGATIVE)


def attend(query, key, value, key_ok):
    scores = scores_of(query, key, key_ok)
    top = jnp.max(scores, axis=-1, keepdims=True)
    total = top + jnp.log(jnp.sum(jnp.exp(scores - top), axis=-1, keepdims=True))
    probs = jnp.exp(scores - total).astype(jnp.bfloat16)
    mixed = jnp.einsum(
        "hqk,khe->qhe", probs, split_heads(value), preferred_element_type=jnp.float32
    )
    return (mixed.reshape(query.shape[0], -1).astype(jnp.bfloat16), total)


def attend_back(query, key, value, grad_mixed, total, key_ok):
    scores = scores_of(query, key, key_ok)
    probs = jnp.exp(scores - total)
    grad_heads = split_heads(grad_mixed)
    grad_probs = jnp.einsum(
        "qhe,khe->hqk", grad_heads, split_heads(value), preferred_element_type=jnp.float32
    )
    grad_value = jnp.einsum(
        "hqk,qhe->khe", probs.astype(jnp.bfloat16), grad_heads, preferred_element_type=jnp.float32
    )
    grad_scores = (
        probs * (grad_probs - jnp.sum(probs * grad_probs, axis=-1, keepdims=True))
    ).astype(jnp.bfloat16)
    grad_query = jnp.einsum(
        "hqk,khe->qhe", grad_scores, split_heads(key), preferred_element_type=jnp.float32
    ) * HDIM ** (-0.5)
    grad_key = jnp.einsum(
        "hqk,qhe->khe", grad_scores, split_heads(query), preferred_element_type=jnp.float32
    ) * HDIM ** (-0.5)
    length = query.shape[0]
    return (
        grad_query.reshape(length, -1).astype(jnp.bfloat16),
        grad_key.reshape(length, -1).astype(jnp.bfloat16),
        grad_value.reshape(length, -1).astype(jnp.bfloat16),
    )


def local(
    images,
    cotangent,
    slot_live,
    first_gain,
    first_shift,
    query_weight,
    query_bias,
    key_weight,
    value_weight,
    value_bias,
    output_weight,
    output_bias,
    second_gain,
    second_shift,
    up_weight,
    up_bias,
    down_weight,
    down_bias,
):
    slots, strip, width = images.shape
    tensor_count = lax.axis_size("tensor")
    tensor_place = lax.axis_index("tensor")
    seq_len = strip * tensor_count
    positions = tensor_place * strip + jnp.arange(strip)
    row_mask = (
        slot_live.astype(jnp.float32)[:, None, None]
        * (positions < VALID).astype(jnp.float32)[None, :, None]
    )
    key_ok = jnp.arange(seq_len) < VALID
    query_full, key_full, value_full, upper_full, output_full, lower_full = (
        lax.all_gather(query_weight, "dp", axis=0, tiled=True),
        lax.all_gather(key_weight, "dp", axis=0, tiled=True),
        lax.all_gather(value_weight, "dp", axis=0, tiled=True),
        lax.all_gather(up_weight, "dp", axis=0, tiled=True),
        lax.all_gather(output_weight, "dp", axis=1, tiled=True),
        lax.all_gather(down_weight, "dp", axis=1, tiled=True),
    )
    head_cols = query_full.shape[1]
    head_start = tensor_place * head_cols
    gain_one = first_gain.astype(jnp.float32)
    shift_one = first_shift.astype(jnp.float32)
    gain_two = second_gain.astype(jnp.float32)
    shift_two = second_shift.astype(jnp.float32)
    query_shift = lax.dynamic_slice_in_dim(query_bias.astype(jnp.float32), head_start, head_cols)
    value_shift = lax.dynamic_slice_in_dim(value_bias.astype(jnp.float32), head_start, head_cols)
    resid = images.astype(jnp.float32)
    normed, unit_one, spread_one = layer_norm(resid, gain_one, shift_one)
    normed_rows = lax.all_gather(normed.astype(jnp.bfloat16), "tensor", axis=1, tiled=True)
    queries = (dense(normed_rows, query_full) + query_shift).astype(jnp.bfloat16)
    keys_low = dense(normed_rows, key_full).astype(jnp.bfloat16)
    values_low = (dense(normed_rows, value_full) + value_shift).astype(jnp.bfloat16)
    mixed, totals = lax.map(
        lambda items: attend(items[0], items[1], items[2], key_ok), (queries, keys_low, values_low)
    )
    attended = lax.psum_scatter(
        dense(mixed, output_full), "tensor", scatter_dimension=1, tiled=True
    ) + output_bias.astype(jnp.float32)
    middle = row_mask * (resid + attended)
    second, unit_two, spread_two = layer_norm(middle, gain_two, shift_two)
    second_low = second.astype(jnp.bfloat16)
    grad_top = row_mask * cotangent.astype(jnp.float32)
    fed_grad = grad_top.astype(jnp.bfloat16)
    down_shift = down_bias.astype(jnp.float32)
    units = upper_full.shape[1]
    second_rows = lax.all_gather(second_low, "tensor", axis=1, tiled=True)
    up_shift = lax.dynamic_slice_in_dim(up_bias.astype(jnp.float32), tensor_place * units, units)
    hidden = dense(second_rows, upper_full) + up_shift
    sigma = jax.nn.sigmoid(SLOPE * hidden)
    active = (hidden * sigma).astype(jnp.bfloat16)
    fed = (
        lax.psum_scatter(
            dense(active, lower_full).astype(jnp.bfloat16),
            "tensor",
            scatter_dimension=1,
            tiled=True,
        ).astype(jnp.float32)
        + down_shift
    )
    fed_rows = lax.all_gather(fed_grad, "tensor", axis=1, tiled=True)
    grad_active = project_back(fed_rows, lower_full)
    lower_grad = outer(active, fed_rows)
    hidden_grad = (grad_active * (sigma + SLOPE * hidden * sigma * (1.0 - sigma))).astype(
        jnp.bfloat16
    )
    upper_grad = outer(second_rows, hidden_grad)
    up_bias_grad = widen(column_sum(hidden_grad), up_bias.shape[0], tensor_place * units)
    second_grad = lax.psum_scatter(
        project_back(hidden_grad, upper_full), "tensor", scatter_dimension=1, tiled=True
    )
    layer_out = (row_mask * (middle + fed)).astype(jnp.bfloat16)
    down_bias_grad = column_sum(fed_grad)
    middle_back, gain_two_grad, shift_two_grad = norm_back(
        second_grad, unit_two, spread_two, gain_two
    )
    middle_grad = row_mask * (grad_top + middle_back)
    attended_grad = middle_grad.astype(jnp.bfloat16)
    output_bias_grad = column_sum(attended_grad)
    attended_rows = lax.all_gather(attended_grad, "tensor", axis=1, tiled=True)
    grad_mixed = project_back(attended_rows, output_full).astype(jnp.bfloat16)
    output_grad = outer(mixed, attended_rows)
    grad_query, grad_key, grad_value = lax.map(
        lambda items: attend_back(items[0], items[1], items[2], items[3], items[4], key_ok),
        (queries, keys_low, values_low, grad_mixed, totals),
    )
    query_grad = outer(normed_rows, grad_query)
    key_grad = outer(normed_rows, grad_key)
    value_grad = outer(normed_rows, grad_value)
    query_bias_grad = widen(column_sum(grad_query), width, head_start)
    value_bias_grad = widen(column_sum(grad_value), width, head_start)
    normed_terms = (
        project_back(grad_query, query_full)
        + project_back(grad_key, key_full)
        + project_back(grad_value, value_full)
    )
    normed_grad = lax.psum_scatter(
        normed_terms.astype(jnp.bfloat16), "tensor", scatter_dimension=1, tiled=True
    ).astype(jnp.float32)
    first_back, gain_one_grad, shift_one_grad = norm_back(
        normed_grad, unit_one, spread_one, gain_one
    )
    images_grad = middle_grad + first_back
    query_owned, key_owned, value_owned, upper_owned, output_owned, lower_owned = (
        lax.psum_scatter(
            query_grad.astype(jnp.bfloat16), "dp", scatter_dimension=0, tiled=True
        ).astype(jnp.float32),
        lax.psum_scatter(
            key_grad.astype(jnp.bfloat16), "dp", scatter_dimension=0, tiled=True
        ).astype(jnp.float32),
        lax.psum_scatter(
            value_grad.astype(jnp.bfloat16), "dp", scatter_dimension=0, tiled=True
        ).astype(jnp.float32),
        lax.psum_scatter(
            upper_grad.astype(jnp.bfloat16), "dp", scatter_dimension=0, tiled=True
        ).astype(jnp.float32),
        lax.psum_scatter(
            output_grad.astype(jnp.bfloat16), "dp", scatter_dimension=1, tiled=True
        ).astype(jnp.float32),
        lax.psum_scatter(
            lower_grad.astype(jnp.bfloat16), "dp", scatter_dimension=1, tiled=True
        ).astype(jnp.float32),
    )
    vector_sums = lax.psum(
        (
            gain_one_grad,
            shift_one_grad,
            query_bias_grad,
            value_bias_grad,
            output_bias_grad,
            gain_two_grad,
            shift_two_grad,
            up_bias_grad,
            down_bias_grad,
        ),
        ("dp", "tensor"),
    )
    (
        gain_one_total,
        shift_one_total,
        query_bias_total,
        value_bias_total,
        output_bias_total,
        gain_two_total,
        shift_two_total,
        up_bias_total,
        down_bias_total,
    ) = vector_sums
    return (
        layer_out,
        images_grad,
        gain_one_total,
        shift_one_total,
        query_owned,
        query_bias_total,
        key_owned,
        value_owned,
        value_bias_total,
        output_owned,
        output_bias_total,
        gain_two_total,
        shift_two_total,
        upper_owned,
        up_bias_total,
        lower_owned,
        down_bias_total,
    )


def solution(mesh):
    in_specs = (
        P("dp", "tensor", None),
        P("dp", "tensor", None),
        P("dp"),
        P(),
        P(),
        P("dp", "tensor"),
        P(),
        P("dp", "tensor"),
        P("dp", "tensor"),
        P(),
        P("tensor", "dp"),
        P(),
        P(),
        P(),
        P("dp", "tensor"),
        P(),
        P("tensor", "dp"),
        P(),
    )
    out_specs = (
        P("dp", "tensor", None),
        P("dp", "tensor", None),
        P(),
        P(),
        P("dp", "tensor"),
        P(),
        P("dp", "tensor"),
        P("dp", "tensor"),
        P(),
        P("tensor", "dp"),
        P(),
        P(),
        P(),
        P("dp", "tensor"),
        P(),
        P("tensor", "dp"),
        P(),
    )
    return jax.shard_map(local, mesh=mesh, in_specs=in_specs, out_specs=out_specs, check_vma=False)
```

profile of v0, /device:TPU:0, one launch (start us, length us, event | category | flops | bytes accessed | tf_op | source)
XLA Modules:
  0.0 1293.3 jit_solution(14458849398330766195)
XLA Ops:
  9.4 2.3 convert_reduce_fusion.2
  14.1 2.9 add_convert_fusion.4
  19.1 31.7 %all-gather.15.cloned.1.call-done = bf16[1024,512]{1,0:T(8,128)(2,1)} async-done(((bf16[64,512]{1,0:T(8,128)(2,1)}), bf16[1024,512]{1,0:T(8,128)(2,1)}) %all-gather.15.cloned.1.call-update) | async-done | bytes 1048592 | tf_op jit(solution)/shard_map/all_gather | solution.py:132
  50.9 37.2 %all-gather.11.cloned.1.call-done = bf16[2,578,1024]{2,0,1:T(2,128)(2,1)} async-done(((bf16[2,289,1024]{2,0,1:T(2,128)(2,1)}), bf16[2,578,1024]{2,0,1:T(2,128)(2,1)}) %all-gather.11.cloned.1.call-update) | async-done | bytes 2367504 | tf_op jit(solution)/shard_map/all_gather | solution.py:149
  88.1 3.4 add_convert_fusion.1
  92.2 36.0 %all-gather.13.cloned.1.call-done = bf16[1024,512]{1,0:T(8,128)(2,1)} async-done(((bf16[64,512]{1,0:T(8,128)(2,1)}), bf16[1024,512]{1,0:T(8,128)(2,1)}) %all-gather.13.cloned.1.call-update) | async-done | bytes 1048592 | tf_op jit(solution)/shard_map/all_gather | solution.py:134
  128.2 4.4 add_convert_fusion.2
  134.3 32.8 %all-gather.17.cloned.1.call-done = bf16[1024,512]{1,0:T(8,128)(2,1)} async-done(((bf16[64,512]{1,0:T(8,128)(2,1)}), bf16[1024,512]{1,0:T(8,128)(2,1)}) %all-gather.17.cloned.1.call-update) | async-done | bytes 1048592 | tf_op jit(solution)/shard_map/all_gather | solution.py:133
  167.1 4.4 convolution_convert_fusion
  171.5 2.4 copy.67
  175.1 22.1 %while.28 = (s32[]{:T(128)}, bf16[2,578,512]{1,2,0:T(8,128)(2,1)}, f32[2,8,578,1]{2,1,3,0:T(8,128)S(1)}, bf16[2,578,512]{1,2,0:T(8,128)(2,1)S(1)}, bf16[2,578,51...) while((s32[]{:T(128)}, bf16[2,578,512]{1,2,0:T(8,128)(2,1)}, ...), condition=%wide.region_5.6_spmd.clone, body=%wide.region_2.5_spmd.clone.sunk | while | flops 713895296 | bytes 48929828 | solution.py:153
  176.6 2.8 fusion.125
  179.4 2.5 exponential_reduce_fusion.2
  182.0 3.0 fusion.126
  187.5 2.8 fusion.125
  190.3 2.6 exponential_reduce_fusion.2
  192.8 3.0 fusion.126
  197.3 8.8 all-gather.19.cloned.1.call-done
  206.0 3.3 fusion.58
  209.4 5.9 copy.69
  219.4 114.6 %all-reduce.10.cloned.1.call-done = f32[2,578,1024]{2,0,1:T(2,128)} async-done(((f32[2,578,1024]{2,0,1:T(2,128)}), f32[2,578,1024]{2,0,1:T(2,128)}) %all-reduce.10.cloned.1.call-update) | async-done | bytes 4734992
  334.0 7.1 convert_reduce_fusion.5
  343.2 2.7 add_convert_fusion.3
  347.4 39.9 %all-gather.23.cloned.1.call-done = bf16[1024,2048]{1,0:T(8,128)(2,1)} async-done(((bf16[64,2048]{1,0:T(8,128)(2,1)}), bf16[1024,2048]{1,0:T(8,128)(2,1)}) %all-gather.23.cloned.1.call-update) | async-done | bytes 4194320 | tf_op jit(solution)/shard_map/all_gather | solution.py:135
  387.3 36.3 %all-gather.21.cloned.1.call-done = bf16[2,578,1024]{2,0,1:T(2,128)(2,1)} async-done(((bf16[2,289,1024]{2,0,1:T(2,128)(2,1)}), bf16[2,578,1024]{2,0,1:T(2,128)(2,1)}) %all-gather.21.cloned.1.call-update) | async-done | bytes 2367504 | tf_op jit(solution)/shard_map/all_gather | solution.py:166
  423.6 12.4 multiply_convert_fusion.2
  435.9 40.6 %all-gather.25.cloned.1.call-done = bf16[2048,1024]{0,1:T(8,128)(2,1)} async-done(((bf16[2048,64]{0,1:T(8,128)(2,1)}), bf16[2048,1024]{0,1:T(8,128)(2,1)}) %all-gather.25.cloned.1.call-update) | async-done | bytes 4194320 | tf_op jit(solution)/shard_map/all_gather | solution.py:137
  476.6 36.7 %all-gather.27.cloned.1.call-done = bf16[2,578,1024]{2,0,1:T(2,128)(2,1)} async-done(((bf16[2,289,1024]{2,0,1:T(2,128)(2,1)}), bf16[2,578,1024]{2,0,1:T(2,128)(2,1)}) %all-gather.27.cloned.1.call-update) | async-done | bytes 2367504 | tf_op jit(solution)/shard_map/all_gather | solution.py:180
  513.3 12.9 convert_reduce_fusion
  526.2 5.2 fusion.24
  531.4 5.9 copy.73
  537.4 119.6 %all-reduce.12.cloned.1.call-done = f32[2,578,1024]{2,0,1:T(2,128)} async-done(((f32[2,578,1024]{2,0,1:T(2,128)}), f32[2,578,1024]{2,0,1:T(2,128)}) %all-reduce.12.cloned.1.call-update) | async-done | bytes 4734992
  657.0 9.9 multiply_reduce_fusion.1
  667.0 8.2 convert_reduce_fusion.6
  675.3 10.4 bitcast_convert_fusion
  687.4 10.2 bitcast_convert_fusion.1
  697.7 14.2 %all-gather.29.cloned.1.call-done = bf16[2,578,1024]{2,0,1:T(2,128)(2,1)} async-done(((bf16[2,289,1024]{2,0,1:T(2,128)(2,1)}), bf16[2,578,1024]{2,0,1:T(2,128)(2,1)}) %all-gather.29.cloned.1.call-update) | async-done | bytes 2367504 | tf_op jit(solution)/shard_map/all_gather | solution.py:199
  711.9 4.3 bitcast_convert_fusion.2
  716.3 4.1 fusion.54
  723.9 54.5 %while.29 = (s32[]{:T(128)}, bf16[2,578,512]{1,2,0:T(8,128)(2,1)}, bf16[2,578,512]{1,2,0:T(8,128)(2,1)}, bf16[2,578,512]{1,2,0:T(8,128)(2,1)}, bf16[2,578,512]{1...) while((s32[]{:T(128)}, bf16[2,578,512]{1,2,0:T(8,128)(2,1)}, ...), condition=%wide.region_15.16_spmd.clone, body=%wide.region_13.15_spmd.clone.sunk | while | flops 1752075776 | bytes 129226720 | solution.py:202
  729.3 2.8 fusion.139
  732.1 6.6 multiply_reduce_fusion.6
  738.8 6.6 multiply_convert_fusion.5
  754.3 2.1 fusion.137
  756.4 2.8 fusion.139
  759.2 6.6 multiply_reduce_fusion.6
  765.8 6.7 multiply_convert_fusion.5
  778.4 4.8 bitcast_convert_fusion.4
  783.3 4.3 bitcast_convert_fusion.3
  787.7 4.7 bitcast_convert_fusion.5
  792.5 8.7 fusion.49
  801.1 3.9 copy.71
  810.3 3.8 copy.82
  819.5 44.7 %reduce-scatter.15.cloned.1.call-done = bf16[64,2048]{1,0:T(8,128)(2,1)} async-done(((bf16[1024,2048]{1,0:T(8,128)(2,1)}), bf16[64,2048]{1,0:T(8,128)(2,1)}) %reduce-scatter.15.cloned.1.call-update) | async-done | bytes 262160 | tf_op jit(solution)/shard_map/reduce_scatter | solution.py:233
  867.2 2.2 convert_reduce_fusion.4
  871.4 52.8 %reduce-scatter.13.cloned.1.call-done = bf16[512,64]{0,1:T(8,128)(2,1)} async-done(((bf16[512,1024]{0,1:T(8,128)(2,1)}), bf16[512,64]{0,1:T(8,128)(2,1)}) %reduce-scatter.13.cloned.1.call-update) | async-done | bytes 65552 | tf_op jit(solution)/shard_map/reduce_scatter | solution.py:236
  925.7 58.9 %reduce-scatter.9.cloned.1.call-done = bf16[64,512]{1,0:T(8,128)(2,1)} async-done(((bf16[1024,512]{1,0:T(8,128)(2,1)}), bf16[64,512]{1,0:T(8,128)(2,1)}) %reduce-scatter.9.cloned.1.call-update) | async-done | bytes 65552 | tf_op jit(solution)/shard_map/reduce_scatter | solution.py:227
  986.1 58.4 %reduce-scatter.11.cloned.1.call-done = bf16[64,512]{1,0:T(8,128)(2,1)} async-done(((bf16[1024,512]{1,0:T(8,128)(2,1)}), bf16[64,512]{1,0:T(8,128)(2,1)}) %reduce-scatter.11.cloned.1.call-update) | async-done | bytes 65552 | tf_op jit(solution)/shard_map/reduce_scatter | solution.py:230
  1045.9 59.5 %reduce-scatter.7.cloned.1.call-done = bf16[64,512]{1,0:T(8,128)(2,1)} async-done(((bf16[1024,512]{1,0:T(8,128)(2,1)}), bf16[64,512]{1,0:T(8,128)(2,1)}) %reduce-scatter.7.cloned.1.call-update) | async-done | bytes 65552 | tf_op jit(solution)/shard_map/reduce_scatter | solution.py:224
  1106.9 120.0 %all-reduce.14.cloned.1.call-done = (bf16[2,578,1024]{2,0,1:T(2,128)(2,1)}, bf16[2,578,1024]{2,0,1:T(2,128)(2,1)}) async-done(((bf16[2,578,1024]{2,0,1:T(2,128)(2,1)}, bf16[2,578,1024]{2,0,1:T(2,128)(2,1)}), (bf16[2,578,1024]{2,0,1:T(2,128)(2,1)}, bf16[2,578,1024]{2,0,1:T(2,128)(2,1)})) %all-reduce.14.cloned.1.call-update) | async-done | bytes 4734992
  1226.9 9.8 fusion.39
  1236.8 3.9 multiply_convert_fusion.3
  1240.8 4.4 fusion.36
  1245.3 41.0 %all-reduce.4 = (f32[1024]{0:T(1024)}, f32[1024]{0:T(1024)}, f32[1024]{0:T(1024)}, f32[1024]{0:T(1024)}, f32[1024]{0:T(1024)}, /*index=5*/f32[1024]{0:T(1024)}, f32[1024]{0:T(1024)}, f32[4096]{0:T(1024)}, f32[1024]{0:T(1024)}) all-reduce(f32[1024]{0:T(1024)S(1)} %copy-done.44, ...), channel_id=1, replica_groups=mesh['dp'=16,'tensor'=2] {'dp','tensor'}, use_global_device_ids=true, to_apply=%region_20.21 | all-reduce | flops 12288 | bytes 98304 | tf_op jit(solution)/shard_map/psum | solution.py:243
  (263 shorter events, 69.2 us)
Async XLA Ops:
  7.2 4.5 copy-start.6
  7.2 43.7 %all-gather.15.cloned.1.call-start = ((), (), s32[]{:S(2)}) async-start(), calls=%async_computation.8 | async-start | bytes 1114112 | tf_op jit(solution)/shard_map/all_gather | solution.py:132
  7.9 80.2 %all-gather.11.cloned.1.call-start = ((), (), s32[]{:S(2)}) async-start(), calls=%async_computation.6 | async-start | bytes 3551232 | tf_op jit(solution)/shard_map/all_gather | solution.py:149
  8.7 4.7 copy-start.38
  13.4 5.6 copy-start.57
  13.4 5.7 copy-start.58
  17.0 111.2 %all-gather.13.cloned.1.call-start = ((), (), s32[]{:S(2)}) async-start(), calls=%async_computation.7 | async-start | bytes 1114112 | tf_op jit(solution)/shard_map/all_gather | solution.py:134
  17.7 149.4 %all-gather.17.cloned.1.call-start = ((), (), s32[]{:S(2)}) async-start(), calls=%async_computation.9 | async-start | bytes 1114112 | tf_op jit(solution)/shard_map/all_gather | solution.py:133
  18.3 187.7 %all-gather.19.cloned.1.call-start = ((), (), s32[]{:S(2)}) async-start(), calls=%async_computation.10 | async-start | bytes 1114112 | tf_op jit(solution)/shard_map/all_gather | solution.py:136
  18.9 315.1 %all-reduce.10.cloned.1.call-start = ((), (), s32[]{:S(2)}) async-start(), calls=%async_computation.22 | async-start | bytes 9469952
  182.0 3.0 copy-start.19
  192.8 3.0 copy-start.19
  197.3 12.1 copy-start.2
  197.3 12.1 copy-start.4
  197.3 12.1 copy-start.36
  215.3 2.1 copy-start.62
  215.3 118.7 %copy-start.7 = (bf16[2,289,1024]{2,0,1:T(2,128)(2,1)S(1)}, bf16[2,289,1024]{2,0,1:T(2,128)(2,1)}, u32[]{:S(2)}) copy-start(bf16[2,289,1024]{2,0,1:T(2,128)(2,1)} %param.22) | copy-start | bytes 3551236
  215.3 172.0 %all-gather.23.cloned.1.call-start = ((), (), s32[]{:S(2)}) async-start(), calls=%async_computation.12 | async-start | bytes 4456448 | tf_op jit(solution)/shard_map/all_gather | solution.py:135
  216.1 207.5 %all-gather.21.cloned.1.call-start = ((), (), s32[]{:S(2)}) async-start(), calls=%async_computation.11 | async-start | bytes 3551232 | tf_op jit(solution)/shard_map/all_gather | solution.py:166
  341.1 325.9 %copy-start = (f32[2,289,1024]{2,0,1:T(2,128)}, f32[2,289,1024]{2,0,1:T(2,128)S(1)}, u32[]{:S(2)}) copy-start(f32[2,289,1024]{2,0,1:T(2,128)S(1)} %get-tuple-element.262) | copy-start | bytes 7102468
  341.1 2.1 copy-start.47
  343.2 4.1 copy-start.52
  346.0 130.6 %all-gather.25.cloned.1.call-start = ((), (), s32[]{:S(2)}) async-start(), calls=%async_computation.13 | async-start | bytes 4456448 | tf_op jit(solution)/shard_map/all_gather | solution.py:137
  346.7 166.6 %all-gather.27.cloned.1.call-start = ((), (), s32[]{:S(2)}) async-start(), calls=%async_computation.14 | async-start | bytes 3551232 | tf_op jit(solution)/shard_map/all_gather | solution.py:180
  347.3 309.7 %all-reduce.12.cloned.1.call-start = ((), (), s32[]{:S(2)}) async-start(), calls=%async_computation.23 | async-start | bytes 9469952
  513.3 12.9 copy-start.59
  526.2 5.2 copy-start.63
  537.3 129.7 %copy-start.23 = (bf16[2,289,1024]{2,0,1:T(2,128)(2,1)S(1)}, bf16[2,289,1024]{2,0,1:T(2,128)(2,1)}, u32[]{:S(2)}) copy-start(bf16[2,289,1024]{2,0,1:T(2,128)(2,1)} %param.23) | copy-start | bytes 3551236
  537.3 174.6 %all-gather.29.cloned.1.call-start = ((), (), s32[]{:S(2)}) async-start(), calls=%async_computation.15 | async-start | bytes 3551232 | tf_op jit(solution)/shard_map/all_gather | solution.py:199
  657.0 10.0 copy-start.22
  675.3 142.4 %reduce-scatter.17.cloned.1.call-start = ((), (), s32[]{:S(2)}) async-start(), calls=%async_computation.21 | async-start | bytes 4456448 | tf_op jit(solution)/shard_map/reduce_scatter | solution.py:239
  685.8 178.5 %reduce-scatter.15.cloned.1.call-start = ((), (), s32[]{:S(2)}) async-start(), calls=%async_computation.20 | async-start | bytes 4456448 | tf_op jit(solution)/shard_map/reduce_scatter | solution.py:233
  697.6 14.3 %copy-start.21 = (bf16[2,578,512]{1,2,0:T(8,128)(2,1)S(1)}, bf16[2,578,512]{1,2,0:T(8,128)(2,1)}, u32[]{:S(2)}) copy-start(bf16[2,578,512]{1,2,0:T(8,128)(2,1)} %get-tuple-element.109) | copy-start | bytes 3551236
  697.6 18.7 %copy-start.35 = (bf16[512,1024]{0,1:T(8,128)(2,1)S(1)}, bf16[512,1024]{0,1:T(8,128)(2,1)}, u32[]{:S(2)}) copy-start(bf16[512,1024]{0,1:T(8,128)(2,1)} %all-gather.19.cloned.1.call-done) | copy-start | bytes 3145732
  697.6 226.6 %reduce-scatter.13.cloned.1.call-start = ((), (), s32[]{:S(2)}) async-start(), calls=%async_computation.19 | async-start | bytes 1114112 | tf_op jit(solution)/shard_map/reduce_scatter | solution.py:236
  716.2 268.3 %reduce-scatter.9.cloned.1.call-start = ((), (), s32[]{:S(2)}) async-start(), calls=%async_computation.17 | async-start | bytes 1114112 | tf_op jit(solution)/shard_map/reduce_scatter | solution.py:227
  720.4 3.5 copy-start.3
  720.4 3.5 copy-start.37
  747.3 2.1 copy-start.16
  774.4 2.1 copy-start.16
  778.4 4.9 copy-start.11
  783.2 261.2 %reduce-scatter.11.cloned.1.call-start = ((), (), s32[]{:S(2)}) async-start(), calls=%async_computation.18 | async-start | bytes 1114112 | tf_op jit(solution)/shard_map/reduce_scatter | solution.py:230
  787.7 317.7 %reduce-scatter.7.cloned.1.call-start = ((), (), s32[]{:S(2)}) async-start(), calls=%async_computation.16 | async-start | bytes 1114112 | tf_op jit(solution)/shard_map/reduce_scatter | solution.py:224
  792.4 434.5 %all-reduce.14.cloned.1.call-start = ((), (), s32[]{:S(2)}) async-start(), calls=%async_computation.24 | async-start | bytes 9469952
  801.1 3.9 copy-start.14
  801.1 3.9 copy-start.32
  814.1 1.9 copy-start.51
  817.6 409.2 %copy-start.8 = (bf16[2,289,1024]{2,0,1:T(2,128)(2,1)S(1)}, bf16[2,289,1024]{2,0,1:T(2,128)(2,1)}, u32[]{:S(2)}) copy-start(bf16[2,289,1024]{2,0,1:T(2,128)(2,1)} %param.22) | copy-start | bytes 3551236
  817.7 409.3 %copy-start.39 = (f32[1024]{0:T(1024)S(1)}, f32[1024]{0:T(1024)}, u32[]{:S(2)}) copy-start(f32[1024]{0:T(1024)} %copy-done.38) | copy-start | bytes 12292
  869.3 367.4 %copy-start.1 = (f32[2,289,1024]{2,0,1:T(2,128)S(1)}, f32[2,289,1024]{2,0,1:T(2,128)}, u32[]{:S(2)}) copy-start(f32[2,289,1024]{2,0,1:T(2,128)} %copy-done) | copy-start | bytes 7102468
  1226.9 9.9 copy-start.29
  1226.9 9.9 copy-start.46
  1236.7 4.0 copy-start.31
  1236.8 3.9 copy-start.15
  1236.8 3.9 copy-start.25
  1236.8 3.9 copy-start.28
  1240.7 4.5 copy-start.40
  1240.7 4.5 copy-start.41
  1240.8 4.5 copy-start.42
  1240.8 4.5 copy-start.43
  1240.8 4.5 copy-start.44
  1240.8 4.5 copy-start.45
  1240.8 4.5 copy-start.48
  1240.8 4.5 copy-start.50
  (28 other events, 35.9 us)
Sparse Core Ops, SparseCore 0:
  10.2 40.6 all-gather.14
  53.0 35.0 all-gather.10
  90.3 37.9 all-gather.12
  130.3 36.8 all-gather.16
  169.2 36.8 all-gather.18
  215.4 118.4 all-reduce.9
  336.3 50.8 all-gather.22
  388.9 34.6 all-gather.20
  426.0 50.5 all-gather.24
  478.6 34.6 all-gather.26
  537.4 119.5 all-reduce.11
  675.4 36.4 all-gather.28
  715.7 72.6 reduce-scatter.16
  792.7 71.5 reduce-scatter.14
  867.7 56.3 reduce-scatter.12
  928.1 56.4 reduce-scatter.8
  988.0 56.3 reduce-scatter.10
  1048.9 56.4 reduce-scatter.6
  1107.9 118.9 all-reduce.13
where the time goes:
time: 1300 us; the launch traced here: 1290 us
  waiting for transfers between devices  947 us (73%)
  matrix products  143 us (11%)
  other arithmetic  89 us (7%)
  local copies, waits for them, and re-layouts  55.3 us (4%)
  blocking collectives  41 us (3%)
  between operations  15.8 us (1%)
    unnamed x22, waiting for transfers between devices  359 us
    reduce_scatter x1, waiting for transfers between devices, local(): lax.psum_scatter(query_grad.astype(jnp.bfloat16), 'dp', scatter_dimension...  59.5 us
    reduce_scatter x1, waiting for transfers between devices, local(): lax.psum_scatter(key_grad.astype(jnp.bfloat16), 'dp', scatter_dimension=0...  58.9 us
    reduce_scatter x1, waiting for transfers between devices, local(): lax.psum_scatter(value_grad.astype(jnp.bfloat16), 'dp', scatter_dimension...  58.4 us
    reduce_scatter x1, waiting for transfers between devices, local(): lax.psum_scatter(output_grad.astype(jnp.bfloat16), 'dp', scatter_dimensio...  52.8 us
    reduce_scatter x1, waiting for transfers between devices, local(): lax.psum_scatter(upper_grad.astype(jnp.bfloat16), 'dp', scatter_dimension...  44.7 us
    psum x1, blocking collectives, local(): lax.psum((gain_one_grad, shift_one_grad, query_bias_grad, value_bias_grad...  41 us
    all_gather x1, waiting for transfers between devices, local(): lax.all_gather(down_weight, 'dp', axis=1, tiled=True)  40.6 us
  transfers between devices with their start and end apart: 19, of which 18 were waited for; matrix products, arithmetic and copies ran while one was open for 16% of the time, Pallas kernels for 0%

commit v1 on v0

--- a/solution.py
+++ b/solution.py
@@ -1,6 +1,8 @@
 import jax
 import jax.numpy as jnp
 from jax import lax
+from jax.experimental import pallas as pl
+from jax.experimental.pallas import tpu as pltpu
 from jax.sharding import PartitionSpec as P
 
 HDIM = 64
@@ -286,6 +288,487 @@
     )
 
 
+BOTH = ("dp", "tensor")
+HALF_PAD = 8
+LANES = 128
+
+
+def exchange(value, far_z=0, far_x=0, far_core=0, far_y=0):
+    pairs = []
+    for place in range(32):
+        other = place ^ (far_z * 8 + far_x * 4 + far_core * 2 + far_y)
+        pairs.append((place, other))
+    return lax.ppermute(value, BOTH, pairs)
+
+
+def pick_two(bit, own, other, axis):
+    first = jnp.where(bit == 0, own, other)
+    last = jnp.where(bit == 0, other, own)
+    return jnp.stack([first, last], axis)
+
+
+def after(value, *others):
+    return lax.optimization_barrier((value, *others))[0]
+
+
+def gather_start(shard, core):
+    keep = jnp.where(core == 0, shard[0], shard[1])
+    send = jnp.where(core == 0, shard[1], shard[0])
+    return pick_two(core, keep, exchange(send, far_core=1), 1)
+
+
+def gather_z(piece, place_z):
+    found = [piece] + [exchange(piece, far_z=step) for step in (1, 2, 3)]
+    ordered = [lax.select_n(place_z ^ spot, *found) for spot in range(4)]
+    return jnp.stack(ordered, 1)
+
+
+def gather_plane_one(ordered):
+    return exchange(ordered[0], far_x=1), exchange(ordered[1], far_y=1)
+
+
+def gather_plane_two(ordered, crossed, place_x):
+    one = pick_two(place_x, ordered[0], crossed[0], 1)
+    two = jnp.stack([ordered[1], crossed[1]])
+    return one, two, exchange(one, far_y=1), exchange(two, far_x=1)
+
+
+def gather_finish(parts, place_x):
+    one, two, one_far, two_far = parts
+    wide = one.shape[-1]
+    two_all = pick_two(place_x, two, two_far, 2)
+    pieces = [one, one_far, two_all[0], two_all[1]]
+    return jnp.concatenate([piece.reshape(-1, wide) for piece in pieces], 1)
+
+
+def scatter_sum(pieces, place_x, place_z, core):
+    rows, wide = pieces[0].shape
+    pieces = [piece.reshape(4, 2, 2, rows // 16, wide) for piece in pieces]
+
+    def low_sum(left, right):
+        return (left.astype(jnp.float32) + right.astype(jnp.float32)).astype(jnp.bfloat16)
+
+    def split_x(value, axis):
+        keep = lax.dynamic_index_in_dim(value, place_x, axis, keepdims=False)
+        send = lax.dynamic_index_in_dim(value, 1 - place_x, axis, keepdims=False)
+        return keep, send
+
+    two_keep, two_send = split_x(jnp.stack(pieces[2:]), 2)
+    one_far = exchange(pieces[1], far_y=1)
+    two_far = exchange(two_send, far_x=1)
+    one_keep, one_send = split_x(low_sum(pieces[0], one_far), 1)
+    two = low_sum(two_keep, two_far)
+    one_far = exchange(one_send, far_x=1)
+    two_far = exchange(two[1], far_y=1)
+    both = jnp.stack([low_sum(one_keep, one_far), low_sum(two[0], two_far)], 1)
+    total = lax.dynamic_index_in_dim(both, place_z, 0, keepdims=False).astype(jnp.float32)
+    for step in (1, 2, 3):
+        piece = lax.dynamic_index_in_dim(both, place_z ^ step, 0, keepdims=False)
+        total = total + exchange(piece, far_z=step).astype(jnp.float32)
+    total = total.astype(jnp.bfloat16)
+    keep = lax.dynamic_index_in_dim(total, core, 1, keepdims=False)
+    send = lax.dynamic_index_in_dim(total, 1 - core, 1, keepdims=False)
+    owned = pick_two(core, keep, exchange(send, far_core=1), 0)
+    return owned.astype(jnp.float32).transpose(2, 0, 1, 3)
+
+
+def lane_of(shape):
+    return lax.broadcasted_iota(jnp.int32, shape, 1)
+
+
+def dot_lanes(left, right):
+    return lax.dot_general(
+        left, right, (((1,), (1,)), ((), ())), preferred_element_type=jnp.float32
+    )
+
+
+def head_views(query, key, bias, head):
+    lane = lane_of(query.shape)
+    mine = (lane >= HDIM) if head else (lane < HDIM)
+    spot = 0 if head else HDIM
+    zero = jnp.zeros_like(query)
+    query_view = jnp.where(mine, query, jnp.where(lane == spot, zero + 1, zero))
+    key_view = jnp.where(lane == spot, bias, key)
+    return mine, query_view, key_view
+
+
+def attend_kernel(qkv_ref, bias_ref, mixed_ref, total_ref):
+    query = qkv_ref[:, 0:LANES] * jnp.bfloat16(HDIM ** (-0.5))
+    key = qkv_ref[:, LANES : 2 * LANES]
+    value = qkv_ref[:, 2 * LANES : 3 * LANES]
+    bias = bias_ref[...]
+    sums, tops = [], []
+    for head in range(2):
+        mine, query_view, key_view = head_views(query, key, bias, head)
+        scores = dot_lanes(query_view, key_view)
+        top = jnp.max(scores, axis=1, keepdims=True)
+        weight = jnp.exp(scores - top).astype(jnp.bfloat16)
+        value_view = jnp.where(mine, value, jnp.ones_like(value))
+        sums.append(jnp.dot(weight, value_view, preferred_element_type=jnp.float32))
+        tops.append(top)
+    low = lane_of(sums[0].shape) < HDIM
+    upper = jnp.where(low, sums[0], sums[1])
+    lower = jnp.where(low, sums[1], sums[0])
+    lower = pltpu.roll(lower, HDIM, 1)
+    mixed_ref[...] = (upper / lower).astype(jnp.bfloat16)
+    total = jnp.where(low, tops[0], tops[1]) + jnp.log(lower)
+    total = jnp.transpose(total)
+    total_ref[0, 0:1, :] = total[0:1]
+    total_ref[0, 1:2, :] = total[HDIM : HDIM + 1]
+
+
+def attend_back_kernel(qkv_ref, bias_ref, grad_ref, mixed_ref, total_ref, out_ref):
+    scale = HDIM ** (-0.5)
+    query = qkv_ref[:, 0:LANES] * jnp.bfloat16(scale)
+    key = qkv_ref[:, LANES : 2 * LANES]
+    value = qkv_ref[:, 2 * LANES : 3 * LANES]
+    bias = bias_ref[...]
+    grad = grad_ref[...]
+    product = grad.astype(jnp.float32) * mixed_ref[...].astype(jnp.float32)
+    grad_query = grad_key = grad_value = None
+    for head in range(2):
+        mine, query_view, key_view = head_views(query, key, bias, head)
+        zero = jnp.zeros_like(query)
+        scores = dot_lanes(key_view, query_view)
+        probs = jnp.exp(scores - total_ref[0, head : head + 1, :])
+        grad_view = jnp.where(mine, grad, zero)
+        grad_probs = dot_lanes(value, grad_view)
+        ones = jnp.where(mine[0:8], 1.0, 0.0)
+        inner = lax.dot_general(
+            ones,
+            product,
+            (((1,), (1,)), ((), ())),
+            precision=lax.Precision.HIGHEST,
+            preferred_element_type=jnp.float32,
+        )
+        grad_scores = (probs * (grad_probs - inner[0:1])).astype(jnp.bfloat16)
+        one_value = jnp.dot(
+            probs.astype(jnp.bfloat16), grad_view, preferred_element_type=jnp.float32
+        )
+        one_key = jnp.dot(
+            grad_scores, jnp.where(mine, query, zero), preferred_element_type=jnp.float32
+        )
+        one_query = lax.dot_general(
+            grad_scores,
+            jnp.where(mine, key, zero),
+            (((0,), (0,)), ((), ())),
+            preferred_element_type=jnp.float32,
+        )
+        grad_query = one_query if head == 0 else grad_query + one_query
+        grad_key = one_key if head == 0 else grad_key + one_key
+        grad_value = one_value if head == 0 else grad_value + one_value
+    out_ref[:, 0:LANES] = (grad_query * scale).astype(jnp.bfloat16)
+    out_ref[:, LANES : 2 * LANES] = grad_key.astype(jnp.bfloat16)
+    out_ref[:, 2 * LANES : 3 * LANES] = grad_value.astype(jnp.bfloat16)
+
+
+def attend_all(qkv, bias, rows):
+    images = qkv.shape[0] // rows
+    blocks = qkv.shape[1] // (3 * LANES)
+    return pl.pallas_call(
+        attend_kernel,
+        grid=(images, blocks),
+        in_specs=[
+            pl.BlockSpec((rows, 3 * LANES), lambda i, j: (i, j)),
+            pl.BlockSpec((rows, LANES), lambda i, j: (0, 0)),
+        ],
+        out_specs=[
+            pl.BlockSpec((rows, LANES), lambda i, j: (i, j)),
+            pl.BlockSpec((1, 8, rows), lambda i, j: (i * blocks + j, 0, 0)),
+        ],
+        out_shape=[
+            jax.ShapeDtypeStruct((images * rows, blocks * LANES), jnp.bfloat16),
+            jax.ShapeDtypeStruct((images * blocks, 8, rows), jnp.float32),
+        ],
+        compiler_params=pltpu.CompilerParams(vmem_limit_bytes=32 * 2**20),
+        cost_estimate=pl.CostEstimate(
+            flops=images * blocks * 2 * 2 * 2 * rows * rows * LANES * 2,
+            transcendentals=images * blocks * 2 * rows * rows,
+            bytes_accessed=images * rows * blocks * LANES * 8,
+        ),
+    )(qkv, bias)
+
+
+def attend_back_all(qkv, bias, grad, mixed, total, rows):
+    images = qkv.shape[0] // rows
+    blocks = qkv.shape[1] // (3 * LANES)
+    return pl.pallas_call(
+        attend_back_kernel,
+        grid=(images, blocks),
+        in_specs=[
+            pl.BlockSpec((rows, 3 * LANES), lambda i, j: (i, j)),
+            pl.BlockSpec((rows, LANES), lambda i, j: (0, 0)),
+            pl.BlockSpec((rows, LANES), lambda i, j: (i, j)),
+            pl.BlockSpec((rows, LANES), lambda i, j: (i, j)),
+            pl.BlockSpec((1, 8, rows), lambda i, j: (i * blocks + j, 0, 0)),
+        ],
+        out_specs=pl.BlockSpec((rows, 3 * LANES), lambda i, j: (i, j)),
+        out_shape=jax.ShapeDtypeStruct(qkv.shape, jnp.bfloat16),
+        compiler_params=pltpu.CompilerParams(vmem_limit_bytes=48 * 2**20),
+        cost_estimate=pl.CostEstimate(
+            flops=images * blocks * 2 * 5 * 2 * rows * rows * LANES * 2,
+            transcendentals=images * blocks * 2 * rows * rows,
+            bytes_accessed=images * rows * blocks * LANES * 16,
+        ),
+    )(qkv, bias, grad, mixed, total)
+
+
+def mat(left, right):
+    return jnp.dot(left, right, preferred_element_type=jnp.float32)
+
+
+def mat_far(left, right):
+    return lax.dot_general(
+        left, right, (((1,), (1,)), ((), ())), preferred_element_type=jnp.float32
+    )
+
+
+def mat_rows(left, right):
+    return lax.dot_general(
+        left, right, (((0,), (0,)), ((), ())), preferred_element_type=jnp.float32
+    )
+
+
+def flat_norm(values, gain, shift):
+    center = values - jnp.mean(values, axis=-1, keepdims=True)
+    spread = lax.rsqrt(jnp.mean(center * center, axis=-1, keepdims=True) + EPS)
+    unit = center * spread
+    return unit * gain + shift, unit, spread
+
+
+def flat_norm_back(upstream, unit, spread, gain):
+    scaled = upstream * gain
+    inner = (
+        scaled
+        - jnp.mean(scaled, axis=-1, keepdims=True)
+        - unit * jnp.mean(scaled * unit, axis=-1, keepdims=True)
+    )
+    return spread * inner, jnp.sum(upstream * unit, axis=0), jnp.sum(upstream, axis=0)
+
+
+def whole_images(
+    images,
+    cotangent,
+    slot_live,
+    first_gain,
+    first_shift,
+    query_weight,
+    query_bias,
+    key_weight,
+    value_weight,
+    value_bias,
+    output_weight,
+    output_bias,
+    second_gain,
+    second_shift,
+    up_weight,
+    up_bias,
+    down_weight,
+    down_bias,
+):
+    low = jnp.bfloat16
+    dp_place = lax.axis_index("dp")
+    place_y = lax.axis_index("tensor")
+    core, place_x, place_z = dp_place % 2, (dp_place // 2) % 2, dp_place // 4
+    strip, width = images.shape[1:]
+    half = -(-strip // HALF_PAD) * HALF_PAD
+    rows = 2 * half
+    depth, head_cols = query_weight.shape
+    units = up_weight.shape[1]
+    head_part, unit_part = head_cols // 4, units // 4
+
+    stacked = jnp.stack([images, cotangent])
+    stacked = jnp.pad(stacked, ((0, 0), (0, 0), (0, half - strip), (0, 0)))
+    mine = lax.dynamic_index_in_dim(stacked, place_y, 1, keepdims=False)
+    theirs = lax.dynamic_index_in_dim(stacked, 1 - place_y, 1, keepdims=False)
+    arrived = exchange(theirs, far_y=1)
+    whole = jnp.stack([mine, arrived], 1).reshape(2, rows, width)
+
+    def four(weight):
+        return weight.reshape(depth, 2, 2, -1)
+
+    def by_core(parts):
+        return jnp.concatenate(parts, 3).transpose(1, 2, 0, 3)
+
+    shard_one = by_core([four(query_weight), four(key_weight), four(value_weight)])
+    shard_two = by_core([four(output_weight.T), four(up_weight)])
+    shard_three = by_core([four(down_weight.T)])
+
+    start_one = gather_start(shard_one, core)
+    line_one = gather_z(start_one, place_z)
+    cross_one = gather_plane_one(line_one)
+    parts_one = gather_plane_two(line_one, cross_one, place_x)
+    qkv_full = gather_finish(parts_one, place_x)
+
+    start_two = after(gather_start(shard_two, core), line_one)
+    line_two = gather_z(start_two, place_z)
+    cross_two = gather_plane_one(after(line_two, *parts_one))
+    parts_two = gather_plane_two(line_two, cross_two, place_x)
+    pair_full = gather_finish(parts_two, place_x)
+    pair_full = pair_full.reshape(width, 4, head_part + unit_part)
+    output_full = pair_full[:, :, :head_part].reshape(width, 4 * head_part)
+    upper_full = pair_full[:, :, head_part:].reshape(width, 4 * unit_part)
+
+    start_three = after(gather_start(shard_three, core), line_two)
+    line_three = gather_z(start_three, place_z)
+    cross_three = gather_plane_one(after(line_three, *parts_two))
+    parts_three = gather_plane_two(line_three, cross_three, place_x)
+    lower_full = gather_finish(parts_three, place_x)
+
+    def local_columns(vector):
+        wide = vector.shape[0] // 8
+        table = vector.astype(jnp.float32).reshape(2, 2, 2, wide)
+        table = lax.dynamic_index_in_dim(table, core, 1, keepdims=False)
+        table = jnp.where(place_y == 0, table, table[::-1])
+        return table.transpose(1, 0, 2)
+
+    def spread_columns(vector):
+        wide = vector.shape[0] // 4
+        table = vector.reshape(2, 2, wide).transpose(1, 0, 2)
+        table = jnp.where(place_y == 0, table, table[::-1])
+        table = jnp.stack(
+            [jnp.where(core == 0, table, 0.0), jnp.where(core == 1, table, 0.0)], 1
+        )
+        return table.reshape(-1)
+
+    gain_one, shift_one = first_gain.astype(jnp.float32), first_shift.astype(jnp.float32)
+    gain_two, shift_two = second_gain.astype(jnp.float32), second_shift.astype(jnp.float32)
+    query_shift = local_columns(query_bias).reshape(4, 1, head_part)
+    value_shift = local_columns(value_bias).reshape(4, 1, head_part)
+    qkv_shift = jnp.concatenate(
+        [query_shift, jnp.zeros_like(query_shift), value_shift], 1
+    ).reshape(-1)
+    up_shift = local_columns(up_bias).reshape(-1)
+
+    row = jnp.arange(rows)
+    in_half = row % half
+    spot = jnp.where(row < half, place_y, 1 - place_y) * strip + in_half
+    ok = (in_half < strip) & (spot < VALID)
+    live = lax.dynamic_index_in_dim(slot_live, place_y, 0, keepdims=False).astype(jnp.float32)
+    row_mask = (live * ok.astype(jnp.float32))[:, None]
+    key_bias = jnp.broadcast_to(
+        jnp.where(ok, 0.0, NEGATIVE).astype(low)[:, None], (rows, LANES)
+    )
+
+    def pair_up(own):
+        return jnp.concatenate([own, exchange(own, far_core=1)], 0)
+
+    def pair_sum(partial):
+        other = exchange(partial[rows:].astype(low), far_core=1)
+        return partial[:rows] + other.astype(jnp.float32)
+
+    resid = whole[0].astype(jnp.float32)
+    grad_top = row_mask * whole[1].astype(jnp.float32)
+    fed_grad = grad_top.astype(low)
+    fed_rows = pair_up(fed_grad)
+    normed, unit_one, spread_one = flat_norm(resid, gain_one, shift_one)
+    normed_rows = pair_up(normed.astype(low))
+    qkv = (mat(normed_rows, qkv_full) + qkv_shift).astype(low)
+    mixed, totals = attend_all(qkv, key_bias, rows)
+    attended = pair_sum(mat_far(mixed, output_full)) + output_bias.astype(jnp.float32)
+    middle = row_mask * (resid + attended)
+    second, unit_two, spread_two = flat_norm(middle, gain_two, shift_two)
+    second_rows = pair_up(second.astype(low))
+    hidden = mat(second_rows, upper_full) + up_shift
+    sigma = jax.nn.sigmoid(SLOPE * hidden)
+    active = (hidden * sigma).astype(low)
+    slope = (sigma + SLOPE * hidden * sigma * (1.0 - sigma)).astype(low)
+
+    def weight_pieces(left, right):
+        wide = right.shape[1] // 4
+        return [
+            mat_rows(left, right[:, at * wide : (at + 1) * wide]).astype(low) for at in range(4)
+        ]
+
+    lower_owned = scatter_sum(weight_pieces(fed_rows, active), place_x, place_z, core)
+    hidden_grad = (mat(fed_rows, lower_full) * slope.astype(jnp.float32)).astype(low)
+    upper_owned = scatter_sum(weight_pieces(second_rows, hidden_grad), place_x, place_z, core)
+    second_grad = pair_sum(mat_far(hidden_grad, upper_full))
+    fed = pair_sum(mat_far(active, lower_full)) + down_bias.astype(jnp.float32)
+    layer_own = (row_mask * (middle + fed)).astype(low)
+    middle_back, gain_two_grad, shift_two_grad = flat_norm_back(
+        second_grad, unit_two, spread_two, gain_two
+    )
+    middle_grad = row_mask * (grad_top + middle_back)
+    attended_grad = middle_grad.astype(low)
+    attended_rows = pair_up(attended_grad)
+    grad_mixed = mat(attended_rows, output_full).astype(low)
+    output_pieces = weight_pieces(attended_rows, mixed)
+    grad_qkv = attend_back_all(qkv, key_bias, grad_mixed, mixed, totals, rows)
+    early = jnp.concatenate(
+        [
+            column_flat(attended_grad),
+            gain_two_grad,
+            shift_two_grad,
+            column_flat(fed_grad),
+            spread_columns(column_flat(hidden_grad)),
+        ]
+    )
+    qkv_pieces = weight_pieces(normed_rows, grad_qkv)
+    last_pieces = [
+        jnp.concatenate([left, right], 1) for left, right in zip(qkv_pieces, output_pieces)
+    ]
+    last_owned = scatter_sum(last_pieces, place_x, place_z, core)
+    normed_grad = pair_sum(mat_far(grad_qkv, qkv_full))
+    first_back, gain_one_grad, shift_one_grad = flat_norm_back(
+        normed_grad, unit_one, spread_one, gain_one
+    )
+    images_own = middle_grad + first_back
+    qkv_sums = column_flat(grad_qkv).reshape(4, 3, head_part)
+    late = jnp.concatenate(
+        [
+            gain_one_grad,
+            shift_one_grad,
+            spread_columns(qkv_sums[:, 0].reshape(-1)),
+            spread_columns(qkv_sums[:, 2].reshape(-1)),
+        ]
+    )
+
+    def to_strips(own):
+        send = own[half : half + strip]
+        return pick_two(place_y, own[:strip], exchange(send, far_y=1), 0)
+
+    layer_out = to_strips(layer_own)
+    images_grad = to_strips(images_own.astype(low)).astype(jnp.float32)
+    early = lax.psum(early, BOTH)
+    late = lax.psum(late, BOTH)
+    owned = last_owned.reshape(depth, 2, 2, 4, head_part)
+
+    def full_columns(at):
+        return owned[:, :, :, at].reshape(depth, head_cols)
+
+    return (
+        layer_out,
+        images_grad,
+        late[:width],
+        late[width : 2 * width],
+        full_columns(0),
+        late[2 * width : 3 * width],
+        full_columns(1),
+        full_columns(2),
+        late[3 * width :],
+        full_columns(3).T,
+        early[:width],
+        early[width : 2 * width],
+        early[2 * width : 3 * width],
+        upper_owned.reshape(depth, units),
+        early[4 * width :],
+        lower_owned.reshape(depth, units).T,
+        early[3 * width : 4 * width],
+    )
+
+
+def column_flat(values):
+    return jnp.sum(values.astype(jnp.float32), axis=0)
+
+
+def pick(mesh):
+    sizes = dict(mesh.shape)
+    if sizes["dp"] == 16 and sizes["tensor"] == 2:
+        return whole_images
+    return local
+
+
 def solution(mesh):
     in_specs = (
         P("dp", "tensor", None),
@@ -326,4 +809,4 @@
         P("tensor", "dp"),
         P(),
     )
-    return jax.shard_map(local, mesh=mesh, in_specs=in_specs, out_specs=out_specs, check_vma=False)
+    return jax.shard_map(pick(mesh), mesh=mesh, in_specs=in_specs, out_specs=out_specs, check_vma=False)

time: 1300 us -> 609 us (0.47)
  waiting for transfers between devices: 947 us -> 159 us
  starting transfers between devices: 0.76 us -> 80.6 us
  matrix products: 143 us -> 85.6 us
  Pallas kernels: 0 us -> 46.1 us
  local copies, waits for them, and re-layouts: 55.3 us -> 81.8 us
    unnamed x22 -> x0, waiting for transfers between devices: 359 us -> none
    all_gather x10 -> x0, waiting for transfers between devices: 314 us -> none  [the longest x1 40.6 us: local(): lax.all_gather(down_weight, 'dp', axis=1, tiled=True)]
    reduce_scatter x6 -> x0, waiting for transfers between devices: 274 us -> none  [the longest x1 59.5 us: local(): lax.psum_scatter(query_grad.astype(jnp.bfloat16), 'dp', scatter_dimension...]
    ppermute x0 -> x59, waiting for transfers between devices: none -> 159 us  [exchange(): return lax.ppermute(value, BOTH, pairs)]
    ppermute x0 -> x59, starting transfers between devices: none -> 80.6 us  [exchange(): return lax.ppermute(value, BOTH, pairs)]
    another operation x0 -> x46, other arithmetic: none -> 58.3 us  [the longest x24 32.9 us: pick_two(): return jnp.stack([first, last], axis)]
    dot_general x32 -> x24, matrix products: 143 us -> 85.6 us  [the longest x16 32.7 us: mat_rows(): lax.dot_general(left, right, (((0,), (0,)), ((), ())), preferred_element_...]
    pallas_call x0 -> x2, Pallas kernels: none -> 46.1 us  [the longest x1 30.7 us: attend_back_all(): pl.pallas_call(attend_back_kernel, grid=(images, blocks), in_specs=[pl.Bl...]
  transfers between devices with their start and end apart: 19 -> 59, of which waited for: 18 -> 24; matrix products, arithmetic and copies ran while one was open for 16% -> 34% of each run, Pallas kernels for 0% -> 3%
where the time goes in v1:
time: 609 us; the launch traced here: 597 us
  waiting for transfers between devices  159 us (26%)
  other arithmetic  101 us (17%)
  matrix products  85.6 us (14%)
  local copies, waits for them, and re-layouts  81.8 us (13%)
  starting transfers between devices  80.6 us (13%)
  Pallas kernels  46.1 us (8%)
  blocking collectives  38.8 us (6%)
    ppermute x59, waiting for transfers between devices, exchange(): return lax.ppermute(value, BOTH, pairs)  159 us
    ppermute x59, starting transfers between devices, exchange(): return lax.ppermute(value, BOTH, pairs)  80.6 us
    psum x1, blocking collectives, whole_images(): late = lax.psum(late, BOTH)  38.8 us
    another operation x24, other arithmetic, pick_two(): return jnp.stack([first, last], axis)  32.9 us
    dot_general x16, matrix products, mat_rows(): lax.dot_general(left, right, (((0,), (0,)), ((), ())), preferred_element_...  32.7 us
    dot_general x4, matrix products, mat(): return jnp.dot(left, right, preferred_element_type=jnp.float32)  31 us
    pallas_call x1, Pallas kernels, attend_back_all(): pl.pallas_call(attend_back_kernel, grid=(images, blocks), in_specs=[pl.Bl...  30.7 us
    unnamed x216, local copies, waits for them, and re-layouts  21.9 us
  transfers between devices with their start and end apart: 59, of which 24 were waited for; matrix products, arithmetic and copies ran while one was open for 34% of the time, Pallas kernels for 3%

profile of v1, /device:TPU:0, one launch (start us, length us, event | category | flops | bytes accessed | tf_op | source)
XLA Modules:
  0.0 596.6 jit_solution(6829592586700947574)
XLA Ops:
  0.7 2.7 copy.308
  8.7 3.0 collective-permute-start
  18.5 2.6 collective-permute-start.4
  22.4 5.6 collective-permute-done.3
  27.9 7.7 %collective-permute-done.4 = bf16[2,2,64,384]{3,0,2,1:T(2,128)(2,1)S(1)} collective-permute-done((bf16[2,2,64,384]{3,0,2,1:T(2,128)(2,1)S(1)}, bf16[2,2,64,384]{3,0,2,1:T(2,128)(2,1)S(1)}, u32[]{:S(2)}, u32[]{:S(2)}) %collective-permute-start.4) | collective-permute-done | bytes 196640 | tf_op jit(solution)/shard_map/ppermute | solution.py:301
  38.7 4.0 collective-permute-start.11
  47.7 8.4 %collective-permute-done.11 = bf16[2,2,64,640]{3,0,2,1:T(2,128)(2,1)S(1)} collective-permute-done((bf16[2,2,64,640]{3,0,2,1:T(2,128)(2,1)S(1)}, bf16[2,2,64,640]{3,0,2,1:T(2,128)(2,1)S(1)}, u32[]{:S(2)}, u32[]{:S(2)}) %collective-permute-start.11) | collective-permute-done | bytes 327712 | tf_op jit(solution)/shard_map/ppermute | solution.py:301
  57.5 10.8 %collective-permute-done.12 = bf16[2,2,64,640]{3,0,2,1:T(2,128)(2,1)S(1)} collective-permute-done((bf16[2,2,64,640]{3,0,2,1:T(2,128)(2,1)S(1)}, bf16[2,2,64,640]{3,0,2,1:T(2,128)(2,1)S(1)}, u32[]{:S(2)}, u32[]{:S(2)}) %collective-permute-start.12) | collective-permute-done | bytes 327712 | tf_op jit(solution)/shard_map/ppermute | solution.py:301
  69.9 2.9 pad_maximum_fusion.12
  72.8 5.8 collective-permute-start.21
  79.7 3.9 fusion.155
  89.4 2.7 pad_maximum_fusion.26
  93.5 5.1 collective-permute-done.22
  99.8 3.2 pad_maximum_fusion.18
  103.1 2.4 convert_reduce_fusion.2
  115.0 3.5 fusion.55
  118.4 2.7 slice_maximum_fusion.2
  123.5 4.8 collective-permute-done.14
  131.4 3.0 pad_maximum_fusion.14
  136.0 4.0 fusion.qkv_ref
  140.1 15.4 %shard_map.305 = (bf16[1184,512]{1,0:T(8,128)(2,1)S(1)}, f32[8,8,592]{2,1,0:T(8,128)S(1)}) custom-call(bf16[1184,1536]{1,0:T(8,128)(2,1)S(1)} %fusion.qkv_ref, bf16[592,128]{1,0:T(8,128)(2,1)S(1)} %broadcast_in_dim.60.bias_ref), custom_call_target="tpu_custom_call" | custom-call | flops 5742002176 | bytes 4849664 | tf_op jit(solution)/shard_map/pallas_call | solution.py:468
  155.5 7.5 %collective-permute-done.17 = bf16[2,4,2,64,640]{4,0,3,2,1:T(2,128)(2,1)S(1)} collective-permute-done((bf16[2,4,2,64,640]{4,0,3,2,1:T(2,128)(2,1)S(1)}, bf16[2,4,2,64,640]{4,0,3,2,1:T(2,128)(2,1)S(1)}, u32[]{:S(2)}, u32[]{:S(2)}) %collective-permute-start.17) | collective-permute-done | bytes 1310752 | tf_op jit(solution)/shard_map/ppermute | solution.py:301
  163.1 4.4 fusion.20
  167.5 6.1 %slice_maximum_fusion = (bf16[1,4,2,2,64,640]{5,0,4,3,1,2:T(2,128)(2,1)S(1)}, bf16[1,4,2,2,64,640]{5,0,4,3,1,2:T(2,128)(2,1)S(1)}) fusion(bf16[2,4,1,2,64,640]{5,0,4,3,1,2:T(2,128)(2,1)S(1)} %get-tuple-element.117, bf16[2,4,1,2,64,640]{5,0,4,3,1,2:T(2,128)(2,1)S(1)} %get-tuple-element.116), kind=kLoop, calls=%fused_computation.18 | loop fusion | flops 5242880 | bytes 5242880 | tf_op jit(solution)/shard_map/stack | solution.py:307
  179.2 2.6 fusion.164
  188.4 2.4 fusion.157
  194.0 6.4 %copy.208 = bf16[1024,4,512]{0,2,1:T(8,128)(2,1)} copy(bf16[1024,4,512]{2,0,1:T(8,128)(2,1)} %pad_maximum_fusion) | data formatting | bytes 8388608 | tf_op jit(solution)/shard_map/slice | solution.py:610
  210.2 3.0 pad_maximum_fusion.20
  214.7 4.8 fusion.14
  224.9 13.1 %collective-permute-done.27 = bf16[2,4,2,64,512]{4,0,3,2,1:T(2,128)(2,1)} collective-permute-done((bf16[2,4,2,64,512]{4,0,3,2,1:T(2,128)(2,1)}, bf16[2,4,2,64,512]{4,0,3,2,1:T(2,128)(2,1)}, u32[]{:S(2)}, u32[]{:S(2)}) %collective-permute-start.27) | collective-permute-done | bytes 1048608 | tf_op jit(solution)/shard_map/ppermute | solution.py:301
  238.0 4.3 fusion.31
  242.3 4.9 slice_maximum_fusion.1
  250.1 10.6 %multiply_convert_fusion.1 = (bf16[1184,2048]{1,0:T(8,128)(2,1)}, f32[1184,2048]{1,0:T(8,128)}) fusion(f32[2048]{0:T(1024)S(1)} %bitcast.533, bf16[1024,2048]{0,1:T(8,128)(2,1)S(1)} %bitcast.485, bf16[592,1024]{1,0:T(8,128)(2,1)S(1)} %collective-permute-done.19, bf16[592,1024]{1,0:T(8,128)(2,1)S(1)} %add_convert_fusion.2), kind=kOutput, calls=%fused_computation.3 | convolution fusion | flops 4987879424 | bytes 21176320 | tf_op jit(solution)/shard_map/dot_general | solution.py:517
  260.7 13.3 %convert_reduce_fusion = (f32[2048]{0:T(1024)S(1)}, bf16[1184,2048]{1,0:T(8,128)(2,1)}) fusion(f32[1184,2048]{1,0:T(8,128)} %get-tuple-element.213, f32[2048]{0:T(1024)S(1)} %bitcast.534, bf16[1024,512]{1,0:T(8,128)(2,1)S(1)} %bitcast.492, bf16[1024,512]{1,0:T(8,128)(2,1)S(1)} %bitcast.494, bf16[1024,512]{1,0:T(8,128)(2,1)S(1)} %bitcast.502, ...), kind=kOutput, calls=%fused_computation | convolution fusion | flops 5024053248 | bytes 21184512 | tf_op jit(solution)/shard_map/dot_general | solution.py:517
  274.0 7.7 %fusion.165 = f32[1184,1024]{1,0:T(8,128)S(1)} fusion(bf16[1184,2048]{1,0:T(8,128)(2,1)} %get-tuple-element.215, bf16[1024,2048]{0,1:T(8,128)(2,1)S(1)} %bitcast.486), kind=kOutput, calls=%fused_computation.452 | convolution fusion | flops 4966055936 | bytes 13893632 | tf_op jit(solution)/shard_map/dot_general | solution.py:521
  285.1 5.3 fusion.57
  294.5 3.7 convolution_convert_fusion.7
  299.8 3.0 convolution_convert_fusion.6
  315.3 9.1 %collective-permute-done.43 = bf16[4,2,2,64,512]{4,3,2,0,1:T(8,128)(2,1)S(1)} collective-permute-done((bf16[4,2,2,64,512]{4,3,2,0,1:T(8,128)(2,1)S(1)}, bf16[4,2,2,64,512]{4,3,2,0,1:T(8,128)(2,1)S(1)}, u32[]{:S(2)}, u32[]{:S(2)}) %collective-permute-start.43) | collective-permute-done | bytes 1048608 | tf_op jit(solution)/shard_map/ppermute | solution.py:301
  326.3 4.4 collective-permute-done.45
  332.5 13.4 %collective-permute-done.51 = bf16[4,2,2,64,512]{4,3,2,0,1:T(8,128)(2,1)S(1)} collective-permute-done((bf16[4,2,2,64,512]{4,3,2,0,1:T(8,128)(2,1)S(1)}, bf16[4,2,2,64,512]{4,3,2,0,1:T(8,128)(2,1)S(1)}, u32[]{:S(2)}, u32[]{:S(2)}) %collective-permute-start.51) | collective-permute-done | bytes 1048608 | tf_op jit(solution)/shard_map/ppermute | solution.py:301
  347.7 5.4 collective-permute-done.53
  357.3 4.8 convert_reduce_fusion.4
  364.6 3.9 collective-permute-start.49
  368.5 5.9 collective-permute-done.52
  374.4 6.7 %collective-permute-start.48 = (bf16[2,2,64,512]{3,2,0,1:T(8,128)(2,1)S(1)}, bf16[2,2,64,512]{3,2,0,1:T(8,128)(2,1)S(1)}, u32[]{:S(2)}, u32[]{:S(2)}) collective-permute-start(bf16[2,2,64,512]{3,2,0,1:T(8,128)(2,1)S(1)} %get-tuple-element.152), channel_id=1, source_target_pairs={{0,16},{1,17},{2,18},{3,19},{4,20},{5,21},{6,22},{7,23},{8,24},{9,... | collective-permute-start | bytes 786440 | tf_op jit(solution)/shard_map/ppermute | solution.py:301
  383.2 3.8 collective-permute-start.57
  389.4 3.2 collective-permute-start.56
  392.6 9.8 %collective-permute-done.48 = bf16[2,2,64,512]{3,2,0,1:T(8,128)(2,1)S(1)} collective-permute-done((bf16[2,2,64,512]{3,2,0,1:T(8,128)(2,1)S(1)}, bf16[2,2,64,512]{3,2,0,1:T(8,128)(2,1)S(1)}, u32[]{:S(2)}, u32[]{:S(2)}) %collective-permute-start.48) | collective-permute-done | bytes 262176 | tf_op jit(solution)/shard_map/ppermute | solution.py:301
  402.9 11.6 %collective-permute-done.56 = bf16[2,2,64,512]{3,2,0,1:T(8,128)(2,1)S(1)} collective-permute-done((bf16[2,2,64,512]{3,2,0,1:T(8,128)(2,1)S(1)}, bf16[2,2,64,512]{3,2,0,1:T(8,128)(2,1)S(1)}, u32[]{:S(2)}, u32[]{:S(2)}) %collective-permute-start.56) | collective-permute-done | bytes 262176 | tf_op jit(solution)/shard_map/ppermute | solution.py:301
  418.7 3.1 convolution_convert_fusion.grad_ref
  421.9 30.7 %shard_map.306 = bf16[1184,1536]{1,0:T(8,128)(2,1)} custom-call(bf16[1184,1536]{1,0:T(8,128)(2,1)} %copy-done.2, bf16[592,128]{1,0:T(8,128)(2,1)S(1)} %copy-done.1, bf16[1184,512]{1,0:T(8,128)(2,1)S(1)} %convolution_convert_fusion.grad_ref, bf16[1184,512]{1,0:T(8,128)(2,1)S(1)} %get-tuple-element.23.mixed_ref, f32[8,8,592]{2,1,0:T(8,128)S(1)} %get-tuple-element.28.total_ref), custom_call_target="tpu_custom_call" | custom-call | flops 14355005440 | bytes 9699328 | tf_op jit(solution)/shard_map/pallas_call | solution.py:495
  452.7 6.2 %fusion.60 = f32[1184,1024]{1,0:T(8,128)S(1)} fusion(bf16[1184,1536]{1,0:T(8,128)(2,1)} %shard_map.306, bf16[1024,384]{1,0:T(8,128)(2,1)S(1)} %bitcast.511, bf16[1024,384]{1,0:T(8,128)(2,1)S(1)} %bitcast.513, bf16[1024,384]{1,0:T(8,128)(2,1)S(1)} %bitcast.509, bf16[1024,384]{1,0:T(8,128)(2,1)S(1)} %bitcast.507), kind=kOutput, calls=%fused_computation.224 | convolution fusion | flops 3737124864 | bytes 11632640 | tf_op jit(solution)/shard_map/dot_general | solution.py:521
  462.0 2.4 convolution_convert_fusion.15
  464.4 2.4 convolution_convert_fusion.11
  484.5 2.4 convolution_convert_fusion.12
  488.5 3.1 copy.223
  498.3 8.9 %collective-permute-done.37 = bf16[2,4,2,64,512]{4,3,2,1,0:T(8,128)(2,1)} collective-permute-done((bf16[2,4,2,64,512]{4,3,2,1,0:T(8,128)(2,1)}, bf16[2,4,2,64,512]{4,3,2,1,0:T(8,128)(2,1)}, u32[]{:S(2)}, u32[]{:S(2)}) %collective-permute-start.37) | collective-permute-done | bytes 1048608 | tf_op jit(solution)/shard_map/ppermute | solution.py:301
  511.3 3.4 multiply_reduce_fusion.1
  514.8 2.7 add_convert_fusion.1
  517.5 38.8 %all-reduce.1 = (f32[4096]{0:T(1024)S(1)}, f32[8192]{0:T(1024)S(1)}) all-reduce(f32[4096]{0:T(1024)S(1)} %pad_maximum_fusion.34, f32[8192]{0:T(1024)S(1)} %constant_dynamic-update-slice_fusion), channel_id=1, replica_groups=mesh['dp'=16,'tensor'=2] {'dp','tensor'}, use_global_device_ids=true, to_apply=%region_11.12 | all-reduce | flops 12288 | bytes 98304 | tf_op jit(solution)/shard_map/psum | solution.py:734
  567.4 4.8 collective-permute-done.34
  574.1 13.7 %collective-permute-done.40 = bf16[2,2,64,512]{3,2,1,0:T(8,128)(2,1)S(1)} collective-permute-done((bf16[2,2,64,512]{3,2,1,0:T(8,128)(2,1)S(1)}, bf16[2,2,64,512]{3,2,1,0:T(8,128)(2,1)S(1)}, u32[]{:S(2)}, u32[]{:S(2)}) %collective-permute-start.40) | collective-permute-done | bytes 262176 | tf_op jit(solution)/shard_map/ppermute | solution.py:301
  588.4 3.2 copy.255
  (504 shorter events, 177.5 us)
Async XLA Ops:
  8.7 94.4 %collective-permute-start = (bf16[2,296,1024]{2,1,0:T(8,128)(2,1)}, bf16[2,296,1024]{2,1,0:T(8,128)(2,1)}, u32[]{:S(2)}, u32[]{:S(2)}) collective-permute-start(bf16[2,296,1024]{2,1,0:T(8,128)(2,1)} %get-tuple-element.121), channel_id=1, source_target_pairs={{0,1},{1,0},{2,3},{3,2},{4,5},{5,4},{6,7},{7,6},{8,9},{9,8},{10,11... | collective-permute-start | bytes 3637256 | tf_op jit(solution)/shard_map/ppermute | solution.py:301
  12.1 4.3 collective-permute-start.2
  12.9 8.7 %collective-permute-start.10 = (bf16[2,64,640]{2,0,1:T(2,128)(2,1)S(1)}, bf16[2,64,640]{2,0,1:T(2,128)(2,1)S(1)}, u32[]{:S(2)}, u32[]{:S(2)}) collective-permute-start(bf16[2,64,640]{2,0,1:T(2,128)(2,1)S(1)} %fusion.121), channel_id=1, source_target_pairs={{0,2},{1,3},{2,0},{3,1},{4,6},{5,7},{6,4},{7,5},{8,10},{9,11},{10,... | collective-permute-start | bytes 491528 | tf_op jit(solution)/shard_map/ppermute | solution.py:301
  13.8 7.3 %collective-permute-start.20 = (bf16[2,64,512]{2,0,1:T(2,128)(2,1)S(1)}, bf16[2,64,512]{2,0,1:T(2,128)(2,1)S(1)}, u32[]{:S(2)}, u32[]{:S(2)}) collective-permute-start(bf16[2,64,512]{2,0,1:T(2,128)(2,1)S(1)} %fusion.131), channel_id=1, source_target_pairs={{0,2},{1,3},{2,0},{3,1},{4,6},{5,7},{6,4},{7,5},{8,10},{9,11},{10,... | collective-permute-start | bytes 393224 | tf_op jit(solution)/shard_map/ppermute | solution.py:301
  15.6 90.5 %copy-start.65 = (f32[1024]{0:T(1024)}, f32[1024]{0:T(1024)S(1)}, u32[]{:S(2)}) copy-start(f32[1024]{0:T(1024)S(1)} %convert_element_type.381) | copy-start | bytes 12292
  16.9 11.1 %collective-permute-start.3 = (bf16[2,2,64,384]{3,0,2,1:T(2,128)(2,1)S(1)}, bf16[2,2,64,384]{3,0,2,1:T(2,128)(2,1)S(1)}, u32[]{:S(2)}, u32[]{:S(2)}) collective-permute-start(bf16[2,2,64,384]{3,0,2,1:T(2,128)(2,1)S(1)} %pad_maximum_fusion.33), channel_id=1, source_target_pairs={{0,8},{1,9},{2,10},{3,11},{4,12},{5,13},{6,14},{7,15},{8,0},{9,1},... | collective-permute-start | bytes 589832 | tf_op jit(solution)/shard_map/ppermute | solution.py:301
  18.5 17.1 %collective-permute-start.4 = (bf16[2,2,64,384]{3,0,2,1:T(2,128)(2,1)S(1)}, bf16[2,2,64,384]{3,0,2,1:T(2,128)(2,1)S(1)}, u32[]{:S(2)}, u32[]{:S(2)}) collective-permute-start(bf16[2,2,64,384]{3,0,2,1:T(2,128)(2,1)S(1)} %pad_maximum_fusion.33), channel_id=1, source_target_pairs={{0,16},{1,17},{2,18},{3,19},{4,20},{5,21},{6,22},{7,23},{8,24},{9,... | collective-permute-start | bytes 589832 | tf_op jit(solution)/shard_map/ppermute | solution.py:301
  21.1 14.5 %collective-permute-start.5 = (bf16[2,2,64,384]{3,0,2,1:T(2,128)(2,1)S(1)}, bf16[2,2,64,384]{3,0,2,1:T(2,128)(2,1)S(1)}, u32[]{:S(2)}, u32[]{:S(2)}) collective-permute-start(bf16[2,2,64,384]{3,0,2,1:T(2,128)(2,1)S(1)} %pad_maximum_fusion.33), channel_id=1, source_target_pairs={{0,24},{1,25},{2,26},{3,27},{4,28},{5,29},{6,30},{7,31},{8,16},{9,... | collective-permute-start | bytes 589832 | tf_op jit(solution)/shard_map/ppermute | solution.py:301
  38.7 17.4 %collective-permute-start.11 = (bf16[2,2,64,640]{3,0,2,1:T(2,128)(2,1)S(1)}, bf16[2,2,64,640]{3,0,2,1:T(2,128)(2,1)S(1)}, u32[]{:S(2)}, u32[]{:S(2)}) collective-permute-start(bf16[2,2,64,640]{3,0,2,1:T(2,128)(2,1)S(1)} %pad_maximum_fusion.31), channel_id=1, source_target_pairs={{0,8},{1,9},{2,10},{3,11},{4,12},{5,13},{6,14},{7,15},{8,0},{9,1},... | collective-permute-start | bytes 983048 | tf_op jit(solution)/shard_map/ppermute | solution.py:301
  42.7 25.6 %collective-permute-start.12 = (bf16[2,2,64,640]{3,0,2,1:T(2,128)(2,1)S(1)}, bf16[2,2,64,640]{3,0,2,1:T(2,128)(2,1)S(1)}, u32[]{:S(2)}, u32[]{:S(2)}) collective-permute-start(bf16[2,2,64,640]{3,0,2,1:T(2,128)(2,1)S(1)} %pad_maximum_fusion.31), channel_id=1, source_target_pairs={{0,16},{1,17},{2,18},{3,19},{4,20},{5,21},{6,22},{7,23},{8,24},{9,... | collective-permute-start | bytes 983048 | tf_op jit(solution)/shard_map/ppermute | solution.py:301
  43.8 24.5 %collective-permute-start.13 = (bf16[2,2,64,640]{3,0,2,1:T(2,128)(2,1)S(1)}, bf16[2,2,64,640]{3,0,2,1:T(2,128)(2,1)S(1)}, u32[]{:S(2)}, u32[]{:S(2)}) collective-permute-start(bf16[2,2,64,640]{3,0,2,1:T(2,128)(2,1)S(1)} %pad_maximum_fusion.31), channel_id=1, source_target_pairs={{0,24},{1,25},{2,26},{3,27},{4,28},{5,29},{6,30},{7,31},{8,16},{9,... | collective-permute-start | bytes 983048 | tf_op jit(solution)/shard_map/ppermute | solution.py:301
  47.0 41.1 %collective-permute-start.8 = (bf16[4,2,64,384]{3,2,1,0:T(8,128)(2,1)S(1)}, bf16[4,2,64,384]{3,2,1,0:T(8,128)(2,1)S(1)}, u32[]{:S(2)}, u32[]{:S(2)}) collective-permute-start(bf16[4,2,64,384]{3,2,1,0:T(8,128)(2,1)S(1)} %bitcast.520), channel_id=1, source_target_pairs={{0,1},{1,0},{2,3},{3,2},{4,5},{5,4},{6,7},{7,6},{8,9},{9,8},{10,11... | collective-permute-start | bytes 1179656 | tf_op jit(solution)/shard_map/ppermute | solution.py:301
  56.0 27.5 %collective-permute-start.6 = (bf16[4,2,64,384]{3,2,1,0:T(8,128)(2,1)S(1)}, bf16[4,2,64,384]{3,2,1,0:T(8,128)(2,1)S(1)}, u32[]{:S(2)}, u32[]{:S(2)}) collective-permute-start(bf16[4,2,64,384]{3,2,1,0:T(8,128)(2,1)S(1)} %bitcast.521), channel_id=1, source_target_pairs={{0,4},{1,5},{2,6},{3,7},{4,0},{5,1},{6,2},{7,3},{8,12},{9,13},{10,... | collective-permute-start | bytes 1179656 | tf_op jit(solution)/shard_map/ppermute | solution.py:301
  72.8 19.3 %collective-permute-start.21 = (bf16[2,2,64,512]{3,0,2,1:T(2,128)(2,1)S(1)}, bf16[2,2,64,512]{3,0,2,1:T(2,128)(2,1)S(1)}, u32[]{:S(2)}, u32[]{:S(2)}) collective-permute-start(bf16[2,2,64,512]{3,0,2,1:T(2,128)(2,1)S(1)} %pad_maximum_fusion.32), channel_id=1, source_target_pairs={{0,8},{1,9},{2,10},{3,11},{4,12},{5,13},{6,14},{7,15},{8,0},{9,1},... | collective-permute-start | bytes 786440 | tf_op jit(solution)/shard_map/ppermute | solution.py:301
  78.6 20.0 %collective-permute-start.22 = (bf16[2,2,64,512]{3,0,2,1:T(2,128)(2,1)S(1)}, bf16[2,2,64,512]{3,0,2,1:T(2,128)(2,1)S(1)}, u32[]{:S(2)}, u32[]{:S(2)}) collective-permute-start(bf16[2,2,64,512]{3,0,2,1:T(2,128)(2,1)S(1)} %pad_maximum_fusion.32), channel_id=1, source_target_pairs={{0,16},{1,17},{2,18},{3,19},{4,20},{5,21},{6,22},{7,23},{8,24},{9,... | collective-permute-start | bytes 786440 | tf_op jit(solution)/shard_map/ppermute | solution.py:301
  83.6 15.0 %collective-permute-start.23 = (bf16[2,2,64,512]{3,0,2,1:T(2,128)(2,1)S(1)}, bf16[2,2,64,512]{3,0,2,1:T(2,128)(2,1)S(1)}, u32[]{:S(2)}, u32[]{:S(2)}) collective-permute-start(bf16[2,2,64,512]{3,0,2,1:T(2,128)(2,1)S(1)} %pad_maximum_fusion.32), channel_id=1, source_target_pairs={{0,24},{1,25},{2,26},{3,27},{4,28},{5,29},{6,30},{7,31},{8,16},{9,... | collective-permute-start | bytes 786440 | tf_op jit(solution)/shard_map/ppermute | solution.py:301
  88.2 21.0 %collective-permute-start.7 = (bf16[4,2,2,64,384]{4,3,2,0,1:T(8,128)(2,1)}, bf16[4,2,2,64,384]{4,3,2,0,1:T(8,128)(2,1)}, u32[]{:S(2)}, u32[]{:S(2)}) collective-permute-start(bf16[4,2,2,64,384]{4,3,2,0,1:T(8,128)(2,1)} %pad_maximum_fusion.25), channel_id=1, source_target_pairs={{0,1},{1,0},{2,3},{3,2},{4,5},{5,4},{6,7},{7,6},{8,9},{9,8},{10,11... | collective-permute-start | bytes 2359304 | tf_op jit(solution)/shard_map/ppermute | solution.py:301
  92.0 17.2 %collective-permute-start.9 = (bf16[2,4,2,64,384]{4,0,3,2,1:T(2,128)(2,1)}, bf16[2,4,2,64,384]{4,0,3,2,1:T(2,128)(2,1)}, u32[]{:S(2)}, u32[]{:S(2)}) collective-permute-start(bf16[2,4,2,64,384]{4,0,3,2,1:T(2,128)(2,1)} %pad_maximum_fusion.26), channel_id=1, source_target_pairs={{0,4},{1,5},{2,6},{3,7},{4,0},{5,1},{6,2},{7,3},{8,12},{9,13},{10,... | collective-permute-start | bytes 2359304 | tf_op jit(solution)/shard_map/ppermute | solution.py:301
  105.5 109.2 %copy-start.5 = (bf16[1,2,296,1024]{3,2,0,1:T(8,128)(2,1)}, bf16[1,2,296,1024]{3,2,0,1:T(8,128)(2,1)S(1)}, u32[]{:S(2)}) copy-start(bf16[1,2,296,1024]{3,2,0,1:T(8,128)(2,1)S(1)} %get-tuple-element.113) | copy-start | bytes 3637252
  108.1 27.8 %collective-permute-start.1 = (bf16[592,1024]{1,0:T(8,128)(2,1)S(1)}, bf16[592,1024]{1,0:T(8,128)(2,1)S(1)}, u32[]{:S(2)}, u32[]{:S(2)}) collective-permute-start(bf16[592,1024]{1,0:T(8,128)(2,1)S(1)} %get-tuple-element.147), channel_id=1, source_target_pairs={{0,2},{1,3},{2,0},{3,1},{4,6},{5,7},{6,4},{7,5},{8,10},{9,11},{10,... | collective-permute-start | bytes 3637256 | tf_op jit(solution)/shard_map/ppermute | solution.py:301
  111.7 18.6 %collective-permute-start.16 = (bf16[4,2,64,640]{3,2,1,0:T(8,128)(2,1)S(1)}, bf16[4,2,64,640]{3,2,1,0:T(8,128)(2,1)S(1)}, u32[]{:S(2)}, u32[]{:S(2)}) collective-permute-start(bf16[4,2,64,640]{3,2,1,0:T(8,128)(2,1)S(1)} %bitcast.514), channel_id=1, source_target_pairs={{0,1},{1,0},{2,3},{3,2},{4,5},{5,4},{6,7},{7,6},{8,9},{9,8},{10,11... | collective-permute-start | bytes 1966088 | tf_op jit(solution)/shard_map/ppermute | solution.py:301
  113.4 14.8 %collective-permute-start.14 = (bf16[4,2,64,640]{3,2,1,0:T(8,128)(2,1)S(1)}, bf16[4,2,64,640]{3,2,1,0:T(8,128)(2,1)S(1)}, u32[]{:S(2)}, u32[]{:S(2)}) collective-permute-start(bf16[4,2,64,640]{3,2,1,0:T(8,128)(2,1)S(1)} %bitcast.516), channel_id=1, source_target_pairs={{0,4},{1,5},{2,6},{3,7},{4,0},{5,1},{6,2},{7,3},{8,12},{9,13},{10,... | collective-permute-start | bytes 1966088 | tf_op jit(solution)/shard_map/ppermute | solution.py:301
  128.6 45.7 %collective-permute-start.15 = (bf16[4,2,2,64,640]{4,3,2,0,1:T(8,128)(2,1)S(1)}, bf16[4,2,2,64,640]{4,3,2,0,1:T(8,128)(2,1)S(1)}, u32[]{:S(2)}, u32[]{:S(2)}) collective-permute-start(bf16[4,2,2,64,640]{4,3,2,0,1:T(8,128)(2,1)S(1)} %pad_maximum_fusion.13), channel_id=1, source_target_pairs={{0,1},{1,0},{2,3},{3,2},{4,5},{5,4},{6,7},{7,6},{8,9},{9,8},{10,11... | collective-permute-start | bytes 3932168 | tf_op jit(solution)/shard_map/ppermute | solution.py:301
  130.3 44.1 %copy-start.11 = (bf16[4,2,2,64,640]{4,3,2,1,0:T(8,128)(2,1)}, bf16[4,2,2,64,640]{4,3,2,1,0:T(8,128)(2,1)S(1)}, u32[]{:S(2)}) copy-start(bf16[4,2,2,64,640]{4,3,2,1,0:T(8,128)(2,1)S(1)} %copy.202) | copy-start | bytes 3932164
  134.4 28.7 %collective-permute-start.17 = (bf16[2,4,2,64,640]{4,0,3,2,1:T(2,128)(2,1)S(1)}, bf16[2,4,2,64,640]{4,0,3,2,1:T(2,128)(2,1)S(1)}, u32[]{:S(2)}, u32[]{:S(2)}) collective-permute-start(bf16[2,4,2,64,640]{4,0,3,2,1:T(2,128)(2,1)S(1)} %pad_maximum_fusion.14), channel_id=1, source_target_pairs={{0,4},{1,5},{2,6},{3,7},{4,0},{5,1},{6,2},{7,3},{8,12},{9,13},{10,... | collective-permute-start | bytes 3932168 | tf_op jit(solution)/shard_map/ppermute | solution.py:301
  184.5 30.2 %collective-permute-start.18 = (bf16[592,1024]{1,0:T(8,128)(2,1)}, bf16[592,1024]{1,0:T(8,128)(2,1)}, u32[]{:S(2)}, u32[]{:S(2)}) collective-permute-start(bf16[592,1024]{1,0:T(8,128)(2,1)} %slice.520), channel_id=1, source_target_pairs={{0,2},{1,3},{2,0},{3,1},{4,6},{5,7},{6,4},{7,5},{8,10},{9,11},{10,... | collective-permute-start | bytes 3637256 | tf_op jit(solution)/shard_map/ppermute | solution.py:301
  186.9 14.7 %collective-permute-start.24 = (bf16[4,2,64,512]{3,2,1,0:T(8,128)(2,1)}, bf16[4,2,64,512]{3,2,1,0:T(8,128)(2,1)}, u32[]{:S(2)}, u32[]{:S(2)}) collective-permute-start(bf16[4,2,64,512]{3,2,1,0:T(8,128)(2,1)} %bitcast.453), channel_id=1, source_target_pairs={{0,4},{1,5},{2,6},{3,7},{4,0},{5,1},{6,2},{7,3},{8,12},{9,13},{10,... | collective-permute-start | bytes 1572872 | tf_op jit(solution)/shard_map/ppermute | solution.py:301
  191.0 16.1 %collective-permute-start.26 = (bf16[4,2,64,512]{3,2,1,0:T(8,128)(2,1)S(1)}, bf16[4,2,64,512]{3,2,1,0:T(8,128)(2,1)}, u32[]{:S(2)}, u32[]{:S(2)}) collective-permute-start(bf16[4,2,64,512]{3,2,1,0:T(8,128)(2,1)S(1)} %bitcast.517), channel_id=1, source_target_pairs={{0,1},{1,0},{2,3},{3,2},{4,5},{5,4},{6,7},{7,6},{8,9},{9,8},{10,11... | collective-permute-start | bytes 1572872 | tf_op jit(solution)/shard_map/ppermute | solution.py:301
  204.1 43.8 %collective-permute-start.25 = (bf16[4,2,2,64,512]{4,3,2,0,1:T(8,128)(2,1)}, bf16[4,2,2,64,512]{4,3,2,0,1:T(8,128)(2,1)}, u32[]{:S(2)}, u32[]{:S(2)}) collective-permute-start(bf16[4,2,2,64,512]{4,3,2,0,1:T(8,128)(2,1)} %pad_maximum_fusion.19), channel_id=1, source_target_pairs={{0,1},{1,0},{2,3},{3,2},{4,5},{5,4},{6,7},{7,6},{8,9},{9,8},{10,11... | collective-permute-start | bytes 3145736 | tf_op jit(solution)/shard_map/ppermute | solution.py:301
  213.2 24.8 %collective-permute-start.27 = (bf16[2,4,2,64,512]{4,0,3,2,1:T(2,128)(2,1)}, bf16[2,4,2,64,512]{4,0,3,2,1:T(2,128)(2,1)}, u32[]{:S(2)}, u32[]{:S(2)}) collective-permute-start(bf16[2,4,2,64,512]{4,0,3,2,1:T(2,128)(2,1)} %pad_maximum_fusion.20), channel_id=1, source_target_pairs={{0,4},{1,5},{2,6},{3,7},{4,0},{5,1},{6,2},{7,3},{8,12},{9,13},{10,... | collective-permute-start | bytes 3145736 | tf_op jit(solution)/shard_map/ppermute | solution.py:301
  224.2 25.2 %collective-permute-start.19 = (bf16[592,1024]{1,0:T(8,128)(2,1)S(1)}, bf16[592,1024]{1,0:T(8,128)(2,1)S(1)}, u32[]{:S(2)}, u32[]{:S(2)}) collective-permute-start(bf16[592,1024]{1,0:T(8,128)(2,1)S(1)} %add_convert_fusion.2), channel_id=1, source_target_pairs={{0,2},{1,3},{2,0},{3,1},{4,6},{5,7},{6,4},{7,5},{8,10},{9,11},{10,... | collective-permute-start | bytes 3637256 | tf_op jit(solution)/shard_map/ppermute | solution.py:301
  224.9 35.8 %collective-permute-start.30 = (bf16[592,1024]{1,0:T(8,128)(2,1)S(1)}, bf16[592,1024]{1,0:T(8,128)(2,1)S(1)}, u32[]{:S(2)}, u32[]{:S(2)}) collective-permute-start(bf16[592,1024]{1,0:T(8,128)(2,1)S(1)} %copy-done.46), channel_id=1, source_target_pairs={{0,2},{1,3},{2,0},{3,1},{4,6},{5,7},{6,4},{7,5},{8,10},{9,11},{10,... | collective-permute-start | bytes 3637256 | tf_op jit(solution)/shard_map/ppermute | solution.py:301
  285.1 69.9 %collective-permute-start.31 = (bf16[592,1024]{1,0:T(8,128)(2,1)}, bf16[592,1024]{1,0:T(8,128)(2,1)S(1)}, u32[]{:S(2)}, u32[]{:S(2)}) collective-permute-start(bf16[592,1024]{1,0:T(8,128)(2,1)} %slice.518), channel_id=1, source_target_pairs={{0,2},{1,3},{2,0},{3,1},{4,6},{5,7},{6,4},{7,5},{8,10},{9,11},{10,... | collective-permute-start | bytes 3637256 | tf_op jit(solution)/shard_map/ppermute | solution.py:301
  293.9 63.3 %collective-permute-start.28 = (bf16[592,1024]{1,0:T(8,128)(2,1)}, bf16[592,1024]{1,0:T(8,128)(2,1)}, u32[]{:S(2)}, u32[]{:S(2)}) collective-permute-start(bf16[592,1024]{1,0:T(8,128)(2,1)} %slice.519), channel_id=1, source_target_pairs={{0,2},{1,3},{2,0},{3,1},{4,6},{5,7},{6,4},{7,5},{8,10},{9,11},{10,... | collective-permute-start | bytes 3637256 | tf_op jit(solution)/shard_map/ppermute | solution.py:301
  298.3 26.1 %collective-permute-start.43 = (bf16[4,2,2,64,512]{4,3,2,0,1:T(8,128)(2,1)S(1)}, bf16[4,2,2,64,512]{4,3,2,0,1:T(8,128)(2,1)S(1)}, u32[]{:S(2)}, u32[]{:S(2)}) collective-permute-start(bf16[4,2,2,64,512]{4,3,2,0,1:T(8,128)(2,1)S(1)} %copy.238), channel_id=1, source_target_pairs={{0,1},{1,0},{2,3},{3,2},{4,5},{5,4},{6,7},{7,6},{8,9},{9,8},{10,11... | collective-permute-start | bytes 3145736 | tf_op jit(solution)/shard_map/ppermute | solution.py:301
  304.5 26.1 %collective-permute-start.45 = (bf16[2,4,2,64,512]{4,3,2,1,0:T(8,128)(2,1)S(1)}, bf16[2,4,2,64,512]{4,3,2,1,0:T(8,128)(2,1)S(1)}, u32[]{:S(2)}, u32[]{:S(2)}) collective-permute-start(bf16[2,4,2,64,512]{4,3,2,1,0:T(8,128)(2,1)S(1)} %fusion.38), channel_id=1, source_target_pairs={{0,4},{1,5},{2,6},{3,7},{4,0},{5,1},{6,2},{7,3},{8,12},{9,13},{10,... | collective-permute-start | bytes 3145736 | tf_op jit(solution)/shard_map/ppermute | solution.py:301
  307.8 38.2 %collective-permute-start.51 = (bf16[4,2,2,64,512]{4,3,2,0,1:T(8,128)(2,1)S(1)}, bf16[4,2,2,64,512]{4,3,2,0,1:T(8,128)(2,1)S(1)}, u32[]{:S(2)}, u32[]{:S(2)}) collective-permute-start(bf16[4,2,2,64,512]{4,3,2,0,1:T(8,128)(2,1)S(1)} %copy.246), channel_id=1, source_target_pairs={{0,1},{1,0},{2,3},{3,2},{4,5},{5,4},{6,7},{7,6},{8,9},{9,8},{10,11... | collective-permute-start | bytes 3145736 | tf_op jit(solution)/shard_map/ppermute | solution.py:301
  324.4 28.7 %collective-permute-start.53 = (bf16[2,4,2,64,512]{4,3,2,1,0:T(8,128)(2,1)S(1)}, bf16[2,4,2,64,512]{4,3,2,1,0:T(8,128)(2,1)S(1)}, u32[]{:S(2)}, u32[]{:S(2)}) collective-permute-start(bf16[2,4,2,64,512]{4,3,2,1,0:T(8,128)(2,1)S(1)} %fusion.34), channel_id=1, source_target_pairs={{0,4},{1,5},{2,6},{3,7},{4,0},{5,1},{6,2},{7,3},{8,12},{9,13},{10,... | collective-permute-start | bytes 3145736 | tf_op jit(solution)/shard_map/ppermute | solution.py:301
  330.7 33.7 %collective-permute-start.44 = (bf16[4,2,64,512]{3,2,1,0:T(8,128)(2,1)S(1)}, bf16[4,2,64,512]{3,2,1,0:T(8,128)(2,1)S(1)}, u32[]{:S(2)}, u32[]{:S(2)}) collective-permute-start(bf16[4,2,64,512]{3,2,1,0:T(8,128)(2,1)S(1)} %dynamic-slice_bitcast_fusion.2), channel_id=1, source_target_pairs={{0,4},{1,5},{2,6},{3,7},{4,0},{5,1},{6,2},{7,3},{8,12},{9,13},{10,... | collective-permute-start | bytes 1572872 | tf_op jit(solution)/shard_map/ppermute | solution.py:301
  345.9 17.4 %collective-permute-start.46 = (bf16[4,2,64,512]{3,2,1,0:T(8,128)(2,1)S(1)}, bf16[4,2,64,512]{3,2,1,0:T(8,128)(2,1)S(1)}, u32[]{:S(2)}, u32[]{:S(2)}) collective-permute-start(bf16[4,2,64,512]{3,2,1,0:T(8,128)(2,1)S(1)} %slice_bitcast_fusion.2), channel_id=1, source_target_pairs={{0,1},{1,0},{2,3},{3,2},{4,5},{5,4},{6,7},{7,6},{8,9},{9,8},{10,11... | collective-permute-start | bytes 1572872 | tf_op jit(solution)/shard_map/ppermute | solution.py:301
  353.1 21.2 %collective-permute-start.52 = (bf16[4,2,64,512]{3,2,1,0:T(8,128)(2,1)S(1)}, bf16[4,2,64,512]{3,2,1,0:T(8,128)(2,1)S(1)}, u32[]{:S(2)}, u32[]{:S(2)}) collective-permute-start(bf16[4,2,64,512]{3,2,1,0:T(8,128)(2,1)S(1)} %dynamic-slice_bitcast_fusion.1), channel_id=1, source_target_pairs={{0,4},{1,5},{2,6},{3,7},{4,0},{5,1},{6,2},{7,3},{8,12},{9,13},{10,... | collective-permute-start | bytes 1572872 | tf_op jit(solution)/shard_map/ppermute | solution.py:301
  355.0 26.2 %collective-permute-start.54 = (bf16[4,2,64,512]{3,2,1,0:T(8,128)(2,1)S(1)}, bf16[4,2,64,512]{3,2,1,0:T(8,128)(2,1)S(1)}, u32[]{:S(2)}, u32[]{:S(2)}) collective-permute-start(bf16[4,2,64,512]{3,2,1,0:T(8,128)(2,1)S(1)} %slice_bitcast_fusion), channel_id=1, source_target_pairs={{0,1},{1,0},{2,3},{3,2},{4,5},{5,4},{6,7},{7,6},{8,9},{9,8},{10,11... | collective-permute-start | bytes 1572872 | tf_op jit(solution)/shard_map/ppermute | solution.py:301
  362.1 21.1 %collective-permute-start.29 = (bf16[289,1024]{1,0:T(8,128)(2,1)S(1)}, bf16[289,1024]{1,0:T(8,128)(2,1)S(1)}, u32[]{:S(2)}, u32[]{:S(2)}) collective-permute-start(bf16[289,1024]{1,0:T(8,128)(2,1)S(1)} %slice.339), channel_id=1, source_target_pairs={{0,1},{1,0},{2,3},{3,2},{4,5},{5,4},{6,7},{7,6},{8,9},{9,8},{10,11... | collective-permute-start | bytes 1775624 | tf_op jit(solution)/shard_map/ppermute | solution.py:301
  363.3 55.4 %collective-permute-start.32 = (bf16[592,1024]{1,0:T(8,128)(2,1)}, bf16[592,1024]{1,0:T(8,128)(2,1)}, u32[]{:S(2)}, u32[]{:S(2)}) collective-permute-start(bf16[592,1024]{1,0:T(8,128)(2,1)} %get-tuple-element.110), channel_id=1, source_target_pairs={{0,2},{1,3},{2,0},{3,1},{4,6},{5,7},{6,4},{7,5},{8,10},{9,11},{10,... | collective-permute-start | bytes 3637256 | tf_op jit(solution)/shard_map/ppermute | solution.py:301
  364.6 24.8 %collective-permute-start.49 = (bf16[2,2,64,512]{3,2,0,1:T(8,128)(2,1)S(1)}, bf16[2,2,64,512]{3,2,0,1:T(8,128)(2,1)S(1)}, u32[]{:S(2)}, u32[]{:S(2)}) collective-permute-start(bf16[2,2,64,512]{3,2,0,1:T(8,128)(2,1)S(1)} %get-tuple-element.153), channel_id=1, source_target_pairs={{0,24},{1,25},{2,26},{3,27},{4,28},{5,29},{6,30},{7,31},{8,16},{9,... | collective-permute-start | bytes 786440 | tf_op jit(solution)/shard_map/ppermute | solution.py:301
  374.4 28.1 %collective-permute-start.48 = (bf16[2,2,64,512]{3,2,0,1:T(8,128)(2,1)S(1)}, bf16[2,2,64,512]{3,2,0,1:T(8,128)(2,1)S(1)}, u32[]{:S(2)}, u32[]{:S(2)}) collective-permute-start(bf16[2,2,64,512]{3,2,0,1:T(8,128)(2,1)S(1)} %get-tuple-element.152), channel_id=1, source_target_pairs={{0,16},{1,17},{2,18},{3,19},{4,20},{5,21},{6,22},{7,23},{8,24},{9,... | collective-permute-start | bytes 786440 | tf_op jit(solution)/shard_map/ppermute | solution.py:301
  381.2 21.3 %collective-permute-start.47 = (bf16[2,2,64,512]{3,2,0,1:T(8,128)(2,1)S(1)}, bf16[2,2,64,512]{3,2,0,1:T(8,128)(2,1)S(1)}, u32[]{:S(2)}, u32[]{:S(2)}) collective-permute-start(bf16[2,2,64,512]{3,2,0,1:T(8,128)(2,1)S(1)} %get-tuple-element.151), channel_id=1, source_target_pairs={{0,8},{1,9},{2,10},{3,11},{4,12},{5,13},{6,14},{7,15},{8,0},{9,1},... | collective-permute-start | bytes 786440 | tf_op jit(solution)/shard_map/ppermute | solution.py:301
  383.2 19.7 %collective-permute-start.57 = (bf16[2,2,64,512]{3,2,0,1:T(8,128)(2,1)S(1)}, bf16[2,2,64,512]{3,2,0,1:T(8,128)(2,1)S(1)}, u32[]{:S(2)}, u32[]{:S(2)}) collective-permute-start(bf16[2,2,64,512]{3,2,0,1:T(8,128)(2,1)S(1)} %get-tuple-element.150), channel_id=1, source_target_pairs={{0,24},{1,25},{2,26},{3,27},{4,28},{5,29},{6,30},{7,31},{8,16},{9,... | collective-permute-start | bytes 786440 | tf_op jit(solution)/shard_map/ppermute | solution.py:301
  389.4 25.1 %collective-permute-start.56 = (bf16[2,2,64,512]{3,2,0,1:T(8,128)(2,1)S(1)}, bf16[2,2,64,512]{3,2,0,1:T(8,128)(2,1)S(1)}, u32[]{:S(2)}, u32[]{:S(2)}) collective-permute-start(bf16[2,2,64,512]{3,2,0,1:T(8,128)(2,1)S(1)} %get-tuple-element.149), channel_id=1, source_target_pairs={{0,16},{1,17},{2,18},{3,19},{4,20},{5,21},{6,22},{7,23},{8,24},{9,... | collective-permute-start | bytes 786440 | tf_op jit(solution)/shard_map/ppermute | solution.py:301
  402.5 12.0 %collective-permute-start.55 = (bf16[2,2,64,512]{3,2,0,1:T(8,128)(2,1)S(1)}, bf16[2,2,64,512]{3,2,0,1:T(8,128)(2,1)S(1)}, u32[]{:S(2)}, u32[]{:S(2)}) collective-permute-start(bf16[2,2,64,512]{3,2,0,1:T(8,128)(2,1)S(1)} %get-tuple-element.148), channel_id=1, source_target_pairs={{0,8},{1,9},{2,10},{3,11},{4,12},{5,13},{6,14},{7,15},{8,0},{9,1},... | collective-permute-start | bytes 786440 | tf_op jit(solution)/shard_map/ppermute | solution.py:301
  402.8 12.1 %collective-permute-start.50 = (bf16[2,64,512]{2,0,1:T(2,128)(2,1)S(1)}, bf16[2,64,512]{2,0,1:T(2,128)(2,1)S(1)}, u32[]{:S(2)}, u32[]{:S(2)}) collective-permute-start(bf16[2,64,512]{2,0,1:T(2,128)(2,1)S(1)} %copy.242), channel_id=1, source_target_pairs={{0,2},{1,3},{2,0},{3,1},{4,6},{5,7},{6,4},{7,5},{8,10},{9,11},{10,... | collective-permute-start | bytes 393224 | tf_op jit(solution)/shard_map/ppermute | solution.py:301
  414.8 2.0 collective-permute-start.58
  461.5 49.8 %collective-permute-start.33 = (bf16[592,1024]{1,0:T(8,128)(2,1)}, bf16[592,1024]{1,0:T(8,128)(2,1)}, u32[]{:S(2)}, u32[]{:S(2)}) collective-permute-start(bf16[592,1024]{1,0:T(8,128)(2,1)} %slice.517), channel_id=1, source_target_pairs={{0,2},{1,3},{2,0},{3,1},{4,6},{5,7},{6,4},{7,5},{8,10},{9,11},{10,... | collective-permute-start | bytes 3637256 | tf_op jit(solution)/shard_map/ppermute | solution.py:301
  468.2 25.4 %collective-permute-start.35 = (bf16[4,2,2,64,512]{4,3,2,1,0:T(8,128)(2,1)}, bf16[4,2,2,64,512]{4,3,2,1,0:T(8,128)(2,1)}, u32[]{:S(2)}, u32[]{:S(2)}) collective-permute-start(bf16[4,2,2,64,512]{4,3,2,1,0:T(8,128)(2,1)} %bitcast.501), channel_id=1, source_target_pairs={{0,1},{1,0},{2,3},{3,2},{4,5},{5,4},{6,7},{7,6},{8,9},{9,8},{10,11... | collective-permute-start | bytes 3145736 | tf_op jit(solution)/shard_map/ppermute | solution.py:301
  480.8 26.4 %collective-permute-start.37 = (bf16[2,4,2,64,512]{4,3,2,1,0:T(8,128)(2,1)}, bf16[2,4,2,64,512]{4,3,2,1,0:T(8,128)(2,1)}, u32[]{:S(2)}, u32[]{:S(2)}) collective-permute-start(bf16[2,4,2,64,512]{4,3,2,1,0:T(8,128)(2,1)} %fusion.42), channel_id=1, source_target_pairs={{0,4},{1,5},{2,6},{3,7},{4,0},{5,1},{6,2},{7,3},{8,12},{9,13},{10,... | collective-permute-start | bytes 3145736 | tf_op jit(solution)/shard_map/ppermute | solution.py:301
  496.8 63.7 %collective-permute-start.36 = (bf16[4,2,64,512]{3,2,1,0:T(8,128)(2,1)}, bf16[4,2,64,512]{3,2,1,0:T(8,128)(2,1)}, u32[]{:S(2)}, u32[]{:S(2)}) collective-permute-start(bf16[4,2,64,512]{3,2,1,0:T(8,128)(2,1)} %dynamic-slice_bitcast_fusion.3), channel_id=1, source_target_pairs={{0,4},{1,5},{2,6},{3,7},{4,0},{5,1},{6,2},{7,3},{8,12},{9,13},{10,... | collective-permute-start | bytes 1572872 | tf_op jit(solution)/shard_map/ppermute | solution.py:301
  509.7 52.0 %collective-permute-start.38 = (bf16[4,2,64,512]{3,2,1,0:T(8,128)(2,1)}, bf16[4,2,64,512]{3,2,1,0:T(8,128)(2,1)}, u32[]{:S(2)}, u32[]{:S(2)}) collective-permute-start(bf16[4,2,64,512]{3,2,1,0:T(8,128)(2,1)} %slice_bitcast_fusion.4), channel_id=1, source_target_pairs={{0,1},{1,0},{2,3},{3,2},{4,5},{5,4},{6,7},{7,6},{8,9},{9,8},{10,11... | collective-permute-start | bytes 1572872 | tf_op jit(solution)/shard_map/ppermute | solution.py:301
  514.8 45.7 %copy-start.35 = (bf16[4,2,2,64,512]{4,3,2,1,0:T(8,128)(2,1)S(1)}, bf16[4,2,2,64,512]{4,3,2,1,0:T(8,128)(2,1)}, u32[]{:S(2)}) copy-start(bf16[4,2,2,64,512]{4,3,2,1,0:T(8,128)(2,1)} %copy-done.34) | copy-start | bytes 3145732
  517.5 44.2 %copy-start.32 = (bf16[2,4,2,64,512]{4,3,2,1,0:T(8,128)(2,1)S(1)}, bf16[2,4,2,64,512]{4,3,2,1,0:T(8,128)(2,1)}, u32[]{:S(2)}) copy-start(bf16[2,4,2,64,512]{4,3,2,1,0:T(8,128)(2,1)} %copy-done.31) | copy-start | bytes 3145732
  557.5 14.7 %collective-permute-start.34 = (bf16[289,1024]{1,0:T(8,128)(2,1)S(1)}, bf16[289,1024]{1,0:T(8,128)(2,1)S(1)}, u32[]{:S(2)}, u32[]{:S(2)}) collective-permute-start(bf16[289,1024]{1,0:T(8,128)(2,1)S(1)} %slice.345), channel_id=1, source_target_pairs={{0,1},{1,0},{2,3},{3,2},{4,5},{5,4},{6,7},{7,6},{8,9},{9,8},{10,11... | collective-permute-start | bytes 1775624 | tf_op jit(solution)/shard_map/ppermute | solution.py:301
  562.9 11.2 %collective-permute-start.41 = (bf16[2,2,64,512]{3,2,1,0:T(8,128)(2,1)S(1)}, bf16[2,2,64,512]{3,2,1,0:T(8,128)(2,1)S(1)}, u32[]{:S(2)}, u32[]{:S(2)}) collective-permute-start(bf16[2,2,64,512]{3,2,1,0:T(8,128)(2,1)S(1)} %get-tuple-element.156), channel_id=1, source_target_pairs={{0,24},{1,25},{2,26},{3,27},{4,28},{5,29},{6,30},{7,31},{8,16},{9,... | collective-permute-start | bytes 786440 | tf_op jit(solution)/shard_map/ppermute | solution.py:301
  564.6 23.3 %collective-permute-start.40 = (bf16[2,2,64,512]{3,2,1,0:T(8,128)(2,1)S(1)}, bf16[2,2,64,512]{3,2,1,0:T(8,128)(2,1)S(1)}, u32[]{:S(2)}, u32[]{:S(2)}) collective-permute-start(bf16[2,2,64,512]{3,2,1,0:T(8,128)(2,1)S(1)} %get-tuple-element.155), channel_id=1, source_target_pairs={{0,16},{1,17},{2,18},{3,19},{4,20},{5,21},{6,22},{7,23},{8,24},{9,... | collective-permute-start | bytes 786440 | tf_op jit(solution)/shard_map/ppermute | solution.py:301
  566.7 21.2 %collective-permute-start.39 = (bf16[2,2,64,512]{3,2,1,0:T(8,128)(2,1)S(1)}, bf16[2,2,64,512]{3,2,1,0:T(8,128)(2,1)S(1)}, u32[]{:S(2)}, u32[]{:S(2)}) collective-permute-start(bf16[2,2,64,512]{3,2,1,0:T(8,128)(2,1)S(1)} %get-tuple-element.154), channel_id=1, source_target_pairs={{0,8},{1,9},{2,10},{3,11},{4,12},{5,13},{6,14},{7,15},{8,0},{9,1},... | collective-permute-start | bytes 786440 | tf_op jit(solution)/shard_map/ppermute | solution.py:301
  588.2 3.5 collective-permute-start.42
  (95 other events, 814.1 us)

commit v2 on v1

--- a/solution.py
+++ b/solution.py
@@ -291,6 +291,8 @@
 BOTH = ("dp", "tensor")
 HALF_PAD = 8
 LANES = 128
+LOW = jnp.bfloat16
+VMEM_ROOM = 56 * 2**20
 
 
 def exchange(value, far_z=0, far_x=0, far_core=0, far_y=0):
@@ -311,75 +313,225 @@
     return lax.optimization_barrier((value, *others))[0]
 
 
-def gather_start(shard, core):
-    keep = jnp.where(core == 0, shard[0], shard[1])
-    send = jnp.where(core == 0, shard[1], shard[0])
-    return pick_two(core, keep, exchange(send, far_core=1), 1)
-
-
-def gather_z(piece, place_z):
-    found = [piece] + [exchange(piece, far_z=step) for step in (1, 2, 3)]
-    ordered = [lax.select_n(place_z ^ spot, *found) for spot in range(4)]
-    return jnp.stack(ordered, 1)
-
-
-def gather_plane_one(ordered):
-    return exchange(ordered[0], far_x=1), exchange(ordered[1], far_y=1)
-
-
-def gather_plane_two(ordered, crossed, place_x):
-    one = pick_two(place_x, ordered[0], crossed[0], 1)
-    two = jnp.stack([ordered[1], crossed[1]])
-    return one, two, exchange(one, far_y=1), exchange(two, far_x=1)
-
-
-def gather_finish(parts, place_x):
-    one, two, one_far, two_far = parts
-    wide = one.shape[-1]
-    two_all = pick_two(place_x, two, two_far, 2)
-    pieces = [one, one_far, two_all[0], two_all[1]]
-    return jnp.concatenate([piece.reshape(-1, wide) for piece in pieces], 1)
-
-
-def scatter_sum(pieces, place_x, place_z, core):
-    rows, wide = pieces[0].shape
-    pieces = [piece.reshape(4, 2, 2, rows // 16, wide) for piece in pieces]
-
-    def low_sum(left, right):
-        return (left.astype(jnp.float32) + right.astype(jnp.float32)).astype(jnp.bfloat16)
-
-    def split_x(value, axis):
-        keep = lax.dynamic_index_in_dim(value, place_x, axis, keepdims=False)
-        send = lax.dynamic_index_in_dim(value, 1 - place_x, axis, keepdims=False)
-        return keep, send
-
-    two_keep, two_send = split_x(jnp.stack(pieces[2:]), 2)
-    one_far = exchange(pieces[1], far_y=1)
-    two_far = exchange(two_send, far_x=1)
-    one_keep, one_send = split_x(low_sum(pieces[0], one_far), 1)
-    two = low_sum(two_keep, two_far)
-    one_far = exchange(one_send, far_x=1)
-    two_far = exchange(two[1], far_y=1)
-    both = jnp.stack([low_sum(one_keep, one_far), low_sum(two[0], two_far)], 1)
-    total = lax.dynamic_index_in_dim(both, place_z, 0, keepdims=False).astype(jnp.float32)
-    for step in (1, 2, 3):
-        piece = lax.dynamic_index_in_dim(both, place_z ^ step, 0, keepdims=False)
-        total = total + exchange(piece, far_z=step).astype(jnp.float32)
-    total = total.astype(jnp.bfloat16)
+def pack(places, sources, shapes, plan):
+    def kernel(places_ref, *refs):
+        ins, outs = refs[: len(sources)], refs[len(sources) :]
+        spots = [places_ref[at] for at in range(4)]
+        for at, take, to, put in plan:
+            outs[to][put(*spots)] = ins[at][take(*spots)]
+
+    return pl.pallas_call(
+        kernel,
+        in_specs=[pl.BlockSpec(memory_space=pltpu.SMEM)]
+        + [pl.BlockSpec(memory_space=pltpu.VMEM)] * len(sources),
+        out_specs=[pl.BlockSpec(memory_space=pltpu.VMEM)] * len(shapes),
+        out_shape=[jax.ShapeDtypeStruct(shape, LOW) for shape in shapes],
+        compiler_params=pltpu.CompilerParams(vmem_limit_bytes=VMEM_ROOM),
+        cost_estimate=pl.CostEstimate(
+            flops=0,
+            transcendentals=0,
+            bytes_accessed=sum(2 * source.size * 2 for source in sources),
+        ),
+    )(places, *sources)
+
+
+def gather_weights(keep, send, places, core):
+    deep, wide = keep.shape[1:]
+    every = slice(None)
+    piece = pick_two(core, keep, exchange(send, far_core=1), 1).reshape(2, 2 * deep, wide)
+    line = [piece] + [exchange(piece, far_z=step) for step in (1, 2, 3)]
+    rows = 2 * deep
+    plan = []
+    for step in range(4):
+        for part in range(2):
+            plan.append(
+                (
+                    step,
+                    lambda z, x, c, y, part=part: part,
+                    part,
+                    lambda z, x, c, y, step=step: z ^ step,
+                )
+            )
+    one, two = pack(places, line, [(4, rows, wide)] * 2, plan)
+    one_x, two_y = exchange(one, far_x=1), exchange(two, far_y=1)
+    plan = [
+        (0, lambda z, x, c, y: every, 0, lambda z, x, c, y: x),
+        (1, lambda z, x, c, y: every, 0, lambda z, x, c, y: 1 - x),
+        (2, lambda z, x, c, y: every, 1, lambda z, x, c, y: 0),
+        (3, lambda z, x, c, y: every, 1, lambda z, x, c, y: 1),
+    ]
+    one_pair, two_pair = pack(places, [one, one_x, two, two_y], [(2, 4, rows, wide)] * 2, plan)
+    one_y, two_x = exchange(one_pair, far_y=1), exchange(two_pair, far_x=1)
+    most = 3 * wide // 4
+    plan = []
+    for to, low, high in ((0, 0, most), (1, most, wide)):
+        span = high - low
+        for place_z in range(4):
+            for far in range(2):
+                for number in range(2):
+                    plan.append(
+                        (
+                            number,
+                            lambda z, x, c, y, a=far, p=place_z, lo=low, hi=high: (
+                                a,
+                                p,
+                                every,
+                                slice(lo, hi),
+                            ),
+                            to,
+                            lambda z, x, c, y, a=far, p=place_z, s=span, n=number: (
+                                p,
+                                a,
+                                every,
+                                slice(n * s, n * s + s),
+                            ),
+                        )
+                    )
+                    plan.append(
+                        (
+                            2 + far,
+                            lambda z, x, c, y, n=number, p=place_z, lo=low, hi=high: (
+                                n,
+                                p,
+                                every,
+                                slice(lo, hi),
+                            ),
+                            to,
+                            lambda z, x, c, y, f=far, p=place_z, s=span, n=number: (
+                                p,
+                                x ^ f,
+                                every,
+                                slice((2 + n) * s, (3 + n) * s),
+                            ),
+                        )
+                    )
+    shapes = [(4, 2, rows, 4 * most), (4, 2, rows, 4 * (wide - most))]
+    full, rest = pack(places, [one_pair, one_y, two_pair, two_x], shapes, plan)
+    return full.reshape(8 * rows, -1), rest.reshape(8 * rows, -1)
+
+
+def low_add(*values):
+    total = values[0].astype(jnp.float32)
+    for value in values[1:]:
+        total = total + value.astype(jnp.float32)
+    return total
+
+
+def line_kernel(one_ref, one_a, one_b, two_ref, two_a, two_b, own_ref, *send_refs):
+    tall = own_ref.shape[1]
+    for step in range(4):
+        rows = slice(step * tall, (step + 1) * tall)
+        one = low_add(one_ref[0, rows], one_a[0, rows], one_b[rows])
+        two = low_add(two_ref[0, rows], two_a[0, rows], two_b[rows])
+        if step == 0:
+            own_ref[0] = one
+            own_ref[1] = two
+        else:
+            send_refs[step - 1][0] = one.astype(LOW)
+            send_refs[step - 1][1] = two.astype(LOW)
+
+
+def scatter_sum(send_one, send_two, keep_one, keep_two, core):
+    lines, wide = send_one.shape[1:]
+    tall = lines // 4
+    one_y, two_x = exchange(send_one, far_y=1), exchange(send_two, far_x=1)
+    one_x = exchange(low_add(keep_one[1], one_y[1]).astype(LOW), far_x=1)
+    two_y = exchange(low_add(keep_two[1], two_x[1]).astype(LOW), far_y=1)
+    first = pl.BlockSpec((1, lines, wide), lambda i: (0, 0, 0))
+    flat = pl.BlockSpec((lines, wide), lambda i: (0, 0))
+    piece = pl.BlockSpec((2, tall, wide), lambda i: (0, 0, 0))
+    sends = pl.pallas_call(
+        line_kernel,
+        grid=(1,),
+        in_specs=[first, first, flat, first, first, flat],
+        out_specs=[piece] * 4,
+        out_shape=[jax.ShapeDtypeStruct((2, tall, wide), jnp.float32)]
+        + [jax.ShapeDtypeStruct((2, tall, wide), LOW)] * 3,
+        compiler_params=pltpu.CompilerParams(vmem_limit_bytes=VMEM_ROOM),
+        cost_estimate=pl.CostEstimate(
+            flops=lines * wide * 4, transcendentals=0, bytes_accessed=lines * wide * 18
+        ),
+    )(keep_one, one_y, one_x, keep_two, two_x, two_y)
+    total = low_add(
+        sends[0], *[exchange(sends[step], far_z=step) for step in (1, 2, 3)]
+    ).reshape(2, 2, tall // 2, wide)
     keep = lax.dynamic_index_in_dim(total, core, 1, keepdims=False)
     send = lax.dynamic_index_in_dim(total, 1 - core, 1, keepdims=False)
-    owned = pick_two(core, keep, exchange(send, far_core=1), 0)
-    return owned.astype(jnp.float32).transpose(2, 0, 1, 3)
+    far = exchange(send.astype(LOW), far_core=1).astype(jnp.float32)
+    return pick_two(core, keep, far, 0)
+
+
+def vector_sum(vector):
+    for step in ({"far_core": 1}, {"far_y": 1}, {"far_x": 1}):
+        vector = vector + exchange(vector, **step)
+    others = [exchange(vector, far_z=step) for step in (1, 2, 3)]
+    return vector + others[0] + others[1] + others[2]
+
+
+def mat_far(left, right):
+    return lax.dot_general(
+        left, right, (((1,), (1,)), ((), ())), preferred_element_type=jnp.float32
+    )
+
+
+def mat_rows(left, right):
+    return lax.dot_general(
+        left, right, (((0,), (0,)), ((), ())), preferred_element_type=jnp.float32
+    )
+
+
+def pair_kernel(places_ref, own_ref, far_ref, rows_ref, turned_ref):
+    spots = [places_ref[0] ^ (block % 4) for block in range(8)]
+    for block in range(8):
+        at = spots[block] * 2 + (places_ref[1] ^ (block // 4))
+        start = pl.multiple_of(at * LANES, LANES)
+        for half, ref in enumerate((own_ref, far_ref)):
+            turned_ref[half, :, block * LANES : (block + 1) * LANES] = ref[:, pl.ds(start, LANES)]
+    rows_ref[0] = own_ref[...]
+    rows_ref[1] = far_ref[...]
+
+
+def pair_up(places, own):
+    rows, width = own.shape
+    made = pl.pallas_call(
+        pair_kernel,
+        in_specs=[pl.BlockSpec(memory_space=pltpu.SMEM)]
+        + [pl.BlockSpec(memory_space=pltpu.VMEM)] * 2,
+        out_specs=[pl.BlockSpec(memory_space=pltpu.VMEM)] * 2,
+        out_shape=[jax.ShapeDtypeStruct((2, rows, width), LOW)] * 2,
+        compiler_params=pltpu.CompilerParams(vmem_limit_bytes=VMEM_ROOM),
+        cost_estimate=pl.CostEstimate(
+            flops=0, transcendentals=0, bytes_accessed=own.size * 12
+        ),
+    )(places, own, exchange(own, far_core=1))
+    return [array.reshape(2 * rows, width) for array in made]
+
+
+def half_sums(left, right, rows):
+    send = mat_far(left[rows:], right).astype(LOW)
+    far = exchange(send, far_core=1)
+    return mat_far(left[:rows], right) + far.astype(jnp.float32)
+
+
+def scatter_grads(pairs, core):
+    lines = pairs[0][0].shape[1] // 2
+
+    def grads(row_far, part, y_far):
+        made = []
+        for left, cut in pairs:
+            left = left if row_far is None else left[:, row_far * lines : (row_far + 1) * lines]
+            made.append(mat_rows(left, cut(part, y_far)).astype(LOW))
+        return made[0] if len(made) == 1 else jnp.concatenate(made, 1)
+
+    send_one = grads(None, 0, 1).reshape(2, lines, -1)
+    send_two = jnp.stack([grads(1, 1, 0), grads(1, 1, 1)])
+    keep_one = grads(None, 0, 0).reshape(2, lines, -1)
+    keep_two = jnp.stack([grads(0, 1, 0), grads(0, 1, 1)])
+    return scatter_sum(send_one, send_two, keep_one, keep_two, core)
 
 
 def lane_of(shape):
     return lax.broadcasted_iota(jnp.int32, shape, 1)
-
-
-def dot_lanes(left, right):
-    return lax.dot_general(
-        left, right, (((1,), (1,)), ((), ())), preferred_element_type=jnp.float32
-    )
 
 
 def head_views(query, key, bias, head):
@@ -400,9 +552,9 @@
     sums, tops = [], []
     for head in range(2):
         mine, query_view, key_view = head_views(query, key, bias, head)
-        scores = dot_lanes(query_view, key_view)
+        scores = mat_far(query_view, key_view)
         top = jnp.max(scores, axis=1, keepdims=True)
-        weight = jnp.exp(scores - top).astype(jnp.bfloat16)
+        weight = jnp.exp(scores - top).astype(LOW)
         value_view = jnp.where(mine, value, jnp.ones_like(value))
         sums.append(jnp.dot(weight, value_view, preferred_element_type=jnp.float32))
         tops.append(top)
@@ -410,7 +562,7 @@
     upper = jnp.where(low, sums[0], sums[1])
     lower = jnp.where(low, sums[1], sums[0])
     lower = pltpu.roll(lower, HDIM, 1)
-    mixed_ref[...] = (upper / lower).astype(jnp.bfloat16)
+    mixed_ref[...] = (upper / lower).astype(LOW)
     total = jnp.where(low, tops[0], tops[1]) + jnp.log(lower)
     total = jnp.transpose(total)
     total_ref[0, 0:1, :] = total[0:1]
@@ -429,10 +581,10 @@
     for head in range(2):
         mine, query_view, key_view = head_views(query, key, bias, head)
         zero = jnp.zeros_like(query)
-        scores = dot_lanes(key_view, query_view)
+        scores = mat_far(key_view, query_view)
         probs = jnp.exp(scores - total_ref[0, head : head + 1, :])
         grad_view = jnp.where(mine, grad, zero)
-        grad_probs = dot_lanes(value, grad_view)
+        grad_probs = mat_far(value, grad_view)
         ones = jnp.where(mine[0:8], 1.0, 0.0)
         inner = lax.dot_general(
             ones,
@@ -441,25 +593,18 @@
             precision=lax.Precision.HIGHEST,
             preferred_element_type=jnp.float32,
         )
-        grad_scores = (probs * (grad_probs - inner[0:1])).astype(jnp.bfloat16)
-        one_value = jnp.dot(
-            probs.astype(jnp.bfloat16), grad_view, preferred_element_type=jnp.float32
-        )
+        grad_scores = (probs * (grad_probs - inner[0:1])).astype(LOW)
+        one_value = jnp.dot(probs.astype(LOW), grad_view, preferred_element_type=jnp.float32)
         one_key = jnp.dot(
             grad_scores, jnp.where(mine, query, zero), preferred_element_type=jnp.float32
         )
-        one_query = lax.dot_general(
-            grad_scores,
-            jnp.where(mine, key, zero),
-            (((0,), (0,)), ((), ())),
-            preferred_element_type=jnp.float32,
-        )
+        one_query = mat_rows(grad_scores, jnp.where(mine, key, zero))
         grad_query = one_query if head == 0 else grad_query + one_query
         grad_key = one_key if head == 0 else grad_key + one_key
         grad_value = one_value if head == 0 else grad_value + one_value
-    out_ref[:, 0:LANES] = (grad_query * scale).astype(jnp.bfloat16)
-    out_ref[:, LANES : 2 * LANES] = grad_key.astype(jnp.bfloat16)
-    out_ref[:, 2 * LANES : 3 * LANES] = grad_value.astype(jnp.bfloat16)
+    out_ref[:, 0:LANES] = (grad_query * scale).astype(LOW)
+    out_ref[:, LANES : 2 * LANES] = grad_key.astype(LOW)
+    out_ref[:, 2 * LANES : 3 * LANES] = grad_value.astype(LOW)
 
 
 def attend_all(qkv, bias, rows):
@@ -477,10 +622,10 @@
             pl.BlockSpec((1, 8, rows), lambda i, j: (i * blocks + j, 0, 0)),
         ],
         out_shape=[
-            jax.ShapeDtypeStruct((images * rows, blocks * LANES), jnp.bfloat16),
+            jax.ShapeDtypeStruct((images * rows, blocks * LANES), LOW),
             jax.ShapeDtypeStruct((images * blocks, 8, rows), jnp.float32),
         ],
-        compiler_params=pltpu.CompilerParams(vmem_limit_bytes=32 * 2**20),
+        compiler_params=pltpu.CompilerParams(vmem_limit_bytes=VMEM_ROOM),
         cost_estimate=pl.CostEstimate(
             flops=images * blocks * 2 * 2 * 2 * rows * rows * LANES * 2,
             transcendentals=images * blocks * 2 * rows * rows,
@@ -503,8 +648,8 @@
             pl.BlockSpec((1, 8, rows), lambda i, j: (i * blocks + j, 0, 0)),
         ],
         out_specs=pl.BlockSpec((rows, 3 * LANES), lambda i, j: (i, j)),
-        out_shape=jax.ShapeDtypeStruct(qkv.shape, jnp.bfloat16),
-        compiler_params=pltpu.CompilerParams(vmem_limit_bytes=48 * 2**20),
+        out_shape=jax.ShapeDtypeStruct(qkv.shape, LOW),
+        compiler_params=pltpu.CompilerParams(vmem_limit_bytes=VMEM_ROOM),
         cost_estimate=pl.CostEstimate(
             flops=images * blocks * 2 * 5 * 2 * rows * rows * LANES * 2,
             transcendentals=images * blocks * 2 * rows * rows,
@@ -517,18 +662,6 @@
     return jnp.dot(left, right, preferred_element_type=jnp.float32)
 
 
-def mat_far(left, right):
-    return lax.dot_general(
-        left, right, (((1,), (1,)), ((), ())), preferred_element_type=jnp.float32
-    )
-
-
-def mat_rows(left, right):
-    return lax.dot_general(
-        left, right, (((0,), (0,)), ((), ())), preferred_element_type=jnp.float32
-    )
-
-
 def flat_norm(values, gain, shift):
     center = values - jnp.mean(values, axis=-1, keepdims=True)
     spread = lax.rsqrt(jnp.mean(center * center, axis=-1, keepdims=True) + EPS)
@@ -544,6 +677,10 @@
         - unit * jnp.mean(scaled * unit, axis=-1, keepdims=True)
     )
     return spread * inner, jnp.sum(upstream * unit, axis=0), jnp.sum(upstream, axis=0)
+
+
+def column_flat(values):
+    return jnp.sum(values.astype(jnp.float32), axis=0)
 
 
 def whole_images(
@@ -566,16 +703,49 @@
     down_weight,
     down_bias,
 ):
-    low = jnp.bfloat16
     dp_place = lax.axis_index("dp")
     place_y = lax.axis_index("tensor")
     core, place_x, place_z = dp_place % 2, (dp_place // 2) % 2, dp_place // 4
+    places = jnp.stack([place_z, place_x, core, place_y]).astype(jnp.int32)
     strip, width = images.shape[1:]
     half = -(-strip // HALF_PAD) * HALF_PAD
     rows = 2 * half
     depth, head_cols = query_weight.shape
     units = up_weight.shape[1]
-    head_part, unit_part = head_cols // 4, units // 4
+
+    def feed_part(place):
+        wide = units // 2
+        return jnp.concatenate(
+            [
+                lax.dynamic_slice_in_dim(up_weight, place * wide, wide, 1),
+                lax.dynamic_slice_in_dim(down_weight, place * wide, wide, 0).T,
+            ],
+            1,
+        )
+
+    feed = pick_two(core, feed_part(core), exchange(feed_part(1 - core), far_core=1), 0)
+    groups = [
+        [place for place in range(32) if (place // 2) % 2 == at] for at in range(2)
+    ]
+    feed_full = lax.all_gather(
+        feed.reshape(2 * depth, units),
+        BOTH,
+        axis=0,
+        tiled=True,
+        axis_index_groups=groups,
+    ).reshape(8, 2, 2 * depth, units)
+    upper_full = feed_full[..., : units // 2].transpose(0, 2, 1, 3).reshape(width, units)
+    lower_full = feed_full[..., units // 2 :].transpose(0, 2, 1, 3).reshape(width, units)
+
+    def core_parts(place):
+        cuts = [
+            lax.dynamic_slice_in_dim(weight, place * (head_cols // 2), head_cols // 2, 1)
+            for weight in (query_weight, key_weight, value_weight, output_weight.T)
+        ]
+        spans = [slice(0, head_cols // 4), slice(head_cols // 4, head_cols // 2)]
+        return jnp.stack([jnp.concatenate([cut[:, span] for cut in cuts], 1) for span in spans])
+
+    qkv_full, output_full = gather_weights(core_parts(core), core_parts(1 - core), places, core)
 
     stacked = jnp.stack([images, cotangent])
     stacked = jnp.pad(stacked, ((0, 0), (0, 0), (0, half - strip), (0, 0)))
@@ -584,61 +754,31 @@
     arrived = exchange(theirs, far_y=1)
     whole = jnp.stack([mine, arrived], 1).reshape(2, rows, width)
 
-    def four(weight):
-        return weight.reshape(depth, 2, 2, -1)
-
-    def by_core(parts):
-        return jnp.concatenate(parts, 3).transpose(1, 2, 0, 3)
-
-    shard_one = by_core([four(query_weight), four(key_weight), four(value_weight)])
-    shard_two = by_core([four(output_weight.T), four(up_weight)])
-    shard_three = by_core([four(down_weight.T)])
-
-    start_one = gather_start(shard_one, core)
-    line_one = gather_z(start_one, place_z)
-    cross_one = gather_plane_one(line_one)
-    parts_one = gather_plane_two(line_one, cross_one, place_x)
-    qkv_full = gather_finish(parts_one, place_x)
-
-    start_two = after(gather_start(shard_two, core), line_one)
-    line_two = gather_z(start_two, place_z)
-    cross_two = gather_plane_one(after(line_two, *parts_one))
-    parts_two = gather_plane_two(line_two, cross_two, place_x)
-    pair_full = gather_finish(parts_two, place_x)
-    pair_full = pair_full.reshape(width, 4, head_part + unit_part)
-    output_full = pair_full[:, :, :head_part].reshape(width, 4 * head_part)
-    upper_full = pair_full[:, :, head_part:].reshape(width, 4 * unit_part)
-
-    start_three = after(gather_start(shard_three, core), line_two)
-    line_three = gather_z(start_three, place_z)
-    cross_three = gather_plane_one(after(line_three, *parts_two))
-    parts_three = gather_plane_two(line_three, cross_three, place_x)
-    lower_full = gather_finish(parts_three, place_x)
-
-    def local_columns(vector):
-        wide = vector.shape[0] // 8
-        table = vector.astype(jnp.float32).reshape(2, 2, 2, wide)
+    def head_columns(vector):
+        table = vector.astype(jnp.float32).reshape(2, 2, 2, -1)
         table = lax.dynamic_index_in_dim(table, core, 1, keepdims=False)
         table = jnp.where(place_y == 0, table, table[::-1])
-        return table.transpose(1, 0, 2)
-
-    def spread_columns(vector):
-        wide = vector.shape[0] // 4
-        table = vector.reshape(2, 2, wide).transpose(1, 0, 2)
-        table = jnp.where(place_y == 0, table, table[::-1])
+        return table.transpose(1, 0, 2).reshape(4, 1, -1)
+
+    def spread_core(table):
         table = jnp.stack(
             [jnp.where(core == 0, table, 0.0), jnp.where(core == 1, table, 0.0)], 1
         )
         return table.reshape(-1)
 
+    def head_spread(vector):
+        table = vector.reshape(2, 2, -1).transpose(1, 0, 2)
+        return spread_core(jnp.where(place_y == 0, table, table[::-1]))
+
     gain_one, shift_one = first_gain.astype(jnp.float32), first_shift.astype(jnp.float32)
     gain_two, shift_two = second_gain.astype(jnp.float32), second_shift.astype(jnp.float32)
-    query_shift = local_columns(query_bias).reshape(4, 1, head_part)
-    value_shift = local_columns(value_bias).reshape(4, 1, head_part)
+    query_shift, value_shift = head_columns(query_bias), head_columns(value_bias)
     qkv_shift = jnp.concatenate(
         [query_shift, jnp.zeros_like(query_shift), value_shift], 1
     ).reshape(-1)
-    up_shift = local_columns(up_bias).reshape(-1)
+    up_shift = lax.dynamic_index_in_dim(
+        up_bias.astype(jnp.float32).reshape(2, 2, -1), core, 1, keepdims=False
+    ).reshape(-1)
 
     row = jnp.arange(rows)
     in_half = row % half
@@ -647,53 +787,58 @@
     live = lax.dynamic_index_in_dim(slot_live, place_y, 0, keepdims=False).astype(jnp.float32)
     row_mask = (live * ok.astype(jnp.float32))[:, None]
     key_bias = jnp.broadcast_to(
-        jnp.where(ok, 0.0, NEGATIVE).astype(low)[:, None], (rows, LANES)
-    )
-
-    def pair_up(own):
-        return jnp.concatenate([own, exchange(own, far_core=1)], 0)
-
-    def pair_sum(partial):
-        other = exchange(partial[rows:].astype(low), far_core=1)
-        return partial[:rows] + other.astype(jnp.float32)
+        jnp.where(ok, 0.0, NEGATIVE).astype(LOW)[:, None], (rows, LANES)
+    )
 
     resid = whole[0].astype(jnp.float32)
     grad_top = row_mask * whole[1].astype(jnp.float32)
-    fed_grad = grad_top.astype(low)
-    fed_rows = pair_up(fed_grad)
+    fed_grad = grad_top.astype(LOW)
+    fed_rows, fed_turned = pair_up(places, fed_grad)
     normed, unit_one, spread_one = flat_norm(resid, gain_one, shift_one)
-    normed_rows = pair_up(normed.astype(low))
-    qkv = (mat(normed_rows, qkv_full) + qkv_shift).astype(low)
+    normed_rows, normed_turned = pair_up(places, normed.astype(LOW))
+    qkv = (mat(normed_rows, qkv_full) + qkv_shift).astype(LOW)
     mixed, totals = attend_all(qkv, key_bias, rows)
-    attended = pair_sum(mat_far(mixed, output_full)) + output_bias.astype(jnp.float32)
+    attended = half_sums(mixed, output_full, rows) + output_bias.astype(jnp.float32)
     middle = row_mask * (resid + attended)
     second, unit_two, spread_two = flat_norm(middle, gain_two, shift_two)
-    second_rows = pair_up(second.astype(low))
+    second_rows, second_turned = pair_up(places, second.astype(LOW))
     hidden = mat(second_rows, upper_full) + up_shift
     sigma = jax.nn.sigmoid(SLOPE * hidden)
-    active = (hidden * sigma).astype(low)
-    slope = (sigma + SLOPE * hidden * sigma * (1.0 - sigma)).astype(low)
-
-    def weight_pieces(left, right):
-        wide = right.shape[1] // 4
-        return [
-            mat_rows(left, right[:, at * wide : (at + 1) * wide]).astype(low) for at in range(4)
-        ]
-
-    lower_owned = scatter_sum(weight_pieces(fed_rows, active), place_x, place_z, core)
-    hidden_grad = (mat(fed_rows, lower_full) * slope.astype(jnp.float32)).astype(low)
-    upper_owned = scatter_sum(weight_pieces(second_rows, hidden_grad), place_x, place_z, core)
-    second_grad = pair_sum(mat_far(hidden_grad, upper_full))
-    fed = pair_sum(mat_far(active, lower_full)) + down_bias.astype(jnp.float32)
-    layer_own = (row_mask * (middle + fed)).astype(low)
+    active = (hidden * sigma).astype(LOW)
+    slope = (sigma + SLOPE * hidden * sigma * (1.0 - sigma)).astype(LOW)
+
+    def unit_cut(array):
+        wide = units // 4
+
+        def cut(part, y_far):
+            start = (place_y ^ y_far) * 2 + part
+            return lax.dynamic_slice_in_dim(array, start * wide, wide, 1)
+
+        return cut
+
+    def head_cut(array):
+        wide = array.shape[1] // 4
+
+        def cut(part, y_far):
+            at = part * 2 + y_far
+            return array[:, at * wide : (at + 1) * wide]
+
+        return cut
+
+    lower_owned = scatter_grads([(fed_turned, unit_cut(active))], core)
+    hidden_grad = (mat(fed_rows, lower_full) * slope.astype(jnp.float32)).astype(LOW)
+    up_bias_sums = column_flat(hidden_grad)
+    upper_owned = scatter_grads([(second_turned, unit_cut(hidden_grad))], core)
+    second_grad = half_sums(hidden_grad, upper_full, rows)
+    fed = half_sums(active, lower_full, rows)
+    layer_own = (row_mask * (middle + fed + down_bias.astype(jnp.float32))).astype(LOW)
     middle_back, gain_two_grad, shift_two_grad = flat_norm_back(
         second_grad, unit_two, spread_two, gain_two
     )
     middle_grad = row_mask * (grad_top + middle_back)
-    attended_grad = middle_grad.astype(low)
-    attended_rows = pair_up(attended_grad)
-    grad_mixed = mat(attended_rows, output_full).astype(low)
-    output_pieces = weight_pieces(attended_rows, mixed)
+    attended_grad = middle_grad.astype(LOW)
+    attended_rows, attended_turned = pair_up(places, attended_grad)
+    grad_mixed = mat(attended_rows, output_full).astype(LOW)
     grad_qkv = attend_back_all(qkv, key_bias, grad_mixed, mixed, totals, rows)
     early = jnp.concatenate(
         [
@@ -701,65 +846,60 @@
             gain_two_grad,
             shift_two_grad,
             column_flat(fed_grad),
-            spread_columns(column_flat(hidden_grad)),
+            spread_core(up_bias_sums.reshape(2, -1)),
         ]
     )
-    qkv_pieces = weight_pieces(normed_rows, grad_qkv)
-    last_pieces = [
-        jnp.concatenate([left, right], 1) for left, right in zip(qkv_pieces, output_pieces)
-    ]
-    last_owned = scatter_sum(last_pieces, place_x, place_z, core)
-    normed_grad = pair_sum(mat_far(grad_qkv, qkv_full))
+    last_owned = scatter_grads(
+        [(normed_turned, head_cut(grad_qkv)), (attended_turned, head_cut(mixed))], core
+    )
+    normed_grad = half_sums(grad_qkv, qkv_full, rows)
     first_back, gain_one_grad, shift_one_grad = flat_norm_back(
         normed_grad, unit_one, spread_one, gain_one
     )
     images_own = middle_grad + first_back
-    qkv_sums = column_flat(grad_qkv).reshape(4, 3, head_part)
+    qkv_sums = column_flat(grad_qkv).reshape(4, 3, -1)
     late = jnp.concatenate(
         [
             gain_one_grad,
             shift_one_grad,
-            spread_columns(qkv_sums[:, 0].reshape(-1)),
-            spread_columns(qkv_sums[:, 2].reshape(-1)),
+            head_spread(qkv_sums[:, 0].reshape(-1)),
+            head_spread(qkv_sums[:, 2].reshape(-1)),
         ]
     )
 
-    def to_strips(own):
-        send = own[half : half + strip]
-        return pick_two(place_y, own[:strip], exchange(send, far_y=1), 0)
-
-    layer_out = to_strips(layer_own)
-    images_grad = to_strips(images_own.astype(low)).astype(jnp.float32)
-    early = lax.psum(early, BOTH)
-    late = lax.psum(late, BOTH)
-    owned = last_owned.reshape(depth, 2, 2, 4, head_part)
-
-    def full_columns(at):
-        return owned[:, :, :, at].reshape(depth, head_cols)
+    def to_strips(own, send):
+        return pick_two(place_y, own[:strip], exchange(send, far_y=1).astype(own.dtype), 0)
+
+    layer_out = to_strips(layer_own, layer_own[half : half + strip])
+    images_grad = to_strips(images_own, images_own[half : half + strip].astype(LOW))
+    early = jnp.sum(lax.all_gather(early, BOTH), axis=0)
+    late = vector_sum(late)
+
+    def full_columns(owned):
+        return owned.transpose(2, 0, 1, 3).reshape(depth, -1)
+
+    def head_grad(at):
+        return full_columns(last_owned[..., at * LANES : (at + 1) * LANES])
 
     return (
         layer_out,
         images_grad,
         late[:width],
         late[width : 2 * width],
-        full_columns(0),
+        head_grad(0),
         late[2 * width : 3 * width],
-        full_columns(1),
-        full_columns(2),
+        head_grad(1),
+        head_grad(2),
         late[3 * width :],
-        full_columns(3).T,
+        head_grad(3).T,
         early[:width],
         early[width : 2 * width],
         early[2 * width : 3 * width],
-        upper_owned.reshape(depth, units),
+        full_columns(upper_owned),
         early[4 * width :],
-        lower_owned.reshape(depth, units).T,
+        full_columns(lower_owned).T,
         early[3 * width : 4 * width],
     )
-
-
-def column_flat(values):
-    return jnp.sum(values.astype(jnp.float32), axis=0)
 
 
 def pick(mesh):

time: 609 us -> 534 us (0.88)
  other arithmetic: 101 us -> 25.7 us
  blocking collectives: 38.8 us -> 0 us
  Pallas kernels: 46.1 us -> 84.4 us
  local copies, waits for them, and re-layouts: 81.8 us -> 60.3 us
  between operations: 4.16 us -> 16.7 us
  matrix products: 85.6 us -> 97.1 us
  waiting for transfers between devices: 159 us -> 166 us
  starting transfers between devices: 80.6 us -> 74.3 us
    psum x1 -> x0, blocking collectives: 38.8 us -> none  [whole_images(): late = lax.psum(late, BOTH)]
    pallas_call x0 -> x10, Pallas kernels: none -> 37.2 us  [the longest x4 18.3 us: pair_up(): pl.pallas_call(pair_kernel, in_specs=[pl.BlockSpec(memory_space=pltpu.SME...]
    another operation x24 -> x11, other arithmetic: 32.9 us -> 3.82 us  [pick_two(): return jnp.stack([first, last], axis)]
    slice x24 -> x7, local copies, waits for them, and re-layouts: 27.8 us -> 0.2 us  [the longest x1 0.08 us: whole_images(): images_own[half:half + strip].astype(LOW)]
    transpose x5 -> x12, local copies, waits for them, and re-layouts: 1.29 us -> 21.9 us  [the longest x2 12.8 us: whole_images(): feed_full[..., :units // 2].transpose(0, 2, 1, 3).reshape(width, units)]
    another operation x21 -> x17, other arithmetic: 23.4 us -> 5.35 us  [the longest x4 3.29 us: scatter_grads(): keep_two = jnp.stack([grads(0, 1, 0), grads(0, 1, 1)])]
    convert_element_type x16 -> x7, other arithmetic: 15.7 us -> 5.43 us  [the longest x3 3.21 us: scatter_sum(): one_x = exchange(low_add(keep_one[1], one_y[1]).astype(LOW), far_x=1)]
    ppermute x59 -> x50, waiting for transfers between devices: 159 us -> 166 us  [exchange(): return lax.ppermute(value, BOTH, pairs)]
  transfers between devices with their start and end apart: 59 -> 52, of which waited for: 24 -> 22; matrix products, arithmetic and copies ran while one was open for 34% -> 19% of each run, Pallas kernels for 3% -> 16%
where the time goes in v2:
time: 534 us; the launch traced here: 525 us
  waiting for transfers between devices  166 us (31%)
  matrix products  97.1 us (18%)
  Pallas kernels  84.4 us (16%)
  starting transfers between devices  74.3 us (14%)
  local copies, waits for them, and re-layouts  60.3 us (11%)
  other arithmetic  25.7 us (5%)
  between operations  16.7 us (3%)
    ppermute x50, waiting for transfers between devices, exchange(): return lax.ppermute(value, BOTH, pairs)  166 us
    ppermute x50, starting transfers between devices, exchange(): return lax.ppermute(value, BOTH, pairs)  74.2 us
    dot_general x4, matrix products, mat(): return jnp.dot(left, right, preferred_element_type=jnp.float32)  37 us
    dot_general x24, matrix products, mat_rows(): lax.dot_general(left, right, (((0,), (0,)), ((), ())), preferred_element_...  34.6 us
    pallas_call x1, Pallas kernels, attend_back_all(): pl.pallas_call(attend_back_kernel, grid=(images, blocks), in_specs=[pl.Bl...  30.3 us
    dot_general x8, matrix products, mat_far(): lax.dot_general(left, right, (((1,), (1,)), ((), ())), preferred_element_...  25.6 us
    unnamed x169, local copies, waits for them, and re-layouts  23.1 us
    pallas_call x4, Pallas kernels, pair_up(): pl.pallas_call(pair_kernel, in_specs=[pl.BlockSpec(memory_space=pltpu.SME...  18.3 us
  transfers between devices with their start and end apart: 52, of which 22 were waited for; matrix products, arithmetic and copies ran while one was open for 19% of the time, Pallas kernels for 16%

profile of v2, /device:TPU:0, one launch (start us, length us, event | category | flops | bytes accessed | tf_op | source)
XLA Modules:
  0.0 525.0 jit_solution(2237246702238873010)
XLA Ops:
  15.6 2.9 collective-permute-start
  21.9 2.6 collective-permute-start.4
  26.6 13.9 %collective-permute-done.3.refs_1_ = bf16[2,128,512]{2,1,0:T(8,128)(2,1)S(1)} collective-permute-done((bf16[2,128,512]{2,1,0:T(8,128)(2,1)S(1)}, bf16[2,128,512]{2,1,0:T(8,128)(2,1)S(1)}, u32[]{:S(2)}, u32[]{:S(2)}) %collective-permute-start.3) | collective-permute-done | bytes 262176 | tf_op jit(solution)/shard_map/ppermute | solution.py:303
  40.5 12.7 %collective-permute-done.4.refs_2_ = bf16[2,128,512]{2,1,0:T(8,128)(2,1)S(1)} collective-permute-done((bf16[2,128,512]{2,1,0:T(8,128)(2,1)S(1)}, bf16[2,128,512]{2,1,0:T(8,128)(2,1)S(1)}, u32[]{:S(2)}, u32[]{:S(2)}) %collective-permute-start.4) | collective-permute-done | bytes 262176 | tf_op jit(solution)/shard_map/ppermute | solution.py:303
  54.7 2.3 shard_map.306
  59.5 2.0 convert_reduce_fusion.2
  62.2 2.4 fusion.27
  64.6 14.8 %collective-permute-done.6.refs_1_ = bf16[4,128,512]{2,1,0:T(8,128)(2,1)S(1)} collective-permute-done((bf16[4,128,512]{2,1,0:T(8,128)(2,1)}, bf16[4,128,512]{2,1,0:T(8,128)(2,1)S(1)}, u32[]{:S(2)}, u32[]{:S(2)}) %collective-permute-start.6) | collective-permute-done | bytes 524320 | tf_op jit(solution)/shard_map/ppermute | solution.py:303
  81.0 2.9 shard_map.307
  83.9 2.4 collective-permute-start.9
  86.5 15.8 %collective-permute-done.8.refs_1_ = bf16[2,4,128,512]{3,2,1,0:T(8,128)(2,1)S(1)} collective-permute-done((bf16[2,4,128,512]{3,2,1,0:T(8,128)(2,1)}, bf16[2,4,128,512]{3,2,1,0:T(8,128)(2,1)S(1)}, u32[]{:S(2)}, u32[]{:S(2)}) %collective-permute-start.8) | collective-permute-done | bytes 1048608 | tf_op jit(solution)/shard_map/ppermute | solution.py:303
  102.4 7.8 %collective-permute-done.9.refs_3_ = bf16[2,4,128,512]{3,2,1,0:T(8,128)(2,1)} collective-permute-done((bf16[2,4,128,512]{3,2,1,0:T(8,128)(2,1)}, bf16[2,4,128,512]{3,2,1,0:T(8,128)(2,1)}, u32[]{:S(2)}, u32[]{:S(2)}) %collective-permute-start.9) | collective-permute-done | bytes 1048608 | tf_op jit(solution)/shard_map/ppermute | solution.py:303
  110.2 4.6 shard_map.308
  114.8 4.5 shard_map.305
  119.3 8.4 %fusion.qkv_ref = bf16[1184,1536]{1,0:T(8,128)(2,1)} fusion(bf16[1184,1024]{1,0:T(8,128)(2,1)} %bitcast.364, bf16[1024,1536]{1,0:T(8,128)(2,1)} %bitcast.334, f32[1536]{0:T(1024)S(1)} %add.299), kind=kOutput, calls=%fused_computation.6 | convolution fusion | flops 3728179200 | bytes 9213952 | tf_op jit(solution)/shard_map/dot_general | solution.py:662
  128.5 16.9 %shard_map.309 = (bf16[1184,512]{1,0:T(8,128)(2,1)}, f32[8,8,592]{2,1,0:T(8,128)}) custom-call(bf16[1184,1536]{1,0:T(8,128)(2,1)} %fusion.qkv_ref, bf16[592,128]{1,0:T(8,128)(2,1)} %broadcast_in_dim.60.bias_ref), custom_call_target="tpu_custom_call" | custom-call | flops 5742002176 | bytes 4849664 | tf_op jit(solution)/shard_map/pallas_call | solution.py:613
  147.6 2.8 collective-permute-done.10
  153.6 2.1 fusion.28
  156.2 2.6 collective-permute-done.15.far_ref
  158.9 4.6 shard_map.311
  163.5 4.6 shard_map.310
  168.1 6.1 %slice_bitcast_fusion.1 = (bf16[8,128,2,1024]{3,1,2,0:T(8,128)(2,1)}, bf16[8,128,2,1024]{3,1,2,0:T(8,128)(2,1)}) fusion(bf16[8,2,128,2048]{3,2,1,0:T(8,128)(2,1)} %bitcast.286), kind=kLoop, calls=%fused_computation.23 | loop fusion | bytes 16777216 | tf_op jit(solution)/shard_map/transpose | solution.py:737
  174.1 6.8 %copy.162 = bf16[8,128,2,1024]{1,0,3,2:T(8,128)(2,1)} copy(bf16[8,128,2,1024]{3,1,2,0:T(8,128)(2,1)} %get-tuple-element.173) | data formatting | bytes 8388608 | tf_op jit(solution)/shard_map/transpose | solution.py:737
  180.9 11.5 %multiply_convert_fusion.1 = (bf16[1184,2048]{1,0:T(8,128)(2,1)S(1)}, f32[1184,2048]{1,0:T(8,128)}) fusion(f32[2048]{0:T(1024)S(1)} %bitcast.326, bf16[1184,1024]{1,0:T(8,128)(2,1)} %bitcast.362, bf16[256,8,8,128]{3,2,1,0:T(8,128)(2,1)} %bitcast.296), kind=kOutput, calls=%fused_computation.3 | convolution fusion | flops 4983029760 | bytes 21176320 | tf_op jit(solution)/shard_map/dot_general | solution.py:662
  192.5 2.2 fusion.52
  196.4 2.5 convolution_convert_fusion.2
  198.9 2.6 convolution_convert_fusion.3
  201.4 6.8 %copy.163 = bf16[8,128,2,1024]{1,0,3,2:T(8,128)(2,1)} copy(bf16[8,128,2,1024]{3,1,2,0:T(8,128)(2,1)} %get-tuple-element.174) | data formatting | bytes 8388608 | tf_op jit(solution)/shard_map/transpose | solution.py:738
  208.3 12.7 %convert_reduce_fusion = (f32[2048]{0:T(1024)S(1)}, bf16[1184,2048]{1,0:T(8,128)(2,1)S(1)}) fusion(f32[1184,2048]{1,0:T(8,128)} %get-tuple-element.241, f32[2048]{0:T(1024)S(1)} %bitcast.327, bf16[1184,1024]{1,0:T(8,128)(2,1)} %bitcast.361, bf16[256,8,8,128]{3,2,1,0:T(8,128)(2,1)} %bitcast.293), kind=kOutput, calls=%fused_computation | convolution fusion | flops 5002426368 | bytes 21184512 | tf_op jit(solution)/shard_map/dot_general | solution.py:662
  224.7 2.7 fusion.35
  227.8 2.7 fusion.40
  231.6 2.6 collective-permute-start.44
  237.3 2.1 collective-permute-start.34
  239.5 18.6 %collective-permute-done.44.two_a = bf16[2,512,512]{2,1,0:T(8,128)(2,1)S(1)} collective-permute-done((bf16[2,512,512]{2,1,0:T(8,128)(2,1)S(1)}, bf16[2,512,512]{2,1,0:T(8,128)(2,1)S(1)}, u32[]{:S(2)}, u32[]{:S(2)}) %collective-permute-start.44) | collective-permute-done | bytes 1048608 | tf_op jit(solution)/shard_map/ppermute | solution.py:303
  263.9 16.2 %collective-permute-done.36.two_a = bf16[2,512,512]{2,1,0:T(8,128)(2,1)S(1)} collective-permute-done((bf16[2,512,512]{2,1,0:T(8,128)(2,1)S(1)}, bf16[2,512,512]{2,1,0:T(8,128)(2,1)S(1)}, u32[]{:S(2)}, u32[]{:S(2)}) %collective-permute-start.36) | collective-permute-done | bytes 1048608 | tf_op jit(solution)/shard_map/ppermute | solution.py:303
  285.0 3.6 multiply_reduce_fusion
  288.6 5.6 %convert_reduce_fusion.4 = (f32[1024]{0:T(1024)S(1)}, bf16[592,1024]{1,0:T(8,128)(2,1)}, f32[592,1024]{1,0:T(8,128)}, bf16[592,1024]{1,0:T(8,128)(2,1)S(1)}) fusion(f32[592]{0:T(1024)S(1)} %broadcast_multiply_fusion.2, f32[592]{0:T(1024)S(1)} %broadcast_multiply_fusion.4, f32[592,1024]{1,0:T(8,128)S(1)} %copy-done.3, f32[592]{0:T(1024)S(1)} %broadcast_multiply_fusion.3, ...), kind=kOutput, calls=%fused_computation.50 | convolution fusion | flops 2497575936 | bytes 21200896 | tf_op jit(solution)/shard_map/dot_general | solution.py:472
  299.1 3.0 shard_map.316
  302.1 18.0 %collective-permute-start.46 = (bf16[2,128,512]{2,1,0:T(8,128)(2,1)}, bf16[2,128,512]{2,1,0:T(8,128)(2,1)S(1)}, u32[]{:S(2)}, u32[]{:S(2)}) collective-permute-start(bf16[2,128,512]{2,1,0:T(8,128)(2,1)} %get-tuple-element.70), channel_id=1, source_target_pairs={{0,8},{1,9},{2,10},{3,11},{4,12},{5,13},{6,14},{7,15},{8,0},{9,1},... | collective-permute-start | bytes 786440 | tf_op jit(solution)/shard_map/ppermute | solution.py:303
  320.1 5.2 collective-permute-start.47
  326.6 3.1 shard_map.315
  329.7 6.7 %collective-permute-start.38 = (bf16[2,128,512]{2,1,0:T(8,128)(2,1)}, bf16[2,128,512]{2,1,0:T(8,128)(2,1)S(1)}, u32[]{:S(2)}, u32[]{:S(2)}) collective-permute-start(bf16[2,128,512]{2,1,0:T(8,128)(2,1)} %get-tuple-element.65), channel_id=1, source_target_pairs={{0,8},{1,9},{2,10},{3,11},{4,12},{5,13},{6,14},{7,15},{8,0},{9,1},... | collective-permute-start | bytes 786440 | tf_op jit(solution)/shard_map/ppermute | solution.py:303
  337.7 2.2 copy.188
  341.0 3.7 collective-permute-done.47
  346.2 3.7 collective-permute-done.38
  349.9 18.8 %collective-permute-done.39 = bf16[2,128,512]{2,1,0:T(8,128)(2,1)S(1)} collective-permute-done((bf16[2,128,512]{2,1,0:T(8,128)(2,1)S(1)}, bf16[2,128,512]{2,1,0:T(8,128)(2,1)S(1)}, u32[]{:S(2)}, u32[]{:S(2)}) %collective-permute-start.39) | collective-permute-done | bytes 262176 | tf_op jit(solution)/shard_map/ppermute | solution.py:303
  375.0 4.6 shard_map.312
  379.7 4.4 convolution_convert_fusion.grad_ref
  384.0 30.3 %shard_map.313 = bf16[1184,1536]{1,0:T(8,128)(2,1)} custom-call(bf16[1184,1536]{1,0:T(8,128)(2,1)} %fusion.qkv_ref, bf16[592,128]{1,0:T(8,128)(2,1)} %broadcast_in_dim.60.bias_ref, bf16[1184,512]{1,0:T(8,128)(2,1)} %convolution_convert_fusion.grad_ref, bf16[1184,512]{1,0:T(8,128)(2,1)} %get-tuple-element.51.mixed_ref, f32[8,8,592]{2,1,0:T(8,128)} %get-tuple-element.56.total_ref), custom_call_target="tpu_custom_call" | custom-call | flops 14355005440 | bytes 9699328 | tf_op jit(solution)/shard_map/pallas_call | solution.py:640
  414.3 2.2 convolution_convert_fusion.16
  424.7 3.1 fusion.45
  432.7 2.6 convolution_convert_fusion.18
  435.2 2.2 convolution_convert_fusion.19
  439.5 2.0 convolution_convert_fusion.21
  446.3 5.0 convert_add_fusion
  459.8 9.2 %collective-permute-done.21 = f32[4096]{0:T(1024)S(1)} collective-permute-done((f32[4096]{0:T(1024)S(1)}, f32[4096]{0:T(1024)S(1)}, u32[]{:S(2)}, u32[]{:S(2)}) %collective-permute-start.21) | collective-permute-done | bytes 16416 | tf_op jit(solution)/shard_map/ppermute | solution.py:303
  469.8 2.9 collective-permute-done.22
  472.7 3.7 collective-permute-start.23
  483.6 2.0 collective-permute-done.25
  487.2 3.0 shard_map.314
  492.2 2.4 collective-permute-start.32
  494.9 6.8 %collective-permute-done.30 = bf16[2,128,512]{2,1,0:T(8,128)(2,1)S(1)} collective-permute-done((bf16[2,128,512]{2,1,0:T(8,128)(2,1)}, bf16[2,128,512]{2,1,0:T(8,128)(2,1)S(1)}, u32[]{:S(2)}, u32[]{:S(2)}) %collective-permute-start.30) | collective-permute-done | bytes 262176 | tf_op jit(solution)/shard_map/ppermute | solution.py:303
  501.7 8.7 %collective-permute-done.31 = bf16[2,128,512]{2,1,0:T(8,128)(2,1)S(1)} collective-permute-done((bf16[2,128,512]{2,1,0:T(8,128)(2,1)}, bf16[2,128,512]{2,1,0:T(8,128)(2,1)S(1)}, u32[]{:S(2)}, u32[]{:S(2)}) %collective-permute-start.31) | collective-permute-done | bytes 262176 | tf_op jit(solution)/shard_map/ppermute | solution.py:303
  510.8 3.2 copy.189
  (393 shorter events, 106.9 us)
Async XLA Ops:
  7.2 160.9 %all-gather.4.cloned.1.call-start = ((), (), s32[]{:S(2)}) async-start(), calls=%async_computation | async-start | bytes 8912896 | tf_op jit(solution)/shard_map/all_gather | solution.py:730
  9.4 1.7 collective-permute-start.12
  12.0 432.1 %all-gather.6.cloned.1.call-start = ((), (), s32[]{:S(2)}) async-start(), calls=%async_computation.1 | async-start | bytes 1081344 | tf_op jit(solution)/shard_map/all_gather | solution.py:875
  15.6 42.8 %collective-permute-start = (bf16[2,296,1024]{2,1,0:T(8,128)(2,1)}, bf16[2,296,1024]{2,1,0:T(8,128)(2,1)S(1)}, u32[]{:S(2)}, u32[]{:S(2)}) collective-permute-start(bf16[2,296,1024]{2,1,0:T(8,128)(2,1)} %get-tuple-element.180), channel_id=1, source_target_pairs={{0,1},{1,0},{2,3},{3,2},{4,5},{5,4},{6,7},{7,6},{8,9},{9,8},{10,11... | collective-permute-start | bytes 3637256 | tf_op jit(solution)/shard_map/ppermute | solution.py:303
  18.7 1.4 collective-permute-start.2
  20.2 33.0 %copy-start.25 = (bf16[2,2,64,512]{3,2,1,0:T(8,128)(2,1)}, bf16[2,2,64,512]{3,2,1,0:T(8,128)(2,1)S(1)}, u32[]{:S(2)}) copy-start(bf16[2,2,64,512]{3,2,1,0:T(8,128)(2,1)S(1)} %copy.158) | copy-start | bytes 786436
  20.2 20.3 %collective-permute-start.3 = (bf16[2,128,512]{2,1,0:T(8,128)(2,1)S(1)}, bf16[2,128,512]{2,1,0:T(8,128)(2,1)S(1)}, u32[]{:S(2)}, u32[]{:S(2)}) collective-permute-start(bf16[2,128,512]{2,1,0:T(8,128)(2,1)S(1)} %bitcast.309), channel_id=1, source_target_pairs={{0,8},{1,9},{2,10},{3,11},{4,12},{5,13},{6,14},{7,15},{8,0},{9,1},... | collective-permute-start | bytes 786440 | tf_op jit(solution)/shard_map/ppermute | solution.py:303
  21.9 31.4 %collective-permute-start.4 = (bf16[2,128,512]{2,1,0:T(8,128)(2,1)S(1)}, bf16[2,128,512]{2,1,0:T(8,128)(2,1)S(1)}, u32[]{:S(2)}, u32[]{:S(2)}) collective-permute-start(bf16[2,128,512]{2,1,0:T(8,128)(2,1)S(1)} %bitcast.310), channel_id=1, source_target_pairs={{0,16},{1,17},{2,18},{3,19},{4,20},{5,21},{6,22},{7,23},{8,24},{9,... | collective-permute-start | bytes 786440 | tf_op jit(solution)/shard_map/ppermute | solution.py:303
  24.5 28.8 %collective-permute-start.5 = (bf16[2,128,512]{2,1,0:T(8,128)(2,1)S(1)}, bf16[2,128,512]{2,1,0:T(8,128)(2,1)S(1)}, u32[]{:S(2)}, u32[]{:S(2)}) collective-permute-start(bf16[2,128,512]{2,1,0:T(8,128)(2,1)S(1)} %bitcast.311), channel_id=1, source_target_pairs={{0,24},{1,25},{2,26},{3,27},{4,28},{5,29},{6,30},{7,31},{8,16},{9,... | collective-permute-start | bytes 786440 | tf_op jit(solution)/shard_map/ppermute | solution.py:303
  26.0 36.2 %copy-start.49 = (f32[1024]{0:T(1024)}, f32[1024]{0:T(1024)S(1)}, u32[]{:S(2)}) copy-start(f32[1024]{0:T(1024)S(1)} %convert_element_type.335) | copy-start | bytes 12292
  57.0 22.4 %collective-permute-start.6 = (bf16[4,128,512]{2,1,0:T(8,128)(2,1)}, bf16[4,128,512]{2,1,0:T(8,128)(2,1)S(1)}, u32[]{:S(2)}, u32[]{:S(2)}) collective-permute-start(bf16[4,128,512]{2,1,0:T(8,128)(2,1)} %get-tuple-element.46.refs_0_), channel_id=1, source_target_pairs={{0,4},{1,5},{2,6},{3,7},{4,0},{5,1},{6,2},{7,3},{8,12},{9,13},{10,... | collective-permute-start | bytes 1572872 | tf_op jit(solution)/shard_map/ppermute | solution.py:303
  58.5 20.9 %collective-permute-start.7 = (bf16[4,128,512]{2,1,0:T(8,128)(2,1)}, bf16[4,128,512]{2,1,0:T(8,128)(2,1)S(1)}, u32[]{:S(2)}, u32[]{:S(2)}) collective-permute-start(bf16[4,128,512]{2,1,0:T(8,128)(2,1)} %get-tuple-element.47.refs_2_), channel_id=1, source_target_pairs={{0,1},{1,0},{2,3},{3,2},{4,5},{5,4},{6,7},{7,6},{8,9},{9,8},{10,11... | collective-permute-start | bytes 1572872 | tf_op jit(solution)/shard_map/ppermute | solution.py:303
  61.5 88.9 %copy-start = (bf16[1,2,296,1024]{3,2,0,1:T(8,128)(2,1)}, bf16[1,2,296,1024]{3,2,0,1:T(8,128)(2,1)S(1)}, u32[]{:S(2)}) copy-start(bf16[1,2,296,1024]{3,2,0,1:T(8,128)(2,1)S(1)} %get-tuple-element.172) | copy-start | bytes 3637252
  62.2 24.1 %copy-start.59 = (bf16[1024]{0:T(1024)(128)(2,1)S(1)}, bf16[1024]{0:T(1024)(128)(2,1)}, u32[]{:S(2)}) copy-start(bf16[1024]{0:T(1024)(128)(2,1)} %param.24) | copy-start | bytes 6148
  62.2 24.1 %copy-start.60 = (bf16[1024]{0:T(1024)(128)(2,1)S(1)}, bf16[1024]{0:T(1024)(128)(2,1)}, u32[]{:S(2)}) copy-start(bf16[1024]{0:T(1024)(128)(2,1)} %param.27) | copy-start | bytes 6148
  64.6 50.2 %collective-permute-start.1 = (bf16[592,1024]{1,0:T(8,128)(2,1)}, bf16[592,1024]{1,0:T(8,128)(2,1)}, u32[]{:S(2)}, u32[]{:S(2)}) collective-permute-start(bf16[592,1024]{1,0:T(8,128)(2,1)} %get-tuple-element.184.own_ref), channel_id=1, source_target_pairs={{0,2},{1,3},{2,0},{3,1},{4,6},{5,7},{6,4},{7,5},{8,10},{9,11},{10,... | collective-permute-start | bytes 3637256 | tf_op jit(solution)/shard_map/ppermute | solution.py:303
  83.9 18.5 %collective-permute-start.8 = (bf16[2,4,128,512]{3,2,1,0:T(8,128)(2,1)}, bf16[2,4,128,512]{3,2,1,0:T(8,128)(2,1)S(1)}, u32[]{:S(2)}, u32[]{:S(2)}) collective-permute-start(bf16[2,4,128,512]{3,2,1,0:T(8,128)(2,1)} %get-tuple-element.48.refs_0_), channel_id=1, source_target_pairs={{0,1},{1,0},{2,3},{3,2},{4,5},{5,4},{6,7},{7,6},{8,9},{9,8},{10,11... | collective-permute-start | bytes 3145736 | tf_op jit(solution)/shard_map/ppermute | solution.py:303
  83.9 26.3 %collective-permute-start.9 = (bf16[2,4,128,512]{3,2,1,0:T(8,128)(2,1)}, bf16[2,4,128,512]{3,2,1,0:T(8,128)(2,1)}, u32[]{:S(2)}, u32[]{:S(2)}) collective-permute-start(bf16[2,4,128,512]{3,2,1,0:T(8,128)(2,1)} %get-tuple-element.49.refs_2_), channel_id=1, source_target_pairs={{0,4},{1,5},{2,6},{3,7},{4,0},{5,1},{6,2},{7,3},{8,12},{9,13},{10,... | collective-permute-start | bytes 3145736 | tf_op jit(solution)/shard_map/ppermute | solution.py:303
  147.5 3.0 collective-permute-start.10
  155.6 3.2 collective-permute-start.15
  155.8 7.7 %collective-permute-start.11 = (bf16[592,1024]{1,0:T(8,128)(2,1)}, bf16[592,1024]{1,0:T(8,128)(2,1)}, u32[]{:S(2)}, u32[]{:S(2)}) collective-permute-start(bf16[592,1024]{1,0:T(8,128)(2,1)} %get-tuple-element.234.own_ref), channel_id=1, source_target_pairs={{0,2},{1,3},{2,0},{3,1},{4,6},{5,7},{6,4},{7,5},{8,10},{9,11},{10,... | collective-permute-start | bytes 3637256 | tf_op jit(solution)/shard_map/ppermute | solution.py:303
  224.7 59.0 %copy-start.12 = (bf16[1024,512]{1,0:T(8,128)(2,1)}, bf16[1024,512]{1,0:T(8,128)(2,1)S(1)}, u32[]{:S(2)}) copy-start(bf16[1024,512]{1,0:T(8,128)(2,1)S(1)} %convolution_convert_fusion.5) | copy-start | bytes 3145732
  231.6 26.5 %collective-permute-start.44 = (bf16[2,512,512]{2,1,0:T(8,128)(2,1)S(1)}, bf16[2,512,512]{2,1,0:T(8,128)(2,1)S(1)}, u32[]{:S(2)}, u32[]{:S(2)}) collective-permute-start(bf16[2,512,512]{2,1,0:T(8,128)(2,1)S(1)} %pad_maximum_fusion.10), channel_id=1, source_target_pairs={{0,4},{1,5},{2,6},{3,7},{4,0},{5,1},{6,2},{7,3},{8,12},{9,13},{10,... | collective-permute-start | bytes 3145736 | tf_op jit(solution)/shard_map/ppermute | solution.py:303
  235.1 26.8 %collective-permute-start.42 = (bf16[2,512,512]{2,1,0:T(8,128)(2,1)S(1)}, bf16[2,512,512]{2,1,0:T(8,128)(2,1)S(1)}, u32[]{:S(2)}, u32[]{:S(2)}) collective-permute-start(bf16[2,512,512]{2,1,0:T(8,128)(2,1)S(1)} %bitcast.369), channel_id=1, source_target_pairs={{0,1},{1,0},{2,3},{3,2},{4,5},{5,4},{6,7},{7,6},{8,9},{9,8},{10,11... | collective-permute-start | bytes 3145736 | tf_op jit(solution)/shard_map/ppermute | solution.py:303
  236.2 43.9 %collective-permute-start.36 = (bf16[2,512,512]{2,1,0:T(8,128)(2,1)S(1)}, bf16[2,512,512]{2,1,0:T(8,128)(2,1)S(1)}, u32[]{:S(2)}, u32[]{:S(2)}) collective-permute-start(bf16[2,512,512]{2,1,0:T(8,128)(2,1)S(1)} %pad_maximum_fusion.8), channel_id=1, source_target_pairs={{0,4},{1,5},{2,6},{3,7},{4,0},{5,1},{6,2},{7,3},{8,12},{9,13},{10,... | collective-permute-start | bytes 3145736 | tf_op jit(solution)/shard_map/ppermute | solution.py:303
  237.3 46.4 %collective-permute-start.34 = (bf16[2,512,512]{2,1,0:T(8,128)(2,1)S(1)}, bf16[2,512,512]{2,1,0:T(8,128)(2,1)S(1)}, u32[]{:S(2)}, u32[]{:S(2)}) collective-permute-start(bf16[2,512,512]{2,1,0:T(8,128)(2,1)S(1)} %bitcast.368), channel_id=1, source_target_pairs={{0,1},{1,0},{2,3},{3,2},{4,5},{5,4},{6,7},{7,6},{8,9},{9,8},{10,11... | collective-permute-start | bytes 3145736 | tf_op jit(solution)/shard_map/ppermute | solution.py:303
  239.4 21.4 %copy-start.35 = (bf16[1,512,512]{2,1,0:T(8,128)(2,1)S(1)}, bf16[1,512,512]{2,1,0:T(8,128)(2,1)}, u32[]{:S(2)}) copy-start(bf16[1,512,512]{2,1,0:T(8,128)(2,1)} %fusion.51) | copy-start | bytes 1572868
  239.5 45.4 %collective-permute-start.16 = (bf16[592,1024]{1,0:T(8,128)(2,1)S(1)}, bf16[592,1024]{1,0:T(8,128)(2,1)S(1)}, u32[]{:S(2)}, u32[]{:S(2)}) collective-permute-start(bf16[592,1024]{1,0:T(8,128)(2,1)S(1)} %fusion.35), channel_id=1, source_target_pairs={{0,2},{1,3},{2,0},{3,1},{4,6},{5,7},{6,4},{7,5},{8,10},{9,11},{10,... | collective-permute-start | bytes 3637256 | tf_op jit(solution)/shard_map/ppermute | solution.py:303
  258.1 30.5 %collective-permute-start.13 = (bf16[592,1024]{1,0:T(8,128)(2,1)S(1)}, bf16[592,1024]{1,0:T(8,128)(2,1)S(1)}, u32[]{:S(2)}, u32[]{:S(2)}) collective-permute-start(bf16[592,1024]{1,0:T(8,128)(2,1)S(1)} %fusion.40), channel_id=1, source_target_pairs={{0,2},{1,3},{2,0},{3,1},{4,6},{5,7},{6,4},{7,5},{8,10},{9,11},{10,... | collective-permute-start | bytes 3637256 | tf_op jit(solution)/shard_map/ppermute | solution.py:303
  262.0 37.0 %collective-permute-start.45 = (bf16[512,512]{1,0:T(8,128)(2,1)}, bf16[512,512]{1,0:T(8,128)(2,1)}, u32[]{:S(2)}, u32[]{:S(2)}) collective-permute-start(bf16[512,512]{1,0:T(8,128)(2,1)} %get-tuple-element.246), channel_id=1, source_target_pairs={{0,1},{1,0},{2,3},{3,2},{4,5},{5,4},{6,7},{7,6},{8,9},{9,8},{10,11... | collective-permute-start | bytes 1572872 | tf_op jit(solution)/shard_map/ppermute | solution.py:303
  263.9 21.1 %copy-start.3 = (f32[592,1024]{1,0:T(8,128)S(1)}, f32[592,1024]{1,0:T(8,128)}, u32[]{:S(2)}) copy-start(f32[592,1024]{1,0:T(8,128)} %copy-done.2) | copy-start | bytes 7274500
  280.1 19.0 %collective-permute-start.43 = (bf16[512,512]{1,0:T(8,128)(2,1)}, bf16[512,512]{1,0:T(8,128)(2,1)}, u32[]{:S(2)}, u32[]{:S(2)}) collective-permute-start(bf16[512,512]{1,0:T(8,128)(2,1)} %fusion.86), channel_id=1, source_target_pairs={{0,4},{1,5},{2,6},{3,7},{4,0},{5,1},{6,2},{7,3},{8,12},{9,13},{10,... | collective-permute-start | bytes 1572872 | tf_op jit(solution)/shard_map/ppermute | solution.py:303
  283.7 36.4 %collective-permute-start.37 = (bf16[512,512]{1,0:T(8,128)(2,1)}, bf16[512,512]{1,0:T(8,128)(2,1)}, u32[]{:S(2)}, u32[]{:S(2)}) collective-permute-start(bf16[512,512]{1,0:T(8,128)(2,1)} %get-tuple-element.244), channel_id=1, source_target_pairs={{0,1},{1,0},{2,3},{3,2},{4,5},{5,4},{6,7},{7,6},{8,9},{9,8},{10,11... | collective-permute-start | bytes 1572872 | tf_op jit(solution)/shard_map/ppermute | solution.py:303
  284.8 40.5 %collective-permute-start.35 = (bf16[512,512]{1,0:T(8,128)(2,1)}, bf16[512,512]{1,0:T(8,128)(2,1)}, u32[]{:S(2)}, u32[]{:S(2)}) collective-permute-start(bf16[512,512]{1,0:T(8,128)(2,1)} %fusion.88), channel_id=1, source_target_pairs={{0,4},{1,5},{2,6},{3,7},{4,0},{5,1},{6,2},{7,3},{8,12},{9,13},{10,... | collective-permute-start | bytes 1572872 | tf_op jit(solution)/shard_map/ppermute | solution.py:303
  295.3 34.4 %collective-permute-start.14 = (bf16[289,1024]{1,0:T(8,128)(2,1)S(1)}, bf16[289,1024]{1,0:T(8,128)(2,1)}, u32[]{:S(2)}, u32[]{:S(2)}) collective-permute-start(bf16[289,1024]{1,0:T(8,128)(2,1)S(1)} %slice.317), channel_id=1, source_target_pairs={{0,1},{1,0},{2,3},{3,2},{4,5},{5,4},{6,7},{7,6},{8,9},{9,8},{10,11... | collective-permute-start | bytes 1775624 | tf_op jit(solution)/shard_map/ppermute | solution.py:303
  299.0 75.0 %collective-permute-start.17 = (bf16[592,1024]{1,0:T(8,128)(2,1)S(1)}, bf16[592,1024]{1,0:T(8,128)(2,1)S(1)}, u32[]{:S(2)}, u32[]{:S(2)}) collective-permute-start(bf16[592,1024]{1,0:T(8,128)(2,1)S(1)} %copy-done.19), channel_id=1, source_target_pairs={{0,2},{1,3},{2,0},{3,1},{4,6},{5,7},{6,4},{7,5},{8,10},{9,11},{10,... | collective-permute-start | bytes 3637256 | tf_op jit(solution)/shard_map/ppermute | solution.py:303
  302.1 37.9 %collective-permute-start.46 = (bf16[2,128,512]{2,1,0:T(8,128)(2,1)}, bf16[2,128,512]{2,1,0:T(8,128)(2,1)S(1)}, u32[]{:S(2)}, u32[]{:S(2)}) collective-permute-start(bf16[2,128,512]{2,1,0:T(8,128)(2,1)} %get-tuple-element.70), channel_id=1, source_target_pairs={{0,8},{1,9},{2,10},{3,11},{4,12},{5,13},{6,14},{7,15},{8,0},{9,1},... | collective-permute-start | bytes 786440 | tf_op jit(solution)/shard_map/ppermute | solution.py:303
  320.1 24.6 %collective-permute-start.47 = (bf16[2,128,512]{2,1,0:T(8,128)(2,1)}, bf16[2,128,512]{2,1,0:T(8,128)(2,1)S(1)}, u32[]{:S(2)}, u32[]{:S(2)}) collective-permute-start(bf16[2,128,512]{2,1,0:T(8,128)(2,1)} %get-tuple-element.71), channel_id=1, source_target_pairs={{0,16},{1,17},{2,18},{3,19},{4,20},{5,21},{6,22},{7,23},{8,24},{9,... | collective-permute-start | bytes 786440 | tf_op jit(solution)/shard_map/ppermute | solution.py:303
  325.3 20.6 %collective-permute-start.48 = (bf16[2,128,512]{2,1,0:T(8,128)(2,1)}, bf16[2,128,512]{2,1,0:T(8,128)(2,1)S(1)}, u32[]{:S(2)}, u32[]{:S(2)}) collective-permute-start(bf16[2,128,512]{2,1,0:T(8,128)(2,1)} %get-tuple-element.72), channel_id=1, source_target_pairs={{0,24},{1,25},{2,26},{3,27},{4,28},{5,29},{6,30},{7,31},{8,16},{9,... | collective-permute-start | bytes 786440 | tf_op jit(solution)/shard_map/ppermute | solution.py:303
  329.7 20.2 %collective-permute-start.38 = (bf16[2,128,512]{2,1,0:T(8,128)(2,1)}, bf16[2,128,512]{2,1,0:T(8,128)(2,1)S(1)}, u32[]{:S(2)}, u32[]{:S(2)}) collective-permute-start(bf16[2,128,512]{2,1,0:T(8,128)(2,1)} %get-tuple-element.65), channel_id=1, source_target_pairs={{0,8},{1,9},{2,10},{3,11},{4,12},{5,13},{6,14},{7,15},{8,0},{9,1},... | collective-permute-start | bytes 786440 | tf_op jit(solution)/shard_map/ppermute | solution.py:303
  337.7 30.9 %copy-start.29 = (f32[2,128,512]{2,1,0:T(8,128)S(1)}, f32[2,128,512]{2,1,0:T(8,128)}, u32[]{:S(2)}) copy-start(f32[2,128,512]{2,1,0:T(8,128)} %get-tuple-element.64) | copy-start | bytes 1572868
  339.9 28.7 %collective-permute-start.39 = (bf16[2,128,512]{2,1,0:T(8,128)(2,1)S(1)}, bf16[2,128,512]{2,1,0:T(8,128)(2,1)S(1)}, u32[]{:S(2)}, u32[]{:S(2)}) collective-permute-start(bf16[2,128,512]{2,1,0:T(8,128)(2,1)S(1)} %copy-done.73), channel_id=1, source_target_pairs={{0,16},{1,17},{2,18},{3,19},{4,20},{5,21},{6,22},{7,23},{8,24},{9,... | collective-permute-start | bytes 786440 | tf_op jit(solution)/shard_map/ppermute | solution.py:303
  344.7 23.9 %collective-permute-start.40 = (bf16[2,128,512]{2,1,0:T(8,128)(2,1)S(1)}, bf16[2,128,512]{2,1,0:T(8,128)(2,1)S(1)}, u32[]{:S(2)}, u32[]{:S(2)}) collective-permute-start(bf16[2,128,512]{2,1,0:T(8,128)(2,1)S(1)} %copy-done.72), channel_id=1, source_target_pairs={{0,24},{1,25},{2,26},{3,27},{4,28},{5,29},{6,30},{7,31},{8,16},{9,... | collective-permute-start | bytes 786440 | tf_op jit(solution)/shard_map/ppermute | solution.py:303
  346.1 23.4 %collective-permute-start.49 = (bf16[2,64,512]{2,1,0:T(8,128)(2,1)S(1)}, bf16[2,64,512]{2,1,0:T(8,128)(2,1)S(1)}, u32[]{:S(2)}, u32[]{:S(2)}) collective-permute-start(bf16[2,64,512]{2,1,0:T(8,128)(2,1)S(1)} %fusion.115), channel_id=1, source_target_pairs={{0,2},{1,3},{2,0},{3,1},{4,6},{5,7},{6,4},{7,5},{8,10},{9,11},{10,... | collective-permute-start | bytes 393224 | tf_op jit(solution)/shard_map/ppermute | solution.py:303
  369.5 1.8 collective-permute-start.41
  384.0 30.3 %copy-start.62 = (bf16[2,592,1024]{2,1,0:T(8,128)(2,1)S(1)}, bf16[2,592,1024]{2,1,0:T(8,128)(2,1)}, u32[]{:S(2)}) copy-start(bf16[2,592,1024]{2,1,0:T(8,128)(2,1)} %get-tuple-element.57) | copy-start | bytes 7274500
  429.0 25.8 %collective-permute-start.28 = (bf16[2,512,512]{2,1,0:T(8,128)(2,1)}, bf16[2,512,512]{2,1,0:T(8,128)(2,1)S(1)}, u32[]{:S(2)}, u32[]{:S(2)}) collective-permute-start(bf16[2,512,512]{2,1,0:T(8,128)(2,1)} %pad_maximum_fusion.6), channel_id=1, source_target_pairs={{0,4},{1,5},{2,6},{3,7},{4,0},{5,1},{6,2},{7,3},{8,12},{9,13},{10,... | collective-permute-start | bytes 3145736 | tf_op jit(solution)/shard_map/ppermute | solution.py:303
  430.7 26.4 %collective-permute-start.26 = (bf16[2,512,512]{2,1,0:T(8,128)(2,1)}, bf16[2,512,512]{2,1,0:T(8,128)(2,1)}, u32[]{:S(2)}, u32[]{:S(2)}) collective-permute-start(bf16[2,512,512]{2,1,0:T(8,128)(2,1)} %bitcast.308), channel_id=1, source_target_pairs={{0,1},{1,0},{2,3},{3,2},{4,5},{5,4},{6,7},{7,6},{8,9},{9,8},{10,11... | collective-permute-start | bytes 3145736 | tf_op jit(solution)/shard_map/ppermute | solution.py:303
  432.4 13.9 %collective-permute-start.18 = (bf16[592,1024]{1,0:T(8,128)(2,1)}, bf16[592,1024]{1,0:T(8,128)(2,1)}, u32[]{:S(2)}, u32[]{:S(2)}) collective-permute-start(bf16[592,1024]{1,0:T(8,128)(2,1)} %fusion.45), channel_id=1, source_target_pairs={{0,2},{1,3},{2,0},{3,1},{4,6},{5,7},{6,4},{7,5},{8,10},{9,11},{10,... | collective-permute-start | bytes 3637256 | tf_op jit(solution)/shard_map/ppermute | solution.py:303
  452.4 24.0 %copy-start.11 = (f32[592,1024]{1,0:T(8,128)S(1)}, f32[592,1024]{1,0:T(8,128)}, u32[]{:S(2)}) copy-start(f32[592,1024]{1,0:T(8,128)} %get-tuple-element.170) | copy-start | bytes 7274500
  452.5 4.1 collective-permute-start.20
  454.8 22.5 %copy-start.13 = (bf16[2,512,512]{2,1,0:T(8,128)(2,1)}, bf16[2,512,512]{2,1,0:T(8,128)(2,1)S(1)}, u32[]{:S(2)}) copy-start(bf16[2,512,512]{2,1,0:T(8,128)(2,1)S(1)} %collective-permute-done.28.two_a) | copy-start | bytes 3145732
  454.9 31.4 %collective-permute-start.29 = (bf16[512,512]{1,0:T(8,128)(2,1)S(1)}, bf16[512,512]{1,0:T(8,128)(2,1)S(1)}, u32[]{:S(2)}, u32[]{:S(2)}) collective-permute-start(bf16[512,512]{1,0:T(8,128)(2,1)S(1)} %fusion.89), channel_id=1, source_target_pairs={{0,1},{1,0},{2,3},{3,2},{4,5},{5,4},{6,7},{7,6},{8,9},{9,8},{10,11... | collective-permute-start | bytes 1572872 | tf_op jit(solution)/shard_map/ppermute | solution.py:303
  456.6 12.4 %collective-permute-start.21 = (f32[4096]{0:T(1024)S(1)}, f32[4096]{0:T(1024)S(1)}, u32[]{:S(2)}, u32[]{:S(2)}) collective-permute-start(f32[4096]{0:T(1024)S(1)} %fusion.144), channel_id=1, source_target_pairs={{0,1},{1,0},{2,3},{3,2},{4,5},{5,4},{6,7},{7,6},{8,9},{9,8},{10,11... | collective-permute-start | bytes 49160 | tf_op jit(solution)/shard_map/ppermute | solution.py:303
  458.2 28.0 %collective-permute-start.27 = (bf16[512,512]{1,0:T(8,128)(2,1)S(1)}, bf16[512,512]{1,0:T(8,128)(2,1)S(1)}, u32[]{:S(2)}, u32[]{:S(2)}) collective-permute-start(bf16[512,512]{1,0:T(8,128)(2,1)S(1)} %fusion.90), channel_id=1, source_target_pairs={{0,4},{1,5},{2,6},{3,7},{4,0},{5,1},{6,2},{7,3},{8,12},{9,13},{10,... | collective-permute-start | bytes 1572872 | tf_op jit(solution)/shard_map/ppermute | solution.py:303
  469.0 3.7 collective-permute-start.22
  472.7 7.4 %collective-permute-start.23 = (f32[4096]{0:T(1024)S(1)}, f32[4096]{0:T(1024)S(1)}, u32[]{:S(2)}, u32[]{:S(2)}) collective-permute-start(f32[4096]{0:T(1024)S(1)} %add.326), channel_id=1, source_target_pairs={{0,8},{1,9},{2,10},{3,11},{4,12},{5,13},{6,14},{7,15},{8,0},{9,1},... | collective-permute-start | bytes 49160 | tf_op jit(solution)/shard_map/ppermute | solution.py:303
  477.3 17.3 %collective-permute-start.19 = (bf16[289,1024]{1,0:T(8,128)(2,1)S(1)}, bf16[289,1024]{1,0:T(8,128)(2,1)S(1)}, u32[]{:S(2)}, u32[]{:S(2)}) collective-permute-start(bf16[289,1024]{1,0:T(8,128)(2,1)S(1)} %slice.508), channel_id=1, source_target_pairs={{0,1},{1,0},{2,3},{3,2},{4,5},{5,4},{6,7},{7,6},{8,9},{9,8},{10,11... | collective-permute-start | bytes 1775624 | tf_op jit(solution)/shard_map/ppermute | solution.py:303
  479.0 4.6 collective-permute-start.24
  480.1 5.5 %collective-permute-start.25 = (f32[4096]{0:T(1024)S(1)}, f32[4096]{0:T(1024)S(1)}, u32[]{:S(2)}, u32[]{:S(2)}) collective-permute-start(f32[4096]{0:T(1024)S(1)} %add.326), channel_id=1, source_target_pairs={{0,24},{1,25},{2,26},{3,27},{4,28},{5,29},{6,30},{7,31},{8,16},{9,... | collective-permute-start | bytes 49160 | tf_op jit(solution)/shard_map/ppermute | solution.py:303
  490.2 11.5 %collective-permute-start.30 = (bf16[2,128,512]{2,1,0:T(8,128)(2,1)}, bf16[2,128,512]{2,1,0:T(8,128)(2,1)S(1)}, u32[]{:S(2)}, u32[]{:S(2)}) collective-permute-start(bf16[2,128,512]{2,1,0:T(8,128)(2,1)} %get-tuple-element.60), channel_id=1, source_target_pairs={{0,8},{1,9},{2,10},{3,11},{4,12},{5,13},{6,14},{7,15},{8,0},{9,1},... | collective-permute-start | bytes 786440 | tf_op jit(solution)/shard_map/ppermute | solution.py:303
  490.4 20.0 %collective-permute-start.31 = (bf16[2,128,512]{2,1,0:T(8,128)(2,1)}, bf16[2,128,512]{2,1,0:T(8,128)(2,1)S(1)}, u32[]{:S(2)}, u32[]{:S(2)}) collective-permute-start(bf16[2,128,512]{2,1,0:T(8,128)(2,1)} %get-tuple-element.61), channel_id=1, source_target_pairs={{0,16},{1,17},{2,18},{3,19},{4,20},{5,21},{6,22},{7,23},{8,24},{9,... | collective-permute-start | bytes 786440 | tf_op jit(solution)/shard_map/ppermute | solution.py:303
  492.2 18.2 %collective-permute-start.32 = (bf16[2,128,512]{2,1,0:T(8,128)(2,1)}, bf16[2,128,512]{2,1,0:T(8,128)(2,1)S(1)}, u32[]{:S(2)}, u32[]{:S(2)}) collective-permute-start(bf16[2,128,512]{2,1,0:T(8,128)(2,1)} %get-tuple-element.62), channel_id=1, source_target_pairs={{0,24},{1,25},{2,26},{3,27},{4,28},{5,29},{6,30},{7,31},{8,16},{9,... | collective-permute-start | bytes 786440 | tf_op jit(solution)/shard_map/ppermute | solution.py:303
  510.6 3.5 collective-permute-start.33
  (68 other events, 310.1 us)
Sparse Core Ops, SparseCore 0:
  12.1 150.9 all-gather.3
  299.1 86.0 all-gather.5

commit v3 on v2

--- a/solution.py
+++ b/solution.py
@@ -335,12 +335,14 @@
     )(places, *sources)
 
 
-def gather_weights(keep, send, places, core):
+def gather_piece(keep, send, core):
     deep, wide = keep.shape[1:]
-    every = slice(None)
-    piece = pick_two(core, keep, exchange(send, far_core=1), 1).reshape(2, 2 * deep, wide)
-    line = [piece] + [exchange(piece, far_z=step) for step in (1, 2, 3)]
-    rows = 2 * deep
+    return pick_two(core, keep, exchange(send, far_core=1), 1).reshape(2, 2 * deep, wide)
+
+
+def gather_line(piece, others, places):
+    rows, wide = piece.shape[1:]
+    line = [piece] + others
     plan = []
     for step in range(4):
         for part in range(2):
@@ -352,17 +354,23 @@
                     lambda z, x, c, y, step=step: z ^ step,
                 )
             )
-    one, two = pack(places, line, [(4, rows, wide)] * 2, plan)
-    one_x, two_y = exchange(one, far_x=1), exchange(two, far_y=1)
+    return pack(places, line, [(4, rows, wide)] * 2, plan)
+
+
+def gather_pairs(places, one, two, one_x, two_y):
+    every = slice(None)
     plan = [
         (0, lambda z, x, c, y: every, 0, lambda z, x, c, y: x),
         (1, lambda z, x, c, y: every, 0, lambda z, x, c, y: 1 - x),
         (2, lambda z, x, c, y: every, 1, lambda z, x, c, y: 0),
         (3, lambda z, x, c, y: every, 1, lambda z, x, c, y: 1),
     ]
-    one_pair, two_pair = pack(places, [one, one_x, two, two_y], [(2, 4, rows, wide)] * 2, plan)
-    one_y, two_x = exchange(one_pair, far_y=1), exchange(two_pair, far_x=1)
-    most = 3 * wide // 4
+    return pack(places, [one, one_x, two, two_y], [(2,) + one.shape] * 2, plan)
+
+
+def gather_all(places, one_pair, two_pair, one_y, two_x, most):
+    every = slice(None)
+    rows, wide = one_pair.shape[2:]
     plan = []
     for to, low, high in ((0, 0, most), (1, most, wide)):
         span = high - low
@@ -379,7 +387,7 @@
                                 slice(lo, hi),
                             ),
                             to,
-                            lambda z, x, c, y, a=far, p=place_z, s=span, n=number: (
+                            lambda z, x, c, y, a=far, p=place_z, n=number, s=span: (
                                 p,
                                 a,
                                 every,
@@ -397,7 +405,7 @@
                                 slice(lo, hi),
                             ),
                             to,
-                            lambda z, x, c, y, f=far, p=place_z, s=span, n=number: (
+                            lambda z, x, c, y, f=far, p=place_z, n=number, s=span: (
                                 p,
                                 x ^ f,
                                 every,
@@ -406,8 +414,8 @@
                         )
                     )
     shapes = [(4, 2, rows, 4 * most), (4, 2, rows, 4 * (wide - most))]
-    full, rest = pack(places, [one_pair, one_y, two_pair, two_x], shapes, plan)
-    return full.reshape(8 * rows, -1), rest.reshape(8 * rows, -1)
+    made = pack(places, [one_pair, one_y, two_pair, two_x], shapes, plan)
+    return [array.reshape(8 * rows, -1) for array in made]
 
 
 def low_add(*values):
@@ -431,16 +439,23 @@
             send_refs[step - 1][1] = two.astype(LOW)
 
 
-def scatter_sum(send_one, send_two, keep_one, keep_two, core):
-    lines, wide = send_one.shape[1:]
+def scatter_first(sends):
+    return exchange(sends[0], far_y=1), exchange(sends[1], far_x=1)
+
+
+def scatter_second(keeps, arrived):
+    one = low_add(keeps[0][1], arrived[0][1]).astype(LOW)
+    two = low_add(keeps[1][1], arrived[1][1]).astype(LOW)
+    return exchange(one, far_x=1), exchange(two, far_y=1)
+
+
+def scatter_line(keeps, arrived, crossed):
+    lines, wide = crossed[0].shape
     tall = lines // 4
-    one_y, two_x = exchange(send_one, far_y=1), exchange(send_two, far_x=1)
-    one_x = exchange(low_add(keep_one[1], one_y[1]).astype(LOW), far_x=1)
-    two_y = exchange(low_add(keep_two[1], two_x[1]).astype(LOW), far_y=1)
     first = pl.BlockSpec((1, lines, wide), lambda i: (0, 0, 0))
     flat = pl.BlockSpec((lines, wide), lambda i: (0, 0))
     piece = pl.BlockSpec((2, tall, wide), lambda i: (0, 0, 0))
-    sends = pl.pallas_call(
+    return pl.pallas_call(
         line_kernel,
         grid=(1,),
         in_specs=[first, first, flat, first, first, flat],
@@ -451,21 +466,32 @@
         cost_estimate=pl.CostEstimate(
             flops=lines * wide * 4, transcendentals=0, bytes_accessed=lines * wide * 18
         ),
-    )(keep_one, one_y, one_x, keep_two, two_x, two_y)
-    total = low_add(
-        sends[0], *[exchange(sends[step], far_z=step) for step in (1, 2, 3)]
-    ).reshape(2, 2, tall // 2, wide)
+    )(keeps[0], arrived[0], crossed[0], keeps[1], arrived[1], crossed[1])
+
+
+def scatter_z(sends):
+    return [exchange(sends[step], far_z=step) for step in (1, 2, 3)]
+
+
+def scatter_last(own, others, core):
+    tall, wide = own.shape[1:]
+    total = low_add(own, *others).reshape(2, 2, tall // 2, wide)
     keep = lax.dynamic_index_in_dim(total, core, 1, keepdims=False)
     send = lax.dynamic_index_in_dim(total, 1 - core, 1, keepdims=False)
     far = exchange(send.astype(LOW), far_core=1).astype(jnp.float32)
     return pick_two(core, keep, far, 0)
 
 
-def vector_sum(vector):
-    for step in ({"far_core": 1}, {"far_y": 1}, {"far_x": 1}):
+def vector_first(vector):
+    vector = vector + exchange(vector, far_core=1)
+    return vector, [exchange(vector, far_z=step) for step in (1, 2, 3)]
+
+
+def vector_last(vector, others):
+    vector = vector + others[0] + others[1] + others[2]
+    for step in ({"far_y": 1}, {"far_x": 1}):
         vector = vector + exchange(vector, **step)
-    others = [exchange(vector, far_z=step) for step in (1, 2, 3)]
-    return vector + others[0] + others[1] + others[2]
+    return vector
 
 
 def mat_far(left, right):
@@ -480,54 +506,229 @@
     )
 
 
-def pair_kernel(places_ref, own_ref, far_ref, rows_ref, turned_ref):
-    spots = [places_ref[0] ^ (block % 4) for block in range(8)]
-    for block in range(8):
-        at = spots[block] * 2 + (places_ref[1] ^ (block // 4))
-        start = pl.multiple_of(at * LANES, LANES)
-        for half, ref in enumerate((own_ref, far_ref)):
-            turned_ref[half, :, block * LANES : (block + 1) * LANES] = ref[:, pl.ds(start, LANES)]
-    rows_ref[0] = own_ref[...]
-    rows_ref[1] = far_ref[...]
-
-
-def pair_up(places, own):
-    rows, width = own.shape
-    made = pl.pallas_call(
-        pair_kernel,
-        in_specs=[pl.BlockSpec(memory_space=pltpu.SMEM)]
-        + [pl.BlockSpec(memory_space=pltpu.VMEM)] * 2,
-        out_specs=[pl.BlockSpec(memory_space=pltpu.VMEM)] * 2,
-        out_shape=[jax.ShapeDtypeStruct((2, rows, width), LOW)] * 2,
+def up_kernel(places_ref, left_ref, right_ref, shift_ref, active_ref, slope_ref):
+    width = left_ref.shape[1]
+    right = right_ref[...].reshape(width, -1)
+    hidden = jnp.dot(left_ref[...], right, preferred_element_type=jnp.float32)
+    hidden = hidden + shift_ref[...]
+    sigma = 1.0 / (1.0 + jnp.exp(-SLOPE * hidden))
+    active = hidden * sigma
+    active_ref[...] = active.astype(LOW)
+    slope_ref[...] = (sigma + SLOPE * active * (1.0 - sigma)).astype(LOW)
+
+
+def feed_spec(gathered, start):
+    lines, _, rows, wide = gathered.shape
+    return pl.BlockSpec(
+        (lines, 1, rows, wide // 4), lambda i, s: (0, s[3] ^ (i % 2), 0, start + i // 2)
+    )
+
+
+def up_call(places, left, gathered, shift):
+    rows, width = left.shape
+    wide = shift.shape[1] // 4
+    piece = pl.BlockSpec((rows, wide), lambda i, s: (0, i))
+    return pl.pallas_call(
+        up_kernel,
+        grid_spec=pltpu.PrefetchScalarGridSpec(
+            num_scalar_prefetch=1,
+            grid=(4,),
+            in_specs=[
+                pl.BlockSpec((rows, width), lambda i, s: (0, 0)),
+                feed_spec(gathered, 0),
+                pl.BlockSpec((1, wide), lambda i, s: (0, i)),
+            ],
+            out_specs=[piece, piece],
+        ),
+        out_shape=[jax.ShapeDtypeStruct((rows, 4 * wide), LOW)] * 2,
         compiler_params=pltpu.CompilerParams(vmem_limit_bytes=VMEM_ROOM),
         cost_estimate=pl.CostEstimate(
-            flops=0, transcendentals=0, bytes_accessed=own.size * 12
-        ),
-    )(places, own, exchange(own, far_core=1))
-    return [array.reshape(2 * rows, width) for array in made]
-
-
-def half_sums(left, right, rows):
-    send = mat_far(left[rows:], right).astype(LOW)
-    far = exchange(send, far_core=1)
-    return mat_far(left[:rows], right) + far.astype(jnp.float32)
-
-
-def scatter_grads(pairs, core):
-    lines = pairs[0][0].shape[1] // 2
-
-    def grads(row_far, part, y_far):
-        made = []
-        for left, cut in pairs:
-            left = left if row_far is None else left[:, row_far * lines : (row_far + 1) * lines]
-            made.append(mat_rows(left, cut(part, y_far)).astype(LOW))
-        return made[0] if len(made) == 1 else jnp.concatenate(made, 1)
-
-    send_one = grads(None, 0, 1).reshape(2, lines, -1)
-    send_two = jnp.stack([grads(1, 1, 0), grads(1, 1, 1)])
-    keep_one = grads(None, 0, 0).reshape(2, lines, -1)
-    keep_two = jnp.stack([grads(0, 1, 0), grads(0, 1, 1)])
-    return scatter_sum(send_one, send_two, keep_one, keep_two, core)
+            flops=8 * rows * wide * width,
+            transcendentals=8 * rows * wide,
+            bytes_accessed=left.size * 2 + 8 * width * wide + 16 * rows * wide,
+        ),
+    )(places, left, gathered, shift)
+
+
+def hidden_kernel(places_ref, left_ref, right_ref, slope_ref, out_ref, sum_ref):
+    width = left_ref.shape[1]
+    right = right_ref[...].reshape(width, -1)
+    grad = jnp.dot(left_ref[...], right, preferred_element_type=jnp.float32)
+    grad = (grad * slope_ref[...].astype(jnp.float32)).astype(LOW)
+    out_ref[...] = grad
+    sum_ref[...] = jnp.sum(grad.astype(jnp.float32), axis=0, keepdims=True)
+
+
+def hidden_call(places, left, gathered, slope):
+    rows, width = left.shape
+    wide = slope.shape[1] // 4
+    piece = pl.BlockSpec((rows, wide), lambda i, s: (0, i))
+    return pl.pallas_call(
+        hidden_kernel,
+        grid_spec=pltpu.PrefetchScalarGridSpec(
+            num_scalar_prefetch=1,
+            grid=(4,),
+            in_specs=[
+                pl.BlockSpec((rows, width), lambda i, s: (0, 0)),
+                feed_spec(gathered, 2),
+                piece,
+            ],
+            out_specs=[piece, pl.BlockSpec((1, wide), lambda i, s: (0, i))],
+        ),
+        out_shape=[
+            jax.ShapeDtypeStruct((rows, 4 * wide), LOW),
+            jax.ShapeDtypeStruct((1, 4 * wide), jnp.float32),
+        ],
+        compiler_params=pltpu.CompilerParams(vmem_limit_bytes=VMEM_ROOM),
+        cost_estimate=pl.CostEstimate(
+            flops=8 * rows * wide * width,
+            transcendentals=0,
+            bytes_accessed=left.size * 2 + 8 * width * wide + 16 * rows * wide,
+        ),
+    )(places, left, gathered, slope)
+
+
+def down_kernel(places_ref, left_ref, right_ref, out_ref):
+    span = right_ref.shape[3] // 2
+    total = None
+    for far in range(2):
+        right = right_ref[:, places_ref[3] ^ far].reshape(-1, 2 * span)
+        for part in range(2):
+            start = (part * 2 + far) * span
+            one = mat_far(
+                left_ref[:, start : start + span], right[:, part * span : (part + 1) * span]
+            )
+            total = one if total is None else total + one
+    out_ref[...] = total.astype(out_ref.dtype)
+
+
+def down_call(places, left, gathered, start, dtype):
+    rows, deep = left.shape
+    lines, _, tall, wide = gathered.shape
+    return pl.pallas_call(
+        down_kernel,
+        grid_spec=pltpu.PrefetchScalarGridSpec(
+            num_scalar_prefetch=1,
+            grid=(lines // 2,),
+            in_specs=[
+                pl.BlockSpec((rows, deep), lambda i, s: (0, 0)),
+                pl.BlockSpec((2, 2, tall, wide // 2), lambda i, s: (i, 0, 0, start)),
+            ],
+            out_specs=pl.BlockSpec((rows, 2 * tall), lambda i, s: (0, i)),
+        ),
+        out_shape=jax.ShapeDtypeStruct((rows, lines * tall), dtype),
+        compiler_params=pltpu.CompilerParams(vmem_limit_bytes=VMEM_ROOM),
+        cost_estimate=pl.CostEstimate(
+            flops=2 * rows * deep * lines * tall,
+            transcendentals=0,
+            bytes_accessed=left.size * 2 + lines * tall * deep * 2 + rows * lines * tall * 4,
+        ),
+    )(places, left, gathered)
+
+
+def owner_kernel(places_ref, left_ref, left_far, right_ref, right_far, out_ref):
+    total = mat_rows(left_ref[...], right_ref[...]) + mat_rows(left_far[...], right_far[...])
+    out_ref[0] = total.astype(LOW)
+
+
+def owner_grads(places, left, right):
+    rows, width = left[0].shape
+    span = right[0].shape[1] // 4
+    whole = pl.BlockSpec((rows, width), lambda i, s: (0, 0))
+    piece = pl.BlockSpec((rows, span), lambda i, s: (0, i))
+    return pl.pallas_call(
+        owner_kernel,
+        grid_spec=pltpu.PrefetchScalarGridSpec(
+            num_scalar_prefetch=1,
+            grid=(4,),
+            in_specs=[whole, whole, piece, piece],
+            out_specs=pl.BlockSpec((1, width, span), lambda i, s: (s[3] ^ (i % 2), 0, i // 2)),
+        ),
+        out_shape=jax.ShapeDtypeStruct((2, width, 2 * span), LOW),
+        compiler_params=pltpu.CompilerParams(vmem_limit_bytes=VMEM_ROOM),
+        cost_estimate=pl.CostEstimate(
+            flops=16 * rows * width * span,
+            transcendentals=0,
+            bytes_accessed=(2 * rows * width + 8 * rows * span + 4 * width * span) * 2,
+        ),
+    )(places, *left, *right)
+
+
+def weight_kernel(pairs, places_ref, *refs):
+    ins, (one_ref, two_ref) = refs[:-2], refs[-2:]
+    step = pl.program_id(0)
+    parts = []
+    for pair in range(pairs):
+        total = None
+        for image in range(2):
+            group = ins[10 * pair + 5 * image : 10 * pair + 5 * image + 5]
+            left = jnp.concatenate([ref[...] for ref in group[:4]], axis=1)
+            one = mat_rows(left, group[4][...])
+            total = one if image == 0 else total + one
+        parts.append(total.astype(LOW))
+    made = parts[0] if pairs == 1 else jnp.concatenate(parts, axis=1)
+
+    @pl.when(step < 2)
+    def _():
+        one_ref[0] = made
+
+    @pl.when(step >= 2)
+    def _():
+        two_ref[0] = made
+
+
+def weight_pieces(places, operands, send):
+    rows = operands[0][0][0].shape[0]
+    line = 4 * LANES
+
+    def x_far(step):
+        if send:
+            return jnp.where(step == 0, 0, 1)
+        return jnp.where(step == 1, 1, 0)
+
+    def y_far(step):
+        if send:
+            return jnp.where(step == 2, 0, 1)
+        return jnp.where(step == 3, 1, 0)
+
+    def left_map(z_far):
+        return lambda i, s: (0, (s[0] ^ z_far) * 2 + (s[1] ^ x_far(i)))
+
+    specs, arrays, wide = [], [], 0
+    for left, right in operands:
+        span = right[0].shape[1] // 4
+        wide += span
+        for image in range(2):
+            for z_far in range(4):
+                specs.append(pl.BlockSpec((rows, LANES), left_map(z_far)))
+                arrays.append(left[image])
+            specs.append(
+                pl.BlockSpec((rows, span), lambda i, s: (0, jnp.where(i < 2, 0, 2) + y_far(i)))
+            )
+            arrays.append(right[image])
+
+    def kernel(*refs):
+        weight_kernel(len(operands), *refs)
+
+    return pl.pallas_call(
+        kernel,
+        grid_spec=pltpu.PrefetchScalarGridSpec(
+            num_scalar_prefetch=1,
+            grid=(4,),
+            in_specs=specs,
+            out_specs=[
+                pl.BlockSpec((1, line, wide), lambda i, s: (jnp.minimum(i, 1), 0, 0)),
+                pl.BlockSpec((1, line, wide), lambda i, s: (jnp.maximum(i - 2, 0), 0, 0)),
+            ],
+        ),
+        out_shape=[jax.ShapeDtypeStruct((2, line, wide), LOW)] * 2,
+        compiler_params=pltpu.CompilerParams(vmem_limit_bytes=VMEM_ROOM),
+        cost_estimate=pl.CostEstimate(
+            flops=16 * rows * line * wide,
+            transcendentals=0,
+            bytes_accessed=rows * wide * 16 + rows * line * 16 + line * wide * 8,
+        ),
+    )(places, *arrays)
 
 
 def lane_of(shape):
@@ -607,53 +808,53 @@
     out_ref[:, 2 * LANES : 3 * LANES] = grad_value.astype(LOW)
 
 
-def attend_all(qkv, bias, rows):
-    images = qkv.shape[0] // rows
+def attend_call(qkv, bias):
+    rows = qkv.shape[0]
     blocks = qkv.shape[1] // (3 * LANES)
     return pl.pallas_call(
         attend_kernel,
-        grid=(images, blocks),
+        grid=(blocks,),
         in_specs=[
-            pl.BlockSpec((rows, 3 * LANES), lambda i, j: (i, j)),
-            pl.BlockSpec((rows, LANES), lambda i, j: (0, 0)),
+            pl.BlockSpec((rows, 3 * LANES), lambda j: (0, j)),
+            pl.BlockSpec((rows, LANES), lambda j: (0, 0)),
         ],
         out_specs=[
-            pl.BlockSpec((rows, LANES), lambda i, j: (i, j)),
-            pl.BlockSpec((1, 8, rows), lambda i, j: (i * blocks + j, 0, 0)),
+            pl.BlockSpec((rows, LANES), lambda j: (0, j)),
+            pl.BlockSpec((1, 8, rows), lambda j: (j, 0, 0)),
         ],
         out_shape=[
-            jax.ShapeDtypeStruct((images * rows, blocks * LANES), LOW),
-            jax.ShapeDtypeStruct((images * blocks, 8, rows), jnp.float32),
+            jax.ShapeDtypeStruct((rows, blocks * LANES), LOW),
+            jax.ShapeDtypeStruct((blocks, 8, rows), jnp.float32),
         ],
         compiler_params=pltpu.CompilerParams(vmem_limit_bytes=VMEM_ROOM),
         cost_estimate=pl.CostEstimate(
-            flops=images * blocks * 2 * 2 * 2 * rows * rows * LANES * 2,
-            transcendentals=images * blocks * 2 * rows * rows,
-            bytes_accessed=images * rows * blocks * LANES * 8,
+            flops=blocks * 2 * 2 * 2 * rows * rows * LANES * 2,
+            transcendentals=blocks * 2 * rows * rows,
+            bytes_accessed=rows * blocks * LANES * 8,
         ),
     )(qkv, bias)
 
 
-def attend_back_all(qkv, bias, grad, mixed, total, rows):
-    images = qkv.shape[0] // rows
+def attend_back_call(qkv, bias, grad, mixed, total):
+    rows = qkv.shape[0]
     blocks = qkv.shape[1] // (3 * LANES)
     return pl.pallas_call(
         attend_back_kernel,
-        grid=(images, blocks),
+        grid=(blocks,),
         in_specs=[
-            pl.BlockSpec((rows, 3 * LANES), lambda i, j: (i, j)),
-            pl.BlockSpec((rows, LANES), lambda i, j: (0, 0)),
-            pl.BlockSpec((rows, LANES), lambda i, j: (i, j)),
-            pl.BlockSpec((rows, LANES), lambda i, j: (i, j)),
-            pl.BlockSpec((1, 8, rows), lambda i, j: (i * blocks + j, 0, 0)),
+            pl.BlockSpec((rows, 3 * LANES), lambda j: (0, j)),
+            pl.BlockSpec((rows, LANES), lambda j: (0, 0)),
+            pl.BlockSpec((rows, LANES), lambda j: (0, j)),
+            pl.BlockSpec((rows, LANES), lambda j: (0, j)),
+            pl.BlockSpec((1, 8, rows), lambda j: (j, 0, 0)),
         ],
-        out_specs=pl.BlockSpec((rows, 3 * LANES), lambda i, j: (i, j)),
+        out_specs=pl.BlockSpec((rows, 3 * LANES), lambda j: (0, j)),
         out_shape=jax.ShapeDtypeStruct(qkv.shape, LOW),
         compiler_params=pltpu.CompilerParams(vmem_limit_bytes=VMEM_ROOM),
         cost_estimate=pl.CostEstimate(
-            flops=images * blocks * 2 * 5 * 2 * rows * rows * LANES * 2,
-            transcendentals=images * blocks * 2 * rows * rows,
-            bytes_accessed=images * rows * blocks * LANES * 16,
+            flops=blocks * 2 * 5 * 2 * rows * rows * LANES * 2,
+            transcendentals=blocks * 2 * rows * rows,
+            bytes_accessed=rows * blocks * LANES * 16,
         ),
     )(qkv, bias, grad, mixed, total)
 
@@ -713,45 +914,49 @@
     depth, head_cols = query_weight.shape
     units = up_weight.shape[1]
 
-    def feed_part(place):
-        wide = units // 2
-        return jnp.concatenate(
-            [
-                lax.dynamic_slice_in_dim(up_weight, place * wide, wide, 1),
-                lax.dynamic_slice_in_dim(down_weight, place * wide, wide, 0).T,
-            ],
-            1,
-        )
-
-    feed = pick_two(core, feed_part(core), exchange(feed_part(1 - core), far_core=1), 0)
-    groups = [
-        [place for place in range(32) if (place // 2) % 2 == at] for at in range(2)
-    ]
-    feed_full = lax.all_gather(
-        feed.reshape(2 * depth, units),
+    def columns_of(weights, place):
+        return [
+            lax.dynamic_slice_in_dim(
+                weight, place * (weight.shape[1] // 2), weight.shape[1] // 2, 1
+            )
+            for weight in weights
+        ]
+
+    def core_parts(weights, place):
+        cuts = columns_of(weights, place)
+        parts = []
+        for part in range(2):
+            spans = [cut.shape[1] // 2 for cut in cuts]
+            parts.append(
+                jnp.concatenate(
+                    [cut[:, part * span : (part + 1) * span] for cut, span in zip(cuts, spans)], 1
+                )
+            )
+        return jnp.stack(parts)
+
+    feeds = [up_weight, down_weight.T]
+    feed_keep = jnp.concatenate(columns_of(feeds, core), 1)
+    feed_send = jnp.concatenate(columns_of(feeds, 1 - core), 1)
+    feed = pick_two(core, feed_keep, exchange(feed_send, far_core=1), 0)
+    groups = [[place for place in range(32) if (place // 2) % 2 == at] for at in range(2)]
+    turned_groups = [sorted(group, key=lambda place: (place % 2, place)) for group in groups]
+    gathered = lax.all_gather(
+        feed.reshape(2 * depth, -1),
         BOTH,
         axis=0,
         tiled=True,
         axis_index_groups=groups,
-    ).reshape(8, 2, 2 * depth, units)
-    upper_full = feed_full[..., : units // 2].transpose(0, 2, 1, 3).reshape(width, units)
-    lower_full = feed_full[..., units // 2 :].transpose(0, 2, 1, 3).reshape(width, units)
-
-    def core_parts(place):
-        cuts = [
-            lax.dynamic_slice_in_dim(weight, place * (head_cols // 2), head_cols // 2, 1)
-            for weight in (query_weight, key_weight, value_weight, output_weight.T)
-        ]
-        spans = [slice(0, head_cols // 4), slice(head_cols // 4, head_cols // 2)]
-        return jnp.stack([jnp.concatenate([cut[:, span] for cut in cuts], 1) for span in spans])
-
-    qkv_full, output_full = gather_weights(core_parts(core), core_parts(1 - core), places, core)
-
-    stacked = jnp.stack([images, cotangent])
+    ).reshape(8, 2, 2 * depth, -1)
+
+    heads = [query_weight, key_weight, value_weight, output_weight.T]
+    piece_one = gather_piece(core_parts(heads, core), core_parts(heads, 1 - core), core)
+    line_one = gather_line(piece_one, scatter_z([None, piece_one, piece_one, piece_one]), places)
+
+    stacked = jnp.stack([images, after(cotangent, piece_one)])
     stacked = jnp.pad(stacked, ((0, 0), (0, 0), (0, half - strip), (0, 0)))
     mine = lax.dynamic_index_in_dim(stacked, place_y, 1, keepdims=False)
     theirs = lax.dynamic_index_in_dim(stacked, 1 - place_y, 1, keepdims=False)
-    arrived = exchange(theirs, far_y=1)
+    arrived = after(exchange(theirs, far_y=1), *line_one)
     whole = jnp.stack([mine, arrived], 1).reshape(2, rows, width)
 
     def head_columns(vector):
@@ -776,9 +981,7 @@
     qkv_shift = jnp.concatenate(
         [query_shift, jnp.zeros_like(query_shift), value_shift], 1
     ).reshape(-1)
-    up_shift = lax.dynamic_index_in_dim(
-        up_bias.astype(jnp.float32).reshape(2, 2, -1), core, 1, keepdims=False
-    ).reshape(-1)
+    up_shift = head_columns(up_bias).reshape(1, -1)
 
     row = jnp.arange(rows)
     in_half = row % half
@@ -793,94 +996,129 @@
     resid = whole[0].astype(jnp.float32)
     grad_top = row_mask * whole[1].astype(jnp.float32)
     fed_grad = grad_top.astype(LOW)
-    fed_rows, fed_turned = pair_up(places, fed_grad)
+    def pair_of(own):
+        return own, exchange(own, far_core=1)
+
+    fed_pair = pair_of(fed_grad)
     normed, unit_one, spread_one = flat_norm(resid, gain_one, shift_one)
-    normed_rows, normed_turned = pair_up(places, normed.astype(LOW))
-    qkv = (mat(normed_rows, qkv_full) + qkv_shift).astype(LOW)
-    mixed, totals = attend_all(qkv, key_bias, rows)
-    attended = half_sums(mixed, output_full, rows) + output_bias.astype(jnp.float32)
+    normed_pair = pair_of(normed.astype(LOW))
+
+    cross_one = exchange(line_one[0], far_x=1), exchange(line_one[1], far_y=1)
+    pair_one = gather_pairs(after(places, *fed_pair, *normed_pair), *line_one, *cross_one)
+    last_one = exchange(pair_one[0], far_y=1), exchange(pair_one[1], far_x=1)
+    qkv_full, output_full = gather_all(places, *pair_one, *last_one, 3 * head_cols // 4)
+
+    def heads_of(one):
+        qkv = (mat(one, qkv_full) + qkv_shift).astype(LOW)
+        return (qkv, *attend_call(qkv, key_bias))
+
+    qkv_far, mixed_far, totals_far = heads_of(normed_pair[1])
+    mixed_sum = exchange(mat_far(mixed_far, output_full).astype(LOW), far_core=1)
+    qkv_own, mixed_own, totals_own = heads_of(normed_pair[0])
+    mixed_pair = mixed_own, mixed_far
+    attended = mat_far(mixed_own, output_full) + mixed_sum.astype(jnp.float32)
+    attended = attended + output_bias.astype(jnp.float32)
     middle = row_mask * (resid + attended)
     second, unit_two, spread_two = flat_norm(middle, gain_two, shift_two)
-    second_rows, second_turned = pair_up(places, second.astype(LOW))
-    hidden = mat(second_rows, upper_full) + up_shift
-    sigma = jax.nn.sigmoid(SLOPE * hidden)
-    active = (hidden * sigma).astype(LOW)
-    slope = (sigma + SLOPE * hidden * sigma * (1.0 - sigma)).astype(LOW)
-
-    def unit_cut(array):
-        wide = units // 4
-
-        def cut(part, y_far):
-            start = (place_y ^ y_far) * 2 + part
-            return lax.dynamic_slice_in_dim(array, start * wide, wide, 1)
-
-        return cut
-
-    def head_cut(array):
-        wide = array.shape[1] // 4
-
-        def cut(part, y_far):
-            at = part * 2 + y_far
-            return array[:, at * wide : (at + 1) * wide]
-
-        return cut
-
-    lower_owned = scatter_grads([(fed_turned, unit_cut(active))], core)
-    hidden_grad = (mat(fed_rows, lower_full) * slope.astype(jnp.float32)).astype(LOW)
-    up_bias_sums = column_flat(hidden_grad)
-    upper_owned = scatter_grads([(second_turned, unit_cut(hidden_grad))], core)
-    second_grad = half_sums(hidden_grad, upper_full, rows)
-    fed = half_sums(active, lower_full, rows)
-    layer_own = (row_mask * (middle + fed + down_bias.astype(jnp.float32))).astype(LOW)
+    second_pair = pair_of(second.astype(LOW))
+    ups = [up_call(places, one, gathered, up_shift) for one in second_pair]
+    active_pair = ups[0][0], ups[1][0]
+
+    def owner_sum(grads):
+        return lax.psum_scatter(
+            grads.reshape(-1, grads.shape[2]),
+            BOTH,
+            scatter_dimension=0,
+            tiled=True,
+            axis_index_groups=turned_groups,
+        ).reshape(2, depth, -1)
+
+    lower_grads = owner_grads(places, fed_pair, active_pair)
+    lower_sum = owner_sum(lower_grads)
+    fed_late = after(fed_pair, lower_grads)
+    hiddens = [
+        hidden_call(places, one, gathered, up[1]) for one, up in zip(fed_late, ups)
+    ]
+    hidden_pair = hiddens[0][0], hiddens[1][0]
+    up_bias_sums = (hiddens[0][1] + hiddens[1][1]).reshape(-1)
+    second_far = exchange(down_call(places, hidden_pair[1], gathered, 0, LOW), far_core=1)
+    second_own = down_call(places, hidden_pair[0], gathered, 0, jnp.float32)
+    second_grad = second_own + second_far.astype(jnp.float32)
     middle_back, gain_two_grad, shift_two_grad = flat_norm_back(
         second_grad, unit_two, spread_two, gain_two
     )
     middle_grad = row_mask * (grad_top + middle_back)
     attended_grad = middle_grad.astype(LOW)
-    attended_rows, attended_turned = pair_up(places, attended_grad)
-    grad_mixed = mat(attended_rows, output_full).astype(LOW)
-    grad_qkv = attend_back_all(qkv, key_bias, grad_mixed, mixed, totals, rows)
-    early = jnp.concatenate(
+    attended_pair = pair_of(attended_grad)
+    upper_grads = owner_grads(places, second_pair, hidden_pair)
+    upper_sum = owner_sum(upper_grads)
+
+    def heads_back(one, qkv, mixed, totals):
+        grad_mixed = mat(one, output_full).astype(LOW)
+        return attend_back_call(qkv, key_bias, grad_mixed, mixed, totals)
+
+    attended_late = after(attended_pair, upper_grads)
+    back_own = heads_back(attended_late[0], qkv_own, mixed_own, totals_own)
+    back_far = heads_back(attended_late[1], qkv_far, mixed_far, totals_far)
+    back_pair = back_own, back_far
+    operands = [(normed_pair, back_pair), (attended_pair, mixed_pair)]
+    last_sends = weight_pieces(places, operands, True)
+    last_first = scatter_first(last_sends)
+    back_late = after(back_pair, last_sends)
+    normed_far = exchange(mat_far(back_late[1], qkv_full).astype(LOW), far_core=1)
+    normed_grad = mat_far(back_late[0], qkv_full) + normed_far.astype(jnp.float32)
+    last_keeps = weight_pieces(places, operands, False)
+    first_back, gain_one_grad, shift_one_grad = flat_norm_back(
+        normed_grad, unit_one, spread_one, gain_one
+    )
+    images_own = middle_grad + first_back
+    qkv_sums = (column_flat(back_own) + column_flat(back_far)).reshape(4, 3, -1)
+    vector = jnp.concatenate(
         [
             column_flat(attended_grad),
             gain_two_grad,
             shift_two_grad,
             column_flat(fed_grad),
-            spread_core(up_bias_sums.reshape(2, -1)),
-        ]
-    )
-    last_owned = scatter_grads(
-        [(normed_turned, head_cut(grad_qkv)), (attended_turned, head_cut(mixed))], core
-    )
-    normed_grad = half_sums(grad_qkv, qkv_full, rows)
-    first_back, gain_one_grad, shift_one_grad = flat_norm_back(
-        normed_grad, unit_one, spread_one, gain_one
-    )
-    images_own = middle_grad + first_back
-    qkv_sums = column_flat(grad_qkv).reshape(4, 3, -1)
-    late = jnp.concatenate(
-        [
+            head_spread(up_bias_sums),
             gain_one_grad,
             shift_one_grad,
             head_spread(qkv_sums[:, 0].reshape(-1)),
             head_spread(qkv_sums[:, 2].reshape(-1)),
         ]
     )
+    last_first = after(last_first, last_keeps)
+    last_second = scatter_second(last_keeps, last_first)
+    vector, vectors = vector_first(vector)
+    last_line = scatter_line(last_keeps, last_first, after(last_second, images_own, *vectors))
+    last_z = scatter_z(last_line)
+    fed_far = exchange(down_call(places, active_pair[1], gathered, 1, LOW), far_core=1)
+    fed = down_call(places, active_pair[0], gathered, 1, jnp.float32)
+    fed = fed + fed_far.astype(jnp.float32)
+    layer_own = (row_mask * (middle + fed + down_bias.astype(jnp.float32))).astype(LOW)
+    vector = vector_last(vector, vectors)
+    last_z = after(tuple(last_z), vector)
+    last_owned = scatter_last(last_line[0], last_z, core)
+
+    def owner_last(total):
+        keep = lax.dynamic_index_in_dim(total, core, 0, keepdims=False)
+        send = lax.dynamic_index_in_dim(total, 1 - core, 0, keepdims=False)
+        both = pick_two(core, keep, exchange(send, far_core=1), 0)
+        return both.astype(jnp.float32).transpose(1, 0, 2).reshape(depth, -1)
+
+    lower_owned, upper_owned = owner_last(lower_sum), owner_last(upper_sum)
 
     def to_strips(own, send):
         return pick_two(place_y, own[:strip], exchange(send, far_y=1).astype(own.dtype), 0)
 
     layer_out = to_strips(layer_own, layer_own[half : half + strip])
     images_grad = to_strips(images_own, images_own[half : half + strip].astype(LOW))
-    early = jnp.sum(lax.all_gather(early, BOTH), axis=0)
-    late = vector_sum(late)
-
     def full_columns(owned):
         return owned.transpose(2, 0, 1, 3).reshape(depth, -1)
 
     def head_grad(at):
         return full_columns(last_owned[..., at * LANES : (at + 1) * LANES])
 
+    early, late = vector[: 4 * width + up_bias.shape[0]], vector[4 * width + up_bias.shape[0] :]
     return (
         layer_out,
         images_grad,
@@ -895,9 +1133,9 @@
         early[:width],
         early[width : 2 * width],
         early[2 * width : 3 * width],
-        full_columns(upper_owned),
+        upper_owned,
         early[4 * width :],
-        full_columns(lower_owned).T,
+        lower_owned.T,
         early[3 * width : 4 * width],
     )
 

time: 534 us -> 492 us (0.921)
  Pallas kernels: 84.4 us -> 172 us
  matrix products: 97.1 us -> 27.2 us
  starting transfers between devices: 74.3 us -> 28.9 us
  local copies, waits for them, and re-layouts: 60.3 us -> 30.3 us
  waiting for transfers between devices: 166 us -> 184 us
    pallas_call x9 -> x17, Pallas kernels: 74.6 us -> 162 us  [the longest x2 32.7 us: attend_back_call(): pl.pallas_call(attend_back_kernel, grid=(blocks,), in_specs=[pl.BlockSpec...]
    ppermute x50 -> x36, starting transfers between devices: 74.2 us -> 28.8 us  [exchange(): return lax.ppermute(value, BOTH, pairs)]
    dot_general x24 -> x0, matrix products: 34.6 us -> none  [mat_rows(): lax.dot_general(left, right, (((0,), (0,)), ((), ())), preferred_element_...]
    dot_general x4, matrix products: 37 us -> 13.3 us  [mat(): return jnp.dot(left, right, preferred_element_type=jnp.float32)]
    transpose x4 -> x1, local copies, waits for them, and re-layouts: 20.6 us -> 0.83 us  [whole_images(): return (layer_out, images_grad, late[:width], late[width:2 * width], head...]
    ppermute x50 -> x36, waiting for transfers between devices: 166 us -> 184 us  [exchange(): return lax.ppermute(value, BOTH, pairs)]
    dot_general x8 -> x4, matrix products: 25.6 us -> 13.9 us  [mat_far(): lax.dot_general(left, right, (((1,), (1,)), ((), ())), preferred_element_...]
    unnamed x169 -> x128, local copies, waits for them, and re-layouts: 23.1 us -> 13.2 us
  transfers between devices with their start and end apart: 52 -> 39, of which waited for: 22 -> 18; matrix products, arithmetic and copies ran while one was open for 19% -> 15% of each run, Pallas kernels for 16% -> 31%
where the time goes in v3:
time: 492 us; the launch traced here: 483 us
  waiting for transfers between devices  184 us (37%)
  Pallas kernels  172 us (35%)
  local copies, waits for them, and re-layouts  30.3 us (6%)
  starting transfers between devices  28.9 us (6%)
  matrix products  27.2 us (6%)
  other arithmetic  25.1 us (5%)
  between operations  16.2 us (3%)
    ppermute x36, waiting for transfers between devices, exchange(): return lax.ppermute(value, BOTH, pairs)  184 us
    pallas_call x2, Pallas kernels, attend_back_call(): pl.pallas_call(attend_back_kernel, grid=(blocks,), in_specs=[pl.BlockSpec...  32.7 us
    pallas_call x4, Pallas kernels, down_call(): pl.pallas_call(down_kernel, grid_spec=pltpu.PrefetchScalarGridSpec(num_sc...  30.3 us
    ppermute x36, starting transfers between devices, exchange(): return lax.ppermute(value, BOTH, pairs)  28.8 us
    pallas_call x2, Pallas kernels, owner_grads(): pl.pallas_call(owner_kernel, grid_spec=pltpu.PrefetchScalarGridSpec(num_s...  22.4 us
    pallas_call x2, Pallas kernels, weight_pieces(): pl.pallas_call(kernel, grid_spec=pltpu.PrefetchScalarGridSpec(num_scalar_...  21.8 us
    pallas_call x2, Pallas kernels, attend_call(): pl.pallas_call(attend_kernel, grid=(blocks,), in_specs=[pl.BlockSpec((row...  18.8 us
    pallas_call x2, Pallas kernels, up_call(): pl.pallas_call(up_kernel, grid_spec=pltpu.PrefetchScalarGridSpec(num_scal...  17.3 us
  transfers between devices with their start and end apart: 39, of which 18 were waited for; matrix products, arithmetic and copies ran while one was open for 15% of the time, Pallas kernels for 31%

profile of v3, /device:TPU:0, one launch (start us, length us, event | category | flops | bytes accessed | tf_op | source)
XLA Modules:
  0.0 483.4 jit_solution(12994096804396021947)
XLA Ops:
  10.0 1.2 collective-permute-done.12
  13.9 1.7 copy.94
  16.0 1.3 constant_dynamic-slice_fusion.10
  17.3 2.9 collective-permute-start.1
  20.2 1.6 collective-permute-start.2
  21.7 2.6 collective-permute-start.3
  26.5 13.5 %collective-permute-done.2.refs_1_ = bf16[2,128,512]{2,1,0:T(8,128)(2,1)S(1)} collective-permute-done((bf16[2,128,512]{2,1,0:T(8,128)(2,1)S(1)}, bf16[2,128,512]{2,1,0:T(8,128)(2,1)S(1)}, u32[]{:S(2)}, u32[]{:S(2)}) %collective-permute-start.2) | collective-permute-done | bytes 262176 | tf_op jit(solution)/shard_map/ppermute | solution.py:303
  40.0 12.9 %collective-permute-done.3.refs_2_ = bf16[2,128,512]{2,1,0:T(8,128)(2,1)S(1)} collective-permute-done((bf16[2,128,512]{2,1,0:T(8,128)(2,1)S(1)}, bf16[2,128,512]{2,1,0:T(8,128)(2,1)S(1)}, u32[]{:S(2)}, u32[]{:S(2)}) %collective-permute-start.3) | collective-permute-done | bytes 262176 | tf_op jit(solution)/shard_map/ppermute | solution.py:303
  54.3 2.3 shard_map.305
  57.6 1.8 convert_reduce_fusion.2
  60.0 2.0 fusion.9
  63.5 1.5 collective-permute-start.7
  65.1 1.7 collective-permute-done.5.left_far.left_ref
  66.7 22.1 %collective-permute-done.7.refs_1_ = bf16[4,128,512]{2,1,0:T(8,128)(2,1)S(1)} collective-permute-done((bf16[4,128,512]{2,1,0:T(8,128)(2,1)S(1)}, bf16[4,128,512]{2,1,0:T(8,128)(2,1)S(1)}, u32[]{:S(2)}, u32[]{:S(2)}) %collective-permute-start.7) | collective-permute-done | bytes 524320 | tf_op jit(solution)/shard_map/ppermute | solution.py:303
  90.5 2.9 shard_map.306
  94.4 37.7 %collective-permute-done.10.refs_3_ = bf16[2,4,128,512]{3,2,1,0:T(8,128)(2,1)S(1)} collective-permute-done((bf16[2,4,128,512]{3,2,1,0:T(8,128)(2,1)}, bf16[2,4,128,512]{3,2,1,0:T(8,128)(2,1)S(1)}, u32[]{:S(2)}, u32[]{:S(2)}) %collective-permute-start.10) | collective-permute-done | bytes 1048608 | tf_op jit(solution)/shard_map/ppermute | solution.py:303
  133.1 4.6 shard_map.307
  137.7 5.2 %add_convert_fusion.qkv_ref = bf16[592,1536]{1,0:T(8,128)(2,1)} fusion(bf16[592,1024]{1,0:T(8,128)(2,1)S(1)} %collective-permute-done.6.refs_6_.refs_7_.refs_8_.refs_9_, bf16[1024,1536]{1,0:T(8,128)(2,1)} %bitcast.244, f32[1536]{0:T(1024)S(1)} %add.252), kind=kOutput, calls=%fused_computation.5 | convolution fusion | flops 1864089600 | bytes 6182912 | tf_op jit(solution)/shard_map/dot_general | solution.py:863
  143.6 9.6 %shard_map.309 = (bf16[592,512]{1,0:T(8,128)(2,1)}, f32[4,8,592]{2,1,0:T(8,128)}) custom-call(bf16[592,1536]{1,0:T(8,128)(2,1)} %add_convert_fusion.qkv_ref, bf16[592,128]{1,0:T(8,128)(2,1)} %broadcast_in_dim.60.bias_ref), custom_call_target="tpu_custom_call" | custom-call | flops 2871001088 | bytes 2424832 | tf_op jit(solution)/shard_map/pallas_call | solution.py:814
  153.2 2.0 convolution_convert_fusion
  156.0 3.3 add_convert_fusion.1.qkv_ref
  159.2 9.2 %shard_map.308 = (bf16[592,512]{1,0:T(8,128)(2,1)}, f32[4,8,592]{2,1,0:T(8,128)}) custom-call(bf16[592,1536]{1,0:T(8,128)(2,1)} %add_convert_fusion.1.qkv_ref, bf16[592,128]{1,0:T(8,128)(2,1)} %broadcast_in_dim.60.bias_ref), custom_call_target="tpu_custom_call" | custom-call | flops 2871001088 | bytes 2424832 | tf_op jit(solution)/shard_map/pallas_call | solution.py:814
  168.5 2.0 bitcast_add_fusion
  171.3 1.6 add_convert_fusion.2.left_ref
  174.1 8.6 %shard_map.310 = (bf16[592,2048]{1,0:T(8,128)(2,1)}, bf16[592,2048]{1,0:T(8,128)(2,1)}) custom-call(s32[4]{0:T(128)} %pad_add_fusion.places_ref.refs_0_, bf16[592,1024]{1,0:T(8,128)(2,1)} %add_convert_fusion.2.left_ref, bf16[8,2,128,2048]{3,2,1,0:T(8,128)(2,1)} %bitcast.201, f32[1,2048]{1,0:T(1,128)} %reshape_reshape.6.shift_ref), custom_call_target="tpu_custom_call" | custom-call | flops 2483027968 | bytes 10256384 | tf_op jit(solution)/shard_map/pallas_call | solution.py:531
  182.7 8.7 %shard_map.312 = (bf16[592,2048]{1,0:T(8,128)(2,1)}, bf16[592,2048]{1,0:T(8,128)(2,1)}) custom-call(s32[4]{0:T(128)} %pad_add_fusion.places_ref.refs_0_, bf16[592,1024]{1,0:T(8,128)(2,1)} %collective-permute-done.13.left_ref.left_far, bf16[8,2,128,2048]{3,2,1,0:T(8,128)(2,1)} %bitcast.202, f32[1,2048]{1,0:T(1,128)} %reshape_reshape.6.shift_ref), custom_call_target="tpu_custom_call" | custom-call | flops 2483027968 | bytes 10256384 | tf_op jit(solution)/shard_map/pallas_call | solution.py:531
  191.4 11.2 %shard_map.314 = bf16[2,1024,1024]{2,1,0:T(8,128)(2,1)} custom-call(s32[4]{0:T(128)} %pad_add_fusion.places_ref.refs_0_, bf16[592,1024]{1,0:T(8,128)(2,1)} %copy-done.21, bf16[592,1024]{1,0:T(8,128)(2,1)} %copy-done.24, bf16[592,2048]{1,0:T(8,128)(2,1)} %get-tuple-element.70.left_ref.right_ref, bf16[592,2048]{1,0:T(8,128)(2,1)} %get-tuple-element.71.left_ref.right_far), custom_call_target="tpu_custom_call" | custom-call | flops 4966055936 | bytes 11468800 | tf_op jit(solution)/shard_map/pallas_call | solution.py:639
  202.7 7.9 %shard_map.317 = (bf16[592,2048]{1,0:T(8,128)(2,1)}, f32[1,2048]{1,0:T(1,128)}) custom-call(s32[4]{0:T(128)} %pad_add_fusion.places_ref.refs_0_, bf16[592,1024]{1,0:T(8,128)(2,1)} %copy-done.24, bf16[8,2,128,2048]{3,2,1,0:T(8,128)(2,1)} %bitcast.203, bf16[592,2048]{1,0:T(8,128)(2,1)} %get-tuple-element.76.slope_ref), custom_call_target="tpu_custom_call" | custom-call | flops 2483027968 | bytes 10256384 | tf_op jit(solution)/shard_map/pallas_call | solution.py:566
  210.6 7.5 %shard_map.318 = bf16[592,1024]{1,0:T(8,128)(2,1)} custom-call(s32[4]{0:T(128)} %pad_add_fusion.places_ref.refs_0_, bf16[592,2048]{1,0:T(8,128)(2,1)} %get-tuple-element.77.left_ref.right_far, bf16[8,2,128,2048]{3,2,1,0:T(8,128)(2,1)} %bitcast.204), custom_call_target="tpu_custom_call" | custom-call | flops 2483027968 | bytes 9043968 | tf_op jit(solution)/shard_map/pallas_call | solution.py:608
  218.2 7.4 %shard_map.313 = bf16[592,1024]{1,0:T(8,128)(2,1)} custom-call(s32[4]{0:T(128)} %pad_add_fusion.places_ref.refs_0_, bf16[592,2048]{1,0:T(8,128)(2,1)} %get-tuple-element.71.left_ref.right_far, bf16[8,2,128,2048]{3,2,1,0:T(8,128)(2,1)} %bitcast.205), custom_call_target="tpu_custom_call" | custom-call | flops 2483027968 | bytes 9043968 | tf_op jit(solution)/shard_map/pallas_call | solution.py:608
  226.0 7.6 %shard_map.311 = f32[592,1024]{1,0:T(8,128)} custom-call(s32[4]{0:T(128)} %pad_add_fusion.places_ref.refs_0_, bf16[592,2048]{1,0:T(8,128)(2,1)} %get-tuple-element.70.left_ref.right_ref, bf16[8,2,128,2048]{3,2,1,0:T(8,128)(2,1)} %bitcast.206), custom_call_target="tpu_custom_call" | custom-call | flops 2483027968 | bytes 9043968 | tf_op jit(solution)/shard_map/pallas_call | solution.py:608
  233.7 7.9 %shard_map.315 = (bf16[592,2048]{1,0:T(8,128)(2,1)}, f32[1,2048]{1,0:T(1,128)}) custom-call(s32[4]{0:T(128)} %pad_add_fusion.places_ref.refs_0_, bf16[592,1024]{1,0:T(8,128)(2,1)} %copy-done.21, bf16[8,2,128,2048]{3,2,1,0:T(8,128)(2,1)} %bitcast.207, bf16[592,2048]{1,0:T(8,128)(2,1)} %get-tuple-element.73.slope_ref), custom_call_target="tpu_custom_call" | custom-call | flops 2483027968 | bytes 10256384 | tf_op jit(solution)/shard_map/pallas_call | solution.py:566
  242.3 7.7 %shard_map.316 = f32[592,1024]{1,0:T(8,128)} custom-call(s32[4]{0:T(128)} %pad_add_fusion.places_ref.refs_0_, bf16[592,2048]{1,0:T(8,128)(2,1)} %get-tuple-element.74.left_ref.right_ref, bf16[8,2,128,2048]{3,2,1,0:T(8,128)(2,1)} %bitcast.208), custom_call_target="tpu_custom_call" | custom-call | flops 2483027968 | bytes 9043968 | tf_op jit(solution)/shard_map/pallas_call | solution.py:608
  250.1 3.4 multiply_reduce_fusion.1
  253.6 5.1 %convert_reduce_fusion.4 = (f32[1024]{0:T(1024)S(1)}, bf16[592,1024]{1,0:T(8,128)(2,1)S(1)}, f32[592,1024]{1,0:T(8,128)}, bf16[592,1024]{1,0:T(8,128)(2,1)}) fusion(f32[592]{0:T(1024)S(1)} %broadcast_multiply_fusion.2, f32[592]{0:T(1024)S(1)} %broadcast_multiply_fusion.4, f32[592,1024]{1,0:T(8,128)} %copy-done.4, f32[592]{0:T(1024)S(1)} %broadcast_multiply_fusion.3, ...), kind=kLoop, calls=%fused_computation.27 | loop fusion | flops 14547968 | bytes 16997952 | tf_op jit(solution)/shard_map/reduce_sum | solution.py:884
  258.9 11.2 %shard_map.319 = bf16[2,1024,1024]{2,1,0:T(8,128)(2,1)} custom-call(s32[4]{0:T(128)} %pad_add_fusion.places_ref.refs_0_, bf16[592,1024]{1,0:T(8,128)(2,1)} %add_convert_fusion.2.left_ref, bf16[592,1024]{1,0:T(8,128)(2,1)} %collective-permute-done.13.left_ref.left_far, bf16[592,2048]{1,0:T(8,128)(2,1)} %get-tuple-element.74.left_ref.right_ref, ...), custom_call_target="tpu_custom_call" | custom-call | flops 4966055936 | bytes 11468800 | tf_op jit(solution)/shard_map/pallas_call | solution.py:639
  271.4 3.3 convolution_convert_fusion.2.grad_ref
  274.7 16.3 %shard_map.321.refs_10_ = bf16[592,1536]{1,0:T(8,128)(2,1)} custom-call(bf16[592,1536]{1,0:T(8,128)(2,1)} %add_convert_fusion.qkv_ref, bf16[592,128]{1,0:T(8,128)(2,1)} %broadcast_in_dim.60.bias_ref, bf16[592,512]{1,0:T(8,128)(2,1)} %convolution_convert_fusion.2.grad_ref, bf16[592,512]{1,0:T(8,128)(2,1)} %get-tuple-element.69.mixed_ref.refs_20_, ...), custom_call_target="tpu_custom_call" | custom-call | flops 7177502720 | bytes 4849664 | tf_op jit(solution)/shard_map/pallas_call | solution.py:841
  291.0 1.6 convolution_convert_fusion.3.grad_ref
  292.6 16.4 %shard_map.320.refs_5_ = bf16[592,1536]{1,0:T(8,128)(2,1)} custom-call(bf16[592,1536]{1,0:T(8,128)(2,1)} %add_convert_fusion.1.qkv_ref, bf16[592,128]{1,0:T(8,128)(2,1)} %broadcast_in_dim.60.bias_ref, bf16[592,512]{1,0:T(8,128)(2,1)} %convolution_convert_fusion.3.grad_ref, bf16[592,512]{1,0:T(8,128)(2,1)} %get-tuple-element.67.mixed_ref.refs_15_, ...), custom_call_target="tpu_custom_call" | custom-call | flops 7177502720 | bytes 4849664 | tf_op jit(solution)/shard_map/pallas_call | solution.py:841
  309.0 10.6 %shard_map.322 = (bf16[2,512,512]{2,1,0:T(8,128)(2,1)}, bf16[2,512,512]{2,1,0:T(8,128)(2,1)}) custom-call(s32[4]{0:T(128)} %pad_add_fusion.places_ref.refs_0_, bf16[592,1024]{1,0:T(8,128)(2,1)} %copy-done.1, bf16[592,1024]{1,0:T(8,128)(2,1)} %copy-done.1, bf16[592,1024]{1,0:T(8,128)(2,1)} %copy-done.1, bf16[592,1024]{1,0:T(8,128)(2,1)} %copy-done.1, ...), custom_call_target="tpu_custom_call" | custom-call | flops 2483027968 | bytes 11796480 | tf_op jit(solution)/shard_map/pallas_call | solution.py:713
  319.6 2.0 collective-permute-start.26
  321.7 1.4 collective-permute-start.27
  323.7 5.0 %convolution_convert_fusion.1 = bf16[592,1024]{1,0:T(8,128)(2,1)} fusion(bf16[592,1536]{1,0:T(8,128)(2,1)S(1)} %copy-done.14, bf16[1024,1536]{1,0:T(8,128)(2,1)} %bitcast.245), kind=kOutput, calls=%fused_computation.44 | convolution fusion | flops 1862877184 | bytes 6176768 | tf_op jit(solution)/shard_map/dot_general | solution.py:498
  328.9 11.2 %shard_map.323 = (bf16[2,512,512]{2,1,0:T(8,128)(2,1)}, bf16[2,512,512]{2,1,0:T(8,128)(2,1)}) custom-call(s32[4]{0:T(128)} %pad_add_fusion.places_ref.refs_0_, bf16[592,1024]{1,0:T(8,128)(2,1)} %copy-done.1, bf16[592,1024]{1,0:T(8,128)(2,1)} %copy-done.1, bf16[592,1024]{1,0:T(8,128)(2,1)} %copy-done.1, bf16[592,1024]{1,0:T(8,128)(2,1)} %copy-done.1, ...), custom_call_target="tpu_custom_call" | custom-call | flops 2483027968 | bytes 11796480 | tf_op jit(solution)/shard_map/pallas_call | solution.py:713
  340.2 17.6 %collective-permute-done.26.one_a = bf16[2,512,512]{2,1,0:T(8,128)(2,1)S(1)} collective-permute-done((bf16[2,512,512]{2,1,0:T(8,128)(2,1)}, bf16[2,512,512]{2,1,0:T(8,128)(2,1)S(1)}, u32[]{:S(2)}, u32[]{:S(2)}) %collective-permute-start.26) | collective-permute-done | bytes 1048608 | tf_op jit(solution)/shard_map/ppermute | solution.py:303
  357.8 35.5 %collective-permute-done.27.two_a = bf16[2,512,512]{2,1,0:T(8,128)(2,1)} collective-permute-done((bf16[2,512,512]{2,1,0:T(8,128)(2,1)}, bf16[2,512,512]{2,1,0:T(8,128)(2,1)}, u32[]{:S(2)}, u32[]{:S(2)}) %collective-permute-start.27) | collective-permute-done | bytes 1048608 | tf_op jit(solution)/shard_map/ppermute | solution.py:303
  393.3 1.3 fusion.15
  394.8 1.2 fusion.14
  396.0 4.8 fusion.41
  400.9 1.2 collective-permute-done.20
  402.1 2.9 collective-permute-start.21
  405.0 1.5 collective-permute-start.22
  406.6 1.4 collective-permute-start.23
  408.9 2.3 collective-permute-start.28
  411.7 3.1 collective-permute-done.23
  416.1 17.5 %collective-permute-done.24 = f32[12288]{0:T(1024)S(1)} collective-permute-done((f32[12288]{0:T(1024)S(1)}, f32[12288]{0:T(1024)S(1)}, u32[]{:S(2)}, u32[]{:S(2)}) %collective-permute-start.24) | collective-permute-done | bytes 49184 | tf_op jit(solution)/shard_map/ppermute | solution.py:303
  433.8 2.2 copy.83
  436.0 1.7 collective-permute-done.25
  440.6 3.0 shard_map.324
  444.5 3.5 collective-permute-start.32
  448.3 6.0 %collective-permute-done.30 = bf16[2,128,512]{2,1,0:T(8,128)(2,1)S(1)} collective-permute-done((bf16[2,128,512]{2,1,0:T(8,128)(2,1)}, bf16[2,128,512]{2,1,0:T(8,128)(2,1)S(1)}, u32[]{:S(2)}, u32[]{:S(2)}) %collective-permute-start.30) | collective-permute-done | bytes 262176 | tf_op jit(solution)/shard_map/ppermute | solution.py:303
  454.2 10.1 %collective-permute-done.31 = bf16[2,128,512]{2,1,0:T(8,128)(2,1)S(1)} collective-permute-done((bf16[2,128,512]{2,1,0:T(8,128)(2,1)}, bf16[2,128,512]{2,1,0:T(8,128)(2,1)S(1)}, u32[]{:S(2)}, u32[]{:S(2)}) %collective-permute-start.31) | collective-permute-done | bytes 262176 | tf_op jit(solution)/shard_map/ppermute | solution.py:303
  464.7 3.2 copy.84
  (293 shorter events, 37.9 us)
Async XLA Ops:
  7.2 166.9 %all-gather.2.cloned.1.call-start = ((), (), s32[]{:S(2)}) async-start(), calls=%async_computation.2 | async-start | bytes 8912896 | tf_op jit(solution)/shard_map/all_gather | solution.py:943
  9.5 1.7 collective-permute-start.12
  12.1 456.0 %reduce-scatter.5.cloned.1.call-start = ((), (), s32[]{:S(2)}) async-start(), calls=%async_computation.4 | async-start | bytes 4456448 | tf_op jit(solution)/shard_map/reduce_scatter | solution.py:1028
  12.4 1.4 collective-permute-start
  13.9 10.4 %copy-start.27 = (bf16[2,2,64,512]{3,2,1,0:T(8,128)(2,1)}, bf16[2,2,64,512]{3,2,1,0:T(8,128)(2,1)S(1)}, u32[]{:S(2)}) copy-start(bf16[2,2,64,512]{3,2,1,0:T(8,128)(2,1)S(1)} %copy.64) | copy-start | bytes 786436
  16.0 9.2 %copy-start.57 = (s32[2]{0:T(128)S(1)}, s32[2]{0:T(128)}, u32[]{:S(2)}) copy-start(s32[2]{0:T(128)} %param.20) | copy-start | bytes 28
  16.0 10.4 %copy-start.46 = (bf16[1024]{0:T(1024)(128)(2,1)S(1)}, bf16[1024]{0:T(1024)(128)(2,1)}, u32[]{:S(2)}) copy-start(bf16[1024]{0:T(1024)(128)(2,1)} %param.21) | copy-start | bytes 6148
  16.0 10.4 %copy-start.47 = (bf16[1024]{0:T(1024)(128)(2,1)S(1)}, bf16[1024]{0:T(1024)(128)(2,1)}, u32[]{:S(2)}) copy-start(bf16[1024]{0:T(1024)(128)(2,1)} %param.22) | copy-start | bytes 6148
  17.3 42.7 %copy-start.9 = (bf16[2,1,296,1024]{3,2,0,1:T(8,128)(2,1)}, bf16[2,1,296,1024]{3,2,0,1:T(8,128)(2,1)S(1)}, u32[]{:S(2)}) copy-start(bf16[2,1,296,1024]{3,2,0,1:T(8,128)(2,1)S(1)} %get-tuple-element.171) | copy-start | bytes 3637252
  17.3 39.3 %collective-permute-start.1 = (bf16[2,296,1024]{2,1,0:T(8,128)(2,1)}, bf16[2,296,1024]{2,1,0:T(8,128)(2,1)S(1)}, u32[]{:S(2)}, u32[]{:S(2)}) collective-permute-start(bf16[2,296,1024]{2,1,0:T(8,128)(2,1)} %get-tuple-element.172), channel_id=1, source_target_pairs={{0,1},{1,0},{2,3},{3,2},{4,5},{5,4},{6,7},{7,6},{8,9},{9,8},{10,11... | collective-permute-start | bytes 3637256 | tf_op jit(solution)/shard_map/ppermute | solution.py:303
  20.2 19.8 %collective-permute-start.2 = (bf16[2,128,512]{2,1,0:T(8,128)(2,1)S(1)}, bf16[2,128,512]{2,1,0:T(8,128)(2,1)S(1)}, u32[]{:S(2)}, u32[]{:S(2)}) collective-permute-start(bf16[2,128,512]{2,1,0:T(8,128)(2,1)S(1)} %bitcast.220), channel_id=1, source_target_pairs={{0,8},{1,9},{2,10},{3,11},{4,12},{5,13},{6,14},{7,15},{8,0},{9,1},... | collective-permute-start | bytes 786440 | tf_op jit(solution)/shard_map/ppermute | solution.py:303
  21.7 31.1 %collective-permute-start.3 = (bf16[2,128,512]{2,1,0:T(8,128)(2,1)S(1)}, bf16[2,128,512]{2,1,0:T(8,128)(2,1)S(1)}, u32[]{:S(2)}, u32[]{:S(2)}) collective-permute-start(bf16[2,128,512]{2,1,0:T(8,128)(2,1)S(1)} %bitcast.221), channel_id=1, source_target_pairs={{0,16},{1,17},{2,18},{3,19},{4,20},{5,21},{6,22},{7,23},{8,24},{9,... | collective-permute-start | bytes 786440 | tf_op jit(solution)/shard_map/ppermute | solution.py:303
  24.3 28.6 %collective-permute-start.4 = (bf16[2,128,512]{2,1,0:T(8,128)(2,1)S(1)}, bf16[2,128,512]{2,1,0:T(8,128)(2,1)S(1)}, u32[]{:S(2)}, u32[]{:S(2)}) collective-permute-start(bf16[2,128,512]{2,1,0:T(8,128)(2,1)S(1)} %bitcast.222), channel_id=1, source_target_pairs={{0,24},{1,25},{2,26},{3,27},{4,28},{5,29},{6,30},{7,31},{8,16},{9,... | collective-permute-start | bytes 786440 | tf_op jit(solution)/shard_map/ppermute | solution.py:303
  40.0 12.9 %copy-start.37 = (bf16[2,128,512]{2,1,0:T(8,128)(2,1)}, bf16[2,128,512]{2,1,0:T(8,128)(2,1)S(1)}, u32[]{:S(2)}) copy-start(bf16[2,128,512]{2,1,0:T(8,128)(2,1)S(1)} %collective-permute-done.2.refs_1_) | copy-start | bytes 786436
  59.4 96.0 %copy-start.5 = (bf16[1,2,296,1024]{3,2,0,1:T(8,128)(2,1)}, bf16[1,2,296,1024]{3,2,0,1:T(8,128)(2,1)S(1)}, u32[]{:S(2)}) copy-start(bf16[1,2,296,1024]{3,2,0,1:T(8,128)(2,1)S(1)} %get-tuple-element.166) | copy-start | bytes 3637252
  62.0 31.3 %copy-start.1 = (bf16[592,1024]{1,0:T(8,128)(2,1)}, bf16[592,1024]{1,0:T(8,128)(2,1)S(1)}, u32[]{:S(2)}) copy-start(bf16[592,1024]{1,0:T(8,128)(2,1)S(1)} %get-tuple-element.176.refs_1_.refs_2_.refs_3_.refs_4_) | copy-start | bytes 3637252
  62.0 32.1 %copy-start.52 = (bf16[1024]{0:T(1024)(128)(2,1)S(1)}, bf16[1024]{0:T(1024)(128)(2,1)}, u32[]{:S(2)}) copy-start(bf16[1024]{0:T(1024)(128)(2,1)} %param.27) | copy-start | bytes 6148
  62.0 32.1 %copy-start.53 = (bf16[1024]{0:T(1024)(128)(2,1)S(1)}, bf16[1024]{0:T(1024)(128)(2,1)}, u32[]{:S(2)}) copy-start(bf16[1024]{0:T(1024)(128)(2,1)} %param.24) | copy-start | bytes 6148
  62.0 3.0 collective-permute-start.6
  63.1 3.6 collective-permute-start.5
  63.5 25.3 %collective-permute-start.7 = (bf16[4,128,512]{2,1,0:T(8,128)(2,1)S(1)}, bf16[4,128,512]{2,1,0:T(8,128)(2,1)S(1)}, u32[]{:S(2)}, u32[]{:S(2)}) collective-permute-start(bf16[4,128,512]{2,1,0:T(8,128)(2,1)S(1)} %copy-done.30), channel_id=1, source_target_pairs={{0,4},{1,5},{2,6},{3,7},{4,0},{5,1},{6,2},{7,3},{8,12},{9,13},{10,... | collective-permute-start | bytes 1572872 | tf_op jit(solution)/shard_map/ppermute | solution.py:303
  65.0 23.8 %collective-permute-start.8 = (bf16[4,128,512]{2,1,0:T(8,128)(2,1)S(1)}, bf16[4,128,512]{2,1,0:T(8,128)(2,1)S(1)}, u32[]{:S(2)}, u32[]{:S(2)}) collective-permute-start(bf16[4,128,512]{2,1,0:T(8,128)(2,1)S(1)} %copy-done.31), channel_id=1, source_target_pairs={{0,1},{1,0},{2,3},{3,2},{4,5},{5,4},{6,7},{7,6},{8,9},{9,8},{10,11... | collective-permute-start | bytes 1572872 | tf_op jit(solution)/shard_map/ppermute | solution.py:303
  65.1 72.6 %copy-start.2 = (bf16[592,1024]{1,0:T(8,128)(2,1)}, bf16[592,1024]{1,0:T(8,128)(2,1)S(1)}, u32[]{:S(2)}) copy-start(bf16[592,1024]{1,0:T(8,128)(2,1)S(1)} %collective-permute-done.6.refs_6_.refs_7_.refs_8_.refs_9_) | copy-start | bytes 3637252
  66.7 26.6 %copy-start.24 = (bf16[592,1024]{1,0:T(8,128)(2,1)}, bf16[592,1024]{1,0:T(8,128)(2,1)S(1)}, u32[]{:S(2)}) copy-start(bf16[592,1024]{1,0:T(8,128)(2,1)S(1)} %collective-permute-done.5.left_far.left_ref) | copy-start | bytes 3637252
  93.4 38.7 %collective-permute-start.10 = (bf16[2,4,128,512]{3,2,1,0:T(8,128)(2,1)}, bf16[2,4,128,512]{3,2,1,0:T(8,128)(2,1)S(1)}, u32[]{:S(2)}, u32[]{:S(2)}) collective-permute-start(bf16[2,4,128,512]{3,2,1,0:T(8,128)(2,1)} %get-tuple-element.65.refs_2_), channel_id=1, source_target_pairs={{0,4},{1,5},{2,6},{3,7},{4,0},{5,1},{6,2},{7,3},{8,12},{9,13},{10,... | collective-permute-start | bytes 3145736 | tf_op jit(solution)/shard_map/ppermute | solution.py:303
  93.8 38.8 %collective-permute-start.9 = (bf16[2,4,128,512]{3,2,1,0:T(8,128)(2,1)}, bf16[2,4,128,512]{3,2,1,0:T(8,128)(2,1)}, u32[]{:S(2)}, u32[]{:S(2)}) collective-permute-start(bf16[2,4,128,512]{3,2,1,0:T(8,128)(2,1)} %get-tuple-element.64.refs_0_), channel_id=1, source_target_pairs={{0,1},{1,0},{2,3},{3,2},{4,5},{5,4},{6,7},{7,6},{8,9},{9,8},{10,11... | collective-permute-start | bytes 3145736 | tf_op jit(solution)/shard_map/ppermute | solution.py:303
  143.6 9.6 %copy-start.55 = (bf16[4,2,128,512]{3,2,1,0:T(8,128)(2,1)S(1)}, bf16[4,2,128,512]{3,2,1,0:T(8,128)(2,1)}, u32[]{:S(2)}) copy-start(bf16[4,2,128,512]{3,2,1,0:T(8,128)(2,1)} %get-tuple-element.68) | copy-start | bytes 3145732
  155.3 13.2 %collective-permute-start.11 = (bf16[592,1024]{1,0:T(8,128)(2,1)S(1)}, bf16[592,1024]{1,0:T(8,128)(2,1)S(1)}, u32[]{:S(2)}, u32[]{:S(2)}) collective-permute-start(bf16[592,1024]{1,0:T(8,128)(2,1)S(1)} %convolution_convert_fusion), channel_id=1, source_target_pairs={{0,2},{1,3},{2,0},{3,1},{4,6},{5,7},{6,4},{7,5},{8,10},{9,11},{10,... | collective-permute-start | bytes 3637256 | tf_op jit(solution)/shard_map/ppermute | solution.py:303
  159.2 9.2 %copy-start.6 = (bf16[1,2,296,1024]{3,2,0,1:T(8,128)(2,1)S(1)}, bf16[1,2,296,1024]{3,2,0,1:T(8,128)(2,1)}, u32[]{:S(2)}) copy-start(bf16[1,2,296,1024]{3,2,0,1:T(8,128)(2,1)} %copy-done.5) | copy-start | bytes 3637252
  170.5 79.6 %copy-start.4 = (f32[592,1024]{1,0:T(8,128)}, f32[592,1024]{1,0:T(8,128)S(1)}, u32[]{:S(2)}) copy-start(f32[592,1024]{1,0:T(8,128)S(1)} %bitcast_add_fusion) | copy-start | bytes 7274500
  172.9 9.8 %collective-permute-start.13 = (bf16[592,1024]{1,0:T(8,128)(2,1)}, bf16[592,1024]{1,0:T(8,128)(2,1)}, u32[]{:S(2)}, u32[]{:S(2)}) collective-permute-start(bf16[592,1024]{1,0:T(8,128)(2,1)} %add_convert_fusion.2.left_ref), channel_id=1, source_target_pairs={{0,2},{1,3},{2,0},{3,1},{4,6},{5,7},{6,4},{7,5},{8,10},{9,11},{10,... | collective-permute-start | bytes 3637256 | tf_op jit(solution)/shard_map/ppermute | solution.py:303
  202.7 270.5 %reduce-scatter.3.cloned.1.call-start = ((), (), s32[]{:S(2)}) async-start(), calls=%async_computation.3 | async-start | bytes 4456448 | tf_op jit(solution)/shard_map/reduce_scatter | solution.py:1028
  218.1 32.0 %collective-permute-start.16 = (bf16[592,1024]{1,0:T(8,128)(2,1)}, bf16[592,1024]{1,0:T(8,128)(2,1)}, u32[]{:S(2)}, u32[]{:S(2)}) collective-permute-start(bf16[592,1024]{1,0:T(8,128)(2,1)} %shard_map.318), channel_id=1, source_target_pairs={{0,2},{1,3},{2,0},{3,1},{4,6},{5,7},{6,4},{7,5},{8,10},{9,11},{10,... | collective-permute-start | bytes 3637256 | tf_op jit(solution)/shard_map/ppermute | solution.py:303
  225.6 28.0 %collective-permute-start.14 = (bf16[592,1024]{1,0:T(8,128)(2,1)}, bf16[592,1024]{1,0:T(8,128)(2,1)}, u32[]{:S(2)}, u32[]{:S(2)}) collective-permute-start(bf16[592,1024]{1,0:T(8,128)(2,1)} %shard_map.313), channel_id=1, source_target_pairs={{0,2},{1,3},{2,0},{3,1},{4,6},{5,7},{6,4},{7,5},{8,10},{9,11},{10,... | collective-permute-start | bytes 3637256 | tf_op jit(solution)/shard_map/ppermute | solution.py:303
  242.3 11.2 %copy-start.18 = (f32[592,1024]{1,0:T(8,128)S(1)}, f32[592,1024]{1,0:T(8,128)}, u32[]{:S(2)}) copy-start(f32[592,1024]{1,0:T(8,128)} %shard_map.311) | copy-start | bytes 7274500
  258.7 32.3 %copy-start = (bf16[592,1024]{1,0:T(8,128)(2,1)}, bf16[592,1024]{1,0:T(8,128)(2,1)S(1)}, u32[]{:S(2)}) copy-start(bf16[592,1024]{1,0:T(8,128)(2,1)S(1)} %get-tuple-element.78.refs_11_.refs_12_.refs_13_.refs_14_) | copy-start | bytes 3637252
  258.7 12.6 %collective-permute-start.17 = (bf16[592,1024]{1,0:T(8,128)(2,1)S(1)}, bf16[592,1024]{1,0:T(8,128)(2,1)S(1)}, u32[]{:S(2)}, u32[]{:S(2)}) collective-permute-start(bf16[592,1024]{1,0:T(8,128)(2,1)S(1)} %get-tuple-element.78.refs_11_.refs_12_.refs_13_.refs_14_), channel_id=1, source_target_pairs={{0,2},{1,3},{2,0},{3,1},{4,6},{5,7},{6,4},{7,5},{8,10},{9,11},{10,... | collective-permute-start | bytes 3637256 | tf_op jit(solution)/shard_map/ppermute | solution.py:303
  271.2 143.7 %collective-permute-start.15 = (bf16[289,1024]{1,0:T(8,128)(2,1)S(1)}, bf16[289,1024]{1,0:T(8,128)(2,1)}, u32[]{:S(2)}, u32[]{:S(2)}) collective-permute-start(bf16[289,1024]{1,0:T(8,128)(2,1)S(1)} %slice.185), channel_id=1, source_target_pairs={{0,1},{1,0},{2,3},{3,2},{4,5},{5,4},{6,7},{7,6},{8,9},{9,8},{10,11... | collective-permute-start | bytes 1775624 | tf_op jit(solution)/shard_map/ppermute | solution.py:303
  274.7 16.3 %copy-start.56 = (bf16[4,2,128,512]{3,2,1,0:T(8,128)(2,1)S(1)}, bf16[4,2,128,512]{3,2,1,0:T(8,128)(2,1)}, u32[]{:S(2)}) copy-start(bf16[4,2,128,512]{3,2,1,0:T(8,128)(2,1)} %get-tuple-element.68) | copy-start | bytes 3145732
  309.0 14.0 %copy-start.14 = (bf16[592,1536]{1,0:T(8,128)(2,1)S(1)}, bf16[592,1536]{1,0:T(8,128)(2,1)}, u32[]{:S(2)}) copy-start(bf16[592,1536]{1,0:T(8,128)(2,1)} %shard_map.321.refs_10_) | copy-start | bytes 5455876
  319.6 38.2 %collective-permute-start.26 = (bf16[2,512,512]{2,1,0:T(8,128)(2,1)}, bf16[2,512,512]{2,1,0:T(8,128)(2,1)S(1)}, u32[]{:S(2)}, u32[]{:S(2)}) collective-permute-start(bf16[2,512,512]{2,1,0:T(8,128)(2,1)} %get-tuple-element.82), channel_id=1, source_target_pairs={{0,1},{1,0},{2,3},{3,2},{4,5},{5,4},{6,7},{7,6},{8,9},{9,8},{10,11... | collective-permute-start | bytes 3145736 | tf_op jit(solution)/shard_map/ppermute | solution.py:303
  321.7 71.7 %collective-permute-start.27 = (bf16[2,512,512]{2,1,0:T(8,128)(2,1)}, bf16[2,512,512]{2,1,0:T(8,128)(2,1)}, u32[]{:S(2)}, u32[]{:S(2)}) collective-permute-start(bf16[2,512,512]{2,1,0:T(8,128)(2,1)} %get-tuple-element.83), channel_id=1, source_target_pairs={{0,4},{1,5},{2,6},{3,7},{4,0},{5,1},{6,2},{7,3},{8,12},{9,13},{10,... | collective-permute-start | bytes 3145736 | tf_op jit(solution)/shard_map/ppermute | solution.py:303
  328.7 67.2 %collective-permute-start.18 = (bf16[592,1024]{1,0:T(8,128)(2,1)}, bf16[592,1024]{1,0:T(8,128)(2,1)S(1)}, u32[]{:S(2)}, u32[]{:S(2)}) collective-permute-start(bf16[592,1024]{1,0:T(8,128)(2,1)} %convolution_convert_fusion.1), channel_id=1, source_target_pairs={{0,2},{1,3},{2,0},{3,1},{4,6},{5,7},{6,4},{7,5},{8,10},{9,11},{10,... | collective-permute-start | bytes 3637256 | tf_op jit(solution)/shard_map/ppermute | solution.py:303
  328.9 67.1 %copy-start.22 = (f32[592,1024]{1,0:T(8,128)S(1)}, f32[592,1024]{1,0:T(8,128)}, u32[]{:S(2)}) copy-start(f32[592,1024]{1,0:T(8,128)} %get-tuple-element.175) | copy-start | bytes 7274500
  340.1 55.8 %copy-start.7 = (bf16[1,2,296,1024]{3,2,0,1:T(8,128)(2,1)S(1)}, bf16[1,2,296,1024]{3,2,0,1:T(8,128)(2,1)}, u32[]{:S(2)}) copy-start(bf16[1,2,296,1024]{3,2,0,1:T(8,128)(2,1)} %copy-done.5) | copy-start | bytes 3637252
  340.1 55.8 %copy-start.13 = (bf16[592,1536]{1,0:T(8,128)(2,1)S(1)}, bf16[592,1536]{1,0:T(8,128)(2,1)}, u32[]{:S(2)}) copy-start(bf16[592,1536]{1,0:T(8,128)(2,1)} %shard_map.320.refs_5_) | copy-start | bytes 5455876
  357.8 43.0 %copy-start.23 = (bf16[2,512,512]{2,1,0:T(8,128)(2,1)}, bf16[2,512,512]{2,1,0:T(8,128)(2,1)S(1)}, u32[]{:S(2)}) copy-start(bf16[2,512,512]{2,1,0:T(8,128)(2,1)S(1)} %collective-permute-done.26.one_a) | copy-start | bytes 3145732
  394.7 44.3 %collective-permute-start.29 = (bf16[512,512]{1,0:T(8,128)(2,1)S(1)}, bf16[512,512]{1,0:T(8,128)(2,1)S(1)}, u32[]{:S(2)}, u32[]{:S(2)}) collective-permute-start(bf16[512,512]{1,0:T(8,128)(2,1)S(1)} %fusion.15), channel_id=1, source_target_pairs={{0,1},{1,0},{2,3},{3,2},{4,5},{5,4},{6,7},{7,6},{8,9},{9,8},{10,11... | collective-permute-start | bytes 1572872 | tf_op jit(solution)/shard_map/ppermute | solution.py:303
  396.0 12.0 %copy-start.19 = (f32[592,1024]{1,0:T(8,128)S(1)}, f32[592,1024]{1,0:T(8,128)}, u32[]{:S(2)}) copy-start(f32[592,1024]{1,0:T(8,128)} %get-tuple-element.164) | copy-start | bytes 7274500
  400.8 1.3 collective-permute-start.20
  402.1 6.8 %collective-permute-start.21 = (f32[12288]{0:T(1024)S(1)}, f32[12288]{0:T(1024)S(1)}, u32[]{:S(2)}, u32[]{:S(2)}) collective-permute-start(f32[12288]{0:T(1024)S(1)} %add.278), channel_id=1, source_target_pairs={{0,8},{1,9},{2,10},{3,11},{4,12},{5,13},{6,14},{7,15},{8,0},{9,1},... | collective-permute-start | bytes 147464 | tf_op jit(solution)/shard_map/ppermute | solution.py:303
  405.0 6.5 %collective-permute-start.22 = (f32[12288]{0:T(1024)S(1)}, f32[12288]{0:T(1024)S(1)}, u32[]{:S(2)}, u32[]{:S(2)}) collective-permute-start(f32[12288]{0:T(1024)S(1)} %add.278), channel_id=1, source_target_pairs={{0,16},{1,17},{2,18},{3,19},{4,20},{5,21},{6,22},{7,23},{8,24},{9,... | collective-permute-start | bytes 147464 | tf_op jit(solution)/shard_map/ppermute | solution.py:303
  406.6 8.3 %collective-permute-start.23 = (f32[12288]{0:T(1024)S(1)}, f32[12288]{0:T(1024)S(1)}, u32[]{:S(2)}, u32[]{:S(2)}) collective-permute-start(f32[12288]{0:T(1024)S(1)} %add.278), channel_id=1, source_target_pairs={{0,24},{1,25},{2,26},{3,27},{4,28},{5,29},{6,30},{7,31},{8,16},{9,... | collective-permute-start | bytes 147464 | tf_op jit(solution)/shard_map/ppermute | solution.py:303
  408.9 30.1 %collective-permute-start.28 = (bf16[512,512]{1,0:T(8,128)(2,1)S(1)}, bf16[512,512]{1,0:T(8,128)(2,1)S(1)}, u32[]{:S(2)}, u32[]{:S(2)}) collective-permute-start(bf16[512,512]{1,0:T(8,128)(2,1)S(1)} %fusion.14), channel_id=1, source_target_pairs={{0,4},{1,5},{2,6},{3,7},{4,0},{5,1},{6,2},{7,3},{8,12},{9,13},{10,... | collective-permute-start | bytes 1572872 | tf_op jit(solution)/shard_map/ppermute | solution.py:303
  411.6 36.4 %collective-permute-start.19 = (bf16[289,1024]{1,0:T(8,128)(2,1)S(1)}, bf16[289,1024]{1,0:T(8,128)(2,1)S(1)}, u32[]{:S(2)}, u32[]{:S(2)}) collective-permute-start(bf16[289,1024]{1,0:T(8,128)(2,1)S(1)} %slice.244), channel_id=1, source_target_pairs={{0,1},{1,0},{2,3},{3,2},{4,5},{5,4},{6,7},{7,6},{8,9},{9,8},{10,11... | collective-permute-start | bytes 1775624 | tf_op jit(solution)/shard_map/ppermute | solution.py:303
  414.8 18.8 %collective-permute-start.24 = (f32[12288]{0:T(1024)S(1)}, f32[12288]{0:T(1024)S(1)}, u32[]{:S(2)}, u32[]{:S(2)}) collective-permute-start(f32[12288]{0:T(1024)S(1)} %add_add_fusion), channel_id=1, source_target_pairs={{0,1},{1,0},{2,3},{3,2},{4,5},{5,4},{6,7},{7,6},{8,9},{9,8},{10,11... | collective-permute-start | bytes 147464 | tf_op jit(solution)/shard_map/ppermute | solution.py:303
  433.6 4.2 collective-permute-start.25
  443.6 20.8 %copy-start.32 = (f32[2,128,512]{2,1,0:T(8,128)S(1)}, f32[2,128,512]{2,1,0:T(8,128)}, u32[]{:S(2)}) copy-start(f32[2,128,512]{2,1,0:T(8,128)} %get-tuple-element.94) | copy-start | bytes 1572868
  443.6 10.7 %collective-permute-start.30 = (bf16[2,128,512]{2,1,0:T(8,128)(2,1)}, bf16[2,128,512]{2,1,0:T(8,128)(2,1)S(1)}, u32[]{:S(2)}, u32[]{:S(2)}) collective-permute-start(bf16[2,128,512]{2,1,0:T(8,128)(2,1)} %get-tuple-element.95), channel_id=1, source_target_pairs={{0,8},{1,9},{2,10},{3,11},{4,12},{5,13},{6,14},{7,15},{8,0},{9,1},... | collective-permute-start | bytes 786440 | tf_op jit(solution)/shard_map/ppermute | solution.py:303
  443.6 20.7 %collective-permute-start.31 = (bf16[2,128,512]{2,1,0:T(8,128)(2,1)}, bf16[2,128,512]{2,1,0:T(8,128)(2,1)S(1)}, u32[]{:S(2)}, u32[]{:S(2)}) collective-permute-start(bf16[2,128,512]{2,1,0:T(8,128)(2,1)} %get-tuple-element.96), channel_id=1, source_target_pairs={{0,16},{1,17},{2,18},{3,19},{4,20},{5,21},{6,22},{7,23},{8,24},{9,... | collective-permute-start | bytes 786440 | tf_op jit(solution)/shard_map/ppermute | solution.py:303
  444.5 19.9 %collective-permute-start.32 = (bf16[2,128,512]{2,1,0:T(8,128)(2,1)}, bf16[2,128,512]{2,1,0:T(8,128)(2,1)S(1)}, u32[]{:S(2)}, u32[]{:S(2)}) collective-permute-start(bf16[2,128,512]{2,1,0:T(8,128)(2,1)} %get-tuple-element.97), channel_id=1, source_target_pairs={{0,24},{1,25},{2,26},{3,27},{4,28},{5,29},{6,30},{7,31},{8,16},{9,... | collective-permute-start | bytes 786440 | tf_op jit(solution)/shard_map/ppermute | solution.py:303
  464.5 3.5 collective-permute-start.33
  469.1 5.2 %collective-permute-start.35 = (bf16[64,1024]{1,0:T(8,128)(2,1)S(1)}, bf16[64,1024]{1,0:T(8,128)(2,1)S(1)}, u32[]{:S(2)}, u32[]{:S(2)}) collective-permute-start(bf16[64,1024]{1,0:T(8,128)(2,1)S(1)} %dynamic-slice_bitcast_fusion.1), channel_id=1, source_target_pairs={{0,2},{1,3},{2,0},{3,1},{4,6},{5,7},{6,4},{7,5},{8,10},{9,11},{10,... | collective-permute-start | bytes 393224 | tf_op jit(solution)/shard_map/ppermute | solution.py:303
  474.1 1.4 collective-permute-start.34
  (33 other events, 102.6 us)
Sparse Core Ops, SparseCore 0:
  12.2 155.8 all-gather.1
  202.8 97.5 reduce-scatter.4
  302.7 118.4 reduce-scatter.2

commit v4 on v3

--- a/solution.py
+++ b/solution.py
@@ -506,12 +506,23 @@
     )
 
 
-def up_kernel(places_ref, left_ref, right_ref, shift_ref, active_ref, slope_ref):
-    width = left_ref.shape[1]
-    right = right_ref[...].reshape(width, -1)
+def fill_rows(made_ref, own_ref, far_ref):
+    rows = own_ref.shape[0]
+
+    @pl.when(pl.program_id(0) == 0)
+    def _():
+        made_ref[:rows] = own_ref[...]
+        made_ref[rows:] = far_ref[...]
+
+
+def up_kernel(
+    places_ref, own_ref, far_ref, right_ref, shift_ref, active_ref, slope_ref, left_ref
+):
+    fill_rows(left_ref, own_ref, far_ref)
+    right = right_ref[...].reshape(left_ref.shape[1], -1)
     hidden = jnp.dot(left_ref[...], right, preferred_element_type=jnp.float32)
     hidden = hidden + shift_ref[...]
-    sigma = 1.0 / (1.0 + jnp.exp(-SLOPE * hidden))
+    sigma = 0.5 * jnp.tanh((0.5 * SLOPE) * hidden) + 0.5
     active = hidden * sigma
     active_ref[...] = active.astype(LOW)
     slope_ref[...] = (sigma + SLOPE * active * (1.0 - sigma)).astype(LOW)
@@ -524,72 +535,76 @@
     )
 
 
-def up_call(places, left, gathered, shift):
-    rows, width = left.shape
+def up_call(places, pair, gathered, shift):
+    rows, width = pair[0].shape
     wide = shift.shape[1] // 4
-    piece = pl.BlockSpec((rows, wide), lambda i, s: (0, i))
+    whole = pl.BlockSpec((rows, width), lambda i, s: (0, 0))
+    piece = pl.BlockSpec((2 * rows, wide), lambda i, s: (0, i))
     return pl.pallas_call(
         up_kernel,
         grid_spec=pltpu.PrefetchScalarGridSpec(
             num_scalar_prefetch=1,
             grid=(4,),
             in_specs=[
-                pl.BlockSpec((rows, width), lambda i, s: (0, 0)),
+                whole,
+                whole,
                 feed_spec(gathered, 0),
                 pl.BlockSpec((1, wide), lambda i, s: (0, i)),
             ],
             out_specs=[piece, piece],
-        ),
-        out_shape=[jax.ShapeDtypeStruct((rows, 4 * wide), LOW)] * 2,
+            scratch_shapes=[pltpu.VMEM((2 * rows, width), LOW)],
+        ),
+        out_shape=[jax.ShapeDtypeStruct((2 * rows, 4 * wide), LOW)] * 2,
         compiler_params=pltpu.CompilerParams(vmem_limit_bytes=VMEM_ROOM),
         cost_estimate=pl.CostEstimate(
-            flops=8 * rows * wide * width,
+            flops=16 * rows * wide * width,
             transcendentals=8 * rows * wide,
-            bytes_accessed=left.size * 2 + 8 * width * wide + 16 * rows * wide,
-        ),
-    )(places, left, gathered, shift)
-
-
-def hidden_kernel(places_ref, left_ref, right_ref, slope_ref, out_ref, sum_ref):
-    width = left_ref.shape[1]
-    right = right_ref[...].reshape(width, -1)
+            bytes_accessed=rows * width * 4 + 8 * width * wide + 32 * rows * wide,
+        ),
+    )(places, *pair, gathered, shift)
+
+
+def hidden_kernel(
+    places_ref, own_ref, far_ref, right_ref, slope_ref, out_ref, sum_ref, left_ref
+):
+    fill_rows(left_ref, own_ref, far_ref)
+    right = right_ref[...].reshape(left_ref.shape[1], -1)
     grad = jnp.dot(left_ref[...], right, preferred_element_type=jnp.float32)
     grad = (grad * slope_ref[...].astype(jnp.float32)).astype(LOW)
     out_ref[...] = grad
     sum_ref[...] = jnp.sum(grad.astype(jnp.float32), axis=0, keepdims=True)
 
 
-def hidden_call(places, left, gathered, slope):
-    rows, width = left.shape
+def hidden_call(places, pair, gathered, slope):
+    rows, width = pair[0].shape
     wide = slope.shape[1] // 4
-    piece = pl.BlockSpec((rows, wide), lambda i, s: (0, i))
+    whole = pl.BlockSpec((rows, width), lambda i, s: (0, 0))
+    piece = pl.BlockSpec((2 * rows, wide), lambda i, s: (0, i))
     return pl.pallas_call(
         hidden_kernel,
         grid_spec=pltpu.PrefetchScalarGridSpec(
             num_scalar_prefetch=1,
             grid=(4,),
-            in_specs=[
-                pl.BlockSpec((rows, width), lambda i, s: (0, 0)),
-                feed_spec(gathered, 2),
-                piece,
-            ],
+            in_specs=[whole, whole, feed_spec(gathered, 2), piece],
             out_specs=[piece, pl.BlockSpec((1, wide), lambda i, s: (0, i))],
+            scratch_shapes=[pltpu.VMEM((2 * rows, width), LOW)],
         ),
         out_shape=[
-            jax.ShapeDtypeStruct((rows, 4 * wide), LOW),
+            jax.ShapeDtypeStruct((2 * rows, 4 * wide), LOW),
             jax.ShapeDtypeStruct((1, 4 * wide), jnp.float32),
         ],
         compiler_params=pltpu.CompilerParams(vmem_limit_bytes=VMEM_ROOM),
         cost_estimate=pl.CostEstimate(
-            flops=8 * rows * wide * width,
+            flops=16 * rows * wide * width,
             transcendentals=0,
-            bytes_accessed=left.size * 2 + 8 * width * wide + 16 * rows * wide,
-        ),
-    )(places, left, gathered, slope)
-
-
-def down_kernel(places_ref, left_ref, right_ref, out_ref):
+            bytes_accessed=rows * width * 4 + 8 * width * wide + 32 * rows * wide,
+        ),
+    )(places, *pair, gathered, slope)
+
+
+def down_kernel(places_ref, left_ref, right_ref, own_ref, send_ref):
     span = right_ref.shape[3] // 2
+    rows = own_ref.shape[0]
     total = None
     for far in range(2):
         right = right_ref[:, places_ref[3] ^ far].reshape(-1, 2 * span)
@@ -599,116 +614,94 @@
                 left_ref[:, start : start + span], right[:, part * span : (part + 1) * span]
             )
             total = one if total is None else total + one
-    out_ref[...] = total.astype(out_ref.dtype)
-
-
-def down_call(places, left, gathered, start, dtype):
-    rows, deep = left.shape
+    own_ref[...] = total[:rows]
+    send_ref[...] = total[rows:].astype(LOW)
+
+
+def down_call(places, left, gathered, start):
+    both, deep = left.shape
+    rows = both // 2
     lines, _, tall, wide = gathered.shape
-    return pl.pallas_call(
+    piece = pl.BlockSpec((rows, 2 * tall), lambda i, s: (0, i))
+    own, send = pl.pallas_call(
         down_kernel,
         grid_spec=pltpu.PrefetchScalarGridSpec(
             num_scalar_prefetch=1,
             grid=(lines // 2,),
             in_specs=[
-                pl.BlockSpec((rows, deep), lambda i, s: (0, 0)),
+                pl.BlockSpec((both, deep), lambda i, s: (0, 0)),
                 pl.BlockSpec((2, 2, tall, wide // 2), lambda i, s: (i, 0, 0, start)),
             ],
-            out_specs=pl.BlockSpec((rows, 2 * tall), lambda i, s: (0, i)),
-        ),
-        out_shape=jax.ShapeDtypeStruct((rows, lines * tall), dtype),
+            out_specs=[piece, piece],
+        ),
+        out_shape=[
+            jax.ShapeDtypeStruct((rows, lines * tall), jnp.float32),
+            jax.ShapeDtypeStruct((rows, lines * tall), LOW),
+        ],
         compiler_params=pltpu.CompilerParams(vmem_limit_bytes=VMEM_ROOM),
         cost_estimate=pl.CostEstimate(
-            flops=2 * rows * deep * lines * tall,
+            flops=2 * both * deep * lines * tall,
             transcendentals=0,
-            bytes_accessed=left.size * 2 + lines * tall * deep * 2 + rows * lines * tall * 4,
+            bytes_accessed=left.size * 2 + lines * tall * deep * 2 + rows * lines * tall * 6,
         ),
     )(places, left, gathered)
-
-
-def owner_kernel(places_ref, left_ref, left_far, right_ref, right_far, out_ref):
-    total = mat_rows(left_ref[...], right_ref[...]) + mat_rows(left_far[...], right_far[...])
-    out_ref[0] = total.astype(LOW)
-
-
-def owner_grads(places, left, right):
-    rows, width = left[0].shape
-    span = right[0].shape[1] // 4
-    whole = pl.BlockSpec((rows, width), lambda i, s: (0, 0))
-    piece = pl.BlockSpec((rows, span), lambda i, s: (0, i))
-    return pl.pallas_call(
-        owner_kernel,
-        grid_spec=pltpu.PrefetchScalarGridSpec(
-            num_scalar_prefetch=1,
-            grid=(4,),
-            in_specs=[whole, whole, piece, piece],
-            out_specs=pl.BlockSpec((1, width, span), lambda i, s: (s[3] ^ (i % 2), 0, i // 2)),
-        ),
-        out_shape=jax.ShapeDtypeStruct((2, width, 2 * span), LOW),
-        compiler_params=pltpu.CompilerParams(vmem_limit_bytes=VMEM_ROOM),
-        cost_estimate=pl.CostEstimate(
-            flops=16 * rows * width * span,
-            transcendentals=0,
-            bytes_accessed=(2 * rows * width + 8 * rows * span + 4 * width * span) * 2,
-        ),
-    )(places, *left, *right)
-
-
-def weight_kernel(pairs, places_ref, *refs):
-    ins, (one_ref, two_ref) = refs[:-2], refs[-2:]
+    return own + exchange(send, far_core=1).astype(jnp.float32)
+
+
+def weight_kernel(send, pairs, places_ref, *refs):
+    ins, outs, lefts = refs[: 3 * pairs], refs[3 * pairs : 3 * pairs + 2], refs[3 * pairs + 2 :]
     step = pl.program_id(0)
-    parts = []
-    for pair in range(pairs):
-        total = None
-        for image in range(2):
-            group = ins[10 * pair + 5 * image : 10 * pair + 5 * image + 5]
-            left = jnp.concatenate([ref[...] for ref in group[:4]], axis=1)
-            one = mat_rows(left, group[4][...])
-            total = one if image == 0 else total + one
-        parts.append(total.astype(LOW))
-    made = parts[0] if pairs == 1 else jnp.concatenate(parts, axis=1)
 
     @pl.when(step < 2)
     def _():
-        one_ref[0] = made
+        x_far = step if send else 1 - step
+        for pair in range(pairs):
+            rows = ins[3 * pair].shape[0]
+            for block in range(4):
+                at = (places_ref[0] ^ block) * 2 + (places_ref[1] ^ x_far)
+                start = pl.multiple_of(at * LANES, LANES)
+                for image in range(2):
+                    lefts[pair][
+                        image * rows : (image + 1) * rows, block * LANES : (block + 1) * LANES
+                    ] = ins[3 * pair + image][:, pl.ds(start, LANES)]
+
+    parts = [
+        mat_rows(lefts[pair][...], ins[3 * pair + 2][...]).astype(LOW) for pair in range(pairs)
+    ]
+    made = parts[0] if pairs == 1 else jnp.concatenate(parts, axis=1)
+
+    @pl.when(step < 2)
+    def _():
+        outs[0][0] = made
 
     @pl.when(step >= 2)
     def _():
-        two_ref[0] = made
+        outs[1][0] = made
 
 
 def weight_pieces(places, operands, send):
-    rows = operands[0][0][0].shape[0]
-    line = 4 * LANES
-
-    def x_far(step):
+    rows, width = operands[0][0][0].shape
+    line = width // 2
+    first = (lambda i: jnp.minimum(i, 1)) if send else (lambda i: 1 - jnp.minimum(i, 1))
+
+    def right_map(i, s):
         if send:
-            return jnp.where(step == 0, 0, 1)
-        return jnp.where(step == 1, 1, 0)
-
-    def y_far(step):
-        if send:
-            return jnp.where(step == 2, 0, 1)
-        return jnp.where(step == 3, 1, 0)
-
-    def left_map(z_far):
-        return lambda i, s: (0, (s[0] ^ z_far) * 2 + (s[1] ^ x_far(i)))
-
-    specs, arrays, wide = [], [], 0
+            return (0, jnp.where(i < 2, 1, i))
+        return (0, jnp.where(i < 2, 0, i))
+
+    specs, arrays, scratch, wide = [], [], [], 0
     for left, right in operands:
-        span = right[0].shape[1] // 4
+        span = right.shape[1] // 4
         wide += span
         for image in range(2):
-            for z_far in range(4):
-                specs.append(pl.BlockSpec((rows, LANES), left_map(z_far)))
-                arrays.append(left[image])
-            specs.append(
-                pl.BlockSpec((rows, span), lambda i, s: (0, jnp.where(i < 2, 0, 2) + y_far(i)))
-            )
-            arrays.append(right[image])
+            specs.append(pl.BlockSpec((rows, width), lambda i, s: (0, 0)))
+            arrays.append(left[image])
+        specs.append(pl.BlockSpec((2 * rows, span), right_map))
+        arrays.append(right)
+        scratch.append(pltpu.VMEM((2 * rows, line), LOW))
 
     def kernel(*refs):
-        weight_kernel(len(operands), *refs)
+        weight_kernel(send, len(operands), *refs)
 
     return pl.pallas_call(
         kernel,
@@ -717,9 +710,10 @@
             grid=(4,),
             in_specs=specs,
             out_specs=[
-                pl.BlockSpec((1, line, wide), lambda i, s: (jnp.minimum(i, 1), 0, 0)),
+                pl.BlockSpec((1, line, wide), lambda i, s: (first(i), 0, 0)),
                 pl.BlockSpec((1, line, wide), lambda i, s: (jnp.maximum(i - 2, 0), 0, 0)),
             ],
+            scratch_shapes=scratch,
         ),
         out_shape=[jax.ShapeDtypeStruct((2, line, wide), LOW)] * 2,
         compiler_params=pltpu.CompilerParams(vmem_limit_bytes=VMEM_ROOM),
@@ -808,55 +802,69 @@
     out_ref[:, 2 * LANES : 3 * LANES] = grad_value.astype(LOW)
 
 
-def attend_call(qkv, bias):
-    rows = qkv.shape[0]
+def attend_image(image, qkv, bias, given):
+    both = qkv.shape[0]
+    rows = both // 2
     blocks = qkv.shape[1] // (3 * LANES)
+
+    def kernel(*refs):
+        attend_kernel(*refs[:2], *refs[-2:])
+
     return pl.pallas_call(
-        attend_kernel,
+        kernel,
         grid=(blocks,),
         in_specs=[
-            pl.BlockSpec((rows, 3 * LANES), lambda j: (0, j)),
+            pl.BlockSpec((rows, 3 * LANES), lambda j: (image, j)),
             pl.BlockSpec((rows, LANES), lambda j: (0, 0)),
-        ],
+        ]
+        + [pl.BlockSpec(memory_space=pl.ANY)] * len(given),
         out_specs=[
-            pl.BlockSpec((rows, LANES), lambda j: (0, j)),
-            pl.BlockSpec((1, 8, rows), lambda j: (j, 0, 0)),
+            pl.BlockSpec((rows, LANES), lambda j: (image, j)),
+            pl.BlockSpec((1, 8, rows), lambda j: (image * blocks + j, 0, 0)),
         ],
         out_shape=[
-            jax.ShapeDtypeStruct((rows, blocks * LANES), LOW),
-            jax.ShapeDtypeStruct((blocks, 8, rows), jnp.float32),
+            jax.ShapeDtypeStruct((both, blocks * LANES), LOW),
+            jax.ShapeDtypeStruct((2 * blocks, 8, rows), jnp.float32),
         ],
+        input_output_aliases={2: 0, 3: 1} if given else {},
         compiler_params=pltpu.CompilerParams(vmem_limit_bytes=VMEM_ROOM),
         cost_estimate=pl.CostEstimate(
             flops=blocks * 2 * 2 * 2 * rows * rows * LANES * 2,
             transcendentals=blocks * 2 * rows * rows,
             bytes_accessed=rows * blocks * LANES * 8,
         ),
-    )(qkv, bias)
-
-
-def attend_back_call(qkv, bias, grad, mixed, total):
-    rows = qkv.shape[0]
+    )(qkv, bias, *given)
+
+
+def attend_back_image(image, qkv, bias, grad, mixed, total, given):
+    both = qkv.shape[0]
+    rows = both // 2
     blocks = qkv.shape[1] // (3 * LANES)
+
+    def kernel(*refs):
+        attend_back_kernel(*refs[:5], refs[-1])
+
     return pl.pallas_call(
-        attend_back_kernel,
+        kernel,
         grid=(blocks,),
         in_specs=[
-            pl.BlockSpec((rows, 3 * LANES), lambda j: (0, j)),
+            pl.BlockSpec((rows, 3 * LANES), lambda j: (image, j)),
             pl.BlockSpec((rows, LANES), lambda j: (0, 0)),
             pl.BlockSpec((rows, LANES), lambda j: (0, j)),
-            pl.BlockSpec((rows, LANES), lambda j: (0, j)),
-            pl.BlockSpec((1, 8, rows), lambda j: (j, 0, 0)),
-        ],
-        out_specs=pl.BlockSpec((rows, 3 * LANES), lambda j: (0, j)),
+            pl.BlockSpec((rows, LANES), lambda j: (image, j)),
+            pl.BlockSpec((1, 8, rows), lambda j: (image * blocks + j, 0, 0)),
+        ]
+        + [pl.BlockSpec(memory_space=pl.ANY)] * len(given),
+        out_specs=pl.BlockSpec((rows, 3 * LANES), lambda j: (image, j)),
         out_shape=jax.ShapeDtypeStruct(qkv.shape, LOW),
+        input_output_aliases={5: 0} if given else {},
         compiler_params=pltpu.CompilerParams(vmem_limit_bytes=VMEM_ROOM),
         cost_estimate=pl.CostEstimate(
             flops=blocks * 2 * 5 * 2 * rows * rows * LANES * 2,
             transcendentals=blocks * 2 * rows * rows,
             bytes_accessed=rows * blocks * LANES * 16,
         ),
-    )(qkv, bias, grad, mixed, total)
+    )(qkv, bias, grad, mixed, total, *given)
 
 
 def mat(left, right):
@@ -939,7 +947,6 @@
     feed_send = jnp.concatenate(columns_of(feeds, 1 - core), 1)
     feed = pick_two(core, feed_keep, exchange(feed_send, far_core=1), 0)
     groups = [[place for place in range(32) if (place // 2) % 2 == at] for at in range(2)]
-    turned_groups = [sorted(group, key=lambda place: (place % 2, place)) for group in groups]
     gathered = lax.all_gather(
         feed.reshape(2 * depth, -1),
         BOTH,
@@ -950,14 +957,22 @@
 
     heads = [query_weight, key_weight, value_weight, output_weight.T]
     piece_one = gather_piece(core_parts(heads, core), core_parts(heads, 1 - core), core)
-    line_one = gather_line(piece_one, scatter_z([None, piece_one, piece_one, piece_one]), places)
-
-    stacked = jnp.stack([images, after(cotangent, piece_one)])
-    stacked = jnp.pad(stacked, ((0, 0), (0, 0), (0, half - strip), (0, 0)))
-    mine = lax.dynamic_index_in_dim(stacked, place_y, 1, keepdims=False)
-    theirs = lax.dynamic_index_in_dim(stacked, 1 - place_y, 1, keepdims=False)
-    arrived = after(exchange(theirs, far_y=1), *line_one)
-    whole = jnp.stack([mine, arrived], 1).reshape(2, rows, width)
+    others_one = scatter_z([None, piece_one, piece_one, piece_one])
+
+    padding = ((0, 0), (0, half - strip), (0, 0))
+
+    def own_and_far(slots, *waits):
+        slots = jnp.pad(slots, padding)
+        mine = lax.dynamic_index_in_dim(slots, place_y, 0, keepdims=False)
+        theirs = lax.dynamic_index_in_dim(slots, 1 - place_y, 0, keepdims=False)
+        return mine, exchange(after(theirs, *waits), far_y=1)
+
+    image_mine, image_far = own_and_far(images, piece_one)
+    line_one = gather_line(piece_one, others_one, places)
+    cross_one = exchange(line_one[0], far_x=1), exchange(line_one[1], far_y=1)
+    pair_one = gather_pairs(places, *line_one, *cross_one)
+    image_far = after(image_far, *pair_one)
+    whole = jnp.concatenate([image_mine, image_far], 0)
 
     def head_columns(vector):
         table = vector.astype(jnp.float32).reshape(2, 2, 2, -1)
@@ -993,93 +1008,93 @@
         jnp.where(ok, 0.0, NEGATIVE).astype(LOW)[:, None], (rows, LANES)
     )
 
-    resid = whole[0].astype(jnp.float32)
-    grad_top = row_mask * whole[1].astype(jnp.float32)
-    fed_grad = grad_top.astype(LOW)
+    resid = whole.astype(jnp.float32)
+
+    def full_columns(owned):
+        return owned.transpose(2, 0, 1, 3).reshape(depth, -1)
+
     def pair_of(own):
         return own, exchange(own, far_core=1)
 
-    fed_pair = pair_of(fed_grad)
     normed, unit_one, spread_one = flat_norm(resid, gain_one, shift_one)
     normed_pair = pair_of(normed.astype(LOW))
 
-    cross_one = exchange(line_one[0], far_x=1), exchange(line_one[1], far_y=1)
-    pair_one = gather_pairs(after(places, *fed_pair, *normed_pair), *line_one, *cross_one)
     last_one = exchange(pair_one[0], far_y=1), exchange(pair_one[1], far_x=1)
-    qkv_full, output_full = gather_all(places, *pair_one, *last_one, 3 * head_cols // 4)
-
-    def heads_of(one):
-        qkv = (mat(one, qkv_full) + qkv_shift).astype(LOW)
-        return (qkv, *attend_call(qkv, key_bias))
-
-    qkv_far, mixed_far, totals_far = heads_of(normed_pair[1])
-    mixed_sum = exchange(mat_far(mixed_far, output_full).astype(LOW), far_core=1)
-    qkv_own, mixed_own, totals_own = heads_of(normed_pair[0])
-    mixed_pair = mixed_own, mixed_far
-    attended = mat_far(mixed_own, output_full) + mixed_sum.astype(jnp.float32)
+    qkv_full, output_full = gather_all(after(places, *normed_pair), *pair_one, *last_one, 3 * head_cols // 4)
+
+    grad_mine, grad_far = own_and_far(cotangent, qkv_full)
+    normed_rows = jnp.concatenate(normed_pair, 0)
+    qkv = (mat(normed_rows, qkv_full) + qkv_shift).astype(LOW)
+    mixed_half = attend_image(1, qkv, key_bias, [])
+    mixed_far = mat_far(mixed_half[0][rows:], output_full).astype(LOW)
+    mixed_sum = exchange(mixed_far, far_core=1)
+    mixed, totals = attend_image(0, qkv, key_bias, list(after(tuple(mixed_half), mixed_far)))
+    grad_far = after(grad_far, mixed)
+    grad_top = row_mask * jnp.concatenate([grad_mine, grad_far], 0).astype(jnp.float32)
+    fed_grad = grad_top.astype(LOW)
+    fed_pair = pair_of(fed_grad)
+    attended = mat_far(mixed[:rows], output_full) + mixed_sum.astype(jnp.float32)
     attended = attended + output_bias.astype(jnp.float32)
     middle = row_mask * (resid + attended)
     second, unit_two, spread_two = flat_norm(middle, gain_two, shift_two)
     second_pair = pair_of(second.astype(LOW))
-    ups = [up_call(places, one, gathered, up_shift) for one in second_pair]
-    active_pair = ups[0][0], ups[1][0]
-
-    def owner_sum(grads):
-        return lax.psum_scatter(
-            grads.reshape(-1, grads.shape[2]),
-            BOTH,
-            scatter_dimension=0,
-            tiled=True,
-            axis_index_groups=turned_groups,
-        ).reshape(2, depth, -1)
-
-    lower_grads = owner_grads(places, fed_pair, active_pair)
-    lower_sum = owner_sum(lower_grads)
-    fed_late = after(fed_pair, lower_grads)
-    hiddens = [
-        hidden_call(places, one, gathered, up[1]) for one, up in zip(fed_late, ups)
-    ]
-    hidden_pair = hiddens[0][0], hiddens[1][0]
-    up_bias_sums = (hiddens[0][1] + hiddens[1][1]).reshape(-1)
-    second_far = exchange(down_call(places, hidden_pair[1], gathered, 0, LOW), far_core=1)
-    second_own = down_call(places, hidden_pair[0], gathered, 0, jnp.float32)
-    second_grad = second_own + second_far.astype(jnp.float32)
+    active, slope = up_call(places, second_pair, gathered, up_shift)
+
+    lower_sends = weight_pieces(places, [(fed_pair, active)], True)
+    lower_first = scatter_first(lower_sends)
+    fed_late = after(fed_pair, *lower_sends)
+    hidden_grad, up_bias_sums = hidden_call(places, fed_late, gathered, slope)
+    up_sends = weight_pieces(places, [(second_pair, hidden_grad)], True)
+    up_first = scatter_first(up_sends)
+    active_late = after(active, *up_sends)
+    lower_keeps = weight_pieces(places, [(fed_pair, active_late)], False)
+    lower_first = after(lower_first, *lower_keeps)
+    lower_second = scatter_second(lower_keeps, lower_first)
+    hidden_late = after(hidden_grad, *lower_first)
+    second_grad = down_call(places, hidden_late, gathered, 0)
     middle_back, gain_two_grad, shift_two_grad = flat_norm_back(
         second_grad, unit_two, spread_two, gain_two
     )
     middle_grad = row_mask * (grad_top + middle_back)
     attended_grad = middle_grad.astype(LOW)
     attended_pair = pair_of(attended_grad)
-    upper_grads = owner_grads(places, second_pair, hidden_pair)
-    upper_sum = owner_sum(upper_grads)
-
-    def heads_back(one, qkv, mixed, totals):
-        grad_mixed = mat(one, output_full).astype(LOW)
-        return attend_back_call(qkv, key_bias, grad_mixed, mixed, totals)
-
-    attended_late = after(attended_pair, upper_grads)
-    back_own = heads_back(attended_late[0], qkv_own, mixed_own, totals_own)
-    back_far = heads_back(attended_late[1], qkv_far, mixed_far, totals_far)
-    back_pair = back_own, back_far
-    operands = [(normed_pair, back_pair), (attended_pair, mixed_pair)]
+    up_keeps = weight_pieces(places, [(second_pair, after(hidden_late, attended_grad))], False)
+    lower_second = after(lower_second, *up_keeps)
+    lower_line = scatter_line(lower_keeps, lower_first, lower_second)
+    lower_z = scatter_z(lower_line)
+    up_first = after(up_first, *up_keeps)
+    up_second = scatter_second(up_keeps, up_first)
+    grad_mixed = [mat(one, output_full).astype(LOW) for one in attended_pair]
+    grad_mixed = after(tuple(grad_mixed), *up_first, *lower_line)
+    back = attend_back_image(0, qkv, key_bias, grad_mixed[0], mixed, totals, [])
+    lower_z = after(tuple(lower_z), back)
+    lower_owned = full_columns(scatter_last(lower_line[0], lower_z, core))
+    up_line = scatter_line(up_keeps, up_first, after(up_second, back))
+    up_z = scatter_z(up_line)
+    back = after(back, *up_line)
+    back = attend_back_image(1, qkv, key_bias, grad_mixed[1], mixed, totals, [back])
+    up_z = after(tuple(up_z), back)
+    back = after(back, *up_z)
+    upper_owned = full_columns(scatter_last(up_line[0], up_z, core))
+    operands = [(normed_pair, back), (attended_pair, mixed)]
     last_sends = weight_pieces(places, operands, True)
     last_first = scatter_first(last_sends)
-    back_late = after(back_pair, last_sends)
-    normed_far = exchange(mat_far(back_late[1], qkv_full).astype(LOW), far_core=1)
-    normed_grad = mat_far(back_late[0], qkv_full) + normed_far.astype(jnp.float32)
+    back_late = after(back, *last_sends)
+    normed_far = exchange(mat_far(back_late[rows:], qkv_full).astype(LOW), far_core=1)
+    normed_grad = mat_far(back_late[:rows], qkv_full) + normed_far.astype(jnp.float32)
     last_keeps = weight_pieces(places, operands, False)
     first_back, gain_one_grad, shift_one_grad = flat_norm_back(
         normed_grad, unit_one, spread_one, gain_one
     )
     images_own = middle_grad + first_back
-    qkv_sums = (column_flat(back_own) + column_flat(back_far)).reshape(4, 3, -1)
+    qkv_sums = column_flat(back).reshape(4, 3, -1)
     vector = jnp.concatenate(
         [
             column_flat(attended_grad),
             gain_two_grad,
             shift_two_grad,
             column_flat(fed_grad),
-            head_spread(up_bias_sums),
+            head_spread(up_bias_sums.reshape(-1)),
             gain_one_grad,
             shift_one_grad,
             head_spread(qkv_sums[:, 0].reshape(-1)),
@@ -1091,30 +1106,17 @@
     vector, vectors = vector_first(vector)
     last_line = scatter_line(last_keeps, last_first, after(last_second, images_own, *vectors))
     last_z = scatter_z(last_line)
-    fed_far = exchange(down_call(places, active_pair[1], gathered, 1, LOW), far_core=1)
-    fed = down_call(places, active_pair[0], gathered, 1, jnp.float32)
-    fed = fed + fed_far.astype(jnp.float32)
+    fed = down_call(places, after(active, last_keeps), gathered, 1)
     layer_own = (row_mask * (middle + fed + down_bias.astype(jnp.float32))).astype(LOW)
     vector = vector_last(vector, vectors)
     last_z = after(tuple(last_z), vector)
     last_owned = scatter_last(last_line[0], last_z, core)
 
-    def owner_last(total):
-        keep = lax.dynamic_index_in_dim(total, core, 0, keepdims=False)
-        send = lax.dynamic_index_in_dim(total, 1 - core, 0, keepdims=False)
-        both = pick_two(core, keep, exchange(send, far_core=1), 0)
-        return both.astype(jnp.float32).transpose(1, 0, 2).reshape(depth, -1)
-
-    lower_owned, upper_owned = owner_last(lower_sum), owner_last(upper_sum)
-
     def to_strips(own, send):
         return pick_two(place_y, own[:strip], exchange(send, far_y=1).astype(own.dtype), 0)
 
     layer_out = to_strips(layer_own, layer_own[half : half + strip])
     images_grad = to_strips(images_own, images_own[half : half + strip].astype(LOW))
-    def full_columns(owned):
-        return owned.transpose(2, 0, 1, 3).reshape(depth, -1)
-
     def head_grad(at):
         return full_columns(last_owned[..., at * LANES : (at + 1) * LANES])
 

time: 492 us -> 466 us (0.947)
  waiting for transfers between devices: 184 us -> 115 us
  starting transfers between devices: 28.9 us -> 63.4 us
  other arithmetic: 25.1 us -> 37.8 us
    ppermute x36 -> x51, waiting for transfers between devices: 184 us -> 103 us  [exchange(): return lax.ppermute(value, BOTH, pairs)]
    pallas_call x2 -> x6, Pallas kernels: 21.8 us -> 56.7 us  [weight_pieces(): pl.pallas_call(kernel, grid_spec=pltpu.PrefetchScalarGridSpec(num_scalar_...]
    ppermute x36 -> x51, starting transfers between devices: 28.8 us -> 63.4 us  [exchange(): return lax.ppermute(value, BOTH, pairs)]
    pallas_call x6 -> x4, Pallas kernels: 73.9 us -> 51.3 us  [the longest x2 32.6 us: attend_back_image(): pl.pallas_call(kernel, grid=(blocks,), in_specs=[pl.BlockSpec((rows, 3 *...]
    all_gather x1, waiting for transfers between devices: 0.01 us -> 11.3 us  [whole_images(): lax.all_gather(feed.reshape(2 * depth, -1), BOTH, axis=0, tiled=True, axi...]
    pallas_call x4 -> x2, Pallas kernels: 30.3 us -> 20.3 us  [down_call(): pl.pallas_call(down_kernel, grid_spec=pltpu.PrefetchScalarGridSpec(num_sc...]
    pallas_call x1 -> x3, Pallas kernels: 2.97 us -> 9.01 us  [scatter_line(): pl.pallas_call(line_kernel, grid=(1,), in_specs=[first, first, flat, firs...]
    pallas_call x2 -> x1, Pallas kernels: 15.8 us -> 11.2 us  [hidden_call(): pl.pallas_call(hidden_kernel, grid_spec=pltpu.PrefetchScalarGridSpec(num_...]
  transfers between devices with their start and end apart: 39 -> 52, of which waited for: 18 -> 22; matrix products, arithmetic and copies ran while one was open for 15% -> 17% of each run, Pallas kernels for 31% -> 31%
where the time goes in v4:
time: 466 us; the launch traced here: 458 us
  Pallas kernels  171 us (37%)
  waiting for transfers between devices  115 us (25%)
  starting transfers between devices  63.4 us (14%)
  other arithmetic  37.8 us (8%)
  matrix products  27.1 us (6%)
  local copies, waits for them, and re-layouts  26.8 us (6%)
  between operations  16.3 us (3%)
    ppermute x51, waiting for transfers between devices, exchange(): return lax.ppermute(value, BOTH, pairs)  103 us
    ppermute x51, starting transfers between devices, exchange(): return lax.ppermute(value, BOTH, pairs)  63.4 us
    pallas_call x6, Pallas kernels, weight_pieces(): pl.pallas_call(kernel, grid_spec=pltpu.PrefetchScalarGridSpec(num_scalar_...  56.7 us
    pallas_call x2, Pallas kernels, attend_back_image(): pl.pallas_call(kernel, grid=(blocks,), in_specs=[pl.BlockSpec((rows, 3 *...  32.6 us
    pallas_call x2, Pallas kernels, down_call(): pl.pallas_call(down_kernel, grid_spec=pltpu.PrefetchScalarGridSpec(num_sc...  20.3 us
    pallas_call x2, Pallas kernels, attend_image(): pl.pallas_call(kernel, grid=(blocks,), in_specs=[pl.BlockSpec((rows, 3 *...  18.8 us
    dot_general x4, matrix products, mat_far(): lax.dot_general(left, right, (((1,), (1,)), ((), ())), preferred_element_...  15.8 us
    pallas_call x1, Pallas kernels, up_call(): pl.pallas_call(up_kernel, grid_spec=pltpu.PrefetchScalarGridSpec(num_scal...  13.1 us
  transfers between devices with their start and end apart: 52, of which 22 were waited for; matrix products, arithmetic and copies ran while one was open for 17% of the time, Pallas kernels for 31%

profile of v4, /device:TPU:0, one launch (start us, length us, event | category | flops | bytes accessed | tf_op | source)
XLA Modules:
  0.0 457.5 jit_solution(10544854912148231944)
XLA Ops:
  13.8 3.0 collective-permute-start.2
  16.8 2.6 collective-permute-start.3
  19.9 1.8 collective-permute-start.1
  22.3 8.3 %collective-permute-done.2.refs_1_ = bf16[2,128,512]{2,1,0:T(8,128)(2,1)S(1)} collective-permute-done((bf16[2,128,512]{2,1,0:T(8,128)(2,1)S(1)}, bf16[2,128,512]{2,1,0:T(8,128)(2,1)S(1)}, u32[]{:S(2)}, u32[]{:S(2)}) %collective-permute-start.2) | collective-permute-done | bytes 262176 | tf_op jit(solution)/shard_map/ppermute | solution.py:303
  30.6 7.2 %collective-permute-done.3.refs_2_ = bf16[2,128,512]{2,1,0:T(8,128)(2,1)} collective-permute-done((bf16[2,128,512]{2,1,0:T(8,128)(2,1)S(1)}, bf16[2,128,512]{2,1,0:T(8,128)(2,1)}, u32[]{:S(2)}, u32[]{:S(2)}) %collective-permute-start.3) | collective-permute-done | bytes 262176 | tf_op jit(solution)/shard_map/ppermute | solution.py:303
  37.8 5.3 %collective-permute-done.4.refs_3_ = bf16[2,128,512]{2,1,0:T(8,128)(2,1)} collective-permute-done((bf16[2,128,512]{2,1,0:T(8,128)(2,1)S(1)}, bf16[2,128,512]{2,1,0:T(8,128)(2,1)}, u32[]{:S(2)}, u32[]{:S(2)}) %collective-permute-start.4) | collective-permute-done | bytes 262176 | tf_op jit(solution)/shard_map/ppermute | solution.py:303
  43.2 2.2 shard_map.305
  48.4 9.9 %collective-permute-done.5.refs_1_ = bf16[4,128,512]{2,1,0:T(8,128)(2,1)S(1)} collective-permute-done((bf16[4,128,512]{2,1,0:T(8,128)(2,1)}, bf16[4,128,512]{2,1,0:T(8,128)(2,1)S(1)}, u32[]{:S(2)}, u32[]{:S(2)}) %collective-permute-start.5) | collective-permute-done | bytes 524320 | tf_op jit(solution)/shard_map/ppermute | solution.py:303
  60.3 2.9 shard_map.306
  67.6 23.2 %collective-permute-done.8.refs_1_ = bf16[2,4,128,512]{3,2,1,0:T(8,128)(2,1)} collective-permute-done((bf16[2,4,128,512]{3,2,1,0:T(8,128)(2,1)S(1)}, bf16[2,4,128,512]{3,2,1,0:T(8,128)(2,1)}, u32[]{:S(2)}, u32[]{:S(2)}) %collective-permute-start.8) | collective-permute-done | bytes 1048608 | tf_op jit(solution)/shard_map/ppermute | solution.py:303
  90.9 7.4 %collective-permute-done.9.refs_3_ = bf16[2,4,128,512]{3,2,1,0:T(8,128)(2,1)} collective-permute-done((bf16[2,4,128,512]{3,2,1,0:T(8,128)(2,1)}, bf16[2,4,128,512]{3,2,1,0:T(8,128)(2,1)}, u32[]{:S(2)}, u32[]{:S(2)}) %collective-permute-start.9) | collective-permute-done | bytes 1048608 | tf_op jit(solution)/shard_map/ppermute | solution.py:303
  98.3 4.7 %shard_map.307 = (bf16[4,2,128,1536]{3,2,1,0:T(8,128)(2,1)}, bf16[4,2,128,512]{3,2,1,0:T(8,128)(2,1)}) custom-call(s32[4]{0:T(128)} %pad_add_fusion.places_ref.refs_0_, bf16[2,4,128,512]{3,2,1,0:T(8,128)(2,1)} %get-tuple-element.101.refs_0_, bf16[2,4,128,512]{3,2,1,0:T(8,128)(2,1)} %collective-permute-done.8.refs_1_, ...), custom_call_target="tpu_custom_call" | custom-call | bytes 8388608 | tf_op jit(solution)/shard_map/pallas_call | solution.py:323
  103.1 8.1 %fusion.refs_0_ = bf16[1184,1536]{1,0:T(8,128)(2,1)} fusion(bf16[1024,1536]{1,0:T(8,128)(2,1)} %bitcast.205, f32[1536]{0:T(1024)S(1)} %add.250, bf16[592,1024]{1,0:T(8,128)(2,1)} %collective-permute-done.7.refs_2_, bf16[592,1024]{1,0:T(8,128)(2,1)S(1)} %fusion.8.refs_1_), kind=kOutput, calls=%fused_computation.1 | convolution fusion | flops 3733028864 | bytes 9213952 | tf_op jit(solution)/shard_map/dot_general | solution.py:871
  112.0 9.7 %shard_map.308 = (bf16[1184,512]{1,0:T(8,128)(2,1)}, f32[8,8,592]{2,1,0:T(8,128)}) custom-call(bf16[1184,1536]{1,0:T(8,128)(2,1)} %fusion.refs_0_, bf16[592,128]{1,0:T(8,128)(2,1)} %broadcast_in_dim.56.refs_1_), custom_call_target="tpu_custom_call" | custom-call | flops 2871001088 | bytes 2424832 | tf_op jit(solution)/shard_map/pallas_call | solution.py:813
  121.7 2.0 convolution_convert_fusion
  127.1 9.1 %shard_map.309 = (bf16[1184,512]{1,0:T(8,128)(2,1)}, f32[8,8,592]{2,1,0:T(8,128)}) custom-call(bf16[1184,1536]{1,0:T(8,128)(2,1)} %fusion.refs_0_, bf16[592,128]{1,0:T(8,128)(2,1)} %broadcast_in_dim.56.refs_1_, bf16[1184,512]{1,0:T(8,128)(2,1)} %get-tuple-element.109.refs_2_, ...), custom_call_target="tpu_custom_call", output_to_operand_aliasing={{0}: (2, {}), {1}: (3, {})} | custom-call | flops 2871001088 | bytes 2424832 | tf_op jit(solution)/shard_map/pallas_call | solution.py:813
  136.2 2.6 fusion.74
  141.1 4.2 collective-permute-done.13
  145.3 2.0 convert_reduce_fusion.2
  148.1 11.3 %all-gather.2.cloned.1.call-done = bf16[2048,2048]{1,0:T(8,128)(2,1)} async-done(((bf16[128,2048]{1,0:T(8,128)(2,1)}), bf16[2048,2048]{1,0:T(8,128)(2,1)}) %all-gather.2.cloned.1.call-update) | async-done | bytes 8388624 | tf_op jit(solution)/shard_map/all_gather | solution.py:950
  159.4 13.1 %shard_map.310 = (bf16[1184,2048]{1,0:T(8,128)(2,1)}, bf16[1184,2048]{1,0:T(8,128)(2,1)}) custom-call(s32[4]{0:T(128)} %pad_add_fusion.places_ref.refs_0_, bf16[592,1024]{1,0:T(8,128)(2,1)} %add_convert_fusion.own_ref.refs_1_, bf16[592,1024]{1,0:T(8,128)(2,1)} %collective-permute-done.11.far_ref.refs_2_, bf16[8,2,128,2048]{3,2,1,0:T(8,128)(2,1)} %bitcast.201, ...), custom_call_target="tpu_custom_call" | custom-call | flops 4966055936 | bytes 16318464 | tf_op jit(solution)/shard_map/pallas_call | solution.py:543
  172.5 8.5 %shard_map.311 = (bf16[2,512,512]{2,1,0:T(8,128)(2,1)}, bf16[2,512,512]{2,1,0:T(8,128)(2,1)}) custom-call(s32[4]{0:T(128)} %pad_add_fusion.places_ref.refs_0_, bf16[592,1024]{1,0:T(8,128)(2,1)} %get-tuple-element.117.refs_1_.own_ref, bf16[592,1024]{1,0:T(8,128)(2,1)} %collective-permute-done.14.refs_2_.far_ref, ...), custom_call_target="tpu_custom_call" | custom-call | flops 2483027968 | bytes 11796480 | tf_op jit(solution)/shard_map/pallas_call | solution.py:706
  181.5 1.7 collective-permute-start.16
  183.2 11.2 %shard_map.312 = (bf16[1184,2048]{1,0:T(8,128)(2,1)}, f32[1,2048]{1,0:T(1,128)}) custom-call(s32[4]{0:T(128)} %pad_add_fusion.places_ref.refs_0_, bf16[592,1024]{1,0:T(8,128)(2,1)} %get-tuple-element.117.refs_1_.own_ref, bf16[592,1024]{1,0:T(8,128)(2,1)} %collective-permute-done.14.refs_2_.far_ref, bf16[8,2,128,2048]{3,2,1,0:T(8,128)(2,1)} %bitcast.202, ...), custom_call_target="tpu_custom_call" | custom-call | flops 4966055936 | bytes 16318464 | tf_op jit(solution)/shard_map/pallas_call | solution.py:583
  194.4 8.7 %shard_map.313 = (bf16[2,512,512]{2,1,0:T(8,128)(2,1)}, bf16[2,512,512]{2,1,0:T(8,128)(2,1)}) custom-call(s32[4]{0:T(128)} %pad_add_fusion.places_ref.refs_0_, bf16[592,1024]{1,0:T(8,128)(2,1)} %add_convert_fusion.own_ref.refs_1_, bf16[592,1024]{1,0:T(8,128)(2,1)} %collective-permute-done.11.far_ref.refs_2_, ...), custom_call_target="tpu_custom_call" | custom-call | flops 2483027968 | bytes 11796480 | tf_op jit(solution)/shard_map/pallas_call | solution.py:706
  203.1 8.5 %shard_map.314 = (bf16[2,512,512]{2,1,0:T(8,128)(2,1)}, bf16[2,512,512]{2,1,0:T(8,128)(2,1)}) custom-call(s32[4]{0:T(128)} %pad_add_fusion.places_ref.refs_0_, bf16[592,1024]{1,0:T(8,128)(2,1)} %get-tuple-element.117.refs_1_.own_ref, bf16[592,1024]{1,0:T(8,128)(2,1)} %collective-permute-done.14.refs_2_.far_ref, ...), custom_call_target="tpu_custom_call" | custom-call | flops 2483027968 | bytes 11796480 | tf_op jit(solution)/shard_map/pallas_call | solution.py:706
  211.7 10.2 %shard_map.315 = (f32[592,1024]{1,0:T(8,128)}, bf16[592,1024]{1,0:T(8,128)(2,1)}) custom-call(s32[4]{0:T(128)} %pad_add_fusion.places_ref.refs_0_, bf16[1184,2048]{1,0:T(8,128)(2,1)} %get-tuple-element.131.refs_3_.left_ref, bf16[8,2,128,2048]{3,2,1,0:T(8,128)(2,1)} %bitcast.203), custom_call_target="tpu_custom_call" | custom-call | flops 4966055936 | bytes 12681216 | tf_op jit(solution)/shard_map/pallas_call | solution.py:626
  225.8 2.3 fusion.38
  228.5 2.1 fusion.37
  230.7 1.7 collective-permute-start.21
  232.5 2.5 multiply_reduce_fusion
  235.1 4.0 convert_reduce_fusion.3
  239.1 8.5 %shard_map.316 = (bf16[2,512,512]{2,1,0:T(8,128)(2,1)}, bf16[2,512,512]{2,1,0:T(8,128)(2,1)}) custom-call(s32[4]{0:T(128)} %pad_add_fusion.places_ref.refs_0_, bf16[592,1024]{1,0:T(8,128)(2,1)} %add_convert_fusion.own_ref.refs_1_, bf16[592,1024]{1,0:T(8,128)(2,1)} %collective-permute-done.11.far_ref.refs_2_, ...), custom_call_target="tpu_custom_call" | custom-call | flops 2483027968 | bytes 11796480 | tf_op jit(solution)/shard_map/pallas_call | solution.py:706
  248.9 1.6 collective-permute-done.20.two_a
  250.6 9.1 %collective-permute-done.22.two_b = bf16[512,512]{1,0:T(8,128)(2,1)S(1)} collective-permute-done((bf16[512,512]{1,0:T(8,128)(2,1)}, bf16[512,512]{1,0:T(8,128)(2,1)S(1)}, u32[]{:S(2)}, u32[]{:S(2)}) %collective-permute-start.22) | collective-permute-done | bytes 524320 | tf_op jit(solution)/shard_map/ppermute | solution.py:303
  261.1 3.0 shard_map.317
  264.0 9.2 %collective-permute-start.47 = (bf16[2,128,512]{2,1,0:T(8,128)(2,1)}, bf16[2,128,512]{2,1,0:T(8,128)(2,1)}, u32[]{:S(2)}, u32[]{:S(2)}) collective-permute-start(bf16[2,128,512]{2,1,0:T(8,128)(2,1)} %get-tuple-element.139), channel_id=1, source_target_pairs={{0,8},{1,9},{2,10},{3,11},{4,12},{5,13},{6,14},{7,15},{8,0},{9,1},... | collective-permute-start | bytes 786440 | tf_op jit(solution)/shard_map/ppermute | solution.py:303
  273.3 3.1 collective-permute-start.48
  280.0 2.0 fusion.39
  282.0 1.7 convolution_convert_fusion.2.refs_2_
  283.7 1.6 convolution_convert_fusion.1.refs_2_
  285.4 16.5 %shard_map.318.refs_5_ = bf16[1184,1536]{1,0:T(8,128)(2,1)} custom-call(bf16[1184,1536]{1,0:T(8,128)(2,1)} %fusion.refs_0_, bf16[592,128]{1,0:T(8,128)(2,1)} %broadcast_in_dim.56.refs_1_, bf16[592,512]{1,0:T(8,128)(2,1)} %convolution_convert_fusion.2.refs_2_, bf16[1184,512]{1,0:T(8,128)(2,1)} %get-tuple-element.111.refs_3_.refs_6_, ...), custom_call_target="tpu_custom_call" | custom-call | flops 7177502720 | bytes 4849664 | tf_op jit(solution)/shard_map/pallas_call | solution.py:847
  304.8 3.0 shard_map.319
  308.4 2.4 collective-permute-start.26
  312.2 16.1 %shard_map.320.refs_3_ = bf16[1184,1536]{1,0:T(8,128)(2,1)} custom-call(bf16[1184,1536]{1,0:T(8,128)(2,1)} %fusion.refs_0_, bf16[592,128]{1,0:T(8,128)(2,1)} %broadcast_in_dim.56.refs_1_, bf16[592,512]{1,0:T(8,128)(2,1)} %convolution_convert_fusion.1.refs_2_, bf16[1184,512]{1,0:T(8,128)(2,1)} %get-tuple-element.111.refs_3_.refs_6_, ...), custom_call_target="tpu_custom_call", output_to_operand_aliasing={{}: (5, {})} | custom-call | flops 7177502720 | bytes 4849664 | tf_op jit(solution)/shard_map/pallas_call | solution.py:847
  331.5 3.2 convert_reduce_fusion
  334.7 11.3 %shard_map.323 = (bf16[2,512,512]{2,1,0:T(8,128)(2,1)}, bf16[2,512,512]{2,1,0:T(8,128)(2,1)}) custom-call(s32[4]{0:T(128)} %pad_add_fusion.places_ref.refs_0_, bf16[592,1024]{1,0:T(8,128)(2,1)} %copy-done, bf16[592,1024]{1,0:T(8,128)(2,1)} %collective-permute-done.7.refs_2_, bf16[1184,1536]{1,0:T(8,128)(2,1)} %shard_map.320.refs_3_, ...), custom_call_target="tpu_custom_call" | custom-call | flops 2483027968 | bytes 11796480 | tf_op jit(solution)/shard_map/pallas_call | solution.py:706
  347.4 1.7 collective-permute-start.39
  351.9 5.5 %fusion.26 = bf16[592,1024]{1,0:T(8,128)(2,1)} fusion(bf16[1024,1536]{1,0:T(8,128)(2,1)} %bitcast.206, bf16[1184,1536]{1,0:T(8,128)(2,1)} %shard_map.320.refs_3_), kind=kOutput, calls=%fused_computation.45 | convolution fusion | flops 1862877184 | bytes 6176768 | tf_op jit(solution)/shard_map/dot_general | solution.py:498
  358.0 11.1 %shard_map.321 = (bf16[2,512,512]{2,1,0:T(8,128)(2,1)}, bf16[2,512,512]{2,1,0:T(8,128)(2,1)}) custom-call(s32[4]{0:T(128)} %pad_add_fusion.places_ref.refs_0_, bf16[592,1024]{1,0:T(8,128)(2,1)} %copy-done, bf16[592,1024]{1,0:T(8,128)(2,1)} %collective-permute-done.7.refs_2_, bf16[1184,1536]{1,0:T(8,128)(2,1)} %shard_map.320.refs_3_, ...), custom_call_target="tpu_custom_call" | custom-call | flops 2483027968 | bytes 11796480 | tf_op jit(solution)/shard_map/pallas_call | solution.py:706
  369.0 10.0 %shard_map.322 = (f32[592,1024]{1,0:T(8,128)}, bf16[592,1024]{1,0:T(8,128)(2,1)}) custom-call(s32[4]{0:T(128)} %pad_add_fusion.places_ref.refs_0_, bf16[1184,2048]{1,0:T(8,128)(2,1)} %get-tuple-element.158.refs_3_.left_ref, bf16[8,2,128,2048]{3,2,1,0:T(8,128)(2,1)} %bitcast.204), custom_call_target="tpu_custom_call" | custom-call | flops 4966055936 | bytes 12681216 | tf_op jit(solution)/shard_map/pallas_call | solution.py:626
  386.9 5.6 %fusion.13 = (f32[1024]{0:T(1024)S(1)}, f32[592]{0:T(1024)S(1)}, f32[592]{0:T(1024)S(1)}, f32[1024]{0:T(1024)S(1)}, f32[592,1024]{1,0:T(8,128)S(1)}) fusion(f32[592]{0:T(1024)S(1)} %copy-done.50, f32[592]{0:T(1024)S(1)} %copy-done.33, bf16[296,1024]{1,0:T(8,128)(2,1)S(1)} %copy-done.6, bf16[296,1024]{1,0:T(8,128)(2,1)S(1)} %get-tuple-element.249, ...), kind=kOutput, calls=%fused_computation.18 | convolution fusion | flops 1871360768 | bytes 9835776 | tf_op jit(solution)/shard_map/dot_general | solution.py:498
  393.9 5.4 %collective-permute-start.33 = (f32[12288]{0:T(1024)S(1)}, f32[12288]{0:T(1024)S(1)}, u32[]{:S(2)}, u32[]{:S(2)}) collective-permute-start(f32[12288]{0:T(1024)S(1)} %add.274), channel_id=1, source_target_pairs={{0,8},{1,9},{2,10},{3,11},{4,12},{5,13},{6,14},{7,15},{8,0},{9,1},... | collective-permute-start | bytes 147464 | tf_op jit(solution)/shard_map/ppermute | solution.py:303
  402.3 3.6 collective-permute-done.34
  408.0 1.9 fusion.12
  411.2 1.8 multiply_convert_fusion
  413.0 1.7 collective-permute-start.29
  414.7 2.1 collective-permute-done.37
  418.8 3.1 shard_map.324
  422.8 2.1 collective-permute-start.43
  428.3 3.2 copy.93
  431.6 5.5 %collective-permute-done.29 = bf16[289,1024]{1,0:T(8,128)(2,1)S(1)} collective-permute-done((bf16[289,1024]{1,0:T(8,128)(2,1)S(1)}, bf16[289,1024]{1,0:T(8,128)(2,1)S(1)}, u32[]{:S(2)}, u32[]{:S(2)}) %collective-permute-start.29) | collective-permute-done | bytes 591904 | tf_op jit(solution)/shard_map/ppermute | solution.py:303
  437.2 7.2 %collective-permute-done.43 = bf16[2,128,512]{2,1,0:T(8,128)(2,1)S(1)} collective-permute-done((bf16[2,128,512]{2,1,0:T(8,128)(2,1)}, bf16[2,128,512]{2,1,0:T(8,128)(2,1)S(1)}, u32[]{:S(2)}, u32[]{:S(2)}) %collective-permute-start.43) | collective-permute-done | bytes 262176 | tf_op jit(solution)/shard_map/ppermute | solution.py:303
  444.7 2.2 copy.92
  (339 shorter events, 72.8 us)
Async XLA Ops:
  7.2 152.2 %all-gather.2.cloned.1.call-start = ((), (), s32[]{:S(2)}) async-start(), calls=%async_computation | async-start | bytes 8912896 | tf_op jit(solution)/shard_map/all_gather | solution.py:950
  9.4 1.7 collective-permute-start.12
  12.3 1.4 collective-permute-start
  13.8 16.8 %collective-permute-start.2 = (bf16[2,128,512]{2,1,0:T(8,128)(2,1)S(1)}, bf16[2,128,512]{2,1,0:T(8,128)(2,1)S(1)}, u32[]{:S(2)}, u32[]{:S(2)}) collective-permute-start(bf16[2,128,512]{2,1,0:T(8,128)(2,1)S(1)} %bitcast.182), channel_id=1, source_target_pairs={{0,8},{1,9},{2,10},{3,11},{4,12},{5,13},{6,14},{7,15},{8,0},{9,1},... | collective-permute-start | bytes 786440 | tf_op jit(solution)/shard_map/ppermute | solution.py:303
  16.8 21.0 %collective-permute-start.3 = (bf16[2,128,512]{2,1,0:T(8,128)(2,1)S(1)}, bf16[2,128,512]{2,1,0:T(8,128)(2,1)}, u32[]{:S(2)}, u32[]{:S(2)}) collective-permute-start(bf16[2,128,512]{2,1,0:T(8,128)(2,1)S(1)} %bitcast.183), channel_id=1, source_target_pairs={{0,16},{1,17},{2,18},{3,19},{4,20},{5,21},{6,22},{7,23},{8,24},{9,... | collective-permute-start | bytes 786440 | tf_op jit(solution)/shard_map/ppermute | solution.py:303
  19.4 23.7 %collective-permute-start.4 = (bf16[2,128,512]{2,1,0:T(8,128)(2,1)S(1)}, bf16[2,128,512]{2,1,0:T(8,128)(2,1)}, u32[]{:S(2)}, u32[]{:S(2)}) collective-permute-start(bf16[2,128,512]{2,1,0:T(8,128)(2,1)S(1)} %bitcast.184), channel_id=1, source_target_pairs={{0,24},{1,25},{2,26},{3,27},{4,28},{5,29},{6,30},{7,31},{8,16},{9,... | collective-permute-start | bytes 786440 | tf_op jit(solution)/shard_map/ppermute | solution.py:303
  19.4 29.0 %copy-start.57 = (bf16[1024]{0:T(1024)(128)(2,1)S(1)}, bf16[1024]{0:T(1024)(128)(2,1)}, u32[]{:S(2)}) copy-start(bf16[1024]{0:T(1024)(128)(2,1)} %param.21) | copy-start | bytes 6148
  19.4 29.0 %copy-start.58 = (bf16[1024]{0:T(1024)(128)(2,1)S(1)}, bf16[1024]{0:T(1024)(128)(2,1)}, u32[]{:S(2)}) copy-start(bf16[1024]{0:T(1024)(128)(2,1)} %param.22) | copy-start | bytes 6148
  19.9 43.3 %collective-permute-start.1 = (bf16[296,1024]{1,0:T(8,128)(2,1)S(1)}, bf16[296,1024]{1,0:T(8,128)(2,1)S(1)}, u32[]{:S(2)}, u32[]{:S(2)}) collective-permute-start(bf16[296,1024]{1,0:T(8,128)(2,1)S(1)} %get-tuple-element.98), channel_id=1, source_target_pairs={{0,1},{1,0},{2,3},{3,2},{4,5},{5,4},{6,7},{7,6},{8,9},{9,8},{10,11... | collective-permute-start | bytes 1818632 | tf_op jit(solution)/shard_map/ppermute | solution.py:303
  45.4 12.9 %collective-permute-start.5 = (bf16[4,128,512]{2,1,0:T(8,128)(2,1)}, bf16[4,128,512]{2,1,0:T(8,128)(2,1)S(1)}, u32[]{:S(2)}, u32[]{:S(2)}) collective-permute-start(bf16[4,128,512]{2,1,0:T(8,128)(2,1)} %get-tuple-element.99.refs_0_), channel_id=1, source_target_pairs={{0,4},{1,5},{2,6},{3,7},{4,0},{5,1},{6,2},{7,3},{8,12},{9,13},{10,... | collective-permute-start | bytes 1572872 | tf_op jit(solution)/shard_map/ppermute | solution.py:303
  46.9 12.6 %collective-permute-start.6 = (bf16[4,128,512]{2,1,0:T(8,128)(2,1)}, bf16[4,128,512]{2,1,0:T(8,128)(2,1)S(1)}, u32[]{:S(2)}, u32[]{:S(2)}) collective-permute-start(bf16[4,128,512]{2,1,0:T(8,128)(2,1)} %get-tuple-element.100.refs_2_), channel_id=1, source_target_pairs={{0,1},{1,0},{2,3},{3,2},{4,5},{5,4},{6,7},{7,6},{8,9},{9,8},{10,11... | collective-permute-start | bytes 1572872 | tf_op jit(solution)/shard_map/ppermute | solution.py:303
  64.5 46.6 %copy-start = (bf16[592,1024]{1,0:T(8,128)(2,1)}, bf16[592,1024]{1,0:T(8,128)(2,1)S(1)}, u32[]{:S(2)}) copy-start(bf16[592,1024]{1,0:T(8,128)(2,1)S(1)} %fusion.8.refs_1_) | copy-start | bytes 3637252
  64.6 3.1 collective-permute-start.7
  64.7 26.2 %collective-permute-start.8 = (bf16[2,4,128,512]{3,2,1,0:T(8,128)(2,1)S(1)}, bf16[2,4,128,512]{3,2,1,0:T(8,128)(2,1)}, u32[]{:S(2)}, u32[]{:S(2)}) collective-permute-start(bf16[2,4,128,512]{3,2,1,0:T(8,128)(2,1)S(1)} %copy-done.19), channel_id=1, source_target_pairs={{0,1},{1,0},{2,3},{3,2},{4,5},{5,4},{6,7},{7,6},{8,9},{9,8},{10,11... | collective-permute-start | bytes 3145736 | tf_op jit(solution)/shard_map/ppermute | solution.py:303
  66.3 32.1 %collective-permute-start.9 = (bf16[2,4,128,512]{3,2,1,0:T(8,128)(2,1)}, bf16[2,4,128,512]{3,2,1,0:T(8,128)(2,1)}, u32[]{:S(2)}, u32[]{:S(2)}) collective-permute-start(bf16[2,4,128,512]{3,2,1,0:T(8,128)(2,1)} %get-tuple-element.102.refs_2_), channel_id=1, source_target_pairs={{0,4},{1,5},{2,6},{3,7},{4,0},{5,1},{6,2},{7,3},{8,12},{9,13},{10,... | collective-permute-start | bytes 3145736 | tf_op jit(solution)/shard_map/ppermute | solution.py:303
  123.7 12.6 %collective-permute-start.10 = (bf16[592,1024]{1,0:T(8,128)(2,1)S(1)}, bf16[592,1024]{1,0:T(8,128)(2,1)S(1)}, u32[]{:S(2)}, u32[]{:S(2)}) collective-permute-start(bf16[592,1024]{1,0:T(8,128)(2,1)S(1)} %convolution_convert_fusion), channel_id=1, source_target_pairs={{0,2},{1,3},{2,0},{3,1},{4,6},{5,7},{6,4},{7,5},{8,10},{9,11},{10,... | collective-permute-start | bytes 3637256 | tf_op jit(solution)/shard_map/ppermute | solution.py:303
  125.4 19.9 %copy-start.34 = (f32[592]{0:T(1024)}, f32[592]{0:T(1024)S(1)}, u32[]{:S(2)}) copy-start(f32[592]{0:T(1024)S(1)} %broadcast_select_fusion) | copy-start | bytes 7108
  125.6 19.8 %copy-start.7 = (bf16[296,1024]{1,0:T(8,128)(2,1)}, bf16[296,1024]{1,0:T(8,128)(2,1)S(1)}, u32[]{:S(2)}) copy-start(bf16[296,1024]{1,0:T(8,128)(2,1)S(1)} %get-tuple-element.247) | copy-start | bytes 1818628
  125.6 19.7 %collective-permute-start.13 = (bf16[296,1024]{1,0:T(8,128)(2,1)S(1)}, bf16[296,1024]{1,0:T(8,128)(2,1)S(1)}, u32[]{:S(2)}, u32[]{:S(2)}) collective-permute-start(bf16[296,1024]{1,0:T(8,128)(2,1)S(1)} %get-tuple-element.113), channel_id=1, source_target_pairs={{0,1},{1,0},{2,3},{3,2},{4,5},{5,4},{6,7},{7,6},{8,9},{9,8},{10,11... | collective-permute-start | bytes 1818632 | tf_op jit(solution)/shard_map/ppermute | solution.py:303
  140.8 7.2 %collective-permute-start.11 = (bf16[592,1024]{1,0:T(8,128)(2,1)}, bf16[592,1024]{1,0:T(8,128)(2,1)}, u32[]{:S(2)}, u32[]{:S(2)}) collective-permute-start(bf16[592,1024]{1,0:T(8,128)(2,1)} %add_convert_fusion.own_ref.refs_1_), channel_id=1, source_target_pairs={{0,2},{1,3},{2,0},{3,1},{4,6},{5,7},{6,4},{7,5},{8,10},{9,11},{10,... | collective-permute-start | bytes 3637256 | tf_op jit(solution)/shard_map/ppermute | solution.py:303
  147.3 25.2 %collective-permute-start.14 = (bf16[592,1024]{1,0:T(8,128)(2,1)}, bf16[592,1024]{1,0:T(8,128)(2,1)}, u32[]{:S(2)}, u32[]{:S(2)}) collective-permute-start(bf16[592,1024]{1,0:T(8,128)(2,1)} %get-tuple-element.117.refs_1_.own_ref), channel_id=1, source_target_pairs={{0,2},{1,3},{2,0},{3,1},{4,6},{5,7},{6,4},{7,5},{8,10},{9,11},{10,... | collective-permute-start | bytes 3637256 | tf_op jit(solution)/shard_map/ppermute | solution.py:303
  181.0 30.6 %collective-permute-start.15 = (bf16[2,512,512]{2,1,0:T(8,128)(2,1)}, bf16[2,512,512]{2,1,0:T(8,128)(2,1)S(1)}, u32[]{:S(2)}, u32[]{:S(2)}) collective-permute-start(bf16[2,512,512]{2,1,0:T(8,128)(2,1)} %get-tuple-element.115), channel_id=1, source_target_pairs={{0,1},{1,0},{2,3},{3,2},{4,5},{5,4},{6,7},{7,6},{8,9},{9,8},{10,11... | collective-permute-start | bytes 3145736 | tf_op jit(solution)/shard_map/ppermute | solution.py:303
  181.5 30.2 %collective-permute-start.16 = (bf16[2,512,512]{2,1,0:T(8,128)(2,1)}, bf16[2,512,512]{2,1,0:T(8,128)(2,1)S(1)}, u32[]{:S(2)}, u32[]{:S(2)}) collective-permute-start(bf16[2,512,512]{2,1,0:T(8,128)(2,1)} %get-tuple-element.116), channel_id=1, source_target_pairs={{0,4},{1,5},{2,6},{3,7},{4,0},{5,1},{6,2},{7,3},{8,12},{9,13},{10,... | collective-permute-start | bytes 3145736 | tf_op jit(solution)/shard_map/ppermute | solution.py:303
  222.0 10.4 %collective-permute-start.17 = (bf16[592,1024]{1,0:T(8,128)(2,1)}, bf16[592,1024]{1,0:T(8,128)(2,1)}, u32[]{:S(2)}, u32[]{:S(2)}) collective-permute-start(bf16[592,1024]{1,0:T(8,128)(2,1)} %get-tuple-element.130), channel_id=1, source_target_pairs={{0,2},{1,3},{2,0},{3,1},{4,6},{5,7},{6,4},{7,5},{8,10},{9,11},{10,... | collective-permute-start | bytes 3637256 | tf_op jit(solution)/shard_map/ppermute | solution.py:303
  222.7 26.3 %collective-permute-start.19 = (bf16[2,512,512]{2,1,0:T(8,128)(2,1)}, bf16[2,512,512]{2,1,0:T(8,128)(2,1)}, u32[]{:S(2)}, u32[]{:S(2)}) collective-permute-start(bf16[2,512,512]{2,1,0:T(8,128)(2,1)} %get-tuple-element.121), channel_id=1, source_target_pairs={{0,1},{1,0},{2,3},{3,2},{4,5},{5,4},{6,7},{7,6},{8,9},{9,8},{10,11... | collective-permute-start | bytes 3145736 | tf_op jit(solution)/shard_map/ppermute | solution.py:303
  224.2 26.3 %collective-permute-start.20 = (bf16[2,512,512]{2,1,0:T(8,128)(2,1)}, bf16[2,512,512]{2,1,0:T(8,128)(2,1)}, u32[]{:S(2)}, u32[]{:S(2)}) collective-permute-start(bf16[2,512,512]{2,1,0:T(8,128)(2,1)} %get-tuple-element.122), channel_id=1, source_target_pairs={{0,4},{1,5},{2,6},{3,7},{4,0},{5,1},{6,2},{7,3},{8,12},{9,13},{10,... | collective-permute-start | bytes 3145736 | tf_op jit(solution)/shard_map/ppermute | solution.py:303
  228.1 31.6 %collective-permute-start.22 = (bf16[512,512]{1,0:T(8,128)(2,1)}, bf16[512,512]{1,0:T(8,128)(2,1)S(1)}, u32[]{:S(2)}, u32[]{:S(2)}) collective-permute-start(bf16[512,512]{1,0:T(8,128)(2,1)} %fusion.38), channel_id=1, source_target_pairs={{0,1},{1,0},{2,3},{3,2},{4,5},{5,4},{6,7},{7,6},{8,9},{9,8},{10,11... | collective-permute-start | bytes 1572872 | tf_op jit(solution)/shard_map/ppermute | solution.py:303
  230.7 30.4 %collective-permute-start.21 = (bf16[512,512]{1,0:T(8,128)(2,1)}, bf16[512,512]{1,0:T(8,128)(2,1)}, u32[]{:S(2)}, u32[]{:S(2)}) collective-permute-start(bf16[512,512]{1,0:T(8,128)(2,1)} %fusion.37), channel_id=1, source_target_pairs={{0,4},{1,5},{2,6},{3,7},{4,0},{5,1},{6,2},{7,3},{8,12},{9,13},{10,... | collective-permute-start | bytes 1572872 | tf_op jit(solution)/shard_map/ppermute | solution.py:303
  239.1 42.9 %copy-start.1 = (bf16[592,1024]{1,0:T(8,128)(2,1)}, bf16[592,1024]{1,0:T(8,128)(2,1)S(1)}, u32[]{:S(2)}) copy-start(bf16[592,1024]{1,0:T(8,128)(2,1)S(1)} %get-tuple-element.241.refs_4_) | copy-start | bytes 3637252
  239.1 44.6 %collective-permute-start.18 = (bf16[592,1024]{1,0:T(8,128)(2,1)S(1)}, bf16[592,1024]{1,0:T(8,128)(2,1)S(1)}, u32[]{:S(2)}, u32[]{:S(2)}) collective-permute-start(bf16[592,1024]{1,0:T(8,128)(2,1)S(1)} %get-tuple-element.241.refs_4_), channel_id=1, source_target_pairs={{0,2},{1,3},{2,0},{3,1},{4,6},{5,7},{6,4},{7,5},{8,10},{9,11},{10,... | collective-permute-start | bytes 3637256 | tf_op jit(solution)/shard_map/ppermute | solution.py:303
  250.6 27.2 %copy-start.16 = (bf16[2,512,512]{2,1,0:T(8,128)(2,1)S(1)}, bf16[2,512,512]{2,1,0:T(8,128)(2,1)}, u32[]{:S(2)}) copy-start(bf16[2,512,512]{2,1,0:T(8,128)(2,1)} %get-tuple-element.133.two_ref) | copy-start | bytes 3145732
  250.6 29.4 %copy-start.52 = (f32[1024]{0:T(1024)S(1)}, f32[1024]{0:T(1024)}, u32[]{:S(2)}) copy-start(f32[1024]{0:T(1024)} %get-tuple-element.238) | copy-start | bytes 12292
  250.6 29.4 %copy-start.15 = (bf16[2,512,512]{2,1,0:T(8,128)(2,1)S(1)}, bf16[2,512,512]{2,1,0:T(8,128)(2,1)}, u32[]{:S(2)}) copy-start(bf16[2,512,512]{2,1,0:T(8,128)(2,1)} %get-tuple-element.132.one_ref) | copy-start | bytes 3145732
  264.0 18.0 %copy-start.66 = (bf16[4,2,128,512]{3,2,1,0:T(8,128)(2,1)S(1)}, bf16[4,2,128,512]{3,2,1,0:T(8,128)(2,1)}, u32[]{:S(2)}) copy-start(bf16[4,2,128,512]{3,2,1,0:T(8,128)(2,1)} %get-tuple-element.108) | copy-start | bytes 3145732
  264.0 37.8 %collective-permute-start.47 = (bf16[2,128,512]{2,1,0:T(8,128)(2,1)}, bf16[2,128,512]{2,1,0:T(8,128)(2,1)}, u32[]{:S(2)}, u32[]{:S(2)}) collective-permute-start(bf16[2,128,512]{2,1,0:T(8,128)(2,1)} %get-tuple-element.139), channel_id=1, source_target_pairs={{0,8},{1,9},{2,10},{3,11},{4,12},{5,13},{6,14},{7,15},{8,0},{9,1},... | collective-permute-start | bytes 786440 | tf_op jit(solution)/shard_map/ppermute | solution.py:303
  273.3 28.6 %collective-permute-start.48 = (bf16[2,128,512]{2,1,0:T(8,128)(2,1)}, bf16[2,128,512]{2,1,0:T(8,128)(2,1)}, u32[]{:S(2)}, u32[]{:S(2)}) collective-permute-start(bf16[2,128,512]{2,1,0:T(8,128)(2,1)} %get-tuple-element.140), channel_id=1, source_target_pairs={{0,16},{1,17},{2,18},{3,19},{4,20},{5,21},{6,22},{7,23},{8,24},{9,... | collective-permute-start | bytes 786440 | tf_op jit(solution)/shard_map/ppermute | solution.py:303
  276.4 25.5 %collective-permute-start.49 = (bf16[2,128,512]{2,1,0:T(8,128)(2,1)}, bf16[2,128,512]{2,1,0:T(8,128)(2,1)}, u32[]{:S(2)}, u32[]{:S(2)}) collective-permute-start(bf16[2,128,512]{2,1,0:T(8,128)(2,1)} %get-tuple-element.141), channel_id=1, source_target_pairs={{0,24},{1,25},{2,26},{3,27},{4,28},{5,29},{6,30},{7,31},{8,16},{9,... | collective-permute-start | bytes 786440 | tf_op jit(solution)/shard_map/ppermute | solution.py:303
  278.9 24.3 %collective-permute-start.24 = (bf16[512,512]{1,0:T(8,128)(2,1)S(1)}, bf16[512,512]{1,0:T(8,128)(2,1)S(1)}, u32[]{:S(2)}, u32[]{:S(2)}) collective-permute-start(bf16[512,512]{1,0:T(8,128)(2,1)S(1)} %fusion.40), channel_id=1, source_target_pairs={{0,1},{1,0},{2,3},{3,2},{4,5},{5,4},{6,7},{7,6},{8,9},{9,8},{10,11... | collective-permute-start | bytes 1572872 | tf_op jit(solution)/shard_map/ppermute | solution.py:303
  283.7 19.6 %collective-permute-start.23 = (bf16[512,512]{1,0:T(8,128)(2,1)}, bf16[512,512]{1,0:T(8,128)(2,1)S(1)}, u32[]{:S(2)}, u32[]{:S(2)}) collective-permute-start(bf16[512,512]{1,0:T(8,128)(2,1)} %fusion.39), channel_id=1, source_target_pairs={{0,4},{1,5},{2,6},{3,7},{4,0},{5,1},{6,2},{7,3},{8,12},{9,13},{10,... | collective-permute-start | bytes 1572872 | tf_op jit(solution)/shard_map/ppermute | solution.py:303
  285.4 16.5 %copy-start.24 = (f32[2,128,512]{2,1,0:T(8,128)S(1)}, f32[2,128,512]{2,1,0:T(8,128)}, u32[]{:S(2)}) copy-start(f32[2,128,512]{2,1,0:T(8,128)} %get-tuple-element.138) | copy-start | bytes 1572868
  303.1 25.2 %collective-permute-start.50 = (bf16[2,64,512]{2,1,0:T(8,128)(2,1)S(1)}, bf16[2,64,512]{2,1,0:T(8,128)(2,1)S(1)}, u32[]{:S(2)}, u32[]{:S(2)}) collective-permute-start(bf16[2,64,512]{2,1,0:T(8,128)(2,1)S(1)} %fusion.51), channel_id=1, source_target_pairs={{0,2},{1,3},{2,0},{3,1},{4,6},{5,7},{6,4},{7,5},{8,10},{9,11},{10,... | collective-permute-start | bytes 393224 | tf_op jit(solution)/shard_map/ppermute | solution.py:303
  307.8 22.3 %collective-permute-start.25 = (bf16[2,128,512]{2,1,0:T(8,128)(2,1)}, bf16[2,128,512]{2,1,0:T(8,128)(2,1)}, u32[]{:S(2)}, u32[]{:S(2)}) collective-permute-start(bf16[2,128,512]{2,1,0:T(8,128)(2,1)} %get-tuple-element.148), channel_id=1, source_target_pairs={{0,8},{1,9},{2,10},{3,11},{4,12},{5,13},{6,14},{7,15},{8,0},{9,1},... | collective-permute-start | bytes 786440 | tf_op jit(solution)/shard_map/ppermute | solution.py:303
  308.4 21.7 %collective-permute-start.26 = (bf16[2,128,512]{2,1,0:T(8,128)(2,1)}, bf16[2,128,512]{2,1,0:T(8,128)(2,1)}, u32[]{:S(2)}, u32[]{:S(2)}) collective-permute-start(bf16[2,128,512]{2,1,0:T(8,128)(2,1)} %get-tuple-element.149), channel_id=1, source_target_pairs={{0,16},{1,17},{2,18},{3,19},{4,20},{5,21},{6,22},{7,23},{8,24},{9,... | collective-permute-start | bytes 786440 | tf_op jit(solution)/shard_map/ppermute | solution.py:303
  310.8 19.3 %collective-permute-start.27 = (bf16[2,128,512]{2,1,0:T(8,128)(2,1)}, bf16[2,128,512]{2,1,0:T(8,128)(2,1)}, u32[]{:S(2)}, u32[]{:S(2)}) collective-permute-start(bf16[2,128,512]{2,1,0:T(8,128)(2,1)} %get-tuple-element.150), channel_id=1, source_target_pairs={{0,24},{1,25},{2,26},{3,27},{4,28},{5,29},{6,30},{7,31},{8,16},{9,... | collective-permute-start | bytes 786440 | tf_op jit(solution)/shard_map/ppermute | solution.py:303
  346.0 37.0 %collective-permute-start.38 = (bf16[2,512,512]{2,1,0:T(8,128)(2,1)}, bf16[2,512,512]{2,1,0:T(8,128)(2,1)}, u32[]{:S(2)}, u32[]{:S(2)}) collective-permute-start(bf16[2,512,512]{2,1,0:T(8,128)(2,1)} %get-tuple-element.161), channel_id=1, source_target_pairs={{0,1},{1,0},{2,3},{3,2},{4,5},{5,4},{6,7},{7,6},{8,9},{9,8},{10,11... | collective-permute-start | bytes 3145736 | tf_op jit(solution)/shard_map/ppermute | solution.py:303
  347.4 35.6 %collective-permute-start.39 = (bf16[2,512,512]{2,1,0:T(8,128)(2,1)}, bf16[2,512,512]{2,1,0:T(8,128)(2,1)}, u32[]{:S(2)}, u32[]{:S(2)}) collective-permute-start(bf16[2,512,512]{2,1,0:T(8,128)(2,1)} %get-tuple-element.162), channel_id=1, source_target_pairs={{0,4},{1,5},{2,6},{3,7},{4,0},{5,1},{6,2},{7,3},{8,12},{9,13},{10,... | collective-permute-start | bytes 3145736 | tf_op jit(solution)/shard_map/ppermute | solution.py:303
  349.8 30.5 %collective-permute-start.46 = (bf16[2,64,512]{2,1,0:T(8,128)(2,1)}, bf16[2,64,512]{2,1,0:T(8,128)(2,1)}, u32[]{:S(2)}, u32[]{:S(2)}) collective-permute-start(bf16[2,64,512]{2,1,0:T(8,128)(2,1)} %fusion.50), channel_id=1, source_target_pairs={{0,2},{1,3},{2,0},{3,1},{4,6},{5,7},{6,4},{7,5},{8,10},{9,11},{10,... | collective-permute-start | bytes 393224 | tf_op jit(solution)/shard_map/ppermute | solution.py:303
  357.4 29.4 %collective-permute-start.30 = (bf16[592,1024]{1,0:T(8,128)(2,1)}, bf16[592,1024]{1,0:T(8,128)(2,1)}, u32[]{:S(2)}, u32[]{:S(2)}) collective-permute-start(bf16[592,1024]{1,0:T(8,128)(2,1)} %fusion.26), channel_id=1, source_target_pairs={{0,2},{1,3},{2,0},{3,1},{4,6},{5,7},{6,4},{7,5},{8,10},{9,11},{10,... | collective-permute-start | bytes 3637256 | tf_op jit(solution)/shard_map/ppermute | solution.py:303
  380.3 30.8 %collective-permute-start.28 = (bf16[592,1024]{1,0:T(8,128)(2,1)}, bf16[592,1024]{1,0:T(8,128)(2,1)}, u32[]{:S(2)}, u32[]{:S(2)}) collective-permute-start(bf16[592,1024]{1,0:T(8,128)(2,1)} %get-tuple-element.160), channel_id=1, source_target_pairs={{0,2},{1,3},{2,0},{3,1},{4,6},{5,7},{6,4},{7,5},{8,10},{9,11},{10,... | collective-permute-start | bytes 3637256 | tf_op jit(solution)/shard_map/ppermute | solution.py:303
  384.4 33.6 %collective-permute-start.41 = (bf16[512,512]{1,0:T(8,128)(2,1)S(1)}, bf16[512,512]{1,0:T(8,128)(2,1)S(1)}, u32[]{:S(2)}, u32[]{:S(2)}) collective-permute-start(bf16[512,512]{1,0:T(8,128)(2,1)S(1)} %fusion.42), channel_id=1, source_target_pairs={{0,1},{1,0},{2,3},{3,2},{4,5},{5,4},{6,7},{7,6},{8,9},{9,8},{10,11... | collective-permute-start | bytes 1572872 | tf_op jit(solution)/shard_map/ppermute | solution.py:303
  386.8 21.2 %copy-start.2 = (f32[592,1024]{1,0:T(8,128)S(1)}, f32[592,1024]{1,0:T(8,128)}, u32[]{:S(2)}) copy-start(f32[592,1024]{1,0:T(8,128)} %get-tuple-element.242) | copy-start | bytes 7274500
  392.6 1.3 collective-permute-start.32
  393.9 8.4 %collective-permute-start.33 = (f32[12288]{0:T(1024)S(1)}, f32[12288]{0:T(1024)S(1)}, u32[]{:S(2)}, u32[]{:S(2)}) collective-permute-start(f32[12288]{0:T(1024)S(1)} %add.274), channel_id=1, source_target_pairs={{0,8},{1,9},{2,10},{3,11},{4,12},{5,13},{6,14},{7,15},{8,0},{9,1},... | collective-permute-start | bytes 147464 | tf_op jit(solution)/shard_map/ppermute | solution.py:303
  399.3 6.5 %collective-permute-start.34 = (f32[12288]{0:T(1024)S(1)}, f32[12288]{0:T(1024)S(1)}, u32[]{:S(2)}, u32[]{:S(2)}) collective-permute-start(f32[12288]{0:T(1024)S(1)} %add.274), channel_id=1, source_target_pairs={{0,16},{1,17},{2,18},{3,19},{4,20},{5,21},{6,22},{7,23},{8,24},{9,... | collective-permute-start | bytes 147464 | tf_op jit(solution)/shard_map/ppermute | solution.py:303
  400.9 6.0 %collective-permute-start.35 = (f32[12288]{0:T(1024)S(1)}, f32[12288]{0:T(1024)S(1)}, u32[]{:S(2)}, u32[]{:S(2)}) collective-permute-start(f32[12288]{0:T(1024)S(1)} %add.274), channel_id=1, source_target_pairs={{0,24},{1,25},{2,26},{3,27},{4,28},{5,29},{6,30},{7,31},{8,16},{9,... | collective-permute-start | bytes 147464 | tf_op jit(solution)/shard_map/ppermute | solution.py:303
  402.3 15.8 %collective-permute-start.40 = (bf16[512,512]{1,0:T(8,128)(2,1)S(1)}, bf16[512,512]{1,0:T(8,128)(2,1)}, u32[]{:S(2)}, u32[]{:S(2)}) collective-permute-start(bf16[512,512]{1,0:T(8,128)(2,1)S(1)} %fusion.41), channel_id=1, source_target_pairs={{0,4},{1,5},{2,6},{3,7},{4,0},{5,1},{6,2},{7,3},{8,12},{9,13},{10,... | collective-permute-start | bytes 1572872 | tf_op jit(solution)/shard_map/ppermute | solution.py:303
  406.9 4.2 collective-permute-start.36
  410.0 16.8 %collective-permute-start.31 = (bf16[289,1024]{1,0:T(8,128)(2,1)S(1)}, bf16[289,1024]{1,0:T(8,128)(2,1)}, u32[]{:S(2)}, u32[]{:S(2)}) collective-permute-start(bf16[289,1024]{1,0:T(8,128)(2,1)S(1)} %slice.294), channel_id=1, source_target_pairs={{0,1},{1,0},{2,3},{3,2},{4,5},{5,4},{6,7},{7,6},{8,9},{9,8},{10,11... | collective-permute-start | bytes 1775624 | tf_op jit(solution)/shard_map/ppermute | solution.py:303
  411.0 5.8 %collective-permute-start.37 = (f32[12288]{0:T(1024)S(1)}, f32[12288]{0:T(1024)S(1)}, u32[]{:S(2)}, u32[]{:S(2)}) collective-permute-start(f32[12288]{0:T(1024)S(1)} %add.278), channel_id=1, source_target_pairs={{0,4},{1,5},{2,6},{3,7},{4,0},{5,1},{6,2},{7,3},{8,12},{9,13},{10,... | collective-permute-start | bytes 147464 | tf_op jit(solution)/shard_map/ppermute | solution.py:303
  413.0 24.0 %collective-permute-start.29 = (bf16[289,1024]{1,0:T(8,128)(2,1)S(1)}, bf16[289,1024]{1,0:T(8,128)(2,1)S(1)}, u32[]{:S(2)}, u32[]{:S(2)}) collective-permute-start(bf16[289,1024]{1,0:T(8,128)(2,1)S(1)} %slice.221), channel_id=1, source_target_pairs={{0,1},{1,0},{2,3},{3,2},{4,5},{5,4},{6,7},{7,6},{8,9},{9,8},{10,11... | collective-permute-start | bytes 1775624 | tf_op jit(solution)/shard_map/ppermute | solution.py:303
  421.9 15.3 %collective-permute-start.42 = (bf16[2,128,512]{2,1,0:T(8,128)(2,1)}, bf16[2,128,512]{2,1,0:T(8,128)(2,1)S(1)}, u32[]{:S(2)}, u32[]{:S(2)}) collective-permute-start(bf16[2,128,512]{2,1,0:T(8,128)(2,1)} %get-tuple-element.170), channel_id=1, source_target_pairs={{0,8},{1,9},{2,10},{3,11},{4,12},{5,13},{6,14},{7,15},{8,0},{9,1},... | collective-permute-start | bytes 786440 | tf_op jit(solution)/shard_map/ppermute | solution.py:303
  422.8 21.6 %collective-permute-start.43 = (bf16[2,128,512]{2,1,0:T(8,128)(2,1)}, bf16[2,128,512]{2,1,0:T(8,128)(2,1)S(1)}, u32[]{:S(2)}, u32[]{:S(2)}) collective-permute-start(bf16[2,128,512]{2,1,0:T(8,128)(2,1)} %get-tuple-element.171), channel_id=1, source_target_pairs={{0,16},{1,17},{2,18},{3,19},{4,20},{5,21},{6,22},{7,23},{8,24},{9,... | collective-permute-start | bytes 786440 | tf_op jit(solution)/shard_map/ppermute | solution.py:303
  424.9 19.5 %collective-permute-start.44 = (bf16[2,128,512]{2,1,0:T(8,128)(2,1)}, bf16[2,128,512]{2,1,0:T(8,128)(2,1)S(1)}, u32[]{:S(2)}, u32[]{:S(2)}) collective-permute-start(bf16[2,128,512]{2,1,0:T(8,128)(2,1)} %get-tuple-element.172), channel_id=1, source_target_pairs={{0,24},{1,25},{2,26},{3,27},{4,28},{5,29},{6,30},{7,31},{8,16},{9,... | collective-permute-start | bytes 786440 | tf_op jit(solution)/shard_map/ppermute | solution.py:303
  444.5 2.4 collective-permute-start.45
  (56 other events, 284.7 us)
Sparse Core Ops, SparseCore 0:
  12.2 147.1 all-gather.1

commit v5 on v4

--- a/solution.py
+++ b/solution.py
@@ -292,7 +292,7 @@
 HALF_PAD = 8
 LANES = 128
 LOW = jnp.bfloat16
-VMEM_ROOM = 56 * 2**20
+VMEM_ROOM = 24 * 2**20
 
 
 def exchange(value, far_z=0, far_x=0, far_core=0, far_y=0):
@@ -487,13 +487,6 @@
     return vector, [exchange(vector, far_z=step) for step in (1, 2, 3)]
 
 
-def vector_last(vector, others):
-    vector = vector + others[0] + others[1] + others[2]
-    for step in ({"far_y": 1}, {"far_x": 1}):
-        vector = vector + exchange(vector, **step)
-    return vector
-
-
 def mat_far(left, right):
     return lax.dot_general(
         left, right, (((1,), (1,)), ((), ())), preferred_element_type=jnp.float32
@@ -648,26 +641,56 @@
     return own + exchange(send, far_core=1).astype(jnp.float32)
 
 
-def weight_kernel(send, pairs, places_ref, *refs):
-    ins, outs, lefts = refs[: 3 * pairs], refs[3 * pairs : 3 * pairs + 2], refs[3 * pairs + 2 :]
+def mat(left, right):
+    return jnp.dot(left, right, preferred_element_type=jnp.float32)
+
+
+def turn_kernel(places_ref, own_ref, far_ref, turned_ref, left_ref):
+    rows = own_ref.shape[0]
+    for block in range(4):
+        at = (places_ref[0] ^ block) * 2 + (places_ref[1] ^ pl.program_id(0))
+        start = pl.multiple_of(at * LANES, LANES)
+        span = slice(block * LANES, (block + 1) * LANES)
+        left_ref[:rows, span] = own_ref[:, pl.ds(start, LANES)]
+        left_ref[rows:, span] = far_ref[:, pl.ds(start, LANES)]
+    turned_ref[0] = jnp.transpose(left_ref[...])
+
+
+def turn(places, pair):
+    rows, width = pair[0].shape
+    line = width // 2
+    whole = pl.BlockSpec((rows, width), lambda i, s: (0, 0))
+    return pl.pallas_call(
+        turn_kernel,
+        grid_spec=pltpu.PrefetchScalarGridSpec(
+            num_scalar_prefetch=1,
+            grid=(2,),
+            in_specs=[whole, whole],
+            out_specs=pl.BlockSpec((1, line, 2 * rows), lambda i, s: (i, 0, 0)),
+            scratch_shapes=[pltpu.VMEM((2 * rows, line), LOW)],
+        ),
+        out_shape=jax.ShapeDtypeStruct((2, line, 2 * rows), LOW),
+        compiler_params=pltpu.CompilerParams(vmem_limit_bytes=VMEM_ROOM),
+        cost_estimate=pl.CostEstimate(
+            flops=0, transcendentals=0, bytes_accessed=rows * width * 8
+        ),
+    )(places, *pair)
+
+
+def weight_cost(operands):
+    rows, line = operands[0][1].shape[0], 4 * LANES
+    wide = sum(right.shape[1] for _, right in operands) // 4
+    return pl.CostEstimate(
+        flops=8 * rows * line * wide,
+        transcendentals=0,
+        bytes_accessed=rows * wide * 8 + rows * line * 8 + line * wide * 8,
+    )
+
+
+def piece_kernel(pairs, *refs):
+    ins, outs = refs[: 2 * pairs], refs[2 * pairs :]
     step = pl.program_id(0)
-
-    @pl.when(step < 2)
-    def _():
-        x_far = step if send else 1 - step
-        for pair in range(pairs):
-            rows = ins[3 * pair].shape[0]
-            for block in range(4):
-                at = (places_ref[0] ^ block) * 2 + (places_ref[1] ^ x_far)
-                start = pl.multiple_of(at * LANES, LANES)
-                for image in range(2):
-                    lefts[pair][
-                        image * rows : (image + 1) * rows, block * LANES : (block + 1) * LANES
-                    ] = ins[3 * pair + image][:, pl.ds(start, LANES)]
-
-    parts = [
-        mat_rows(lefts[pair][...], ins[3 * pair + 2][...]).astype(LOW) for pair in range(pairs)
-    ]
+    parts = [mat(ins[2 * pair][0], ins[2 * pair + 1][...]).astype(LOW) for pair in range(pairs)]
     made = parts[0] if pairs == 1 else jnp.concatenate(parts, axis=1)
 
     @pl.when(step < 2)
@@ -679,50 +702,37 @@
         outs[1][0] = made
 
 
-def weight_pieces(places, operands, send):
-    rows, width = operands[0][0][0].shape
-    line = width // 2
-    first = (lambda i: jnp.minimum(i, 1)) if send else (lambda i: 1 - jnp.minimum(i, 1))
-
-    def right_map(i, s):
-        if send:
-            return (0, jnp.where(i < 2, 1, i))
-        return (0, jnp.where(i < 2, 0, i))
-
-    specs, arrays, scratch, wide = [], [], [], 0
-    for left, right in operands:
+def weight_pieces(operands, send):
+    line, rows = operands[0][0].shape[1:]
+    if send:
+        first = lambda i: jnp.minimum(i, 1)
+        column = lambda i: jnp.maximum(i, 1)
+    else:
+        first = lambda i: 1 - jnp.minimum(i, 1)
+        column = lambda i: jnp.where(i < 2, 0, i)
+    specs, arrays, wide = [], [], 0
+    for turned, right in operands:
         span = right.shape[1] // 4
         wide += span
-        for image in range(2):
-            specs.append(pl.BlockSpec((rows, width), lambda i, s: (0, 0)))
-            arrays.append(left[image])
-        specs.append(pl.BlockSpec((2 * rows, span), right_map))
-        arrays.append(right)
-        scratch.append(pltpu.VMEM((2 * rows, line), LOW))
+        specs.append(pl.BlockSpec((1, line, rows), lambda i: (first(i), 0, 0)))
+        specs.append(pl.BlockSpec((rows, span), lambda i: (0, column(i))))
+        arrays += [turned, right]
 
     def kernel(*refs):
-        weight_kernel(send, len(operands), *refs)
+        piece_kernel(len(operands), *refs)
 
     return pl.pallas_call(
         kernel,
-        grid_spec=pltpu.PrefetchScalarGridSpec(
-            num_scalar_prefetch=1,
-            grid=(4,),
-            in_specs=specs,
-            out_specs=[
-                pl.BlockSpec((1, line, wide), lambda i, s: (first(i), 0, 0)),
-                pl.BlockSpec((1, line, wide), lambda i, s: (jnp.maximum(i - 2, 0), 0, 0)),
-            ],
-            scratch_shapes=scratch,
-        ),
+        grid=(4,),
+        in_specs=specs,
+        out_specs=[
+            pl.BlockSpec((1, line, wide), lambda i: (first(i), 0, 0)),
+            pl.BlockSpec((1, line, wide), lambda i: (jnp.maximum(i - 2, 0), 0, 0)),
+        ],
         out_shape=[jax.ShapeDtypeStruct((2, line, wide), LOW)] * 2,
         compiler_params=pltpu.CompilerParams(vmem_limit_bytes=VMEM_ROOM),
-        cost_estimate=pl.CostEstimate(
-            flops=16 * rows * line * wide,
-            transcendentals=0,
-            bytes_accessed=rows * wide * 16 + rows * line * 16 + line * wide * 8,
-        ),
-    )(places, *arrays)
+        cost_estimate=weight_cost(operands),
+    )(*arrays)
 
 
 def lane_of(shape):
@@ -867,10 +877,6 @@
     )(qkv, bias, grad, mixed, total, *given)
 
 
-def mat(left, right):
-    return jnp.dot(left, right, preferred_element_type=jnp.float32)
-
-
 def flat_norm(values, gain, shift):
     center = values - jnp.mean(values, axis=-1, keepdims=True)
     spread = lax.rsqrt(jnp.mean(center * center, axis=-1, keepdims=True) + EPS)
@@ -947,13 +953,11 @@
     feed_send = jnp.concatenate(columns_of(feeds, 1 - core), 1)
     feed = pick_two(core, feed_keep, exchange(feed_send, far_core=1), 0)
     groups = [[place for place in range(32) if (place // 2) % 2 == at] for at in range(2)]
+
     gathered = lax.all_gather(
-        feed.reshape(2 * depth, -1),
-        BOTH,
-        axis=0,
-        tiled=True,
-        axis_index_groups=groups,
+        feed.reshape(2 * depth, -1), BOTH, axis=0, tiled=True, axis_index_groups=groups
     ).reshape(8, 2, 2 * depth, -1)
+    gathered = pltpu.with_memory_space_constraint(gathered, pltpu.HBM)
 
     heads = [query_weight, key_weight, value_weight, output_weight.T]
     piece_one = gather_piece(core_parts(heads, core), core_parts(heads, 1 - core), core)
@@ -968,10 +972,11 @@
         return mine, exchange(after(theirs, *waits), far_y=1)
 
     image_mine, image_far = own_and_far(images, piece_one)
+    grad_mine, grad_far = own_and_far(cotangent, piece_one)
     line_one = gather_line(piece_one, others_one, places)
     cross_one = exchange(line_one[0], far_x=1), exchange(line_one[1], far_y=1)
     pair_one = gather_pairs(places, *line_one, *cross_one)
-    image_far = after(image_far, *pair_one)
+    image_far, grad_far = after((image_far, grad_far), *pair_one)
     whole = jnp.concatenate([image_mine, image_far], 0)
 
     def head_columns(vector):
@@ -1019,20 +1024,20 @@
     normed, unit_one, spread_one = flat_norm(resid, gain_one, shift_one)
     normed_pair = pair_of(normed.astype(LOW))
 
+    normed_turned = turn(places, normed_pair)
+    grad_top = row_mask * jnp.concatenate([grad_mine, grad_far], 0).astype(jnp.float32)
+    fed_grad = grad_top.astype(LOW)
+    fed_pair = pair_of(fed_grad)
+    fed_turned = turn(places, fed_pair)
     last_one = exchange(pair_one[0], far_y=1), exchange(pair_one[1], far_x=1)
-    qkv_full, output_full = gather_all(after(places, *normed_pair), *pair_one, *last_one, 3 * head_cols // 4)
-
-    grad_mine, grad_far = own_and_far(cotangent, qkv_full)
+    qkv_full, output_full = gather_all(after(places, normed_turned, fed_turned), *pair_one, *last_one, 3 * head_cols // 4)
+
     normed_rows = jnp.concatenate(normed_pair, 0)
     qkv = (mat(normed_rows, qkv_full) + qkv_shift).astype(LOW)
     mixed_half = attend_image(1, qkv, key_bias, [])
     mixed_far = mat_far(mixed_half[0][rows:], output_full).astype(LOW)
     mixed_sum = exchange(mixed_far, far_core=1)
     mixed, totals = attend_image(0, qkv, key_bias, list(after(tuple(mixed_half), mixed_far)))
-    grad_far = after(grad_far, mixed)
-    grad_top = row_mask * jnp.concatenate([grad_mine, grad_far], 0).astype(jnp.float32)
-    fed_grad = grad_top.astype(LOW)
-    fed_pair = pair_of(fed_grad)
     attended = mat_far(mixed[:rows], output_full) + mixed_sum.astype(jnp.float32)
     attended = attended + output_bias.astype(jnp.float32)
     middle = row_mask * (resid + attended)
@@ -1040,15 +1045,15 @@
     second_pair = pair_of(second.astype(LOW))
     active, slope = up_call(places, second_pair, gathered, up_shift)
 
-    lower_sends = weight_pieces(places, [(fed_pair, active)], True)
+    lower_sends = weight_pieces([(fed_turned, active)], True)
     lower_first = scatter_first(lower_sends)
-    fed_late = after(fed_pair, *lower_sends)
+    lower_keeps = weight_pieces([(fed_turned, after(active, *lower_sends))], False)
+    fed_late = after(fed_pair, *lower_keeps)
     hidden_grad, up_bias_sums = hidden_call(places, fed_late, gathered, slope)
-    up_sends = weight_pieces(places, [(second_pair, hidden_grad)], True)
+    second_turned = turn(places, second_pair)
+    up_sends = weight_pieces([(second_turned, hidden_grad)], True)
     up_first = scatter_first(up_sends)
-    active_late = after(active, *up_sends)
-    lower_keeps = weight_pieces(places, [(fed_pair, active_late)], False)
-    lower_first = after(lower_first, *lower_keeps)
+    lower_first = after(lower_first, *up_sends)
     lower_second = scatter_second(lower_keeps, lower_first)
     hidden_late = after(hidden_grad, *lower_first)
     second_grad = down_call(places, hidden_late, gathered, 0)
@@ -1058,8 +1063,9 @@
     middle_grad = row_mask * (grad_top + middle_back)
     attended_grad = middle_grad.astype(LOW)
     attended_pair = pair_of(attended_grad)
-    up_keeps = weight_pieces(places, [(second_pair, after(hidden_late, attended_grad))], False)
-    lower_second = after(lower_second, *up_keeps)
+    up_keeps = weight_pieces([(second_turned, after(hidden_late, attended_grad))], False)
+    attended_turned = turn(places, attended_pair)
+    lower_second = after(lower_second, *up_keeps, attended_turned)
     lower_line = scatter_line(lower_keeps, lower_first, lower_second)
     lower_z = scatter_z(lower_line)
     up_first = after(up_first, *up_keeps)
@@ -1068,26 +1074,23 @@
     grad_mixed = after(tuple(grad_mixed), *up_first, *lower_line)
     back = attend_back_image(0, qkv, key_bias, grad_mixed[0], mixed, totals, [])
     lower_z = after(tuple(lower_z), back)
-    lower_owned = full_columns(scatter_last(lower_line[0], lower_z, core))
     up_line = scatter_line(up_keeps, up_first, after(up_second, back))
     up_z = scatter_z(up_line)
     back = after(back, *up_line)
     back = attend_back_image(1, qkv, key_bias, grad_mixed[1], mixed, totals, [back])
     up_z = after(tuple(up_z), back)
     back = after(back, *up_z)
-    upper_owned = full_columns(scatter_last(up_line[0], up_z, core))
-    operands = [(normed_pair, back), (attended_pair, mixed)]
-    last_sends = weight_pieces(places, operands, True)
+    last_sends = weight_pieces([(normed_turned, back), (attended_turned, mixed)], True)
     last_first = scatter_first(last_sends)
     back_late = after(back, *last_sends)
     normed_far = exchange(mat_far(back_late[rows:], qkv_full).astype(LOW), far_core=1)
+    last_keeps = weight_pieces([(normed_turned, back_late), (attended_turned, mixed)], False)
     normed_grad = mat_far(back_late[:rows], qkv_full) + normed_far.astype(jnp.float32)
-    last_keeps = weight_pieces(places, operands, False)
     first_back, gain_one_grad, shift_one_grad = flat_norm_back(
         normed_grad, unit_one, spread_one, gain_one
     )
     images_own = middle_grad + first_back
-    qkv_sums = column_flat(back).reshape(4, 3, -1)
+    qkv_sums = column_flat(back_late).reshape(4, 3, -1)
     vector = jnp.concatenate(
         [
             column_flat(attended_grad),
@@ -1101,22 +1104,31 @@
             head_spread(qkv_sums[:, 2].reshape(-1)),
         ]
     )
-    last_first = after(last_first, last_keeps)
+    vector, vectors = vector_first(vector)
+    last_first = after(last_first, *last_keeps, images_own, *vectors)
     last_second = scatter_second(last_keeps, last_first)
-    vector, vectors = vector_first(vector)
-    last_line = scatter_line(last_keeps, last_first, after(last_second, images_own, *vectors))
+    vector = vector + vectors[0] + vectors[1] + vectors[2]
+    vector_y = exchange(vector, far_y=1)
+    fed = down_call(places, after(active, *last_first), gathered, 1)
+    vector = vector + after(vector_y, fed)
+    vector_x = exchange(vector, far_x=1)
+    layer_own = (row_mask * (middle + fed + down_bias.astype(jnp.float32))).astype(LOW)
+    last_line = scatter_line(last_keeps, last_first, after(last_second, layer_own))
     last_z = scatter_z(last_line)
-    fed = down_call(places, after(active, last_keeps), gathered, 1)
-    layer_own = (row_mask * (middle + fed + down_bias.astype(jnp.float32))).astype(LOW)
-    vector = vector_last(vector, vectors)
-    last_z = after(tuple(last_z), vector)
+    vector = vector + after(vector_x, *last_line)
+    lower_z, up_z = after((tuple(lower_z), tuple(up_z)), *last_line)
+    lower_owned = full_columns(scatter_last(lower_line[0], lower_z, core)).T
+    upper_owned = full_columns(scatter_last(up_line[0], up_z, core))
+    layer_late, images_late = after((layer_own, images_own), *last_line)
+
+    def to_strips(own, send):
+        far = exchange(send, far_y=1).astype(own.dtype)
+        return pick_two(place_y, own[:strip], far, 1).transpose(1, 0, 2)
+
+    layer_out = to_strips(layer_late, layer_late[half : half + strip])
+    images_grad = to_strips(images_late, images_late[half : half + strip].astype(LOW))
+    last_z = after(tuple(last_z), vector, layer_out, images_grad, lower_owned, upper_owned)
     last_owned = scatter_last(last_line[0], last_z, core)
-
-    def to_strips(own, send):
-        return pick_two(place_y, own[:strip], exchange(send, far_y=1).astype(own.dtype), 0)
-
-    layer_out = to_strips(layer_own, layer_own[half : half + strip])
-    images_grad = to_strips(images_own, images_own[half : half + strip].astype(LOW))
     def head_grad(at):
         return full_columns(last_owned[..., at * LANES : (at + 1) * LANES])
 
@@ -1137,7 +1149,7 @@
         early[2 * width : 3 * width],
         upper_owned,
         early[4 * width :],
-        lower_owned.T,
+        lower_owned,
         early[3 * width : 4 * width],
     )
 

time: 466 us -> 425 us (0.912)
  Pallas kernels: 171 us -> 132 us
  waiting for transfers between devices: 115 us -> 128 us
  local copies, waits for them, and re-layouts: 26.8 us -> 39.4 us
  matrix products: 27.1 us -> 18.1 us
  starting transfers between devices: 63.4 us -> 54.9 us
  other arithmetic: 37.8 us -> 31.6 us
    pallas_call x6 -> x10, Pallas kernels: 56.7 us -> 39.3 us  [the longest x6 28 us: weight_pieces(): pl.pallas_call(kernel, grid=(4,), in_specs=specs, out_specs=[pl.BlockSpec...]
    unnamed x149 -> x211, local copies, waits for them, and re-layouts: 9.63 us -> 22.3 us
    ppermute x51, waiting for transfers between devices: 103 us -> 115 us  [exchange(): return lax.ppermute(value, BOTH, pairs)]
    ppermute x51, starting transfers between devices: 63.4 us -> 54.8 us  [exchange(): return lax.ppermute(value, BOTH, pairs)]
    dot_general x4, matrix products: 15.8 us -> 10.1 us  [mat_far(): lax.dot_general(left, right, (((1,), (1,)), ((), ())), preferred_element_...]
    pallas_call x3, Pallas kernels: 9.01 us -> 3.5 us  [scatter_line(): pl.pallas_call(line_kernel, grid=(1,), in_specs=[first, first, flat, firs...]
  transfers between devices with their start and end apart: 52 -> 52, of which waited for: 22 -> 22; matrix products, arithmetic and copies ran while one was open for 17% -> 15% of each run, Pallas kernels for 31% -> 22%
where the time goes in v5:
time: 425 us; the launch traced here: 420 us
  Pallas kernels  132 us (31%)
  waiting for transfers between devices  128 us (30%)
  starting transfers between devices  54.9 us (13%)
  local copies, waits for them, and re-layouts  39.4 us (9%)
  other arithmetic  31.6 us (7%)
  matrix products  18.1 us (4%)
  between operations  17 us (4%)
    ppermute x51, waiting for transfers between devices, exchange(): return lax.ppermute(value, BOTH, pairs)  115 us
    ppermute x51, starting transfers between devices, exchange(): return lax.ppermute(value, BOTH, pairs)  54.8 us
    pallas_call x2, Pallas kernels, attend_back_image(): pl.pallas_call(kernel, grid=(blocks,), in_specs=[pl.BlockSpec((rows, 3 *...  29.4 us
    pallas_call x6, Pallas kernels, weight_pieces(): pl.pallas_call(kernel, grid=(4,), in_specs=specs, out_specs=[pl.BlockSpec...  28 us
    unnamed x211, local copies, waits for them, and re-layouts  22.3 us
    pallas_call x2, Pallas kernels, down_call(): pl.pallas_call(down_kernel, grid_spec=pltpu.PrefetchScalarGridSpec(num_sc...  17.2 us
    pallas_call x2, Pallas kernels, attend_image(): pl.pallas_call(kernel, grid=(blocks,), in_specs=[pl.BlockSpec((rows, 3 *...  15.4 us
    pallas_call x1, Pallas kernels, up_call(): pl.pallas_call(up_kernel, grid_spec=pltpu.PrefetchScalarGridSpec(num_scal...  12.3 us
  transfers between devices with their start and end apart: 52, of which 22 were waited for; matrix products, arithmetic and copies ran while one was open for 15% of the time, Pallas kernels for 22%

profile of v5, /device:TPU:0, one launch (start us, length us, event | category | flops | bytes accessed | tf_op | source)
XLA Modules:
  0.0 420.2 jit_solution(2314498432496881295)
XLA Ops:
  13.9 3.0 collective-permute-start.3
  16.9 2.6 collective-permute-start.4
  20.4 2.9 copy.70
  24.7 1.8 collective-permute-start.2
  26.9 3.8 collective-permute-done.3.refs_1_
  30.6 7.1 %collective-permute-done.4.refs_2_ = bf16[2,128,512]{2,1,0:T(8,128)(2,1)S(1)} collective-permute-done((bf16[2,128,512]{2,1,0:T(8,128)(2,1)S(1)}, bf16[2,128,512]{2,1,0:T(8,128)(2,1)S(1)}, u32[]{:S(2)}, u32[]{:S(2)}) %collective-permute-start.4) | collective-permute-done | bytes 262176 | tf_op jit(solution)/shard_map/ppermute | solution.py:303
  37.8 5.3 %collective-permute-done.5.refs_3_ = bf16[2,128,512]{2,1,0:T(8,128)(2,1)S(1)} collective-permute-done((bf16[2,128,512]{2,1,0:T(8,128)(2,1)S(1)}, bf16[2,128,512]{2,1,0:T(8,128)(2,1)S(1)}, u32[]{:S(2)}, u32[]{:S(2)}) %collective-permute-start.5) | collective-permute-done | bytes 262176 | tf_op jit(solution)/shard_map/ppermute | solution.py:303
  48.1 8.4 %collective-permute-done.6.refs_1_ = bf16[4,128,512]{2,1,0:T(8,128)(2,1)S(1)} collective-permute-done((bf16[4,128,512]{2,1,0:T(8,128)(2,1)S(1)}, bf16[4,128,512]{2,1,0:T(8,128)(2,1)S(1)}, u32[]{:S(2)}, u32[]{:S(2)}) %collective-permute-start.6) | collective-permute-done | bytes 524320 | tf_op jit(solution)/shard_map/ppermute | solution.py:303
  56.4 17.8 %collective-permute-done.7.refs_3_ = bf16[4,128,512]{2,1,0:T(8,128)(2,1)S(1)} collective-permute-done((bf16[4,128,512]{2,1,0:T(8,128)(2,1)S(1)}, bf16[4,128,512]{2,1,0:T(8,128)(2,1)S(1)}, u32[]{:S(2)}, u32[]{:S(2)}) %collective-permute-start.7) | collective-permute-done | bytes 524320 | tf_op jit(solution)/shard_map/ppermute | solution.py:303
  74.2 2.0 shard_map.306
  78.8 1.7 collective-permute-start.11
  80.8 3.4 shard_map.308.refs_0_
  84.3 2.2 copy-done.10
  86.5 2.9 shard_map.307.refs_0_
  89.5 19.8 %collective-permute-done.10.refs_1_ = bf16[2,4,128,512]{3,2,1,0:T(8,128)(2,1)} collective-permute-done((bf16[2,4,128,512]{3,2,1,0:T(8,128)(2,1)}, bf16[2,4,128,512]{3,2,1,0:T(8,128)(2,1)}, u32[]{:S(2)}, u32[]{:S(2)}) %collective-permute-start.10) | collective-permute-done | bytes 1048608 | tf_op jit(solution)/shard_map/ppermute | solution.py:303
  110.2 2.6 shard_map.309
  112.9 6.4 %fusion.refs_0_ = bf16[1184,1536]{1,0:T(8,128)(2,1)S(1)} fusion(bf16[1024,1536]{1,0:T(8,128)(2,1)S(1)} %bitcast.183, f32[1536]{0:T(1024)S(1)} %add.250, bf16[592,1024]{1,0:T(8,128)(2,1)} %collective-permute-done.8.far_ref, bf16[592,1024]{1,0:T(8,128)(2,1)S(1)} %copy-done.11), kind=kOutput, calls=%fused_computation.1 | convolution fusion | flops 3733028864 | bytes 9213952 | tf_op jit(solution)/shard_map/dot_general | solution.py:645
  119.4 7.7 %shard_map.310 = (bf16[1184,512]{1,0:T(8,128)(2,1)S(1)}, f32[8,8,592]{2,1,0:T(8,128)S(1)}) custom-call(bf16[1184,1536]{1,0:T(8,128)(2,1)S(1)} %fusion.refs_0_, bf16[592,128]{1,0:T(8,128)(2,1)S(1)} %broadcast_in_dim.56.refs_1_), custom_call_target="tpu_custom_call" | custom-call | flops 2871001088 | bytes 2424832 | tf_op jit(solution)/shard_map/pallas_call | solution.py:823
  128.2 7.7 %shard_map.311 = (bf16[1184,512]{1,0:T(8,128)(2,1)S(1)}, f32[8,8,592]{2,1,0:T(8,128)S(1)}) custom-call(bf16[1184,1536]{1,0:T(8,128)(2,1)S(1)} %fusion.refs_0_, bf16[592,128]{1,0:T(8,128)(2,1)S(1)} %broadcast_in_dim.56.refs_1_, bf16[1184,512]{1,0:T(8,128)(2,1)S(1)} %get-tuple-element.121.refs_2_, ...), custom_call_target="tpu_custom_call", output_to_operand_aliasing={{0}: (2, {}), {1}: (3, {})} | custom-call | flops 2871001088 | bytes 2424832 | tf_op jit(solution)/shard_map/pallas_call | solution.py:823
  139.6 2.8 collective-permute-done.13.far_ref
  142.4 12.3 %all-gather.2.cloned.1.call-done = bf16[2048,2048]{1,0:T(8,128)(2,1)} async-done(((bf16[128,2048]{1,0:T(8,128)(2,1)}), bf16[2048,2048]{1,0:T(8,128)(2,1)}) %all-gather.2.cloned.1.call-update) | async-done | bytes 8388624 | tf_op jit(solution)/shard_map/all_gather | solution.py:957
  154.8 12.3 %shard_map.312 = (bf16[1184,2048]{1,0:T(8,128)(2,1)S(1)}, bf16[1184,2048]{1,0:T(8,128)(2,1)S(1)}) custom-call(s32[4]{0:T(128)S(1)} %pad_add_fusion.places_ref, bf16[592,1024]{1,0:T(8,128)(2,1)} %add_convert_fusion.own_ref, bf16[592,1024]{1,0:T(8,128)(2,1)} %collective-permute-done.13.far_ref, bf16[8,2,128,2048]{3,2,1,0:T(8,128)(2,1)} %bitcast.216, ...), custom_call_target="tpu_custom_call" | custom-call | flops 4966055936 | bytes 16318464 | tf_op jit(solution)/shard_map/pallas_call | solution.py:536
  167.1 4.1 shard_map.313
  174.3 3.3 shard_map.316.refs_0_
  177.7 3.9 shard_map.314
  183.6 9.4 %shard_map.315 = (bf16[1184,2048]{1,0:T(8,128)(2,1)S(1)}, f32[1,2048]{1,0:T(1,128)S(1)}) custom-call(s32[4]{0:T(128)S(1)} %pad_add_fusion.places_ref, bf16[592,1024]{1,0:T(8,128)(2,1)S(1)} %copy-done.8, bf16[592,1024]{1,0:T(8,128)(2,1)} %collective-permute-done.9.far_ref, bf16[8,2,128,2048]{3,2,1,0:T(8,128)(2,1)} %bitcast.217, ...), custom_call_target="tpu_custom_call" | custom-call | flops 4966055936 | bytes 16318464 | tf_op jit(solution)/shard_map/pallas_call | solution.py:576
  193.0 3.9 shard_map.317
  198.9 8.6 %shard_map.318 = (f32[592,1024]{1,0:T(8,128)S(1)}, bf16[592,1024]{1,0:T(8,128)(2,1)}) custom-call(s32[4]{0:T(128)S(1)} %pad_add_fusion.places_ref, bf16[1184,2048]{1,0:T(8,128)(2,1)S(1)} %get-tuple-element.141.refs_1_.left_ref, bf16[8,2,128,2048]{3,2,1,0:T(8,128)(2,1)} %bitcast.218), custom_call_target="tpu_custom_call" | custom-call | flops 4966055936 | bytes 12681216 | tf_op jit(solution)/shard_map/pallas_call | solution.py:619
  217.4 3.3 multiply_reduce_fusion
  220.8 4.2 %convert_reduce_fusion.3 = (f32[1024]{0:T(1024)S(1)}, bf16[592,1024]{1,0:T(8,128)(2,1)S(1)}, f32[592,1024]{1,0:T(8,128)}) fusion(f32[592]{0:T(1024)S(1)} %broadcast_multiply_fusion.2, f32[592,1024]{1,0:T(8,128)S(1)} %copy-done.47, f32[592]{0:T(1024)S(1)} %broadcast_multiply_fusion.4, f32[592]{0:T(1024)S(1)} %broadcast_multiply_fusion.3, ...), kind=kLoop, calls=%fused_computation.29 | loop fusion | flops 11516928 | bytes 10931776 | tf_op jit(solution)/shard_map/reduce_sum | solution.py:898
  225.0 3.9 shard_map.319
  229.0 6.3 %collective-permute-done.19.one_a = bf16[2,512,512]{2,1,0:T(8,128)(2,1)} collective-permute-done((bf16[2,512,512]{2,1,0:T(8,128)(2,1)}, bf16[2,512,512]{2,1,0:T(8,128)(2,1)}, u32[]{:S(2)}, u32[]{:S(2)}) %collective-permute-start.19) | collective-permute-done | bytes 1048608 | tf_op jit(solution)/shard_map/ppermute | solution.py:303
  236.9 1.6 collective-permute-start.24
  241.3 1.7 shard_map.320.refs_2_
  242.9 3.4 collective-permute-done.22.two_b
  247.4 2.7 collective-permute-start.46
  250.1 1.6 collective-permute-start.47
  252.6 14.9 %shard_map.322.refs_5_ = bf16[1184,1536]{1,0:T(8,128)(2,1)S(1)} custom-call(bf16[1184,1536]{1,0:T(8,128)(2,1)S(1)} %copy-done.45, bf16[592,128]{1,0:T(8,128)(2,1)S(1)} %broadcast_in_dim.56.refs_1_, bf16[592,512]{1,0:T(8,128)(2,1)S(1)} %convolution_convert_fusion.2.refs_2_, bf16[1184,512]{1,0:T(8,128)(2,1)S(1)} %copy-done.13, ...), custom_call_target="tpu_custom_call" | custom-call | flops 7177502720 | bytes 4849664 | tf_op jit(solution)/shard_map/pallas_call | solution.py:857
  269.2 2.7 collective-permute-start.26
  271.9 1.6 collective-permute-start.27
  273.6 14.5 %shard_map.324.refs_1_ = bf16[1184,1536]{1,0:T(8,128)(2,1)S(1)} custom-call(bf16[1184,1536]{1,0:T(8,128)(2,1)S(1)} %copy-done.45, bf16[592,128]{1,0:T(8,128)(2,1)S(1)} %broadcast_in_dim.56.refs_1_, bf16[592,512]{1,0:T(8,128)(2,1)S(1)} %convolution_convert_fusion.1.refs_2_, bf16[1184,512]{1,0:T(8,128)(2,1)S(1)} %copy-done.13, ...), custom_call_target="tpu_custom_call", output_to_operand_aliasing={{}: (5, {})} | custom-call | flops 7177502720 | bytes 4849664 | tf_op jit(solution)/shard_map/pallas_call | solution.py:857
  288.1 2.5 collective-permute-done.26
  290.6 6.5 %shard_map.325 = (bf16[2,512,512]{2,1,0:T(8,128)(2,1)}, bf16[2,512,512]{2,1,0:T(8,128)(2,1)}) custom-call(bf16[2,512,1184]{2,1,0:T(8,128)(2,1)S(1)} %shard_map.307.refs_0_, bf16[1184,1536]{1,0:T(8,128)(2,1)S(1)} %shard_map.324.refs_1_, bf16[2,512,1184]{2,1,0:T(8,128)(2,1)S(1)} %shard_map.320.refs_2_, bf16[1184,512]{1,0:T(8,128)(2,1)S(1)} %copy-done.13), custom_call_target="tpu_custom_call" | custom-call | flops 2483027968 | bytes 11796480 | tf_op jit(solution)/shard_map/pallas_call | solution.py:724
  297.2 3.1 fusion.26
  303.0 2.0 copy-done.1
  305.1 1.7 copy-done.4
  308.1 5.6 %shard_map.326 = (bf16[2,512,512]{2,1,0:T(8,128)(2,1)S(1)}, bf16[2,512,512]{2,1,0:T(8,128)(2,1)S(1)}) custom-call(bf16[2,512,1184]{2,1,0:T(8,128)(2,1)S(1)} %shard_map.307.refs_0_, bf16[1184,1536]{1,0:T(8,128)(2,1)S(1)} %copy-done.1, bf16[2,512,1184]{2,1,0:T(8,128)(2,1)S(1)} %copy-done.4, bf16[1184,512]{1,0:T(8,128)(2,1)S(1)} %copy-done.14), custom_call_target="tpu_custom_call" | custom-call | flops 2483027968 | bytes 11796480 | tf_op jit(solution)/shard_map/pallas_call | solution.py:724
  313.8 5.0 %fusion.13 = (f32[1024]{0:T(1024)S(1)}, f32[592]{0:T(1024)S(1)}, f32[592]{0:T(1024)S(1)}, f32[1024]{0:T(1024)S(1)}, f32[592,1024]{1,0:T(8,128)S(1)}) fusion(f32[592]{0:T(1024)S(1)} %add_rsqrt_fusion.1, f32[592]{0:T(1024)S(1)} %broadcast_multiply_fusion.5, bf16[296,1024]{1,0:T(8,128)(2,1)} %copy-done.53, bf16[296,1024]{1,0:T(8,128)(2,1)S(1)} %copy-done.51, ...), kind=kOutput, calls=%fused_computation.18 | convolution fusion | flops 1871360768 | bytes 9839232 | tf_op jit(solution)/shard_map/dot_general | solution.py:491
  320.2 4.8 %collective-permute-start.32 = (f32[12288]{0:T(1024)S(1)}, f32[12288]{0:T(1024)S(1)}, u32[]{:S(2)}, u32[]{:S(2)}) collective-permute-start(f32[12288]{0:T(1024)S(1)} %add.270), channel_id=1, source_target_pairs={{0,8},{1,9},{2,10},{3,11},{4,12},{5,13},{6,14},{7,15},{8,0},{9,1},... | collective-permute-start | bytes 147464 | tf_op jit(solution)/shard_map/ppermute | solution.py:303
  325.3 2.2 collective-permute-start.34
  327.5 2.4 fusion.12
  329.9 2.0 collective-permute-done.33
  332.5 8.5 %shard_map.327 = (f32[592,1024]{1,0:T(8,128)S(1)}, bf16[592,1024]{1,0:T(8,128)(2,1)}) custom-call(s32[4]{0:T(128)S(1)} %pad_add_fusion.places_ref, bf16[1184,2048]{1,0:T(8,128)(2,1)S(1)} %bitcast.191, bf16[8,2,128,2048]{3,2,1,0:T(8,128)(2,1)} %bitcast.219), custom_call_target="tpu_custom_call" | custom-call | flops 4966055936 | bytes 12681216 | tf_op jit(solution)/shard_map/pallas_call | solution.py:619
  344.4 1.6 collective-permute-start.36
  347.5 1.8 multiply_convert_fusion
  349.4 8.0 %collective-permute-done.37.two_b = bf16[512,512]{1,0:T(8,128)(2,1)S(1)} collective-permute-done((bf16[512,512]{1,0:T(8,128)(2,1)S(1)}, bf16[512,512]{1,0:T(8,128)(2,1)S(1)}, u32[]{:S(2)}, u32[]{:S(2)}) %collective-permute-start.37) | collective-permute-done | bytes 524320 | tf_op jit(solution)/shard_map/ppermute | solution.py:303
  362.7 1.9 collective-permute-start.44
  365.8 1.6 collective-permute-start.41
  367.7 2.2 slice.291
  377.1 11.2 %collective-permute-done.39 = bf16[289,1024]{1,0:T(8,128)(2,1)} collective-permute-done((bf16[289,1024]{1,0:T(8,128)(2,1)}, bf16[289,1024]{1,0:T(8,128)(2,1)}, u32[]{:S(2)}, u32[]{:S(2)}) %collective-permute-start.39) | collective-permute-done | bytes 591904 | tf_op jit(solution)/shard_map/ppermute | solution.py:303
  388.4 1.8 fusion.29
  390.1 10.6 %collective-permute-done.38 = bf16[289,1024]{1,0:T(8,128)(2,1)} collective-permute-done((bf16[289,1024]{1,0:T(8,128)(2,1)}, bf16[289,1024]{1,0:T(8,128)(2,1)}, u32[]{:S(2)}, u32[]{:S(2)}) %collective-permute-start.38) | collective-permute-done | bytes 591904 | tf_op jit(solution)/shard_map/ppermute | solution.py:303
  404.1 3.2 copy.93
  407.4 2.2 copy.92
  (407 shorter events, 78.2 us)
Async XLA Ops:
  7.2 147.5 %all-gather.2.cloned.1.call-start = ((), (), s32[]{:S(2)}) async-start(), calls=%async_computation | async-start | bytes 8912896 | tf_op jit(solution)/shard_map/all_gather | solution.py:957
  9.5 1.7 collective-permute-start.14
  12.3 1.4 collective-permute-start
  13.9 16.8 %collective-permute-start.3 = (bf16[2,128,512]{2,1,0:T(8,128)(2,1)S(1)}, bf16[2,128,512]{2,1,0:T(8,128)(2,1)S(1)}, u32[]{:S(2)}, u32[]{:S(2)}) collective-permute-start(bf16[2,128,512]{2,1,0:T(8,128)(2,1)S(1)} %bitcast.179), channel_id=1, source_target_pairs={{0,8},{1,9},{2,10},{3,11},{4,12},{5,13},{6,14},{7,15},{8,0},{9,1},... | collective-permute-start | bytes 786440 | tf_op jit(solution)/shard_map/ppermute | solution.py:303
  16.9 20.9 %collective-permute-start.4 = (bf16[2,128,512]{2,1,0:T(8,128)(2,1)S(1)}, bf16[2,128,512]{2,1,0:T(8,128)(2,1)S(1)}, u32[]{:S(2)}, u32[]{:S(2)}) collective-permute-start(bf16[2,128,512]{2,1,0:T(8,128)(2,1)S(1)} %bitcast.180), channel_id=1, source_target_pairs={{0,16},{1,17},{2,18},{3,19},{4,20},{5,21},{6,22},{7,23},{8,24},{9,... | collective-permute-start | bytes 786440 | tf_op jit(solution)/shard_map/ppermute | solution.py:303
  19.4 23.6 %collective-permute-start.5 = (bf16[2,128,512]{2,1,0:T(8,128)(2,1)S(1)}, bf16[2,128,512]{2,1,0:T(8,128)(2,1)S(1)}, u32[]{:S(2)}, u32[]{:S(2)}) collective-permute-start(bf16[2,128,512]{2,1,0:T(8,128)(2,1)S(1)} %bitcast.181), channel_id=1, source_target_pairs={{0,24},{1,25},{2,26},{3,27},{4,28},{5,29},{6,30},{7,31},{8,16},{9,... | collective-permute-start | bytes 786440 | tf_op jit(solution)/shard_map/ppermute | solution.py:303
  20.4 55.9 %copy-start.56 = (bf16[296,1024]{1,0:T(8,128)(2,1)}, bf16[296,1024]{1,0:T(8,128)(2,1)S(1)}, u32[]{:S(2)}) copy-start(bf16[296,1024]{1,0:T(8,128)(2,1)S(1)} %get-tuple-element.269) | copy-start | bytes 1818628
  20.4 26.4 %copy-start.94 = (s32[2]{0:T(128)S(1)}, s32[2]{0:T(128)}, u32[]{:S(2)}) copy-start(s32[2]{0:T(128)} %param.20) | copy-start | bytes 28
  20.4 27.6 %copy-start.86 = (bf16[1024]{0:T(1024)(128)(2,1)S(1)}, bf16[1024]{0:T(1024)(128)(2,1)}, u32[]{:S(2)}) copy-start(bf16[1024]{0:T(1024)(128)(2,1)} %param.21) | copy-start | bytes 6148
  20.4 27.7 %copy-start.87 = (bf16[1024]{0:T(1024)(128)(2,1)S(1)}, bf16[1024]{0:T(1024)(128)(2,1)}, u32[]{:S(2)}) copy-start(bf16[1024]{0:T(1024)(128)(2,1)} %param.22) | copy-start | bytes 6148
  24.7 52.8 %copy-start.49 = (bf16[296,1024]{1,0:T(8,128)(2,1)}, bf16[296,1024]{1,0:T(8,128)(2,1)S(1)}, u32[]{:S(2)}) copy-start(bf16[296,1024]{1,0:T(8,128)(2,1)S(1)} %get-tuple-element.271) | copy-start | bytes 1818628
  24.7 51.6 %collective-permute-start.2 = (bf16[296,1024]{1,0:T(8,128)(2,1)}, bf16[296,1024]{1,0:T(8,128)(2,1)S(1)}, u32[]{:S(2)}, u32[]{:S(2)}) collective-permute-start(bf16[296,1024]{1,0:T(8,128)(2,1)} %get-tuple-element.109), channel_id=1, source_target_pairs={{0,1},{1,0},{2,3},{3,2},{4,5},{5,4},{6,7},{7,6},{8,9},{9,8},{10,11... | collective-permute-start | bytes 1818632 | tf_op jit(solution)/shard_map/ppermute | solution.py:303
  26.5 49.7 %collective-permute-start.1 = (bf16[296,1024]{1,0:T(8,128)(2,1)S(1)}, bf16[296,1024]{1,0:T(8,128)(2,1)S(1)}, u32[]{:S(2)}, u32[]{:S(2)}) collective-permute-start(bf16[296,1024]{1,0:T(8,128)(2,1)S(1)} %get-tuple-element.108), channel_id=1, source_target_pairs={{0,1},{1,0},{2,3},{3,2},{4,5},{5,4},{6,7},{7,6},{8,9},{9,8},{10,11... | collective-permute-start | bytes 1818632 | tf_op jit(solution)/shard_map/ppermute | solution.py:303
  43.7 12.7 %collective-permute-start.6 = (bf16[4,128,512]{2,1,0:T(8,128)(2,1)S(1)}, bf16[4,128,512]{2,1,0:T(8,128)(2,1)S(1)}, u32[]{:S(2)}, u32[]{:S(2)}) collective-permute-start(bf16[4,128,512]{2,1,0:T(8,128)(2,1)S(1)} %get-tuple-element.110.refs_0_), channel_id=1, source_target_pairs={{0,4},{1,5},{2,6},{3,7},{4,0},{5,1},{6,2},{7,3},{8,12},{9,13},{10,... | collective-permute-start | bytes 1572872 | tf_op jit(solution)/shard_map/ppermute | solution.py:303
  45.3 29.0 %collective-permute-start.7 = (bf16[4,128,512]{2,1,0:T(8,128)(2,1)S(1)}, bf16[4,128,512]{2,1,0:T(8,128)(2,1)S(1)}, u32[]{:S(2)}, u32[]{:S(2)}) collective-permute-start(bf16[4,128,512]{2,1,0:T(8,128)(2,1)S(1)} %get-tuple-element.111.refs_2_), channel_id=1, source_target_pairs={{0,1},{1,0},{2,3},{3,2},{4,5},{5,4},{6,7},{7,6},{8,9},{9,8},{10,11... | collective-permute-start | bytes 1572872 | tf_op jit(solution)/shard_map/ppermute | solution.py:303
  76.6 4.2 collective-permute-start.9
  78.0 6.2 %collective-permute-start.8 = (bf16[592,1024]{1,0:T(8,128)(2,1)S(1)}, bf16[592,1024]{1,0:T(8,128)(2,1)}, u32[]{:S(2)}, u32[]{:S(2)}) collective-permute-start(bf16[592,1024]{1,0:T(8,128)(2,1)S(1)} %fusion.8.own_ref), channel_id=1, source_target_pairs={{0,2},{1,3},{2,0},{3,1},{4,6},{5,7},{6,4},{7,5},{8,10},{9,11},{10,... | collective-permute-start | bytes 3637256 | tf_op jit(solution)/shard_map/ppermute | solution.py:303
  78.6 30.7 %collective-permute-start.10 = (bf16[2,4,128,512]{3,2,1,0:T(8,128)(2,1)}, bf16[2,4,128,512]{3,2,1,0:T(8,128)(2,1)}, u32[]{:S(2)}, u32[]{:S(2)}) collective-permute-start(bf16[2,4,128,512]{3,2,1,0:T(8,128)(2,1)} %get-tuple-element.112.refs_0_), channel_id=1, source_target_pairs={{0,1},{1,0},{2,3},{3,2},{4,5},{5,4},{6,7},{7,6},{8,9},{9,8},{10,11... | collective-permute-start | bytes 3145736 | tf_op jit(solution)/shard_map/ppermute | solution.py:303
  78.8 31.4 %collective-permute-start.11 = (bf16[2,4,128,512]{3,2,1,0:T(8,128)(2,1)}, bf16[2,4,128,512]{3,2,1,0:T(8,128)(2,1)}, u32[]{:S(2)}, u32[]{:S(2)}) collective-permute-start(bf16[2,4,128,512]{3,2,1,0:T(8,128)(2,1)} %get-tuple-element.113.refs_2_), channel_id=1, source_target_pairs={{0,4},{1,5},{2,6},{3,7},{4,0},{5,1},{6,2},{7,3},{8,12},{9,13},{10,... | collective-permute-start | bytes 3145736 | tf_op jit(solution)/shard_map/ppermute | solution.py:303
  89.4 23.4 %copy-start.11 = (bf16[592,1024]{1,0:T(8,128)(2,1)S(1)}, bf16[592,1024]{1,0:T(8,128)(2,1)}, u32[]{:S(2)}) copy-start(bf16[592,1024]{1,0:T(8,128)(2,1)} %copy-done.9) | copy-start | bytes 3637252
  112.9 23.1 %copy-start.38 = (bf16[4,2,128,512]{3,2,1,0:T(8,128)(2,1)}, bf16[4,2,128,512]{3,2,1,0:T(8,128)(2,1)S(1)}, u32[]{:S(2)}) copy-start(bf16[4,2,128,512]{3,2,1,0:T(8,128)(2,1)S(1)} %get-tuple-element.120) | copy-start | bytes 3145732
  128.0 7.9 %collective-permute-start.12 = (bf16[592,1024]{1,0:T(8,128)(2,1)S(1)}, bf16[592,1024]{1,0:T(8,128)(2,1)S(1)}, u32[]{:S(2)}, u32[]{:S(2)}) collective-permute-start(bf16[592,1024]{1,0:T(8,128)(2,1)S(1)} %convolution_convert_fusion), channel_id=1, source_target_pairs={{0,2},{1,3},{2,0},{3,1},{4,6},{5,7},{6,4},{7,5},{8,10},{9,11},{10,... | collective-permute-start | bytes 3637256 | tf_op jit(solution)/shard_map/ppermute | solution.py:303
  139.1 3.3 collective-permute-start.13
  171.2 27.7 %collective-permute-start.15 = (bf16[2,512,512]{2,1,0:T(8,128)(2,1)S(1)}, bf16[2,512,512]{2,1,0:T(8,128)(2,1)S(1)}, u32[]{:S(2)}, u32[]{:S(2)}) collective-permute-start(bf16[2,512,512]{2,1,0:T(8,128)(2,1)S(1)} %get-tuple-element.125), channel_id=1, source_target_pairs={{0,1},{1,0},{2,3},{3,2},{4,5},{5,4},{6,7},{7,6},{8,9},{9,8},{10,11... | collective-permute-start | bytes 3145736 | tf_op jit(solution)/shard_map/ppermute | solution.py:303
  172.9 26.1 %collective-permute-start.16 = (bf16[2,512,512]{2,1,0:T(8,128)(2,1)S(1)}, bf16[2,512,512]{2,1,0:T(8,128)(2,1)S(1)}, u32[]{:S(2)}, u32[]{:S(2)}) collective-permute-start(bf16[2,512,512]{2,1,0:T(8,128)(2,1)S(1)} %get-tuple-element.126), channel_id=1, source_target_pairs={{0,4},{1,5},{2,6},{3,7},{4,0},{5,1},{6,2},{7,3},{8,12},{9,13},{10,... | collective-permute-start | bytes 3145736 | tf_op jit(solution)/shard_map/ppermute | solution.py:303
  209.0 8.5 %collective-permute-start.17 = (bf16[592,1024]{1,0:T(8,128)(2,1)}, bf16[592,1024]{1,0:T(8,128)(2,1)}, u32[]{:S(2)}, u32[]{:S(2)}) collective-permute-start(bf16[592,1024]{1,0:T(8,128)(2,1)} %get-tuple-element.140), channel_id=1, source_target_pairs={{0,2},{1,3},{2,0},{3,1},{4,6},{5,7},{6,4},{7,5},{8,10},{9,11},{10,... | collective-permute-start | bytes 3637256 | tf_op jit(solution)/shard_map/ppermute | solution.py:303
  209.0 26.3 %collective-permute-start.19 = (bf16[2,512,512]{2,1,0:T(8,128)(2,1)}, bf16[2,512,512]{2,1,0:T(8,128)(2,1)}, u32[]{:S(2)}, u32[]{:S(2)}) collective-permute-start(bf16[2,512,512]{2,1,0:T(8,128)(2,1)} %copy-done.41), channel_id=1, source_target_pairs={{0,1},{1,0},{2,3},{3,2},{4,5},{5,4},{6,7},{7,6},{8,9},{9,8},{10,11... | collective-permute-start | bytes 3145736 | tf_op jit(solution)/shard_map/ppermute | solution.py:303
  209.4 26.3 %collective-permute-start.20 = (bf16[2,512,512]{2,1,0:T(8,128)(2,1)}, bf16[2,512,512]{2,1,0:T(8,128)(2,1)}, u32[]{:S(2)}, u32[]{:S(2)}) collective-permute-start(bf16[2,512,512]{2,1,0:T(8,128)(2,1)} %copy-done.40), channel_id=1, source_target_pairs={{0,4},{1,5},{2,6},{3,7},{4,0},{5,1},{6,2},{7,3},{8,12},{9,13},{10,... | collective-permute-start | bytes 3145736 | tf_op jit(solution)/shard_map/ppermute | solution.py:303
  212.8 33.6 %collective-permute-start.22 = (bf16[512,512]{1,0:T(8,128)(2,1)S(1)}, bf16[512,512]{1,0:T(8,128)(2,1)S(1)}, u32[]{:S(2)}, u32[]{:S(2)}) collective-permute-start(bf16[512,512]{1,0:T(8,128)(2,1)S(1)} %fusion.38), channel_id=1, source_target_pairs={{0,1},{1,0},{2,3},{3,2},{4,5},{5,4},{6,7},{7,6},{8,9},{9,8},{10,11... | collective-permute-start | bytes 1572872 | tf_op jit(solution)/shard_map/ppermute | solution.py:303
  215.9 31.0 %collective-permute-start.21 = (bf16[512,512]{1,0:T(8,128)(2,1)S(1)}, bf16[512,512]{1,0:T(8,128)(2,1)S(1)}, u32[]{:S(2)}, u32[]{:S(2)}) collective-permute-start(bf16[512,512]{1,0:T(8,128)(2,1)S(1)} %fusion.37), channel_id=1, source_target_pairs={{0,4},{1,5},{2,6},{3,7},{4,0},{5,1},{6,2},{7,3},{8,12},{9,13},{10,... | collective-permute-start | bytes 1572872 | tf_op jit(solution)/shard_map/ppermute | solution.py:303
  225.0 16.2 %collective-permute-start.18 = (bf16[592,1024]{1,0:T(8,128)(2,1)S(1)}, bf16[592,1024]{1,0:T(8,128)(2,1)S(1)}, u32[]{:S(2)}, u32[]{:S(2)}) collective-permute-start(bf16[592,1024]{1,0:T(8,128)(2,1)S(1)} %get-tuple-element.263.own_ref), channel_id=1, source_target_pairs={{0,2},{1,3},{2,0},{3,1},{4,6},{5,7},{6,4},{7,5},{8,10},{9,11},{10,... | collective-permute-start | bytes 3637256 | tf_op jit(solution)/shard_map/ppermute | solution.py:303
  236.9 30.5 %collective-permute-start.24 = (bf16[512,512]{1,0:T(8,128)(2,1)S(1)}, bf16[512,512]{1,0:T(8,128)(2,1)S(1)}, u32[]{:S(2)}, u32[]{:S(2)}) collective-permute-start(bf16[512,512]{1,0:T(8,128)(2,1)S(1)} %fusion.40), channel_id=1, source_target_pairs={{0,1},{1,0},{2,3},{3,2},{4,5},{5,4},{6,7},{7,6},{8,9},{9,8},{10,11... | collective-permute-start | bytes 1572872 | tf_op jit(solution)/shard_map/ppermute | solution.py:303
  239.7 27.7 %collective-permute-start.23 = (bf16[512,512]{1,0:T(8,128)(2,1)S(1)}, bf16[512,512]{1,0:T(8,128)(2,1)S(1)}, u32[]{:S(2)}, u32[]{:S(2)}) collective-permute-start(bf16[512,512]{1,0:T(8,128)(2,1)S(1)} %fusion.39), channel_id=1, source_target_pairs={{0,4},{1,5},{2,6},{3,7},{4,0},{5,1},{6,2},{7,3},{8,12},{9,13},{10,... | collective-permute-start | bytes 1572872 | tf_op jit(solution)/shard_map/ppermute | solution.py:303
  242.9 47.7 %copy-start.3 = (bf16[2,512,1184]{2,1,0:T(8,128)(2,1)}, bf16[2,512,1184]{2,1,0:T(8,128)(2,1)S(1)}, u32[]{:S(2)}) copy-start(bf16[2,512,1184]{2,1,0:T(8,128)(2,1)S(1)} %shard_map.320.refs_2_) | copy-start | bytes 7274500
  247.3 24.6 %collective-permute-start.45 = (bf16[2,128,512]{2,1,0:T(8,128)(2,1)S(1)}, bf16[2,128,512]{2,1,0:T(8,128)(2,1)S(1)}, u32[]{:S(2)}, u32[]{:S(2)}) collective-permute-start(bf16[2,128,512]{2,1,0:T(8,128)(2,1)S(1)} %get-tuple-element.149), channel_id=1, source_target_pairs={{0,8},{1,9},{2,10},{3,11},{4,12},{5,13},{6,14},{7,15},{8,0},{9,1},... | collective-permute-start | bytes 786440 | tf_op jit(solution)/shard_map/ppermute | solution.py:303
  247.4 26.2 %collective-permute-start.46 = (bf16[2,128,512]{2,1,0:T(8,128)(2,1)S(1)}, bf16[2,128,512]{2,1,0:T(8,128)(2,1)S(1)}, u32[]{:S(2)}, u32[]{:S(2)}) collective-permute-start(bf16[2,128,512]{2,1,0:T(8,128)(2,1)S(1)} %get-tuple-element.150), channel_id=1, source_target_pairs={{0,16},{1,17},{2,18},{3,19},{4,20},{5,21},{6,22},{7,23},{8,24},{9,... | collective-permute-start | bytes 786440 | tf_op jit(solution)/shard_map/ppermute | solution.py:303
  250.1 23.4 %collective-permute-start.47 = (bf16[2,128,512]{2,1,0:T(8,128)(2,1)S(1)}, bf16[2,128,512]{2,1,0:T(8,128)(2,1)S(1)}, u32[]{:S(2)}, u32[]{:S(2)}) collective-permute-start(bf16[2,128,512]{2,1,0:T(8,128)(2,1)S(1)} %get-tuple-element.151), channel_id=1, source_target_pairs={{0,24},{1,25},{2,26},{3,27},{4,28},{5,29},{6,30},{7,31},{8,16},{9,... | collective-permute-start | bytes 786440 | tf_op jit(solution)/shard_map/ppermute | solution.py:303
  269.1 19.0 %copy-start.33 = (f32[2,128,512]{2,1,0:T(8,128)}, f32[2,128,512]{2,1,0:T(8,128)S(1)}, u32[]{:S(2)}) copy-start(f32[2,128,512]{2,1,0:T(8,128)S(1)} %get-tuple-element.157) | copy-start | bytes 1572868
  269.1 19.0 %collective-permute-start.25 = (bf16[2,128,512]{2,1,0:T(8,128)(2,1)S(1)}, bf16[2,128,512]{2,1,0:T(8,128)(2,1)S(1)}, u32[]{:S(2)}, u32[]{:S(2)}) collective-permute-start(bf16[2,128,512]{2,1,0:T(8,128)(2,1)S(1)} %get-tuple-element.158), channel_id=1, source_target_pairs={{0,8},{1,9},{2,10},{3,11},{4,12},{5,13},{6,14},{7,15},{8,0},{9,1},... | collective-permute-start | bytes 786440 | tf_op jit(solution)/shard_map/ppermute | solution.py:303
  269.2 21.5 %collective-permute-start.26 = (bf16[2,128,512]{2,1,0:T(8,128)(2,1)S(1)}, bf16[2,128,512]{2,1,0:T(8,128)(2,1)S(1)}, u32[]{:S(2)}, u32[]{:S(2)}) collective-permute-start(bf16[2,128,512]{2,1,0:T(8,128)(2,1)S(1)} %get-tuple-element.159), channel_id=1, source_target_pairs={{0,16},{1,17},{2,18},{3,19},{4,20},{5,21},{6,22},{7,23},{8,24},{9,... | collective-permute-start | bytes 786440 | tf_op jit(solution)/shard_map/ppermute | solution.py:303
  271.9 18.7 %collective-permute-start.27 = (bf16[2,128,512]{2,1,0:T(8,128)(2,1)S(1)}, bf16[2,128,512]{2,1,0:T(8,128)(2,1)}, u32[]{:S(2)}, u32[]{:S(2)}) collective-permute-start(bf16[2,128,512]{2,1,0:T(8,128)(2,1)S(1)} %get-tuple-element.160), channel_id=1, source_target_pairs={{0,24},{1,25},{2,26},{3,27},{4,28},{5,29},{6,30},{7,31},{8,16},{9,... | collective-permute-start | bytes 786440 | tf_op jit(solution)/shard_map/ppermute | solution.py:303
  300.3 13.5 %collective-permute-start.30 = (bf16[592,1024]{1,0:T(8,128)(2,1)}, bf16[592,1024]{1,0:T(8,128)(2,1)}, u32[]{:S(2)}, u32[]{:S(2)}) collective-permute-start(bf16[592,1024]{1,0:T(8,128)(2,1)} %fusion.26), channel_id=1, source_target_pairs={{0,2},{1,3},{2,0},{3,1},{4,6},{5,7},{6,4},{7,5},{8,10},{9,11},{10,... | collective-permute-start | bytes 3637256 | tf_op jit(solution)/shard_map/ppermute | solution.py:303
  300.8 29.0 %collective-permute-start.28 = (bf16[2,512,512]{2,1,0:T(8,128)(2,1)}, bf16[2,512,512]{2,1,0:T(8,128)(2,1)}, u32[]{:S(2)}, u32[]{:S(2)}) collective-permute-start(bf16[2,512,512]{2,1,0:T(8,128)(2,1)} %get-tuple-element.166), channel_id=1, source_target_pairs={{0,1},{1,0},{2,3},{3,2},{4,5},{5,4},{6,7},{7,6},{8,9},{9,8},{10,11... | collective-permute-start | bytes 3145736 | tf_op jit(solution)/shard_map/ppermute | solution.py:303
  302.4 27.5 %collective-permute-start.29 = (bf16[2,512,512]{2,1,0:T(8,128)(2,1)}, bf16[2,512,512]{2,1,0:T(8,128)(2,1)}, u32[]{:S(2)}, u32[]{:S(2)}) collective-permute-start(bf16[2,512,512]{2,1,0:T(8,128)(2,1)} %get-tuple-element.167), channel_id=1, source_target_pairs={{0,4},{1,5},{2,6},{3,7},{4,0},{5,1},{6,2},{7,3},{8,12},{9,13},{10,... | collective-permute-start | bytes 3145736 | tf_op jit(solution)/shard_map/ppermute | solution.py:303
  308.1 24.4 %slice-start = ((s8[4849664]{0:T(1024)(128)(4,1)}), s8[4194304]{0:T(1024)(128)(4,1)S(1)}, s32[]{:S(2)}) async-start(s8[4849664]{0:T(1024)(128)(4,1)} %bitcast.190), calls=%async_computation.1 | async-start | bytes 8388608
  318.9 1.3 collective-permute-start.31
  320.2 9.6 %collective-permute-start.32 = (f32[12288]{0:T(1024)S(1)}, f32[12288]{0:T(1024)S(1)}, u32[]{:S(2)}, u32[]{:S(2)}) collective-permute-start(f32[12288]{0:T(1024)S(1)} %add.270), channel_id=1, source_target_pairs={{0,8},{1,9},{2,10},{3,11},{4,12},{5,13},{6,14},{7,15},{8,0},{9,1},... | collective-permute-start | bytes 147464 | tf_op jit(solution)/shard_map/ppermute | solution.py:303
  325.0 6.8 %collective-permute-start.33 = (f32[12288]{0:T(1024)S(1)}, f32[12288]{0:T(1024)S(1)}, u32[]{:S(2)}, u32[]{:S(2)}) collective-permute-start(f32[12288]{0:T(1024)S(1)} %add.270), channel_id=1, source_target_pairs={{0,16},{1,17},{2,18},{3,19},{4,20},{5,21},{6,22},{7,23},{8,24},{9,... | collective-permute-start | bytes 147464 | tf_op jit(solution)/shard_map/ppermute | solution.py:303
  325.3 6.6 %collective-permute-start.34 = (f32[12288]{0:T(1024)S(1)}, f32[12288]{0:T(1024)S(1)}, u32[]{:S(2)}, u32[]{:S(2)}) collective-permute-start(f32[12288]{0:T(1024)S(1)} %add.270), channel_id=1, source_target_pairs={{0,24},{1,25},{2,26},{3,27},{4,28},{5,29},{6,30},{7,31},{8,16},{9,... | collective-permute-start | bytes 147464 | tf_op jit(solution)/shard_map/ppermute | solution.py:303
  341.1 6.4 %collective-permute-start.35 = (bf16[592,1024]{1,0:T(8,128)(2,1)}, bf16[592,1024]{1,0:T(8,128)(2,1)}, u32[]{:S(2)}, u32[]{:S(2)}) collective-permute-start(bf16[592,1024]{1,0:T(8,128)(2,1)} %get-tuple-element.176), channel_id=1, source_target_pairs={{0,2},{1,3},{2,0},{3,1},{4,6},{5,7},{6,4},{7,5},{8,10},{9,11},{10,... | collective-permute-start | bytes 3637256 | tf_op jit(solution)/shard_map/ppermute | solution.py:303
  342.6 14.8 %collective-permute-start.37 = (bf16[512,512]{1,0:T(8,128)(2,1)S(1)}, bf16[512,512]{1,0:T(8,128)(2,1)S(1)}, u32[]{:S(2)}, u32[]{:S(2)}) collective-permute-start(bf16[512,512]{1,0:T(8,128)(2,1)S(1)} %fusion.42), channel_id=1, source_target_pairs={{0,1},{1,0},{2,3},{3,2},{4,5},{5,4},{6,7},{7,6},{8,9},{9,8},{10,11... | collective-permute-start | bytes 1572872 | tf_op jit(solution)/shard_map/ppermute | solution.py:303
  344.4 14.1 %collective-permute-start.36 = (bf16[512,512]{1,0:T(8,128)(2,1)S(1)}, bf16[512,512]{1,0:T(8,128)(2,1)S(1)}, u32[]{:S(2)}, u32[]{:S(2)}) collective-permute-start(bf16[512,512]{1,0:T(8,128)(2,1)S(1)} %fusion.41), channel_id=1, source_target_pairs={{0,4},{1,5},{2,6},{3,7},{4,0},{5,1},{6,2},{7,3},{8,12},{9,13},{10,... | collective-permute-start | bytes 1572872 | tf_op jit(solution)/shard_map/ppermute | solution.py:303
  346.1 19.7 %collective-permute-start.40 = (f32[12288]{0:T(1024)S(1)}, f32[12288]{0:T(1024)S(1)}, u32[]{:S(2)}, u32[]{:S(2)}) collective-permute-start(f32[12288]{0:T(1024)S(1)} %add_add_fusion), channel_id=1, source_target_pairs={{0,1},{1,0},{2,3},{3,2},{4,5},{5,4},{6,7},{7,6},{8,9},{9,8},{10,11... | collective-permute-start | bytes 147464 | tf_op jit(solution)/shard_map/ppermute | solution.py:303
  349.4 20.5 %copy-start.58 = (bf16[592,1024]{1,0:T(8,128)(2,1)}, bf16[592,1024]{1,0:T(8,128)(2,1)S(1)}, u32[]{:S(2)}) copy-start(bf16[592,1024]{1,0:T(8,128)(2,1)S(1)} %multiply_convert_fusion) | copy-start | bytes 3637252
  360.1 42.0 %collective-permute-start.42 = (bf16[2,128,512]{2,1,0:T(8,128)(2,1)S(1)}, bf16[2,128,512]{2,1,0:T(8,128)(2,1)S(1)}, u32[]{:S(2)}, u32[]{:S(2)}) collective-permute-start(bf16[2,128,512]{2,1,0:T(8,128)(2,1)S(1)} %get-tuple-element.180), channel_id=1, source_target_pairs={{0,8},{1,9},{2,10},{3,11},{4,12},{5,13},{6,14},{7,15},{8,0},{9,1},... | collective-permute-start | bytes 786440 | tf_op jit(solution)/shard_map/ppermute | solution.py:303
  361.3 40.9 %collective-permute-start.43 = (bf16[2,128,512]{2,1,0:T(8,128)(2,1)S(1)}, bf16[2,128,512]{2,1,0:T(8,128)(2,1)}, u32[]{:S(2)}, u32[]{:S(2)}) collective-permute-start(bf16[2,128,512]{2,1,0:T(8,128)(2,1)S(1)} %get-tuple-element.181), channel_id=1, source_target_pairs={{0,16},{1,17},{2,18},{3,19},{4,20},{5,21},{6,22},{7,23},{8,24},{9,... | collective-permute-start | bytes 786440 | tf_op jit(solution)/shard_map/ppermute | solution.py:303
  362.7 39.5 %collective-permute-start.44 = (bf16[2,128,512]{2,1,0:T(8,128)(2,1)S(1)}, bf16[2,128,512]{2,1,0:T(8,128)(2,1)}, u32[]{:S(2)}, u32[]{:S(2)}) collective-permute-start(bf16[2,128,512]{2,1,0:T(8,128)(2,1)S(1)} %get-tuple-element.182), channel_id=1, source_target_pairs={{0,24},{1,25},{2,26},{3,27},{4,28},{5,29},{6,30},{7,31},{8,16},{9,... | collective-permute-start | bytes 786440 | tf_op jit(solution)/shard_map/ppermute | solution.py:303
  365.7 5.8 %collective-permute-start.49 = (bf16[2,64,512]{2,1,0:T(8,128)(2,1)S(1)}, bf16[2,64,512]{2,1,0:T(8,128)(2,1)S(1)}, u32[]{:S(2)}, u32[]{:S(2)}) collective-permute-start(bf16[2,64,512]{2,1,0:T(8,128)(2,1)S(1)} %fusion.50), channel_id=1, source_target_pairs={{0,2},{1,3},{2,0},{3,1},{4,6},{5,7},{6,4},{7,5},{8,10},{9,11},{10,... | collective-permute-start | bytes 393224 | tf_op jit(solution)/shard_map/ppermute | solution.py:303
  365.8 4.9 %collective-permute-start.41 = (f32[12288]{0:T(1024)S(1)}, f32[12288]{0:T(1024)S(1)}, u32[]{:S(2)}, u32[]{:S(2)}) collective-permute-start(f32[12288]{0:T(1024)S(1)} %add.280), channel_id=1, source_target_pairs={{0,4},{1,5},{2,6},{3,7},{4,0},{5,1},{6,2},{7,3},{8,12},{9,13},{10,... | collective-permute-start | bytes 147464 | tf_op jit(solution)/shard_map/ppermute | solution.py:303
  370.7 3.9 collective-permute-start.48
  371.5 16.8 %collective-permute-start.39 = (bf16[289,1024]{1,0:T(8,128)(2,1)}, bf16[289,1024]{1,0:T(8,128)(2,1)}, u32[]{:S(2)}, u32[]{:S(2)}) collective-permute-start(bf16[289,1024]{1,0:T(8,128)(2,1)} %slice.291), channel_id=1, source_target_pairs={{0,1},{1,0},{2,3},{3,2},{4,5},{5,4},{6,7},{7,6},{8,9},{9,8},{10,11... | collective-permute-start | bytes 1775624 | tf_op jit(solution)/shard_map/ppermute | solution.py:303
  374.7 26.1 %collective-permute-start.38 = (bf16[289,1024]{1,0:T(8,128)(2,1)}, bf16[289,1024]{1,0:T(8,128)(2,1)}, u32[]{:S(2)}, u32[]{:S(2)}) collective-permute-start(bf16[289,1024]{1,0:T(8,128)(2,1)} %slice.200), channel_id=1, source_target_pairs={{0,1},{1,0},{2,3},{3,2},{4,5},{5,4},{6,7},{7,6},{8,9},{9,8},{10,11... | collective-permute-start | bytes 1775624 | tf_op jit(solution)/shard_map/ppermute | solution.py:303
  375.9 24.9 %copy-start.59 = (bf16[592,1024]{1,0:T(8,128)(2,1)S(1)}, bf16[592,1024]{1,0:T(8,128)(2,1)}, u32[]{:S(2)}) copy-start(bf16[592,1024]{1,0:T(8,128)(2,1)} %copy-done.58) | copy-start | bytes 3637252
  403.4 6.2 %collective-permute-start.50 = (bf16[2,64,512]{2,1,0:T(8,128)(2,1)S(1)}, bf16[2,64,512]{2,1,0:T(8,128)(2,1)S(1)}, u32[]{:S(2)}, u32[]{:S(2)}) collective-permute-start(bf16[2,64,512]{2,1,0:T(8,128)(2,1)S(1)} %fusion.51), channel_id=1, source_target_pairs={{0,2},{1,3},{2,0},{3,1},{4,6},{5,7},{6,4},{7,5},{8,10},{9,11},{10,... | collective-permute-start | bytes 393224 | tf_op jit(solution)/shard_map/ppermute | solution.py:303
  (87 other events, 560.2 us)
Sparse Core Ops, SparseCore 0:
  12.2 142.4 all-gather.1

commit v6 on v5

--- a/solution.py
+++ b/solution.py
@@ -293,6 +293,7 @@
 LANES = 128
 LOW = jnp.bfloat16
 VMEM_ROOM = 24 * 2**20
+SMALL = pl.CostEstimate(flops=1024, transcendentals=0, bytes_accessed=1024)
 
 
 def exchange(value, far_z=0, far_x=0, far_core=0, far_y=0):
@@ -443,10 +444,12 @@
     return exchange(sends[0], far_y=1), exchange(sends[1], far_x=1)
 
 
-def scatter_second(keeps, arrived):
-    one = low_add(keeps[0][1], arrived[0][1]).astype(LOW)
-    two = low_add(keeps[1][1], arrived[1][1]).astype(LOW)
-    return exchange(one, far_x=1), exchange(two, far_y=1)
+def scatter_adds(keeps, arrived):
+    return [low_add(keeps[at][1], arrived[at][1]).astype(LOW) for at in range(2)]
+
+
+def scatter_second(adds):
+    return exchange(adds[0], far_x=1), exchange(adds[1], far_y=1)
 
 
 def scatter_line(keeps, arrived, crossed):
@@ -632,11 +635,7 @@
             jax.ShapeDtypeStruct((rows, lines * tall), LOW),
         ],
         compiler_params=pltpu.CompilerParams(vmem_limit_bytes=VMEM_ROOM),
-        cost_estimate=pl.CostEstimate(
-            flops=2 * both * deep * lines * tall,
-            transcendentals=0,
-            bytes_accessed=left.size * 2 + lines * tall * deep * 2 + rows * lines * tall * 6,
-        ),
+        cost_estimate=SMALL,
     )(places, left, gathered)
     return own + exchange(send, far_core=1).astype(jnp.float32)
 
@@ -1054,7 +1053,7 @@
     up_sends = weight_pieces([(second_turned, hidden_grad)], True)
     up_first = scatter_first(up_sends)
     lower_first = after(lower_first, *up_sends)
-    lower_second = scatter_second(lower_keeps, lower_first)
+    lower_second = scatter_second(scatter_adds(lower_keeps, lower_first))
     hidden_late = after(hidden_grad, *lower_first)
     second_grad = down_call(places, hidden_late, gathered, 0)
     middle_back, gain_two_grad, shift_two_grad = flat_norm_back(
@@ -1063,28 +1062,29 @@
     middle_grad = row_mask * (grad_top + middle_back)
     attended_grad = middle_grad.astype(LOW)
     attended_pair = pair_of(attended_grad)
-    up_keeps = weight_pieces([(second_turned, after(hidden_late, attended_grad))], False)
-    attended_turned = turn(places, attended_pair)
-    lower_second = after(lower_second, *up_keeps, attended_turned)
+    grad_mixed = mat(attended_pair[0], output_full).astype(LOW)
+    back = attend_back_image(0, qkv, key_bias, grad_mixed, mixed, totals, [])
+    up_keeps = weight_pieces([(second_turned, after(hidden_late, back))], False)
+    up_first = after(up_first, back)
+    up_adds = scatter_adds(up_keeps, up_first)
+    up_second = scatter_second(up_adds)
+    lower_second = after(lower_second, back, *up_keeps)
     lower_line = scatter_line(lower_keeps, lower_first, lower_second)
     lower_z = scatter_z(lower_line)
-    up_first = after(up_first, *up_keeps)
-    up_second = scatter_second(up_keeps, up_first)
-    grad_mixed = [mat(one, output_full).astype(LOW) for one in attended_pair]
-    grad_mixed = after(tuple(grad_mixed), *up_first, *lower_line)
-    back = attend_back_image(0, qkv, key_bias, grad_mixed[0], mixed, totals, [])
-    lower_z = after(tuple(lower_z), back)
-    up_line = scatter_line(up_keeps, up_first, after(up_second, back))
+    attended_turned = turn(places, attended_pair)
+    grad_mixed = mat(attended_pair[1], output_full).astype(LOW)
+    grad_mixed = after(grad_mixed, *up_adds, *lower_line, attended_turned)
+    back = attend_back_image(1, qkv, key_bias, grad_mixed, mixed, totals, [back])
+    up_second, lower_z = after((up_second, tuple(lower_z)), back)
+    up_line = scatter_line(up_keeps, up_first, up_second)
     up_z = scatter_z(up_line)
     back = after(back, *up_line)
-    back = attend_back_image(1, qkv, key_bias, grad_mixed[1], mixed, totals, [back])
-    up_z = after(tuple(up_z), back)
-    back = after(back, *up_z)
     last_sends = weight_pieces([(normed_turned, back), (attended_turned, mixed)], True)
     last_first = scatter_first(last_sends)
     back_late = after(back, *last_sends)
+    last_keeps = weight_pieces([(normed_turned, back_late), (attended_turned, mixed)], False)
+    back_late = after(back_late, *last_keeps)
     normed_far = exchange(mat_far(back_late[rows:], qkv_full).astype(LOW), far_core=1)
-    last_keeps = weight_pieces([(normed_turned, back_late), (attended_turned, mixed)], False)
     normed_grad = mat_far(back_late[:rows], qkv_full) + normed_far.astype(jnp.float32)
     first_back, gain_one_grad, shift_one_grad = flat_norm_back(
         normed_grad, unit_one, spread_one, gain_one
@@ -1106,27 +1106,27 @@
     )
     vector, vectors = vector_first(vector)
     last_first = after(last_first, *last_keeps, images_own, *vectors)
-    last_second = scatter_second(last_keeps, last_first)
-    vector = vector + vectors[0] + vectors[1] + vectors[2]
-    vector_y = exchange(vector, far_y=1)
-    fed = down_call(places, after(active, *last_first), gathered, 1)
-    vector = vector + after(vector_y, fed)
+    last_adds = scatter_adds(last_keeps, last_first)
+    last_second = scatter_second(last_adds)
+    fed = down_call(places, after(active, *last_adds), gathered, 1)
+    layer_own = (row_mask * (middle + fed + down_bias.astype(jnp.float32))).astype(LOW)
+    vector = after(vector, *last_adds) + vectors[0] + vectors[1] + vectors[2]
+    vector = vector + after(exchange(vector, far_y=1), layer_own)
     vector_x = exchange(vector, far_x=1)
-    layer_own = (row_mask * (middle + fed + down_bias.astype(jnp.float32))).astype(LOW)
-    last_line = scatter_line(last_keeps, last_first, after(last_second, layer_own))
+    last_line = scatter_line(last_keeps, last_first, after(last_second, layer_own, *up_z))
     last_z = scatter_z(last_line)
-    vector = vector + after(vector_x, *last_line)
+    images_far = exchange(after(images_own, *last_adds)[half : half + strip].astype(LOW), far_y=1)
+    layer_far = exchange(after(layer_own, *last_second)[half : half + strip], far_y=1)
+    vector = vector + after(vector_x, *last_line, images_far, layer_far)
     lower_z, up_z = after((tuple(lower_z), tuple(up_z)), *last_line)
     lower_owned = full_columns(scatter_last(lower_line[0], lower_z, core)).T
     upper_owned = full_columns(scatter_last(up_line[0], up_z, core))
-    layer_late, images_late = after((layer_own, images_own), *last_line)
-
-    def to_strips(own, send):
-        far = exchange(send, far_y=1).astype(own.dtype)
+
+    def to_strips(own, far):
         return pick_two(place_y, own[:strip], far, 1).transpose(1, 0, 2)
 
-    layer_out = to_strips(layer_late, layer_late[half : half + strip])
-    images_grad = to_strips(images_late, images_late[half : half + strip].astype(LOW))
+    layer_out = to_strips(layer_own, layer_far)
+    images_grad = to_strips(after(images_own, *last_line), images_far.astype(jnp.float32))
     last_z = after(tuple(last_z), vector, layer_out, images_grad, lower_owned, upper_owned)
     last_owned = scatter_last(last_line[0], last_z, core)
     def head_grad(at):

time: 425 us -> 407 us (0.958)
  waiting for transfers between devices: 128 us -> 112 us
    ppermute x51, waiting for transfers between devices: 115 us -> 100 us  [exchange(): return lax.ppermute(value, BOTH, pairs)]
    unnamed x211 -> x203, local copies, waits for them, and re-layouts: 22.3 us -> 19.9 us
  transfers between devices with their start and end apart: 52 -> 52, of which waited for: 22 -> 21; matrix products, arithmetic and copies ran while one was open for 15% -> 15% of each run, Pallas kernels for 22% -> 21%
where the time goes in v6:
time: 407 us; the launch traced here: 403 us
  Pallas kernels  132 us (32%)
  waiting for transfers between devices  112 us (28%)
  starting transfers between devices  55.9 us (14%)
  local copies, waits for them, and re-layouts  36.2 us (9%)
  other arithmetic  32.3 us (8%)
  matrix products  17.4 us (4%)
  between operations  17 us (4%)
    ppermute x51, waiting for transfers between devices, exchange(): return lax.ppermute(value, BOTH, pairs)  100 us
    ppermute x51, starting transfers between devices, exchange(): return lax.ppermute(value, BOTH, pairs)  55.8 us
    pallas_call x2, Pallas kernels, attend_back_image(): pl.pallas_call(kernel, grid=(blocks,), in_specs=[pl.BlockSpec((rows, 3 *...  29 us
    pallas_call x6, Pallas kernels, weight_pieces(): pl.pallas_call(kernel, grid=(4,), in_specs=specs, out_specs=[pl.BlockSpec...  28.2 us
    unnamed x203, local copies, waits for them, and re-layouts  19.9 us
    pallas_call x2, Pallas kernels, down_call(): pl.pallas_call(down_kernel, grid_spec=pltpu.PrefetchScalarGridSpec(num_sc...  17.3 us
    pallas_call x2, Pallas kernels, attend_image(): pl.pallas_call(kernel, grid=(blocks,), in_specs=[pl.BlockSpec((rows, 3 *...  15.4 us
    all_gather x1, waiting for transfers between devices, whole_images(): lax.all_gather(feed.reshape(2 * depth, -1), BOTH, axis=0, tiled=True, axi...  12.5 us
  transfers between devices with their start and end apart: 52, of which 21 were waited for; matrix products, arithmetic and copies ran while one was open for 15% of the time, Pallas kernels for 21%

profile of v6, /device:TPU:0, one launch (start us, length us, event | category | flops | bytes accessed | tf_op | source)
XLA Modules:
  0.0 402.8 jit_solution(13801868235873993308)
XLA Ops:
  13.9 3.0 collective-permute-start.3
  16.9 2.6 collective-permute-start.4
  20.4 2.9 copy.72
  24.7 1.8 collective-permute-start.1
  26.8 3.8 collective-permute-done.3.refs_1_
  30.6 7.1 %collective-permute-done.4.refs_2_ = bf16[2,128,512]{2,1,0:T(8,128)(2,1)S(1)} collective-permute-done((bf16[2,128,512]{2,1,0:T(8,128)(2,1)S(1)}, bf16[2,128,512]{2,1,0:T(8,128)(2,1)S(1)}, u32[]{:S(2)}, u32[]{:S(2)}) %collective-permute-start.4) | collective-permute-done | bytes 262176 | tf_op jit(solution)/shard_map/ppermute | solution.py:304
  37.8 5.3 %collective-permute-done.5.refs_3_ = bf16[2,128,512]{2,1,0:T(8,128)(2,1)S(1)} collective-permute-done((bf16[2,128,512]{2,1,0:T(8,128)(2,1)S(1)}, bf16[2,128,512]{2,1,0:T(8,128)(2,1)S(1)}, u32[]{:S(2)}, u32[]{:S(2)}) %collective-permute-start.5) | collective-permute-done | bytes 262176 | tf_op jit(solution)/shard_map/ppermute | solution.py:304
  43.7 1.6 collective-permute-start.6
  45.3 1.5 collective-permute-start.7
  48.1 8.4 %collective-permute-done.6.refs_1_ = bf16[4,128,512]{2,1,0:T(8,128)(2,1)S(1)} collective-permute-done((bf16[4,128,512]{2,1,0:T(8,128)(2,1)S(1)}, bf16[4,128,512]{2,1,0:T(8,128)(2,1)S(1)}, u32[]{:S(2)}, u32[]{:S(2)}) %collective-permute-start.6) | collective-permute-done | bytes 524320 | tf_op jit(solution)/shard_map/ppermute | solution.py:304
  56.4 17.8 %collective-permute-done.7.refs_3_ = bf16[4,128,512]{2,1,0:T(8,128)(2,1)S(1)} collective-permute-done((bf16[4,128,512]{2,1,0:T(8,128)(2,1)S(1)}, bf16[4,128,512]{2,1,0:T(8,128)(2,1)S(1)}, u32[]{:S(2)}, u32[]{:S(2)}) %collective-permute-start.7) | collective-permute-done | bytes 524320 | tf_op jit(solution)/shard_map/ppermute | solution.py:304
  74.2 2.0 shard_map.306
  79.8 1.7 collective-permute-start.11
  85.4 1.8 shard_map.307.refs_0_
  87.2 3.3 shard_map.308.refs_0_
  92.0 19.0 %collective-permute-done.10.refs_1_ = bf16[2,4,128,512]{3,2,1,0:T(8,128)(2,1)} collective-permute-done((bf16[2,4,128,512]{3,2,1,0:T(8,128)(2,1)}, bf16[2,4,128,512]{3,2,1,0:T(8,128)(2,1)}, u32[]{:S(2)}, u32[]{:S(2)}) %collective-permute-start.10) | collective-permute-done | bytes 1048608 | tf_op jit(solution)/shard_map/ppermute | solution.py:304
  112.1 2.7 shard_map.309
  114.8 5.2 %fusion.refs_0_ = bf16[1184,1536]{1,0:T(8,128)(2,1)S(1)} fusion(bf16[1024,1536]{1,0:T(8,128)(2,1)S(1)} %bitcast.187, f32[1536]{0:T(1024)S(1)} %add.250, bf16[592,1024]{1,0:T(8,128)(2,1)S(1)} %copy-done.29, bf16[592,1024]{1,0:T(8,128)(2,1)S(1)} %copy-done.7), kind=kOutput, calls=%fused_computation.1 | convolution fusion | flops 3733028864 | bytes 9213952 | tf_op jit(solution)/shard_map/dot_general | solution.py:644
  120.2 7.7 %shard_map.310 = (bf16[1184,512]{1,0:T(8,128)(2,1)S(1)}, f32[8,8,592]{2,1,0:T(8,128)S(1)}) custom-call(bf16[1184,1536]{1,0:T(8,128)(2,1)S(1)} %fusion.refs_0_, bf16[592,128]{1,0:T(8,128)(2,1)S(1)} %broadcast_in_dim.56.refs_1_), custom_call_target="tpu_custom_call" | custom-call | flops 2871001088 | bytes 2424832 | tf_op jit(solution)/shard_map/pallas_call | solution.py:822
  128.9 7.7 %shard_map.311 = (bf16[1184,512]{1,0:T(8,128)(2,1)S(1)}, f32[8,8,592]{2,1,0:T(8,128)S(1)}) custom-call(bf16[1184,1536]{1,0:T(8,128)(2,1)S(1)} %fusion.refs_0_, bf16[592,128]{1,0:T(8,128)(2,1)S(1)} %broadcast_in_dim.56.refs_1_, bf16[1184,512]{1,0:T(8,128)(2,1)S(1)} %get-tuple-element.119.refs_2_, ...), custom_call_target="tpu_custom_call", output_to_operand_aliasing={{0}: (2, {}), {1}: (3, {})} | custom-call | flops 2871001088 | bytes 2424832 | tf_op jit(solution)/shard_map/pallas_call | solution.py:822
  138.3 1.5 add_convert_fusion.own_ref
  140.4 2.8 collective-permute-done.13.far_ref
  143.1 12.5 %all-gather.2.cloned.1.call-done = bf16[2048,2048]{1,0:T(8,128)(2,1)} async-done(((bf16[128,2048]{1,0:T(8,128)(2,1)}), bf16[2048,2048]{1,0:T(8,128)(2,1)}) %all-gather.2.cloned.1.call-update) | async-done | bytes 8388624 | tf_op jit(solution)/shard_map/all_gather | solution.py:956
  155.7 12.3 %shard_map.312 = (bf16[1184,2048]{1,0:T(8,128)(2,1)S(1)}, bf16[1184,2048]{1,0:T(8,128)(2,1)S(1)}) custom-call(s32[4]{0:T(128)S(1)} %pad_add_fusion.places_ref, bf16[592,1024]{1,0:T(8,128)(2,1)} %add_convert_fusion.own_ref, bf16[592,1024]{1,0:T(8,128)(2,1)} %collective-permute-done.13.far_ref, bf16[8,2,128,2048]{3,2,1,0:T(8,128)(2,1)} %bitcast.194, ...), custom_call_target="tpu_custom_call" | custom-call | flops 4966055936 | bytes 16318464 | tf_op jit(solution)/shard_map/pallas_call | solution.py:539
  168.0 4.3 %shard_map.313 = (bf16[2,512,512]{2,1,0:T(8,128)(2,1)S(1)}, bf16[2,512,512]{2,1,0:T(8,128)(2,1)S(1)}) custom-call(bf16[2,512,1184]{2,1,0:T(8,128)(2,1)S(1)} %copy-done.13, bf16[1184,2048]{1,0:T(8,128)(2,1)S(1)} %get-tuple-element.168.refs_1_.left_ref), custom_call_target="tpu_custom_call" | custom-call | flops 2483027968 | bytes 11796480 | tf_op jit(solution)/shard_map/pallas_call | solution.py:723
  172.3 1.6 collective-permute-start.15
  175.4 3.3 shard_map.316.refs_0_
  178.8 3.9 shard_map.314
  184.6 9.7 %shard_map.315 = (bf16[1184,2048]{1,0:T(8,128)(2,1)S(1)}, f32[1,2048]{1,0:T(1,128)S(1)}) custom-call(s32[4]{0:T(128)S(1)} %pad_add_fusion.places_ref, bf16[592,1024]{1,0:T(8,128)(2,1)} %get-tuple-element.128.own_ref, bf16[592,1024]{1,0:T(8,128)(2,1)} %collective-permute-done.9.far_ref, bf16[8,2,128,2048]{3,2,1,0:T(8,128)(2,1)} %bitcast.195, ...), custom_call_target="tpu_custom_call" | custom-call | flops 4966055936 | bytes 16318464 | tf_op jit(solution)/shard_map/pallas_call | solution.py:579
  194.4 3.9 shard_map.317
  198.9 8.5 %shard_map.318 = (f32[592,1024]{1,0:T(8,128)S(1)}, bf16[592,1024]{1,0:T(8,128)(2,1)}) custom-call(s32[4]{0:T(128)S(1)} %pad_add_fusion.places_ref, bf16[1184,2048]{1,0:T(8,128)(2,1)S(1)} %get-tuple-element.140.refs_1_.left_ref, bf16[8,2,128,2048]{3,2,1,0:T(8,128)(2,1)} %bitcast.196), custom_call_target="tpu_custom_call" | custom-call | flops 1024 | bytes 1024 | tf_op jit(solution)/shard_map/pallas_call | solution.py:622
  212.1 1.5 fusion.39
  215.5 1.6 collective-permute-start.22
  217.2 3.3 multiply_reduce_fusion
  220.5 4.2 %convert_reduce_fusion.3 = (f32[1024]{0:T(1024)S(1)}, bf16[592,1024]{1,0:T(8,128)(2,1)S(1)}, f32[592,1024]{1,0:T(8,128)}) fusion(f32[592]{0:T(1024)S(1)} %broadcast_multiply_fusion.2, f32[592,1024]{1,0:T(8,128)S(1)} %copy-done.48, f32[592]{0:T(1024)S(1)} %broadcast_multiply_fusion.4, f32[592]{0:T(1024)S(1)} %broadcast_multiply_fusion.3, ...), kind=kLoop, calls=%fused_computation.28 | loop fusion | flops 11516928 | bytes 10931776 | tf_op jit(solution)/shard_map/reduce_sum | solution.py:897
  227.1 14.5 %shard_map.319.refs_5_ = bf16[1184,1536]{1,0:T(8,128)(2,1)S(1)} custom-call(bf16[1184,1536]{1,0:T(8,128)(2,1)S(1)} %copy-done.44, bf16[592,128]{1,0:T(8,128)(2,1)S(1)} %broadcast_in_dim.56.refs_1_, bf16[592,512]{1,0:T(8,128)(2,1)S(1)} %convolution_convert_fusion.1.refs_2_, bf16[1184,512]{1,0:T(8,128)(2,1)S(1)} %copy-done.9, f32[8,8,592]{2,1,0:T(8,128)S(1)} %copy-done.46), custom_call_target="tpu_custom_call" | custom-call | flops 7177502720 | bytes 4849664 | tf_op jit(solution)/shard_map/pallas_call | solution.py:856
  241.6 4.1 %shard_map.320 = (bf16[2,512,512]{2,1,0:T(8,128)(2,1)S(1)}, bf16[2,512,512]{2,1,0:T(8,128)(2,1)S(1)}) custom-call(bf16[2,512,1184]{2,1,0:T(8,128)(2,1)S(1)} %copy-done.11, bf16[1184,2048]{1,0:T(8,128)(2,1)S(1)} %bitcast.182), custom_call_target="tpu_custom_call" | custom-call | flops 2483027968 | bytes 11796480 | tf_op jit(solution)/shard_map/pallas_call | solution.py:723
  247.5 1.5 collective-permute-start.23
  250.1 1.5 collective-permute-start.24
  251.6 1.6 shard_map.321
  253.3 1.6 collective-permute-start.26
  254.9 2.8 collective-permute-start.27
  258.5 1.7 shard_map.322.refs_2_
  260.2 14.5 %shard_map.323.refs_1_ = bf16[1184,1536]{1,0:T(8,128)(2,1)S(1)} custom-call(bf16[1184,1536]{1,0:T(8,128)(2,1)S(1)} %copy-done.44, bf16[592,128]{1,0:T(8,128)(2,1)S(1)} %broadcast_in_dim.56.refs_1_, bf16[592,512]{1,0:T(8,128)(2,1)S(1)} %convolution_convert_fusion.2.refs_2_, bf16[1184,512]{1,0:T(8,128)(2,1)S(1)} %copy-done.9, ...), custom_call_target="tpu_custom_call", output_to_operand_aliasing={{}: (5, {})} | custom-call | flops 7177502720 | bytes 4849664 | tf_op jit(solution)/shard_map/pallas_call | solution.py:856
  274.8 2.4 shard_map.324
  277.2 6.5 %shard_map.325 = (bf16[2,512,512]{2,1,0:T(8,128)(2,1)}, bf16[2,512,512]{2,1,0:T(8,128)(2,1)}) custom-call(bf16[2,512,1184]{2,1,0:T(8,128)(2,1)S(1)} %shard_map.307.refs_0_, bf16[1184,1536]{1,0:T(8,128)(2,1)S(1)} %shard_map.323.refs_1_, bf16[2,512,1184]{2,1,0:T(8,128)(2,1)S(1)} %shard_map.322.refs_2_, bf16[1184,512]{1,0:T(8,128)(2,1)S(1)} %copy-done.9), custom_call_target="tpu_custom_call" | custom-call | flops 2483027968 | bytes 11796480 | tf_op jit(solution)/shard_map/pallas_call | solution.py:723
  283.8 5.5 %shard_map.326 = (bf16[2,512,512]{2,1,0:T(8,128)(2,1)S(1)}, bf16[2,512,512]{2,1,0:T(8,128)(2,1)S(1)}) custom-call(bf16[2,512,1184]{2,1,0:T(8,128)(2,1)S(1)} %shard_map.307.refs_0_, bf16[1184,1536]{1,0:T(8,128)(2,1)S(1)} %shard_map.323.refs_1_, bf16[2,512,1184]{2,1,0:T(8,128)(2,1)S(1)} %shard_map.322.refs_2_, bf16[1184,512]{1,0:T(8,128)(2,1)S(1)} %copy-done.9), custom_call_target="tpu_custom_call" | custom-call | flops 2483027968 | bytes 11796480 | tf_op jit(solution)/shard_map/pallas_call | solution.py:723
  289.3 3.1 fusion.26
  295.7 5.5 %fusion.13 = (f32[1024]{0:T(1024)S(1)}, f32[592]{0:T(1024)S(1)}, f32[592]{0:T(1024)S(1)}, f32[1024]{0:T(1024)S(1)}, f32[592,1024]{1,0:T(8,128)S(1)}) fusion(f32[592]{0:T(1024)S(1)} %add_rsqrt_fusion.1, f32[592]{0:T(1024)S(1)} %broadcast_multiply_fusion.5, bf16[296,1024]{1,0:T(8,128)(2,1)S(1)} %copy-done.56, bf16[296,1024]{1,0:T(8,128)(2,1)S(1)} %copy-done.51, ...), kind=kOutput, calls=%fused_computation.18 | convolution fusion | flops 1871360768 | bytes 9835776 | tf_op jit(solution)/shard_map/dot_general | solution.py:494
  302.5 3.3 collective-permute-start.32
  306.1 2.2 collective-permute-start.34
  308.3 2.4 fusion.12
  310.7 7.5 %collective-permute-done.28.one_a = bf16[2,512,512]{2,1,0:T(8,128)(2,1)S(1)} collective-permute-done((bf16[2,512,512]{2,1,0:T(8,128)(2,1)}, bf16[2,512,512]{2,1,0:T(8,128)(2,1)S(1)}, u32[]{:S(2)}, u32[]{:S(2)}) %collective-permute-start.28) | collective-permute-done | bytes 1048608 | tf_op jit(solution)/shard_map/ppermute | solution.py:304
  321.5 8.8 %shard_map.327 = (f32[592,1024]{1,0:T(8,128)S(1)}, bf16[592,1024]{1,0:T(8,128)(2,1)}) custom-call(s32[4]{0:T(128)S(1)} %pad_add_fusion.places_ref, bf16[1184,2048]{1,0:T(8,128)(2,1)S(1)} %bitcast.180, bf16[8,2,128,2048]{3,2,1,0:T(8,128)(2,1)} %bitcast.197), custom_call_target="tpu_custom_call" | custom-call | flops 1024 | bytes 1024 | tf_op jit(solution)/shard_map/pallas_call | solution.py:622
  330.4 3.5 collective-permute-start.39
  338.0 2.5 collective-permute-start.41
  340.5 2.6 multiply_convert_fusion
  343.1 2.7 collective-permute-done.39
  346.6 8.8 %collective-permute-done.40 = bf16[2,128,512]{2,1,0:T(8,128)(2,1)S(1)} collective-permute-done((bf16[2,128,512]{2,1,0:T(8,128)(2,1)}, bf16[2,128,512]{2,1,0:T(8,128)(2,1)S(1)}, u32[]{:S(2)}, u32[]{:S(2)}) %collective-permute-start.40) | collective-permute-done | bytes 262176 | tf_op jit(solution)/shard_map/ppermute | solution.py:304
  357.1 4.1 %collective-permute-start.45 = (bf16[2,128,512]{2,1,0:T(8,128)(2,1)S(1)}, bf16[2,128,512]{2,1,0:T(8,128)(2,1)S(1)}, u32[]{:S(2)}, u32[]{:S(2)}) collective-permute-start(bf16[2,128,512]{2,1,0:T(8,128)(2,1)S(1)} %get-tuple-element.175), channel_id=1, source_target_pairs={{0,8},{1,9},{2,10},{3,11},{4,12},{5,13},{6,14},{7,15},{8,0},{9,1},... | collective-permute-start | bytes 786440 | tf_op jit(solution)/shard_map/ppermute | solution.py:304
  361.8 1.9 collective-permute-start.47
  365.7 3.2 copy.93
  375.7 9.6 %collective-permute-done.38 = bf16[289,1024]{1,0:T(8,128)(2,1)} collective-permute-done((bf16[289,1024]{1,0:T(8,128)(2,1)}, bf16[289,1024]{1,0:T(8,128)(2,1)}, u32[]{:S(2)}, u32[]{:S(2)}) %collective-permute-start.38) | collective-permute-done | bytes 591904 | tf_op jit(solution)/shard_map/ppermute | solution.py:304
  386.6 2.2 copy.92
  (399 shorter events, 71.9 us)
Async XLA Ops:
  7.2 148.4 %all-gather.2.cloned.1.call-start = ((), (), s32[]{:S(2)}) async-start(), calls=%async_computation | async-start | bytes 8912896 | tf_op jit(solution)/shard_map/all_gather | solution.py:956
  9.5 1.7 collective-permute-start.14
  12.3 1.4 collective-permute-start
  13.9 16.8 %collective-permute-start.3 = (bf16[2,128,512]{2,1,0:T(8,128)(2,1)S(1)}, bf16[2,128,512]{2,1,0:T(8,128)(2,1)S(1)}, u32[]{:S(2)}, u32[]{:S(2)}) collective-permute-start(bf16[2,128,512]{2,1,0:T(8,128)(2,1)S(1)} %bitcast.183), channel_id=1, source_target_pairs={{0,8},{1,9},{2,10},{3,11},{4,12},{5,13},{6,14},{7,15},{8,0},{9,1},... | collective-permute-start | bytes 786440 | tf_op jit(solution)/shard_map/ppermute | solution.py:304
  16.9 20.9 %collective-permute-start.4 = (bf16[2,128,512]{2,1,0:T(8,128)(2,1)S(1)}, bf16[2,128,512]{2,1,0:T(8,128)(2,1)S(1)}, u32[]{:S(2)}, u32[]{:S(2)}) collective-permute-start(bf16[2,128,512]{2,1,0:T(8,128)(2,1)S(1)} %bitcast.184), channel_id=1, source_target_pairs={{0,16},{1,17},{2,18},{3,19},{4,20},{5,21},{6,22},{7,23},{8,24},{9,... | collective-permute-start | bytes 786440 | tf_op jit(solution)/shard_map/ppermute | solution.py:304
  19.4 23.6 %collective-permute-start.5 = (bf16[2,128,512]{2,1,0:T(8,128)(2,1)S(1)}, bf16[2,128,512]{2,1,0:T(8,128)(2,1)S(1)}, u32[]{:S(2)}, u32[]{:S(2)}) collective-permute-start(bf16[2,128,512]{2,1,0:T(8,128)(2,1)S(1)} %bitcast.185), channel_id=1, source_target_pairs={{0,24},{1,25},{2,26},{3,27},{4,28},{5,29},{6,30},{7,31},{8,16},{9,... | collective-permute-start | bytes 786440 | tf_op jit(solution)/shard_map/ppermute | solution.py:304
  20.4 56.6 %copy-start.49 = (bf16[296,1024]{1,0:T(8,128)(2,1)}, bf16[296,1024]{1,0:T(8,128)(2,1)S(1)}, u32[]{:S(2)}) copy-start(bf16[296,1024]{1,0:T(8,128)(2,1)S(1)} %get-tuple-element.265) | copy-start | bytes 1818628
  20.4 26.4 %copy-start.82 = (bf16[1024]{0:T(1024)(128)(2,1)S(1)}, bf16[1024]{0:T(1024)(128)(2,1)}, u32[]{:S(2)}) copy-start(bf16[1024]{0:T(1024)(128)(2,1)} %param.22) | copy-start | bytes 6148
  20.4 26.4 %copy-start.83 = (bf16[1024]{0:T(1024)(128)(2,1)S(1)}, bf16[1024]{0:T(1024)(128)(2,1)}, u32[]{:S(2)}) copy-start(bf16[1024]{0:T(1024)(128)(2,1)} %param.21) | copy-start | bytes 6148
  20.4 26.4 %copy-start.90 = (s32[2]{0:T(128)S(1)}, s32[2]{0:T(128)}, u32[]{:S(2)}) copy-start(s32[2]{0:T(128)} %param.20) | copy-start | bytes 28
  24.6 53.0 %copy-start.59 = (bf16[296,1024]{1,0:T(8,128)(2,1)}, bf16[296,1024]{1,0:T(8,128)(2,1)S(1)}, u32[]{:S(2)}) copy-start(bf16[296,1024]{1,0:T(8,128)(2,1)S(1)} %get-tuple-element.263) | copy-start | bytes 1818628
  24.7 51.6 %collective-permute-start.1 = (bf16[296,1024]{1,0:T(8,128)(2,1)S(1)}, bf16[296,1024]{1,0:T(8,128)(2,1)S(1)}, u32[]{:S(2)}, u32[]{:S(2)}) collective-permute-start(bf16[296,1024]{1,0:T(8,128)(2,1)S(1)} %copy-done.67), channel_id=1, source_target_pairs={{0,1},{1,0},{2,3},{3,2},{4,5},{5,4},{6,7},{7,6},{8,9},{9,8},{10,11... | collective-permute-start | bytes 1818632 | tf_op jit(solution)/shard_map/ppermute | solution.py:304
  26.5 49.7 %collective-permute-start.2 = (bf16[296,1024]{1,0:T(8,128)(2,1)S(1)}, bf16[296,1024]{1,0:T(8,128)(2,1)S(1)}, u32[]{:S(2)}, u32[]{:S(2)}) collective-permute-start(bf16[296,1024]{1,0:T(8,128)(2,1)S(1)} %get-tuple-element.107), channel_id=1, source_target_pairs={{0,1},{1,0},{2,3},{3,2},{4,5},{5,4},{6,7},{7,6},{8,9},{9,8},{10,11... | collective-permute-start | bytes 1818632 | tf_op jit(solution)/shard_map/ppermute | solution.py:304
  43.7 12.7 %collective-permute-start.6 = (bf16[4,128,512]{2,1,0:T(8,128)(2,1)S(1)}, bf16[4,128,512]{2,1,0:T(8,128)(2,1)S(1)}, u32[]{:S(2)}, u32[]{:S(2)}) collective-permute-start(bf16[4,128,512]{2,1,0:T(8,128)(2,1)S(1)} %get-tuple-element.108.refs_0_), channel_id=1, source_target_pairs={{0,4},{1,5},{2,6},{3,7},{4,0},{5,1},{6,2},{7,3},{8,12},{9,13},{10,... | collective-permute-start | bytes 1572872 | tf_op jit(solution)/shard_map/ppermute | solution.py:304
  45.3 29.0 %collective-permute-start.7 = (bf16[4,128,512]{2,1,0:T(8,128)(2,1)S(1)}, bf16[4,128,512]{2,1,0:T(8,128)(2,1)S(1)}, u32[]{:S(2)}, u32[]{:S(2)}) collective-permute-start(bf16[4,128,512]{2,1,0:T(8,128)(2,1)S(1)} %get-tuple-element.109.refs_2_), channel_id=1, source_target_pairs={{0,1},{1,0},{2,3},{3,2},{4,5},{5,4},{6,7},{7,6},{8,9},{9,8},{10,11... | collective-permute-start | bytes 1572872 | tf_op jit(solution)/shard_map/ppermute | solution.py:304
  77.5 4.2 %collective-permute-start.8 = (bf16[592,1024]{1,0:T(8,128)(2,1)S(1)}, bf16[592,1024]{1,0:T(8,128)(2,1)S(1)}, u32[]{:S(2)}, u32[]{:S(2)}) collective-permute-start(bf16[592,1024]{1,0:T(8,128)(2,1)S(1)} %fusion.8.own_ref), channel_id=1, source_target_pairs={{0,2},{1,3},{2,0},{3,1},{4,6},{5,7},{6,4},{7,5},{8,10},{9,11},{10,... | collective-permute-start | bytes 3637256 | tf_op jit(solution)/shard_map/ppermute | solution.py:304
  79.0 8.2 %collective-permute-start.9 = (bf16[592,1024]{1,0:T(8,128)(2,1)}, bf16[592,1024]{1,0:T(8,128)(2,1)}, u32[]{:S(2)}, u32[]{:S(2)}) collective-permute-start(bf16[592,1024]{1,0:T(8,128)(2,1)} %get-tuple-element.128.own_ref), channel_id=1, source_target_pairs={{0,2},{1,3},{2,0},{3,1},{4,6},{5,7},{6,4},{7,5},{8,10},{9,11},{10,... | collective-permute-start | bytes 3637256 | tf_op jit(solution)/shard_map/ppermute | solution.py:304
  79.5 31.6 %collective-permute-start.10 = (bf16[2,4,128,512]{3,2,1,0:T(8,128)(2,1)}, bf16[2,4,128,512]{3,2,1,0:T(8,128)(2,1)}, u32[]{:S(2)}, u32[]{:S(2)}) collective-permute-start(bf16[2,4,128,512]{3,2,1,0:T(8,128)(2,1)} %get-tuple-element.110.refs_0_), channel_id=1, source_target_pairs={{0,1},{1,0},{2,3},{3,2},{4,5},{5,4},{6,7},{7,6},{8,9},{9,8},{10,11... | collective-permute-start | bytes 3145736 | tf_op jit(solution)/shard_map/ppermute | solution.py:304
  79.8 32.3 %collective-permute-start.11 = (bf16[2,4,128,512]{3,2,1,0:T(8,128)(2,1)}, bf16[2,4,128,512]{3,2,1,0:T(8,128)(2,1)}, u32[]{:S(2)}, u32[]{:S(2)}) collective-permute-start(bf16[2,4,128,512]{3,2,1,0:T(8,128)(2,1)} %get-tuple-element.111.refs_2_), channel_id=1, source_target_pairs={{0,4},{1,5},{2,6},{3,7},{4,0},{5,1},{6,2},{7,3},{8,12},{9,13},{10,... | collective-permute-start | bytes 3145736 | tf_op jit(solution)/shard_map/ppermute | solution.py:304
  92.0 22.8 %copy-start.7 = (bf16[592,1024]{1,0:T(8,128)(2,1)S(1)}, bf16[592,1024]{1,0:T(8,128)(2,1)}, u32[]{:S(2)}) copy-start(bf16[592,1024]{1,0:T(8,128)(2,1)} %copy-done.5) | copy-start | bytes 3637252
  92.0 22.8 %copy-start.29 = (bf16[592,1024]{1,0:T(8,128)(2,1)S(1)}, bf16[592,1024]{1,0:T(8,128)(2,1)}, u32[]{:S(2)}) copy-start(bf16[592,1024]{1,0:T(8,128)(2,1)} %copy-done.27) | copy-start | bytes 3637252
  114.8 21.9 %copy-start.36 = (bf16[4,2,128,512]{3,2,1,0:T(8,128)(2,1)}, bf16[4,2,128,512]{3,2,1,0:T(8,128)(2,1)S(1)}, u32[]{:S(2)}) copy-start(bf16[4,2,128,512]{3,2,1,0:T(8,128)(2,1)S(1)} %get-tuple-element.118) | copy-start | bytes 3145732
  128.7 7.9 %collective-permute-start.12 = (bf16[592,1024]{1,0:T(8,128)(2,1)S(1)}, bf16[592,1024]{1,0:T(8,128)(2,1)S(1)}, u32[]{:S(2)}, u32[]{:S(2)}) collective-permute-start(bf16[592,1024]{1,0:T(8,128)(2,1)S(1)} %convolution_convert_fusion), channel_id=1, source_target_pairs={{0,2},{1,3},{2,0},{3,1},{4,6},{5,7},{6,4},{7,5},{8,10},{9,11},{10,... | collective-permute-start | bytes 3637256 | tf_op jit(solution)/shard_map/ppermute | solution.py:304
  139.8 3.3 collective-permute-start.13
  172.3 26.0 %collective-permute-start.15 = (bf16[2,512,512]{2,1,0:T(8,128)(2,1)S(1)}, bf16[2,512,512]{2,1,0:T(8,128)(2,1)}, u32[]{:S(2)}, u32[]{:S(2)}) collective-permute-start(bf16[2,512,512]{2,1,0:T(8,128)(2,1)S(1)} %get-tuple-element.123), channel_id=1, source_target_pairs={{0,1},{1,0},{2,3},{3,2},{4,5},{5,4},{6,7},{7,6},{8,9},{9,8},{10,11... | collective-permute-start | bytes 3145736 | tf_op jit(solution)/shard_map/ppermute | solution.py:304
  174.0 24.9 %collective-permute-start.16 = (bf16[2,512,512]{2,1,0:T(8,128)(2,1)S(1)}, bf16[2,512,512]{2,1,0:T(8,128)(2,1)}, u32[]{:S(2)}, u32[]{:S(2)}) collective-permute-start(bf16[2,512,512]{2,1,0:T(8,128)(2,1)S(1)} %get-tuple-element.124), channel_id=1, source_target_pairs={{0,4},{1,5},{2,6},{3,7},{4,0},{5,1},{6,2},{7,3},{8,12},{9,13},{10,... | collective-permute-start | bytes 3145736 | tf_op jit(solution)/shard_map/ppermute | solution.py:304
  208.9 8.3 %collective-permute-start.17 = (bf16[592,1024]{1,0:T(8,128)(2,1)}, bf16[592,1024]{1,0:T(8,128)(2,1)}, u32[]{:S(2)}, u32[]{:S(2)}) collective-permute-start(bf16[592,1024]{1,0:T(8,128)(2,1)} %get-tuple-element.138), channel_id=1, source_target_pairs={{0,2},{1,3},{2,0},{3,1},{4,6},{5,7},{6,4},{7,5},{8,10},{9,11},{10,... | collective-permute-start | bytes 3637256 | tf_op jit(solution)/shard_map/ppermute | solution.py:304
  208.9 32.7 %collective-permute-start.19 = (bf16[2,512,512]{2,1,0:T(8,128)(2,1)}, bf16[2,512,512]{2,1,0:T(8,128)(2,1)}, u32[]{:S(2)}, u32[]{:S(2)}) collective-permute-start(bf16[2,512,512]{2,1,0:T(8,128)(2,1)} %copy-done.39), channel_id=1, source_target_pairs={{0,1},{1,0},{2,3},{3,2},{4,5},{5,4},{6,7},{7,6},{8,9},{9,8},{10,11... | collective-permute-start | bytes 3145736 | tf_op jit(solution)/shard_map/ppermute | solution.py:304
  209.4 32.2 %collective-permute-start.20 = (bf16[2,512,512]{2,1,0:T(8,128)(2,1)}, bf16[2,512,512]{2,1,0:T(8,128)(2,1)}, u32[]{:S(2)}, u32[]{:S(2)}) collective-permute-start(bf16[2,512,512]{2,1,0:T(8,128)(2,1)} %copy-done.38), channel_id=1, source_target_pairs={{0,4},{1,5},{2,6},{3,7},{4,0},{5,1},{6,2},{7,3},{8,12},{9,13},{10,... | collective-permute-start | bytes 3145736 | tf_op jit(solution)/shard_map/ppermute | solution.py:304
  213.6 32.5 %collective-permute-start.21 = (bf16[512,512]{1,0:T(8,128)(2,1)S(1)}, bf16[512,512]{1,0:T(8,128)(2,1)S(1)}, u32[]{:S(2)}, u32[]{:S(2)}) collective-permute-start(bf16[512,512]{1,0:T(8,128)(2,1)S(1)} %fusion.39), channel_id=1, source_target_pairs={{0,4},{1,5},{2,6},{3,7},{4,0},{5,1},{6,2},{7,3},{8,12},{9,13},{10,... | collective-permute-start | bytes 1572872 | tf_op jit(solution)/shard_map/ppermute | solution.py:304
  215.5 30.6 %collective-permute-start.22 = (bf16[512,512]{1,0:T(8,128)(2,1)S(1)}, bf16[512,512]{1,0:T(8,128)(2,1)S(1)}, u32[]{:S(2)}, u32[]{:S(2)}) collective-permute-start(bf16[512,512]{1,0:T(8,128)(2,1)S(1)} %fusion.40), channel_id=1, source_target_pairs={{0,1},{1,0},{2,3},{3,2},{4,5},{5,4},{6,7},{7,6},{8,9},{9,8},{10,11... | collective-permute-start | bytes 1572872 | tf_op jit(solution)/shard_map/ppermute | solution.py:304
  224.7 30.2 %collective-permute-start.18 = (bf16[592,1024]{1,0:T(8,128)(2,1)S(1)}, bf16[592,1024]{1,0:T(8,128)(2,1)S(1)}, u32[]{:S(2)}, u32[]{:S(2)}) collective-permute-start(bf16[592,1024]{1,0:T(8,128)(2,1)S(1)} %get-tuple-element.257.own_ref), channel_id=1, source_target_pairs={{0,2},{1,3},{2,0},{3,1},{4,6},{5,7},{6,4},{7,5},{8,10},{9,11},{10,... | collective-permute-start | bytes 3637256 | tf_op jit(solution)/shard_map/ppermute | solution.py:304
  247.5 27.3 %collective-permute-start.23 = (bf16[512,512]{1,0:T(8,128)(2,1)S(1)}, bf16[512,512]{1,0:T(8,128)(2,1)S(1)}, u32[]{:S(2)}, u32[]{:S(2)}) collective-permute-start(bf16[512,512]{1,0:T(8,128)(2,1)S(1)} %fusion.37), channel_id=1, source_target_pairs={{0,4},{1,5},{2,6},{3,7},{4,0},{5,1},{6,2},{7,3},{8,12},{9,13},{10,... | collective-permute-start | bytes 1572872 | tf_op jit(solution)/shard_map/ppermute | solution.py:304
  250.1 24.6 %collective-permute-start.24 = (bf16[512,512]{1,0:T(8,128)(2,1)S(1)}, bf16[512,512]{1,0:T(8,128)(2,1)S(1)}, u32[]{:S(2)}, u32[]{:S(2)}) collective-permute-start(bf16[512,512]{1,0:T(8,128)(2,1)S(1)} %fusion.38), channel_id=1, source_target_pairs={{0,1},{1,0},{2,3},{3,2},{4,5},{5,4},{6,7},{7,6},{8,9},{9,8},{10,11... | collective-permute-start | bytes 1572872 | tf_op jit(solution)/shard_map/ppermute | solution.py:304
  253.2 21.5 %collective-permute-start.25 = (bf16[2,128,512]{2,1,0:T(8,128)(2,1)S(1)}, bf16[2,128,512]{2,1,0:T(8,128)(2,1)S(1)}, u32[]{:S(2)}, u32[]{:S(2)}) collective-permute-start(bf16[2,128,512]{2,1,0:T(8,128)(2,1)S(1)} %get-tuple-element.148), channel_id=1, source_target_pairs={{0,8},{1,9},{2,10},{3,11},{4,12},{5,13},{6,14},{7,15},{8,0},{9,1},... | collective-permute-start | bytes 786440 | tf_op jit(solution)/shard_map/ppermute | solution.py:304
  253.3 21.5 %collective-permute-start.26 = (bf16[2,128,512]{2,1,0:T(8,128)(2,1)S(1)}, bf16[2,128,512]{2,1,0:T(8,128)(2,1)S(1)}, u32[]{:S(2)}, u32[]{:S(2)}) collective-permute-start(bf16[2,128,512]{2,1,0:T(8,128)(2,1)S(1)} %get-tuple-element.149), channel_id=1, source_target_pairs={{0,16},{1,17},{2,18},{3,19},{4,20},{5,21},{6,22},{7,23},{8,24},{9,... | collective-permute-start | bytes 786440 | tf_op jit(solution)/shard_map/ppermute | solution.py:304
  254.9 19.8 %collective-permute-start.27 = (bf16[2,128,512]{2,1,0:T(8,128)(2,1)S(1)}, bf16[2,128,512]{2,1,0:T(8,128)(2,1)S(1)}, u32[]{:S(2)}, u32[]{:S(2)}) collective-permute-start(bf16[2,128,512]{2,1,0:T(8,128)(2,1)S(1)} %get-tuple-element.150), channel_id=1, source_target_pairs={{0,24},{1,25},{2,26},{3,27},{4,28},{5,29},{6,30},{7,31},{8,16},{9,... | collective-permute-start | bytes 786440 | tf_op jit(solution)/shard_map/ppermute | solution.py:304
  292.4 3.3 collective-permute-start.30
  292.5 25.8 %collective-permute-start.28 = (bf16[2,512,512]{2,1,0:T(8,128)(2,1)}, bf16[2,512,512]{2,1,0:T(8,128)(2,1)S(1)}, u32[]{:S(2)}, u32[]{:S(2)}) collective-permute-start(bf16[2,512,512]{2,1,0:T(8,128)(2,1)} %get-tuple-element.159), channel_id=1, source_target_pairs={{0,1},{1,0},{2,3},{3,2},{4,5},{5,4},{6,7},{7,6},{8,9},{9,8},{10,11... | collective-permute-start | bytes 3145736 | tf_op jit(solution)/shard_map/ppermute | solution.py:304
  293.2 25.4 %collective-permute-start.29 = (bf16[2,512,512]{2,1,0:T(8,128)(2,1)}, bf16[2,512,512]{2,1,0:T(8,128)(2,1)S(1)}, u32[]{:S(2)}, u32[]{:S(2)}) collective-permute-start(bf16[2,512,512]{2,1,0:T(8,128)(2,1)} %get-tuple-element.160), channel_id=1, source_target_pairs={{0,4},{1,5},{2,6},{3,7},{4,0},{5,1},{6,2},{7,3},{8,12},{9,13},{10,... | collective-permute-start | bytes 3145736 | tf_op jit(solution)/shard_map/ppermute | solution.py:304
  301.2 1.3 collective-permute-start.31
  302.5 16.1 %collective-permute-start.32 = (f32[12288]{0:T(1024)S(1)}, f32[12288]{0:T(1024)S(1)}, u32[]{:S(2)}, u32[]{:S(2)}) collective-permute-start(f32[12288]{0:T(1024)S(1)} %add.270), channel_id=1, source_target_pairs={{0,8},{1,9},{2,10},{3,11},{4,12},{5,13},{6,14},{7,15},{8,0},{9,1},... | collective-permute-start | bytes 147464 | tf_op jit(solution)/shard_map/ppermute | solution.py:304
  305.9 12.8 %collective-permute-start.33 = (f32[12288]{0:T(1024)S(1)}, f32[12288]{0:T(1024)S(1)}, u32[]{:S(2)}, u32[]{:S(2)}) collective-permute-start(f32[12288]{0:T(1024)S(1)} %add.270), channel_id=1, source_target_pairs={{0,16},{1,17},{2,18},{3,19},{4,20},{5,21},{6,22},{7,23},{8,24},{9,... | collective-permute-start | bytes 147464 | tf_op jit(solution)/shard_map/ppermute | solution.py:304
  306.1 12.5 %collective-permute-start.34 = (f32[12288]{0:T(1024)S(1)}, f32[12288]{0:T(1024)S(1)}, u32[]{:S(2)}, u32[]{:S(2)}) collective-permute-start(f32[12288]{0:T(1024)S(1)} %add.270), channel_id=1, source_target_pairs={{0,24},{1,25},{2,26},{3,27},{4,28},{5,29},{6,30},{7,31},{8,16},{9,... | collective-permute-start | bytes 147464 | tf_op jit(solution)/shard_map/ppermute | solution.py:304
  330.3 7.7 %collective-permute-start.35 = (bf16[592,1024]{1,0:T(8,128)(2,1)}, bf16[592,1024]{1,0:T(8,128)(2,1)}, u32[]{:S(2)}, u32[]{:S(2)}) collective-permute-start(bf16[592,1024]{1,0:T(8,128)(2,1)} %get-tuple-element.170), channel_id=1, source_target_pairs={{0,2},{1,3},{2,0},{3,1},{4,6},{5,7},{6,4},{7,5},{8,10},{9,11},{10,... | collective-permute-start | bytes 3637256 | tf_op jit(solution)/shard_map/ppermute | solution.py:304
  330.4 15.4 %collective-permute-start.39 = (bf16[2,128,512]{2,1,0:T(8,128)(2,1)}, bf16[2,128,512]{2,1,0:T(8,128)(2,1)S(1)}, u32[]{:S(2)}, u32[]{:S(2)}) collective-permute-start(bf16[2,128,512]{2,1,0:T(8,128)(2,1)} %copy-done.42), channel_id=1, source_target_pairs={{0,8},{1,9},{2,10},{3,11},{4,12},{5,13},{6,14},{7,15},{8,0},{9,1},... | collective-permute-start | bytes 786440 | tf_op jit(solution)/shard_map/ppermute | solution.py:304
  333.9 21.5 %collective-permute-start.40 = (bf16[2,128,512]{2,1,0:T(8,128)(2,1)}, bf16[2,128,512]{2,1,0:T(8,128)(2,1)S(1)}, u32[]{:S(2)}, u32[]{:S(2)}) collective-permute-start(bf16[2,128,512]{2,1,0:T(8,128)(2,1)} %copy-done.41), channel_id=1, source_target_pairs={{0,16},{1,17},{2,18},{3,19},{4,20},{5,21},{6,22},{7,23},{8,24},{9,... | collective-permute-start | bytes 786440 | tf_op jit(solution)/shard_map/ppermute | solution.py:304
  334.4 22.3 %collective-permute-start.36 = (bf16[512,512]{1,0:T(8,128)(2,1)}, bf16[512,512]{1,0:T(8,128)(2,1)S(1)}, u32[]{:S(2)}, u32[]{:S(2)}) collective-permute-start(bf16[512,512]{1,0:T(8,128)(2,1)} %fusion.41), channel_id=1, source_target_pairs={{0,4},{1,5},{2,6},{3,7},{4,0},{5,1},{6,2},{7,3},{8,12},{9,13},{10,... | collective-permute-start | bytes 1572872 | tf_op jit(solution)/shard_map/ppermute | solution.py:304
  334.8 22.0 %collective-permute-start.37 = (bf16[512,512]{1,0:T(8,128)(2,1)}, bf16[512,512]{1,0:T(8,128)(2,1)S(1)}, u32[]{:S(2)}, u32[]{:S(2)}) collective-permute-start(bf16[512,512]{1,0:T(8,128)(2,1)} %fusion.42), channel_id=1, source_target_pairs={{0,1},{1,0},{2,3},{3,2},{4,5},{5,4},{6,7},{7,6},{8,9},{9,8},{10,11... | collective-permute-start | bytes 1572872 | tf_op jit(solution)/shard_map/ppermute | solution.py:304
  338.0 18.8 %collective-permute-start.41 = (bf16[2,128,512]{2,1,0:T(8,128)(2,1)}, bf16[2,128,512]{2,1,0:T(8,128)(2,1)S(1)}, u32[]{:S(2)}, u32[]{:S(2)}) collective-permute-start(bf16[2,128,512]{2,1,0:T(8,128)(2,1)} %copy-done.40), channel_id=1, source_target_pairs={{0,24},{1,25},{2,26},{3,27},{4,28},{5,29},{6,30},{7,31},{8,16},{9,... | collective-permute-start | bytes 786440 | tf_op jit(solution)/shard_map/ppermute | solution.py:304
  343.1 21.8 %copy-start.61 = (bf16[592,1024]{1,0:T(8,128)(2,1)}, bf16[592,1024]{1,0:T(8,128)(2,1)S(1)}, u32[]{:S(2)}) copy-start(bf16[592,1024]{1,0:T(8,128)(2,1)S(1)} %multiply_convert_fusion) | copy-start | bytes 3637252
  343.1 20.6 %copy-start.31 = (f32[2,128,512]{2,1,0:T(8,128)S(1)}, f32[2,128,512]{2,1,0:T(8,128)}, u32[]{:S(2)}) copy-start(f32[2,128,512]{2,1,0:T(8,128)} %copy-done.30) | copy-start | bytes 1572868
  343.1 20.6 %copy-start.69 = (bf16[2,128,512]{2,1,0:T(8,128)(2,1)S(1)}, bf16[2,128,512]{2,1,0:T(8,128)(2,1)}, u32[]{:S(2)}) copy-start(bf16[2,128,512]{2,1,0:T(8,128)(2,1)} %copy-done.68) | copy-start | bytes 786436
  343.1 20.8 %copy-start.33 = (f32[2,128,512]{2,1,0:T(8,128)S(1)}, f32[2,128,512]{2,1,0:T(8,128)}, u32[]{:S(2)}) copy-start(f32[2,128,512]{2,1,0:T(8,128)} %copy-done.32) | copy-start | bytes 1572868
  345.8 18.3 %collective-permute-start.42 = (bf16[289,1024]{1,0:T(8,128)(2,1)S(1)}, bf16[289,1024]{1,0:T(8,128)(2,1)S(1)}, u32[]{:S(2)}, u32[]{:S(2)}) collective-permute-start(bf16[289,1024]{1,0:T(8,128)(2,1)S(1)} %slice.292), channel_id=1, source_target_pairs={{0,1},{1,0},{2,3},{3,2},{4,5},{5,4},{6,7},{7,6},{8,9},{9,8},{10,11... | collective-permute-start | bytes 1775624 | tf_op jit(solution)/shard_map/ppermute | solution.py:304
  355.4 13.6 %collective-permute-start.43 = (f32[12288]{0:T(1024)S(1)}, f32[12288]{0:T(1024)S(1)}, u32[]{:S(2)}, u32[]{:S(2)}) collective-permute-start(f32[12288]{0:T(1024)S(1)} %add_add_fusion), channel_id=1, source_target_pairs={{0,1},{1,0},{2,3},{3,2},{4,5},{5,4},{6,7},{7,6},{8,9},{9,8},{10,11... | collective-permute-start | bytes 147464 | tf_op jit(solution)/shard_map/ppermute | solution.py:304
  357.1 32.4 %collective-permute-start.45 = (bf16[2,128,512]{2,1,0:T(8,128)(2,1)S(1)}, bf16[2,128,512]{2,1,0:T(8,128)(2,1)S(1)}, u32[]{:S(2)}, u32[]{:S(2)}) collective-permute-start(bf16[2,128,512]{2,1,0:T(8,128)(2,1)S(1)} %get-tuple-element.175), channel_id=1, source_target_pairs={{0,8},{1,9},{2,10},{3,11},{4,12},{5,13},{6,14},{7,15},{8,0},{9,1},... | collective-permute-start | bytes 786440 | tf_op jit(solution)/shard_map/ppermute | solution.py:304
  361.3 28.2 %collective-permute-start.46 = (bf16[2,128,512]{2,1,0:T(8,128)(2,1)S(1)}, bf16[2,128,512]{2,1,0:T(8,128)(2,1)}, u32[]{:S(2)}, u32[]{:S(2)}) collective-permute-start(bf16[2,128,512]{2,1,0:T(8,128)(2,1)S(1)} %get-tuple-element.176), channel_id=1, source_target_pairs={{0,16},{1,17},{2,18},{3,19},{4,20},{5,21},{6,22},{7,23},{8,24},{9,... | collective-permute-start | bytes 786440 | tf_op jit(solution)/shard_map/ppermute | solution.py:304
  361.8 27.7 %collective-permute-start.47 = (bf16[2,128,512]{2,1,0:T(8,128)(2,1)S(1)}, bf16[2,128,512]{2,1,0:T(8,128)(2,1)}, u32[]{:S(2)}, u32[]{:S(2)}) collective-permute-start(bf16[2,128,512]{2,1,0:T(8,128)(2,1)S(1)} %get-tuple-element.177), channel_id=1, source_target_pairs={{0,24},{1,25},{2,26},{3,27},{4,28},{5,29},{6,30},{7,31},{8,16},{9,... | collective-permute-start | bytes 786440 | tf_op jit(solution)/shard_map/ppermute | solution.py:304
  364.1 6.2 %collective-permute-start.48 = (bf16[2,64,512]{2,1,0:T(8,128)(2,1)S(1)}, bf16[2,64,512]{2,1,0:T(8,128)(2,1)S(1)}, u32[]{:S(2)}, u32[]{:S(2)}) collective-permute-start(bf16[2,64,512]{2,1,0:T(8,128)(2,1)S(1)} %fusion.49), channel_id=1, source_target_pairs={{0,2},{1,3},{2,0},{3,1},{4,6},{5,7},{6,4},{7,5},{8,10},{9,11},{10,... | collective-permute-start | bytes 393224 | tf_op jit(solution)/shard_map/ppermute | solution.py:304
  369.0 16.4 %collective-permute-start.38 = (bf16[289,1024]{1,0:T(8,128)(2,1)}, bf16[289,1024]{1,0:T(8,128)(2,1)}, u32[]{:S(2)}, u32[]{:S(2)}) collective-permute-start(bf16[289,1024]{1,0:T(8,128)(2,1)} %slice.200), channel_id=1, source_target_pairs={{0,1},{1,0},{2,3},{3,2},{4,5},{5,4},{6,7},{7,6},{8,9},{9,8},{10,11... | collective-permute-start | bytes 1775624 | tf_op jit(solution)/shard_map/ppermute | solution.py:304
  370.3 2.1 collective-permute-start.49
  372.4 16.5 %collective-permute-start.44 = (f32[12288]{0:T(1024)S(1)}, f32[12288]{0:T(1024)S(1)}, u32[]{:S(2)}, u32[]{:S(2)}) collective-permute-start(f32[12288]{0:T(1024)S(1)} %add.280), channel_id=1, source_target_pairs={{0,4},{1,5},{2,6},{3,7},{4,0},{5,1},{6,2},{7,3},{8,12},{9,13},{10,... | collective-permute-start | bytes 147464 | tf_op jit(solution)/shard_map/ppermute | solution.py:304
  390.7 1.4 collective-permute-start.50
  (83 other events, 534.1 us)
Sparse Core Ops, SparseCore 0:
  12.2 143.3 all-gather.1

commit v7 on v6

--- a/solution.py
+++ b/solution.py
@@ -637,7 +637,7 @@
         compiler_params=pltpu.CompilerParams(vmem_limit_bytes=VMEM_ROOM),
         cost_estimate=SMALL,
     )(places, left, gathered)
-    return own + exchange(send, far_core=1).astype(jnp.float32)
+    return own, send
 
 
 def mat(left, right):
@@ -701,7 +701,7 @@
         outs[1][0] = made
 
 
-def weight_pieces(operands, send):
+def weight_pieces(operands, send, cost=None):
     line, rows = operands[0][0].shape[1:]
     if send:
         first = lambda i: jnp.minimum(i, 1)
@@ -730,7 +730,7 @@
         ],
         out_shape=[jax.ShapeDtypeStruct((2, line, wide), LOW)] * 2,
         compiler_params=pltpu.CompilerParams(vmem_limit_bytes=VMEM_ROOM),
-        cost_estimate=weight_cost(operands),
+        cost_estimate=cost or weight_cost(operands),
     )(*arrays)
 
 
@@ -1042,20 +1042,22 @@
     middle = row_mask * (resid + attended)
     second, unit_two, spread_two = flat_norm(middle, gain_two, shift_two)
     second_pair = pair_of(second.astype(LOW))
-    active, slope = up_call(places, second_pair, gathered, up_shift)
+    second_turned = turn(places, second_pair)
+    up_pair = after(second_pair, second_turned)
+    active, slope = up_call(places, up_pair, gathered, up_shift)
 
     lower_sends = weight_pieces([(fed_turned, active)], True)
     lower_first = scatter_first(lower_sends)
     lower_keeps = weight_pieces([(fed_turned, after(active, *lower_sends))], False)
     fed_late = after(fed_pair, *lower_keeps)
     hidden_grad, up_bias_sums = hidden_call(places, fed_late, gathered, slope)
-    second_turned = turn(places, second_pair)
     up_sends = weight_pieces([(second_turned, hidden_grad)], True)
     up_first = scatter_first(up_sends)
     lower_first = after(lower_first, *up_sends)
     lower_second = scatter_second(scatter_adds(lower_keeps, lower_first))
     hidden_late = after(hidden_grad, *lower_first)
-    second_grad = down_call(places, hidden_late, gathered, 0)
+    second_grad, second_send = down_call(places, hidden_late, gathered, 0)
+    second_grad = second_grad + exchange(second_send, far_core=1).astype(jnp.float32)
     middle_back, gain_two_grad, shift_two_grad = flat_norm_back(
         second_grad, unit_two, spread_two, gain_two
     )
@@ -1079,12 +1081,24 @@
     up_line = scatter_line(up_keeps, up_first, up_second)
     up_z = scatter_z(up_line)
     back = after(back, *up_line)
-    last_sends = weight_pieces([(normed_turned, back), (attended_turned, mixed)], True)
+    last_sends = weight_pieces(
+        [(normed_turned, back), (attended_turned, mixed)], True, SMALL
+    )
     last_first = scatter_first(last_sends)
     back_late = after(back, *last_sends)
-    last_keeps = weight_pieces([(normed_turned, back_late), (attended_turned, mixed)], False)
-    back_late = after(back_late, *last_keeps)
-    normed_far = exchange(mat_far(back_late[rows:], qkv_full).astype(LOW), far_core=1)
+    last_keeps = weight_pieces(
+        [(normed_turned, back_late), (attended_turned, mixed)], False, SMALL
+    )
+    fed, fed_send = down_call(places, after(active, *last_keeps), gathered, 1)
+    back_late = after(back_late, fed, fed_send, *up_z)
+    normed_send = mat_far(back_late[rows:], qkv_full).astype(LOW)
+    last_first = after(last_first, normed_send)
+    last_adds = scatter_adds(last_keeps, last_first)
+    last_second = scatter_second(last_adds)
+    back_late = after(back_late, *last_adds)
+    normed_far = exchange(normed_send, far_core=1)
+    fed = fed + exchange(fed_send, far_core=1).astype(jnp.float32)
+    layer_own = (row_mask * (middle + fed + down_bias.astype(jnp.float32))).astype(LOW)
     normed_grad = mat_far(back_late[:rows], qkv_full) + normed_far.astype(jnp.float32)
     first_back, gain_one_grad, shift_one_grad = flat_norm_back(
         normed_grad, unit_one, spread_one, gain_one
@@ -1105,20 +1119,16 @@
         ]
     )
     vector, vectors = vector_first(vector)
-    last_first = after(last_first, *last_keeps, images_own, *vectors)
-    last_adds = scatter_adds(last_keeps, last_first)
-    last_second = scatter_second(last_adds)
-    fed = down_call(places, after(active, *last_adds), gathered, 1)
-    layer_own = (row_mask * (middle + fed + down_bias.astype(jnp.float32))).astype(LOW)
-    vector = after(vector, *last_adds) + vectors[0] + vectors[1] + vectors[2]
-    vector = vector + after(exchange(vector, far_y=1), layer_own)
-    vector_x = exchange(vector, far_x=1)
-    last_line = scatter_line(last_keeps, last_first, after(last_second, layer_own, *up_z))
+    last_line = scatter_line(last_keeps, last_first, after(last_second, images_own))
     last_z = scatter_z(last_line)
-    images_far = exchange(after(images_own, *last_adds)[half : half + strip].astype(LOW), far_y=1)
-    layer_far = exchange(after(layer_own, *last_second)[half : half + strip], far_y=1)
-    vector = vector + after(vector_x, *last_line, images_far, layer_far)
-    lower_z, up_z = after((tuple(lower_z), tuple(up_z)), *last_line)
+    images_far = exchange(
+        after(images_own, *last_second)[half : half + strip].astype(LOW), far_y=1
+    )
+    layer_far = exchange(after(layer_own, *last_adds)[half : half + strip], far_y=1)
+    vector = vector + vectors[0] + vectors[1] + vectors[2]
+    vector = vector + after(exchange(vector, far_x=1), images_far, *last_line)
+    vector = vector + after(exchange(vector, far_y=1), layer_far)
+    lower_z, up_z = after((tuple(lower_z), tuple(up_z)), *last_line, images_far)
     lower_owned = full_columns(scatter_last(lower_line[0], lower_z, core)).T
     upper_owned = full_columns(scatter_last(up_line[0], up_z, core))
 

time: 407 us -> 383 us (0.941)
  waiting for transfers between devices: 112 us -> 92.7 us
    ppermute x51, waiting for transfers between devices: 100 us -> 85 us  [exchange(): return lax.ppermute(value, BOTH, pairs)]
    all_gather x1, waiting for transfers between devices: 12.5 us -> 7.68 us  [whole_images(): lax.all_gather(feed.reshape(2 * depth, -1), BOTH, axis=0, tiled=True, axi...]
    unnamed x203 -> x195, local copies, waits for them, and re-layouts: 19.9 us -> 23.7 us
  transfers between devices with their start and end apart: 52 -> 52, of which waited for: 21 -> 20; matrix products, arithmetic and copies ran while one was open for 15% -> 16% of each run, Pallas kernels for 21% -> 26%
where the time goes in v7:
time: 383 us; the launch traced here: 377 us
  Pallas kernels  132 us (34%)
  waiting for transfers between devices  92.7 us (24%)
  starting transfers between devices  53.4 us (14%)
  local copies, waits for them, and re-layouts  37.9 us (10%)
  other arithmetic  28.5 us (7%)
  between operations  16.8 us (4%)
  matrix products  16 us (4%)
    ppermute x51, waiting for transfers between devices, exchange(): return lax.ppermute(value, BOTH, pairs)  85 us
    ppermute x51, starting transfers between devices, exchange(): return lax.ppermute(value, BOTH, pairs)  53.4 us
    pallas_call x2, Pallas kernels, attend_back_image(): pl.pallas_call(kernel, grid=(blocks,), in_specs=[pl.BlockSpec((rows, 3 *...  29.2 us
    pallas_call x6, Pallas kernels, weight_pieces(): pl.pallas_call(kernel, grid=(4,), in_specs=specs, out_specs=[pl.BlockSpec...  26.6 us
    unnamed x195, local copies, waits for them, and re-layouts  23.7 us
    pallas_call x2, Pallas kernels, down_call(): pl.pallas_call(down_kernel, grid_spec=pltpu.PrefetchScalarGridSpec(num_sc...  18.1 us
    pallas_call x2, Pallas kernels, attend_image(): pl.pallas_call(kernel, grid=(blocks,), in_specs=[pl.BlockSpec((rows, 3 *...  15.4 us
    pallas_call x1, Pallas kernels, up_call(): pl.pallas_call(up_kernel, grid_spec=pltpu.PrefetchScalarGridSpec(num_scal...  12.3 us
  transfers between devices with their start and end apart: 52, of which 20 were waited for; matrix products, arithmetic and copies ran while one was open for 16% of the time, Pallas kernels for 26%

profile of v7, /device:TPU:0, one launch (start us, length us, event | category | flops | bytes accessed | tf_op | source)
XLA Modules:
  0.0 376.8 jit_solution(4277973538384960178)
XLA Ops:
  13.9 3.0 collective-permute-start.3
  16.9 2.6 collective-permute-start.4
  20.4 2.9 copy.72
  24.7 1.8 collective-permute-start.1
  26.8 3.8 %collective-permute-done.3.refs_1_ = bf16[2,128,512]{2,1,0:T(8,128)(2,1)S(1)} collective-permute-done((bf16[2,128,512]{2,1,0:T(8,128)(2,1)S(1)}, bf16[2,128,512]{2,1,0:T(8,128)(2,1)S(1)}, u32[]{:S(2)}, u32[]{:S(2)}) %collective-permute-start.3) | collective-permute-done | bytes 262176 | tf_op jit(solution)/shard_map/ppermute | solution.py:304
  30.7 7.1 %collective-permute-done.4.refs_2_ = bf16[2,128,512]{2,1,0:T(8,128)(2,1)S(1)} collective-permute-done((bf16[2,128,512]{2,1,0:T(8,128)(2,1)S(1)}, bf16[2,128,512]{2,1,0:T(8,128)(2,1)S(1)}, u32[]{:S(2)}, u32[]{:S(2)}) %collective-permute-start.4) | collective-permute-done | bytes 262176 | tf_op jit(solution)/shard_map/ppermute | solution.py:304
  37.8 5.3 %collective-permute-done.5.refs_3_ = bf16[2,128,512]{2,1,0:T(8,128)(2,1)S(1)} collective-permute-done((bf16[2,128,512]{2,1,0:T(8,128)(2,1)S(1)}, bf16[2,128,512]{2,1,0:T(8,128)(2,1)S(1)}, u32[]{:S(2)}, u32[]{:S(2)}) %collective-permute-start.5) | collective-permute-done | bytes 262176 | tf_op jit(solution)/shard_map/ppermute | solution.py:304
  43.7 1.6 collective-permute-start.6
  45.3 1.5 collective-permute-start.7
  48.1 8.4 %collective-permute-done.6.refs_1_ = bf16[4,128,512]{2,1,0:T(8,128)(2,1)S(1)} collective-permute-done((bf16[4,128,512]{2,1,0:T(8,128)(2,1)S(1)}, bf16[4,128,512]{2,1,0:T(8,128)(2,1)S(1)}, u32[]{:S(2)}, u32[]{:S(2)}) %collective-permute-start.6) | collective-permute-done | bytes 524320 | tf_op jit(solution)/shard_map/ppermute | solution.py:304
  56.4 17.8 %collective-permute-done.7.refs_3_ = bf16[4,128,512]{2,1,0:T(8,128)(2,1)S(1)} collective-permute-done((bf16[4,128,512]{2,1,0:T(8,128)(2,1)S(1)}, bf16[4,128,512]{2,1,0:T(8,128)(2,1)S(1)}, u32[]{:S(2)}, u32[]{:S(2)}) %collective-permute-start.7) | collective-permute-done | bytes 524320 | tf_op jit(solution)/shard_map/ppermute | solution.py:304
  74.2 2.0 shard_map.306
  79.8 1.7 collective-permute-start.11
  85.4 2.2 shard_map.307.refs_0_
  87.6 3.3 shard_map.308.refs_0_
  90.9 1.5 copy-done.14
  92.4 18.7 %collective-permute-done.10.refs_1_ = bf16[2,4,128,512]{3,2,1,0:T(8,128)(2,1)} collective-permute-done((bf16[2,4,128,512]{3,2,1,0:T(8,128)(2,1)}, bf16[2,4,128,512]{3,2,1,0:T(8,128)(2,1)}, u32[]{:S(2)}, u32[]{:S(2)}) %collective-permute-start.10) | collective-permute-done | bytes 1048608 | tf_op jit(solution)/shard_map/ppermute | solution.py:304
  112.1 2.7 shard_map.309
  114.8 5.2 %fusion.refs_0_ = bf16[1184,1536]{1,0:T(8,128)(2,1)S(1)} fusion(bf16[1024,1536]{1,0:T(8,128)(2,1)S(1)} %bitcast.187, f32[1536]{0:T(1024)S(1)} %add.250, bf16[592,1024]{1,0:T(8,128)(2,1)S(1)} %copy-done.34, bf16[592,1024]{1,0:T(8,128)(2,1)S(1)} %copy-done.8), kind=kOutput, calls=%fused_computation.1 | convolution fusion | flops 3733028864 | bytes 9213952 | tf_op jit(solution)/shard_map/dot_general | solution.py:644
  120.2 7.7 %shard_map.310 = (bf16[1184,512]{1,0:T(8,128)(2,1)S(1)}, f32[8,8,592]{2,1,0:T(8,128)S(1)}) custom-call(bf16[1184,1536]{1,0:T(8,128)(2,1)S(1)} %fusion.refs_0_, bf16[592,128]{1,0:T(8,128)(2,1)S(1)} %broadcast_in_dim.56.refs_1_), custom_call_target="tpu_custom_call" | custom-call | flops 2871001088 | bytes 2424832 | tf_op jit(solution)/shard_map/pallas_call | solution.py:822
  128.9 7.7 %shard_map.311 = (bf16[1184,512]{1,0:T(8,128)(2,1)S(1)}, f32[8,8,592]{2,1,0:T(8,128)S(1)}) custom-call(bf16[1184,1536]{1,0:T(8,128)(2,1)S(1)} %fusion.refs_0_, bf16[592,128]{1,0:T(8,128)(2,1)S(1)} %broadcast_in_dim.56.refs_1_, bf16[1184,512]{1,0:T(8,128)(2,1)S(1)} %get-tuple-element.121.refs_2_, ...), custom_call_target="tpu_custom_call", output_to_operand_aliasing={{0}: (2, {}), {1}: (3, {})} | custom-call | flops 2871001088 | bytes 2424832 | tf_op jit(solution)/shard_map/pallas_call | solution.py:822
  140.4 2.8 collective-permute-done.13.far_ref
  143.1 3.3 shard_map.312.refs_0_
  146.5 1.5 copy-done.11
  148.0 7.7 %all-gather.2.cloned.1.call-done = bf16[2048,2048]{1,0:T(8,128)(2,1)} async-done(((bf16[128,2048]{1,0:T(8,128)(2,1)}), bf16[2048,2048]{1,0:T(8,128)(2,1)}) %all-gather.2.cloned.1.call-update) | async-done | bytes 8388624 | tf_op jit(solution)/shard_map/all_gather | solution.py:956
  155.7 12.3 %shard_map.313 = (bf16[1184,2048]{1,0:T(8,128)(2,1)S(1)}, bf16[1184,2048]{1,0:T(8,128)(2,1)S(1)}) custom-call(s32[4]{0:T(128)S(1)} %pad_add_fusion.places_ref, bf16[592,1024]{1,0:T(8,128)(2,1)} %add_convert_fusion.own_ref, bf16[592,1024]{1,0:T(8,128)(2,1)} %collective-permute-done.13.far_ref, bf16[8,2,128,2048]{3,2,1,0:T(8,128)(2,1)} %bitcast.194, ...), custom_call_target="tpu_custom_call" | custom-call | flops 4966055936 | bytes 16318464 | tf_op jit(solution)/shard_map/pallas_call | solution.py:539
  168.0 3.9 %shard_map.314 = (bf16[2,512,512]{2,1,0:T(8,128)(2,1)S(1)}, bf16[2,512,512]{2,1,0:T(8,128)(2,1)S(1)}) custom-call(bf16[2,512,1184]{2,1,0:T(8,128)(2,1)S(1)} %copy-done.15, bf16[1184,2048]{1,0:T(8,128)(2,1)S(1)} %get-tuple-element.168.refs_1_.left_ref), custom_call_target="tpu_custom_call" | custom-call | flops 2483027968 | bytes 11796480 | tf_op jit(solution)/shard_map/pallas_call | solution.py:723
  171.9 1.6 collective-permute-start.15
  175.0 3.9 %shard_map.315 = (bf16[2,512,512]{2,1,0:T(8,128)(2,1)S(1)}, bf16[2,512,512]{2,1,0:T(8,128)(2,1)S(1)}) custom-call(bf16[2,512,1184]{2,1,0:T(8,128)(2,1)S(1)} %copy-done.15, bf16[1184,2048]{1,0:T(8,128)(2,1)S(1)} %get-tuple-element.168.refs_1_.left_ref), custom_call_target="tpu_custom_call" | custom-call | flops 2483027968 | bytes 11796480 | tf_op jit(solution)/shard_map/pallas_call | solution.py:723
  181.0 9.9 %shard_map.316 = (bf16[1184,2048]{1,0:T(8,128)(2,1)S(1)}, f32[1,2048]{1,0:T(1,128)S(1)}) custom-call(s32[4]{0:T(128)S(1)} %pad_add_fusion.places_ref, bf16[592,1024]{1,0:T(8,128)(2,1)} %get-tuple-element.132.own_ref, bf16[592,1024]{1,0:T(8,128)(2,1)} %collective-permute-done.9.far_ref, bf16[8,2,128,2048]{3,2,1,0:T(8,128)(2,1)} %bitcast.195, ...), custom_call_target="tpu_custom_call" | custom-call | flops 4966055936 | bytes 16318464 | tf_op jit(solution)/shard_map/pallas_call | solution.py:579
  190.9 3.9 %shard_map.317 = (bf16[2,512,512]{2,1,0:T(8,128)(2,1)S(1)}, bf16[2,512,512]{2,1,0:T(8,128)(2,1)S(1)}) custom-call(bf16[2,512,1184]{2,1,0:T(8,128)(2,1)S(1)} %copy-done.12, bf16[1184,2048]{1,0:T(8,128)(2,1)S(1)} %get-tuple-element.144.refs_1_.left_ref), custom_call_target="tpu_custom_call" | custom-call | flops 2483027968 | bytes 11796480 | tf_op jit(solution)/shard_map/pallas_call | solution.py:723
  198.4 8.5 %shard_map.318 = (f32[592,1024]{1,0:T(8,128)S(1)}, bf16[592,1024]{1,0:T(8,128)(2,1)}) custom-call(s32[4]{0:T(128)S(1)} %pad_add_fusion.places_ref, bf16[1184,2048]{1,0:T(8,128)(2,1)S(1)} %get-tuple-element.144.refs_1_.left_ref, bf16[8,2,128,2048]{3,2,1,0:T(8,128)(2,1)} %bitcast.196), custom_call_target="tpu_custom_call" | custom-call | flops 1024 | bytes 1024 | tf_op jit(solution)/shard_map/pallas_call | solution.py:622
  215.0 1.6 collective-permute-start.22
  216.7 3.3 multiply_reduce_fusion
  220.1 4.1 %convert_reduce_fusion.3 = (f32[1024]{0:T(1024)S(1)}, bf16[592,1024]{1,0:T(8,128)(2,1)S(1)}, f32[592,1024]{1,0:T(8,128)}) fusion(f32[592]{0:T(1024)S(1)} %broadcast_multiply_fusion.2, f32[592,1024]{1,0:T(8,128)S(1)} %copy-done.47, f32[592]{0:T(1024)S(1)} %broadcast_multiply_fusion.4, f32[592]{0:T(1024)S(1)} %broadcast_multiply_fusion.3, ...), kind=kLoop, calls=%fused_computation.27 | loop fusion | flops 11516928 | bytes 10931776 | tf_op jit(solution)/shard_map/reduce_sum | solution.py:897
  226.6 14.7 %shard_map.319.refs_5_ = bf16[1184,1536]{1,0:T(8,128)(2,1)S(1)} custom-call(bf16[1184,1536]{1,0:T(8,128)(2,1)S(1)} %copy-done.45, bf16[592,128]{1,0:T(8,128)(2,1)S(1)} %broadcast_in_dim.56.refs_1_, bf16[592,512]{1,0:T(8,128)(2,1)S(1)} %convolution_convert_fusion.1.refs_2_, bf16[1184,512]{1,0:T(8,128)(2,1)S(1)} %copy-done.10, ...), custom_call_target="tpu_custom_call" | custom-call | flops 7177502720 | bytes 4849664 | tf_op jit(solution)/shard_map/pallas_call | solution.py:856
  241.3 3.9 %shard_map.320 = (bf16[2,512,512]{2,1,0:T(8,128)(2,1)S(1)}, bf16[2,512,512]{2,1,0:T(8,128)(2,1)S(1)}) custom-call(bf16[2,512,1184]{2,1,0:T(8,128)(2,1)S(1)} %copy-done.13, bf16[1184,2048]{1,0:T(8,128)(2,1)S(1)} %bitcast.182), custom_call_target="tpu_custom_call" | custom-call | flops 2483027968 | bytes 11796480 | tf_op jit(solution)/shard_map/pallas_call | solution.py:723
  246.9 1.5 collective-permute-start.23
  249.6 1.5 collective-permute-start.24
  251.6 1.8 collective-permute-start.26
  253.3 2.6 collective-permute-start.27
  256.8 1.6 shard_map.322.refs_2_
  258.4 14.5 %shard_map.323.refs_1_ = bf16[1184,1536]{1,0:T(8,128)(2,1)S(1)} custom-call(bf16[1184,1536]{1,0:T(8,128)(2,1)S(1)} %copy-done.45, bf16[592,128]{1,0:T(8,128)(2,1)S(1)} %broadcast_in_dim.56.refs_1_, bf16[592,512]{1,0:T(8,128)(2,1)S(1)} %convolution_convert_fusion.2.refs_2_, bf16[1184,512]{1,0:T(8,128)(2,1)S(1)} %copy-done.10, ...), custom_call_target="tpu_custom_call", output_to_operand_aliasing={{}: (5, {})} | custom-call | flops 7177502720 | bytes 4849664 | tf_op jit(solution)/shard_map/pallas_call | solution.py:856
  273.7 2.4 shard_map.324
  276.1 5.5 %shard_map.325 = (bf16[2,512,512]{2,1,0:T(8,128)(2,1)S(1)}, bf16[2,512,512]{2,1,0:T(8,128)(2,1)S(1)}) custom-call(bf16[2,512,1184]{2,1,0:T(8,128)(2,1)S(1)} %shard_map.307.refs_0_, bf16[1184,1536]{1,0:T(8,128)(2,1)S(1)} %shard_map.323.refs_1_, bf16[2,512,1184]{2,1,0:T(8,128)(2,1)S(1)} %shard_map.322.refs_2_, bf16[1184,512]{1,0:T(8,128)(2,1)S(1)} %copy-done.10), custom_call_target="tpu_custom_call" | custom-call | flops 1024 | bytes 1024 | tf_op jit(solution)/shard_map/pallas_call | solution.py:723
  282.8 2.9 collective-permute-start.31
  285.8 2.2 collective-permute-start.33
  288.0 5.5 %shard_map.326 = (bf16[2,512,512]{2,1,0:T(8,128)(2,1)S(1)}, bf16[2,512,512]{2,1,0:T(8,128)(2,1)S(1)}) custom-call(bf16[2,512,1184]{2,1,0:T(8,128)(2,1)S(1)} %shard_map.307.refs_0_, bf16[1184,1536]{1,0:T(8,128)(2,1)S(1)} %shard_map.323.refs_1_, bf16[2,512,1184]{2,1,0:T(8,128)(2,1)S(1)} %shard_map.322.refs_2_, bf16[1184,512]{1,0:T(8,128)(2,1)S(1)} %copy-done.10), custom_call_target="tpu_custom_call" | custom-call | flops 1024 | bytes 1024 | tf_op jit(solution)/shard_map/pallas_call | solution.py:723
  293.6 9.6 %shard_map.327 = (f32[592,1024]{1,0:T(8,128)S(1)}, bf16[592,1024]{1,0:T(8,128)(2,1)}) custom-call(s32[4]{0:T(128)S(1)} %pad_add_fusion.places_ref, bf16[1184,2048]{1,0:T(8,128)(2,1)S(1)} %bitcast.180, bf16[8,2,128,2048]{3,2,1,0:T(8,128)(2,1)} %bitcast.197), custom_call_target="tpu_custom_call" | custom-call | flops 1024 | bytes 1024 | tf_op jit(solution)/shard_map/pallas_call | solution.py:622
  303.2 2.3 collective-permute-done.32
  305.5 3.1 fusion.26
  311.9 1.6 collective-permute-start.36
  315.1 2.6 multiply_convert_fusion
  319.4 4.0 %fusion.13 = (f32[1024]{0:T(1024)S(1)}, f32[592]{0:T(1024)S(1)}, f32[592]{0:T(1024)S(1)}, f32[1024]{0:T(1024)S(1)}, f32[592,1024]{1,0:T(8,128)S(1)}) fusion(f32[592]{0:T(1024)S(1)} %add_rsqrt_fusion.1, f32[592]{0:T(1024)S(1)} %broadcast_multiply_fusion.5, bf16[296,1024]{1,0:T(8,128)(2,1)S(1)} %copy-done.54, bf16[296,1024]{1,0:T(8,128)(2,1)S(1)} %copy-done.50, ...), kind=kOutput, calls=%fused_computation.18 | convolution fusion | flops 1871360768 | bytes 9839232 | tf_op jit(solution)/shard_map/dot_general | solution.py:494
  324.8 1.9 collective-permute-start.42
  326.7 3.7 collective-permute-start.41
  330.5 1.5 fusion.12
  333.4 1.6 shard_map.328
  335.1 1.7 collective-permute-start.45
  337.0 2.5 collective-permute-start.47
  339.5 1.9 collective-permute-done.34
  342.3 2.2 copy.92
  345.6 8.2 %collective-permute-done.38 = bf16[289,1024]{1,0:T(8,128)(2,1)S(1)} collective-permute-done((bf16[289,1024]{1,0:T(8,128)(2,1)S(1)}, bf16[289,1024]{1,0:T(8,128)(2,1)S(1)}, u32[]{:S(2)}, u32[]{:S(2)}) %collective-permute-start.38) | collective-permute-done | bytes 591904 | tf_op jit(solution)/shard_map/ppermute | solution.py:304
  355.7 3.2 copy.93
  (391 shorter events, 70.9 us)
Async XLA Ops:
  7.2 148.4 %all-gather.2.cloned.1.call-start = ((), (), s32[]{:S(2)}) async-start(), calls=%async_computation | async-start | bytes 8912896 | tf_op jit(solution)/shard_map/all_gather | solution.py:956
  9.5 1.7 collective-permute-start.14
  12.3 1.4 collective-permute-start
  13.9 16.8 %collective-permute-start.3 = (bf16[2,128,512]{2,1,0:T(8,128)(2,1)S(1)}, bf16[2,128,512]{2,1,0:T(8,128)(2,1)S(1)}, u32[]{:S(2)}, u32[]{:S(2)}) collective-permute-start(bf16[2,128,512]{2,1,0:T(8,128)(2,1)S(1)} %bitcast.183), channel_id=1, source_target_pairs={{0,8},{1,9},{2,10},{3,11},{4,12},{5,13},{6,14},{7,15},{8,0},{9,1},... | collective-permute-start | bytes 786440 | tf_op jit(solution)/shard_map/ppermute | solution.py:304
  16.9 20.9 %collective-permute-start.4 = (bf16[2,128,512]{2,1,0:T(8,128)(2,1)S(1)}, bf16[2,128,512]{2,1,0:T(8,128)(2,1)S(1)}, u32[]{:S(2)}, u32[]{:S(2)}) collective-permute-start(bf16[2,128,512]{2,1,0:T(8,128)(2,1)S(1)} %bitcast.184), channel_id=1, source_target_pairs={{0,16},{1,17},{2,18},{3,19},{4,20},{5,21},{6,22},{7,23},{8,24},{9,... | collective-permute-start | bytes 786440 | tf_op jit(solution)/shard_map/ppermute | solution.py:304
  19.5 23.6 %collective-permute-start.5 = (bf16[2,128,512]{2,1,0:T(8,128)(2,1)S(1)}, bf16[2,128,512]{2,1,0:T(8,128)(2,1)S(1)}, u32[]{:S(2)}, u32[]{:S(2)}) collective-permute-start(bf16[2,128,512]{2,1,0:T(8,128)(2,1)S(1)} %bitcast.185), channel_id=1, source_target_pairs={{0,24},{1,25},{2,26},{3,27},{4,28},{5,29},{6,30},{7,31},{8,16},{9,... | collective-permute-start | bytes 786440 | tf_op jit(solution)/shard_map/ppermute | solution.py:304
  20.4 56.6 %copy-start.48 = (bf16[296,1024]{1,0:T(8,128)(2,1)}, bf16[296,1024]{1,0:T(8,128)(2,1)S(1)}, u32[]{:S(2)}) copy-start(bf16[296,1024]{1,0:T(8,128)(2,1)S(1)} %get-tuple-element.269) | copy-start | bytes 1818628
  20.4 26.4 %copy-start.78 = (bf16[1024]{0:T(1024)(128)(2,1)S(1)}, bf16[1024]{0:T(1024)(128)(2,1)}, u32[]{:S(2)}) copy-start(bf16[1024]{0:T(1024)(128)(2,1)} %param.22) | copy-start | bytes 6148
  20.4 26.4 %copy-start.79 = (bf16[1024]{0:T(1024)(128)(2,1)S(1)}, bf16[1024]{0:T(1024)(128)(2,1)}, u32[]{:S(2)}) copy-start(bf16[1024]{0:T(1024)(128)(2,1)} %param.21) | copy-start | bytes 6148
  20.4 26.4 %copy-start.86 = (s32[2]{0:T(128)S(1)}, s32[2]{0:T(128)}, u32[]{:S(2)}) copy-start(s32[2]{0:T(128)} %param.20) | copy-start | bytes 28
  24.6 53.0 %copy-start.55 = (bf16[296,1024]{1,0:T(8,128)(2,1)}, bf16[296,1024]{1,0:T(8,128)(2,1)S(1)}, u32[]{:S(2)}) copy-start(bf16[296,1024]{1,0:T(8,128)(2,1)S(1)} %get-tuple-element.267) | copy-start | bytes 1818628
  24.7 51.6 %collective-permute-start.1 = (bf16[296,1024]{1,0:T(8,128)(2,1)S(1)}, bf16[296,1024]{1,0:T(8,128)(2,1)S(1)}, u32[]{:S(2)}, u32[]{:S(2)}) collective-permute-start(bf16[296,1024]{1,0:T(8,128)(2,1)S(1)} %copy-done.60), channel_id=1, source_target_pairs={{0,1},{1,0},{2,3},{3,2},{4,5},{5,4},{6,7},{7,6},{8,9},{9,8},{10,11... | collective-permute-start | bytes 1818632 | tf_op jit(solution)/shard_map/ppermute | solution.py:304
  26.5 49.7 %collective-permute-start.2 = (bf16[296,1024]{1,0:T(8,128)(2,1)S(1)}, bf16[296,1024]{1,0:T(8,128)(2,1)S(1)}, u32[]{:S(2)}, u32[]{:S(2)}) collective-permute-start(bf16[296,1024]{1,0:T(8,128)(2,1)S(1)} %get-tuple-element.109), channel_id=1, source_target_pairs={{0,1},{1,0},{2,3},{3,2},{4,5},{5,4},{6,7},{7,6},{8,9},{9,8},{10,11... | collective-permute-start | bytes 1818632 | tf_op jit(solution)/shard_map/ppermute | solution.py:304
  43.7 12.7 %collective-permute-start.6 = (bf16[4,128,512]{2,1,0:T(8,128)(2,1)S(1)}, bf16[4,128,512]{2,1,0:T(8,128)(2,1)S(1)}, u32[]{:S(2)}, u32[]{:S(2)}) collective-permute-start(bf16[4,128,512]{2,1,0:T(8,128)(2,1)S(1)} %get-tuple-element.110.refs_0_), channel_id=1, source_target_pairs={{0,4},{1,5},{2,6},{3,7},{4,0},{5,1},{6,2},{7,3},{8,12},{9,13},{10,... | collective-permute-start | bytes 1572872 | tf_op jit(solution)/shard_map/ppermute | solution.py:304
  45.3 29.0 %collective-permute-start.7 = (bf16[4,128,512]{2,1,0:T(8,128)(2,1)S(1)}, bf16[4,128,512]{2,1,0:T(8,128)(2,1)S(1)}, u32[]{:S(2)}, u32[]{:S(2)}) collective-permute-start(bf16[4,128,512]{2,1,0:T(8,128)(2,1)S(1)} %get-tuple-element.111.refs_2_), channel_id=1, source_target_pairs={{0,1},{1,0},{2,3},{3,2},{4,5},{5,4},{6,7},{7,6},{8,9},{9,8},{10,11... | collective-permute-start | bytes 1572872 | tf_op jit(solution)/shard_map/ppermute | solution.py:304
  77.5 4.2 %collective-permute-start.8 = (bf16[592,1024]{1,0:T(8,128)(2,1)S(1)}, bf16[592,1024]{1,0:T(8,128)(2,1)S(1)}, u32[]{:S(2)}, u32[]{:S(2)}) collective-permute-start(bf16[592,1024]{1,0:T(8,128)(2,1)S(1)} %fusion.8.own_ref), channel_id=1, source_target_pairs={{0,2},{1,3},{2,0},{3,1},{4,6},{5,7},{6,4},{7,5},{8,10},{9,11},{10,... | collective-permute-start | bytes 3637256 | tf_op jit(solution)/shard_map/ppermute | solution.py:304
  79.0 8.6 %collective-permute-start.9 = (bf16[592,1024]{1,0:T(8,128)(2,1)}, bf16[592,1024]{1,0:T(8,128)(2,1)}, u32[]{:S(2)}, u32[]{:S(2)}) collective-permute-start(bf16[592,1024]{1,0:T(8,128)(2,1)} %get-tuple-element.132.own_ref), channel_id=1, source_target_pairs={{0,2},{1,3},{2,0},{3,1},{4,6},{5,7},{6,4},{7,5},{8,10},{9,11},{10,... | collective-permute-start | bytes 3637256 | tf_op jit(solution)/shard_map/ppermute | solution.py:304
  79.5 31.6 %collective-permute-start.10 = (bf16[2,4,128,512]{3,2,1,0:T(8,128)(2,1)}, bf16[2,4,128,512]{3,2,1,0:T(8,128)(2,1)}, u32[]{:S(2)}, u32[]{:S(2)}) collective-permute-start(bf16[2,4,128,512]{3,2,1,0:T(8,128)(2,1)} %get-tuple-element.112.refs_0_), channel_id=1, source_target_pairs={{0,1},{1,0},{2,3},{3,2},{4,5},{5,4},{6,7},{7,6},{8,9},{9,8},{10,11... | collective-permute-start | bytes 3145736 | tf_op jit(solution)/shard_map/ppermute | solution.py:304
  79.8 32.3 %collective-permute-start.11 = (bf16[2,4,128,512]{3,2,1,0:T(8,128)(2,1)}, bf16[2,4,128,512]{3,2,1,0:T(8,128)(2,1)}, u32[]{:S(2)}, u32[]{:S(2)}) collective-permute-start(bf16[2,4,128,512]{3,2,1,0:T(8,128)(2,1)} %get-tuple-element.113.refs_2_), channel_id=1, source_target_pairs={{0,4},{1,5},{2,6},{3,7},{4,0},{5,1},{6,2},{7,3},{8,12},{9,13},{10,... | collective-permute-start | bytes 3145736 | tf_op jit(solution)/shard_map/ppermute | solution.py:304
  92.4 22.4 %copy-start.8 = (bf16[592,1024]{1,0:T(8,128)(2,1)S(1)}, bf16[592,1024]{1,0:T(8,128)(2,1)}, u32[]{:S(2)}) copy-start(bf16[592,1024]{1,0:T(8,128)(2,1)} %copy-done.6) | copy-start | bytes 3637252
  92.4 22.4 %copy-start.34 = (bf16[592,1024]{1,0:T(8,128)(2,1)S(1)}, bf16[592,1024]{1,0:T(8,128)(2,1)}, u32[]{:S(2)}) copy-start(bf16[592,1024]{1,0:T(8,128)(2,1)} %copy-done.32) | copy-start | bytes 3637252
  114.8 21.9 %copy-start.40 = (bf16[4,2,128,512]{3,2,1,0:T(8,128)(2,1)}, bf16[4,2,128,512]{3,2,1,0:T(8,128)(2,1)S(1)}, u32[]{:S(2)}) copy-start(bf16[4,2,128,512]{3,2,1,0:T(8,128)(2,1)S(1)} %get-tuple-element.120) | copy-start | bytes 3145732
  128.8 7.9 %collective-permute-start.12 = (bf16[592,1024]{1,0:T(8,128)(2,1)S(1)}, bf16[592,1024]{1,0:T(8,128)(2,1)S(1)}, u32[]{:S(2)}, u32[]{:S(2)}) collective-permute-start(bf16[592,1024]{1,0:T(8,128)(2,1)S(1)} %convolution_convert_fusion), channel_id=1, source_target_pairs={{0,2},{1,3},{2,0},{3,1},{4,6},{5,7},{6,4},{7,5},{8,10},{9,11},{10,... | collective-permute-start | bytes 3637256 | tf_op jit(solution)/shard_map/ppermute | solution.py:304
  139.8 3.3 collective-permute-start.13
  171.9 25.2 %collective-permute-start.15 = (bf16[2,512,512]{2,1,0:T(8,128)(2,1)S(1)}, bf16[2,512,512]{2,1,0:T(8,128)(2,1)S(1)}, u32[]{:S(2)}, u32[]{:S(2)}) collective-permute-start(bf16[2,512,512]{2,1,0:T(8,128)(2,1)S(1)} %get-tuple-element.127), channel_id=1, source_target_pairs={{0,1},{1,0},{2,3},{3,2},{4,5},{5,4},{6,7},{7,6},{8,9},{9,8},{10,11... | collective-permute-start | bytes 3145736 | tf_op jit(solution)/shard_map/ppermute | solution.py:304
  173.6 24.8 %collective-permute-start.16 = (bf16[2,512,512]{2,1,0:T(8,128)(2,1)S(1)}, bf16[2,512,512]{2,1,0:T(8,128)(2,1)S(1)}, u32[]{:S(2)}, u32[]{:S(2)}) collective-permute-start(bf16[2,512,512]{2,1,0:T(8,128)(2,1)S(1)} %get-tuple-element.128), channel_id=1, source_target_pairs={{0,4},{1,5},{2,6},{3,7},{4,0},{5,1},{6,2},{7,3},{8,12},{9,13},{10,... | collective-permute-start | bytes 3145736 | tf_op jit(solution)/shard_map/ppermute | solution.py:304
  208.3 8.4 %collective-permute-start.17 = (bf16[592,1024]{1,0:T(8,128)(2,1)}, bf16[592,1024]{1,0:T(8,128)(2,1)}, u32[]{:S(2)}, u32[]{:S(2)}) collective-permute-start(bf16[592,1024]{1,0:T(8,128)(2,1)} %get-tuple-element.142), channel_id=1, source_target_pairs={{0,2},{1,3},{2,0},{3,1},{4,6},{5,7},{6,4},{7,5},{8,10},{9,11},{10,... | collective-permute-start | bytes 3637256 | tf_op jit(solution)/shard_map/ppermute | solution.py:304
  208.3 32.9 %collective-permute-start.19 = (bf16[2,512,512]{2,1,0:T(8,128)(2,1)}, bf16[2,512,512]{2,1,0:T(8,128)(2,1)}, u32[]{:S(2)}, u32[]{:S(2)}) collective-permute-start(bf16[2,512,512]{2,1,0:T(8,128)(2,1)} %copy-done.43), channel_id=1, source_target_pairs={{0,1},{1,0},{2,3},{3,2},{4,5},{5,4},{6,7},{7,6},{8,9},{9,8},{10,11... | collective-permute-start | bytes 3145736 | tf_op jit(solution)/shard_map/ppermute | solution.py:304
  208.9 32.4 %collective-permute-start.20 = (bf16[2,512,512]{2,1,0:T(8,128)(2,1)}, bf16[2,512,512]{2,1,0:T(8,128)(2,1)}, u32[]{:S(2)}, u32[]{:S(2)}) collective-permute-start(bf16[2,512,512]{2,1,0:T(8,128)(2,1)} %copy-done.42), channel_id=1, source_target_pairs={{0,4},{1,5},{2,6},{3,7},{4,0},{5,1},{6,2},{7,3},{8,12},{9,13},{10,... | collective-permute-start | bytes 3145736 | tf_op jit(solution)/shard_map/ppermute | solution.py:304
  213.1 32.5 %collective-permute-start.21 = (bf16[512,512]{1,0:T(8,128)(2,1)S(1)}, bf16[512,512]{1,0:T(8,128)(2,1)S(1)}, u32[]{:S(2)}, u32[]{:S(2)}) collective-permute-start(bf16[512,512]{1,0:T(8,128)(2,1)S(1)} %fusion.39), channel_id=1, source_target_pairs={{0,4},{1,5},{2,6},{3,7},{4,0},{5,1},{6,2},{7,3},{8,12},{9,13},{10,... | collective-permute-start | bytes 1572872 | tf_op jit(solution)/shard_map/ppermute | solution.py:304
  215.0 30.5 %collective-permute-start.22 = (bf16[512,512]{1,0:T(8,128)(2,1)S(1)}, bf16[512,512]{1,0:T(8,128)(2,1)S(1)}, u32[]{:S(2)}, u32[]{:S(2)}) collective-permute-start(bf16[512,512]{1,0:T(8,128)(2,1)S(1)} %fusion.40), channel_id=1, source_target_pairs={{0,1},{1,0},{2,3},{3,2},{4,5},{5,4},{6,7},{7,6},{8,9},{9,8},{10,11... | collective-permute-start | bytes 1572872 | tf_op jit(solution)/shard_map/ppermute | solution.py:304
  224.2 29.2 %collective-permute-start.18 = (bf16[592,1024]{1,0:T(8,128)(2,1)S(1)}, bf16[592,1024]{1,0:T(8,128)(2,1)S(1)}, u32[]{:S(2)}, u32[]{:S(2)}) collective-permute-start(bf16[592,1024]{1,0:T(8,128)(2,1)S(1)} %get-tuple-element.261.own_ref), channel_id=1, source_target_pairs={{0,2},{1,3},{2,0},{3,1},{4,6},{5,7},{6,4},{7,5},{8,10},{9,11},{10,... | collective-permute-start | bytes 3637256 | tf_op jit(solution)/shard_map/ppermute | solution.py:304
  224.2 17.1 %slice-start.2 = ((s8[4849664]{0:T(1024)(128)(4,1)}), s8[4194304]{0:T(1024)(128)(4,1)S(1)}, s32[]{:S(2)}) async-start(s8[4849664]{0:T(1024)(128)(4,1)} %bitcast.181), calls=%async_computation.3 | async-start | bytes 8388608
  246.9 26.1 %collective-permute-start.23 = (bf16[512,512]{1,0:T(8,128)(2,1)S(1)}, bf16[512,512]{1,0:T(8,128)(2,1)S(1)}, u32[]{:S(2)}, u32[]{:S(2)}) collective-permute-start(bf16[512,512]{1,0:T(8,128)(2,1)S(1)} %fusion.37), channel_id=1, source_target_pairs={{0,4},{1,5},{2,6},{3,7},{4,0},{5,1},{6,2},{7,3},{8,12},{9,13},{10,... | collective-permute-start | bytes 1572872 | tf_op jit(solution)/shard_map/ppermute | solution.py:304
  249.6 24.1 %collective-permute-start.24 = (bf16[512,512]{1,0:T(8,128)(2,1)S(1)}, bf16[512,512]{1,0:T(8,128)(2,1)S(1)}, u32[]{:S(2)}, u32[]{:S(2)}) collective-permute-start(bf16[512,512]{1,0:T(8,128)(2,1)S(1)} %fusion.38), channel_id=1, source_target_pairs={{0,1},{1,0},{2,3},{3,2},{4,5},{5,4},{6,7},{7,6},{8,9},{9,8},{10,11... | collective-permute-start | bytes 1572872 | tf_op jit(solution)/shard_map/ppermute | solution.py:304
  251.5 21.4 %collective-permute-start.25 = (bf16[2,128,512]{2,1,0:T(8,128)(2,1)S(1)}, bf16[2,128,512]{2,1,0:T(8,128)(2,1)S(1)}, u32[]{:S(2)}, u32[]{:S(2)}) collective-permute-start(bf16[2,128,512]{2,1,0:T(8,128)(2,1)S(1)} %get-tuple-element.152), channel_id=1, source_target_pairs={{0,8},{1,9},{2,10},{3,11},{4,12},{5,13},{6,14},{7,15},{8,0},{9,1},... | collective-permute-start | bytes 786440 | tf_op jit(solution)/shard_map/ppermute | solution.py:304
  251.6 21.4 %collective-permute-start.26 = (bf16[2,128,512]{2,1,0:T(8,128)(2,1)S(1)}, bf16[2,128,512]{2,1,0:T(8,128)(2,1)S(1)}, u32[]{:S(2)}, u32[]{:S(2)}) collective-permute-start(bf16[2,128,512]{2,1,0:T(8,128)(2,1)S(1)} %get-tuple-element.153), channel_id=1, source_target_pairs={{0,16},{1,17},{2,18},{3,19},{4,20},{5,21},{6,22},{7,23},{8,24},{9,... | collective-permute-start | bytes 786440 | tf_op jit(solution)/shard_map/ppermute | solution.py:304
  253.3 19.6 %collective-permute-start.27 = (bf16[2,128,512]{2,1,0:T(8,128)(2,1)S(1)}, bf16[2,128,512]{2,1,0:T(8,128)(2,1)S(1)}, u32[]{:S(2)}, u32[]{:S(2)}) collective-permute-start(bf16[2,128,512]{2,1,0:T(8,128)(2,1)S(1)} %get-tuple-element.154), channel_id=1, source_target_pairs={{0,24},{1,25},{2,26},{3,27},{4,28},{5,29},{6,30},{7,31},{8,16},{9,... | collective-permute-start | bytes 786440 | tf_op jit(solution)/shard_map/ppermute | solution.py:304
  272.9 41.5 %copy-start = (bf16[1184,1536]{1,0:T(8,128)(2,1)}, bf16[1184,1536]{1,0:T(8,128)(2,1)S(1)}, u32[]{:S(2)}) copy-start(bf16[1184,1536]{1,0:T(8,128)(2,1)S(1)} %shard_map.323.refs_1_) | copy-start | bytes 10911748
  281.5 27.2 %collective-permute-start.29 = (bf16[2,512,512]{2,1,0:T(8,128)(2,1)S(1)}, bf16[2,512,512]{2,1,0:T(8,128)(2,1)S(1)}, u32[]{:S(2)}, u32[]{:S(2)}) collective-permute-start(bf16[2,512,512]{2,1,0:T(8,128)(2,1)S(1)} %get-tuple-element.163), channel_id=1, source_target_pairs={{0,1},{1,0},{2,3},{3,2},{4,5},{5,4},{6,7},{7,6},{8,9},{9,8},{10,11... | collective-permute-start | bytes 3145736 | tf_op jit(solution)/shard_map/ppermute | solution.py:304
  282.2 26.6 %collective-permute-start.30 = (bf16[2,512,512]{2,1,0:T(8,128)(2,1)S(1)}, bf16[2,512,512]{2,1,0:T(8,128)(2,1)S(1)}, u32[]{:S(2)}, u32[]{:S(2)}) collective-permute-start(bf16[2,512,512]{2,1,0:T(8,128)(2,1)S(1)} %get-tuple-element.164), channel_id=1, source_target_pairs={{0,4},{1,5},{2,6},{3,7},{4,0},{5,1},{6,2},{7,3},{8,12},{9,13},{10,... | collective-permute-start | bytes 3145736 | tf_op jit(solution)/shard_map/ppermute | solution.py:304
  282.8 20.4 %collective-permute-start.31 = (bf16[2,128,512]{2,1,0:T(8,128)(2,1)S(1)}, bf16[2,128,512]{2,1,0:T(8,128)(2,1)S(1)}, u32[]{:S(2)}, u32[]{:S(2)}) collective-permute-start(bf16[2,128,512]{2,1,0:T(8,128)(2,1)S(1)} %get-tuple-element.159), channel_id=1, source_target_pairs={{0,8},{1,9},{2,10},{3,11},{4,12},{5,13},{6,14},{7,15},{8,0},{9,1},... | collective-permute-start | bytes 786440 | tf_op jit(solution)/shard_map/ppermute | solution.py:304
  285.6 19.9 %collective-permute-start.32 = (bf16[2,128,512]{2,1,0:T(8,128)(2,1)S(1)}, bf16[2,128,512]{2,1,0:T(8,128)(2,1)S(1)}, u32[]{:S(2)}, u32[]{:S(2)}) collective-permute-start(bf16[2,128,512]{2,1,0:T(8,128)(2,1)S(1)} %get-tuple-element.160), channel_id=1, source_target_pairs={{0,16},{1,17},{2,18},{3,19},{4,20},{5,21},{6,22},{7,23},{8,24},{9,... | collective-permute-start | bytes 786440 | tf_op jit(solution)/shard_map/ppermute | solution.py:304
  285.8 19.7 %collective-permute-start.33 = (bf16[2,128,512]{2,1,0:T(8,128)(2,1)S(1)}, bf16[2,128,512]{2,1,0:T(8,128)(2,1)S(1)}, u32[]{:S(2)}, u32[]{:S(2)}) collective-permute-start(bf16[2,128,512]{2,1,0:T(8,128)(2,1)S(1)} %get-tuple-element.161), channel_id=1, source_target_pairs={{0,24},{1,25},{2,26},{3,27},{4,28},{5,29},{6,30},{7,31},{8,16},{9,... | collective-permute-start | bytes 786440 | tf_op jit(solution)/shard_map/ppermute | solution.py:304
  293.5 15.3 %copy-start.20 = (bf16[2,512,512]{2,1,0:T(8,128)(2,1)}, bf16[2,512,512]{2,1,0:T(8,128)(2,1)S(1)}, u32[]{:S(2)}) copy-start(bf16[2,512,512]{2,1,0:T(8,128)(2,1)S(1)} %get-tuple-element.166.one_ref) | copy-start | bytes 3145732
  293.5 16.4 %copy-start.22 = (bf16[2,512,512]{2,1,0:T(8,128)(2,1)}, bf16[2,512,512]{2,1,0:T(8,128)(2,1)S(1)}, u32[]{:S(2)}) copy-start(bf16[2,512,512]{2,1,0:T(8,128)(2,1)S(1)} %get-tuple-element.167.two_ref) | copy-start | bytes 3145732
  303.2 12.0 %collective-permute-start.28 = (bf16[592,1024]{1,0:T(8,128)(2,1)}, bf16[592,1024]{1,0:T(8,128)(2,1)}, u32[]{:S(2)}, u32[]{:S(2)}) collective-permute-start(bf16[592,1024]{1,0:T(8,128)(2,1)} %get-tuple-element.170), channel_id=1, source_target_pairs={{0,2},{1,3},{2,0},{3,1},{4,6},{5,7},{6,4},{7,5},{8,10},{9,11},{10,... | collective-permute-start | bytes 3637256 | tf_op jit(solution)/shard_map/ppermute | solution.py:304
  308.7 10.4 %collective-permute-start.35 = (bf16[592,1024]{1,0:T(8,128)(2,1)}, bf16[592,1024]{1,0:T(8,128)(2,1)}, u32[]{:S(2)}, u32[]{:S(2)}) collective-permute-start(bf16[592,1024]{1,0:T(8,128)(2,1)} %fusion.26), channel_id=1, source_target_pairs={{0,2},{1,3},{2,0},{3,1},{4,6},{5,7},{6,4},{7,5},{8,10},{9,11},{10,... | collective-permute-start | bytes 3637256 | tf_op jit(solution)/shard_map/ppermute | solution.py:304
  311.9 18.4 %collective-permute-start.36 = (bf16[512,512]{1,0:T(8,128)(2,1)}, bf16[512,512]{1,0:T(8,128)(2,1)}, u32[]{:S(2)}, u32[]{:S(2)}) collective-permute-start(bf16[512,512]{1,0:T(8,128)(2,1)} %fusion.41), channel_id=1, source_target_pairs={{0,4},{1,5},{2,6},{3,7},{4,0},{5,1},{6,2},{7,3},{8,12},{9,13},{10,... | collective-permute-start | bytes 1572872 | tf_op jit(solution)/shard_map/ppermute | solution.py:304
  313.5 18.6 %collective-permute-start.37 = (bf16[512,512]{1,0:T(8,128)(2,1)}, bf16[512,512]{1,0:T(8,128)(2,1)}, u32[]{:S(2)}, u32[]{:S(2)}) collective-permute-start(bf16[512,512]{1,0:T(8,128)(2,1)} %fusion.42), channel_id=1, source_target_pairs={{0,1},{1,0},{2,3},{3,2},{4,5},{5,4},{6,7},{7,6},{8,9},{9,8},{10,11... | collective-permute-start | bytes 1572872 | tf_op jit(solution)/shard_map/ppermute | solution.py:304
  317.8 23.7 %collective-permute-start.34 = (bf16[289,1024]{1,0:T(8,128)(2,1)S(1)}, bf16[289,1024]{1,0:T(8,128)(2,1)S(1)}, u32[]{:S(2)}, u32[]{:S(2)}) collective-permute-start(bf16[289,1024]{1,0:T(8,128)(2,1)S(1)} %slice.197), channel_id=1, source_target_pairs={{0,1},{1,0},{2,3},{3,2},{4,5},{5,4},{6,7},{7,6},{8,9},{9,8},{10,11... | collective-permute-start | bytes 1775624 | tf_op jit(solution)/shard_map/ppermute | solution.py:304
  323.5 1.3 collective-permute-start.39
  324.8 10.3 %collective-permute-start.42 = (f32[12288]{0:T(1024)S(1)}, f32[12288]{0:T(1024)S(1)}, u32[]{:S(2)}, u32[]{:S(2)}) collective-permute-start(f32[12288]{0:T(1024)S(1)} %add.276), channel_id=1, source_target_pairs={{0,24},{1,25},{2,26},{3,27},{4,28},{5,29},{6,30},{7,31},{8,16},{9,... | collective-permute-start | bytes 147464 | tf_op jit(solution)/shard_map/ppermute | solution.py:304
  326.7 10.1 %collective-permute-start.41 = (f32[12288]{0:T(1024)S(1)}, f32[12288]{0:T(1024)S(1)}, u32[]{:S(2)}, u32[]{:S(2)}) collective-permute-start(f32[12288]{0:T(1024)S(1)} %add.276), channel_id=1, source_target_pairs={{0,16},{1,17},{2,18},{3,19},{4,20},{5,21},{6,22},{7,23},{8,24},{9,... | collective-permute-start | bytes 147464 | tf_op jit(solution)/shard_map/ppermute | solution.py:304
  330.4 6.7 %collective-permute-start.40 = (f32[12288]{0:T(1024)S(1)}, f32[12288]{0:T(1024)S(1)}, u32[]{:S(2)}, u32[]{:S(2)}) collective-permute-start(f32[12288]{0:T(1024)S(1)} %add.276), channel_id=1, source_target_pairs={{0,8},{1,9},{2,10},{3,11},{4,12},{5,13},{6,14},{7,15},{8,0},{9,1},... | collective-permute-start | bytes 147464 | tf_op jit(solution)/shard_map/ppermute | solution.py:304
  332.2 21.5 %collective-permute-start.38 = (bf16[289,1024]{1,0:T(8,128)(2,1)S(1)}, bf16[289,1024]{1,0:T(8,128)(2,1)S(1)}, u32[]{:S(2)}, u32[]{:S(2)}) collective-permute-start(bf16[289,1024]{1,0:T(8,128)(2,1)S(1)} %slice.292), channel_id=1, source_target_pairs={{0,1},{1,0},{2,3},{3,2},{4,5},{5,4},{6,7},{7,6},{8,9},{9,8},{10,11... | collective-permute-start | bytes 1775624 | tf_op jit(solution)/shard_map/ppermute | solution.py:304
  335.1 28.5 %collective-permute-start.45 = (bf16[2,128,512]{2,1,0:T(8,128)(2,1)S(1)}, bf16[2,128,512]{2,1,0:T(8,128)(2,1)S(1)}, u32[]{:S(2)}, u32[]{:S(2)}) collective-permute-start(bf16[2,128,512]{2,1,0:T(8,128)(2,1)S(1)} %get-tuple-element.179), channel_id=1, source_target_pairs={{0,8},{1,9},{2,10},{3,11},{4,12},{5,13},{6,14},{7,15},{8,0},{9,1},... | collective-permute-start | bytes 786440 | tf_op jit(solution)/shard_map/ppermute | solution.py:304
  336.8 26.8 %collective-permute-start.46 = (bf16[2,128,512]{2,1,0:T(8,128)(2,1)S(1)}, bf16[2,128,512]{2,1,0:T(8,128)(2,1)}, u32[]{:S(2)}, u32[]{:S(2)}) collective-permute-start(bf16[2,128,512]{2,1,0:T(8,128)(2,1)S(1)} %get-tuple-element.180), channel_id=1, source_target_pairs={{0,16},{1,17},{2,18},{3,19},{4,20},{5,21},{6,22},{7,23},{8,24},{9,... | collective-permute-start | bytes 786440 | tf_op jit(solution)/shard_map/ppermute | solution.py:304
  337.0 26.5 %collective-permute-start.47 = (bf16[2,128,512]{2,1,0:T(8,128)(2,1)S(1)}, bf16[2,128,512]{2,1,0:T(8,128)(2,1)}, u32[]{:S(2)}, u32[]{:S(2)}) collective-permute-start(bf16[2,128,512]{2,1,0:T(8,128)(2,1)S(1)} %get-tuple-element.181), channel_id=1, source_target_pairs={{0,24},{1,25},{2,26},{3,27},{4,28},{5,29},{6,30},{7,31},{8,16},{9,... | collective-permute-start | bytes 786440 | tf_op jit(solution)/shard_map/ppermute | solution.py:304
  341.5 4.1 %collective-permute-start.43 = (f32[12288]{0:T(1024)S(1)}, f32[12288]{0:T(1024)S(1)}, u32[]{:S(2)}, u32[]{:S(2)}) collective-permute-start(f32[12288]{0:T(1024)S(1)} %add_add_fusion), channel_id=1, source_target_pairs={{0,4},{1,5},{2,6},{3,7},{4,0},{5,1},{6,2},{7,3},{8,12},{9,13},{10,... | collective-permute-start | bytes 147464 | tf_op jit(solution)/shard_map/ppermute | solution.py:304
  353.7 5.2 %collective-permute-start.44 = (f32[12288]{0:T(1024)S(1)}, f32[12288]{0:T(1024)S(1)}, u32[]{:S(2)}, u32[]{:S(2)}) collective-permute-start(f32[12288]{0:T(1024)S(1)} %add.280), channel_id=1, source_target_pairs={{0,1},{1,0},{2,3},{3,2},{4,5},{5,4},{6,7},{7,6},{8,9},{9,8},{10,11... | collective-permute-start | bytes 147464 | tf_op jit(solution)/shard_map/ppermute | solution.py:304
  354.9 5.1 %collective-permute-start.48 = (bf16[2,64,512]{2,1,0:T(8,128)(2,1)S(1)}, bf16[2,64,512]{2,1,0:T(8,128)(2,1)S(1)}, u32[]{:S(2)}, u32[]{:S(2)}) collective-permute-start(bf16[2,64,512]{2,1,0:T(8,128)(2,1)S(1)} %fusion.49), channel_id=1, source_target_pairs={{0,2},{1,3},{2,0},{3,1},{4,6},{5,7},{6,4},{7,5},{8,10},{9,11},{10,... | collective-permute-start | bytes 393224 | tf_op jit(solution)/shard_map/ppermute | solution.py:304
  358.9 2.9 collective-permute-start.49
  364.7 1.4 collective-permute-start.50
  (79 other events, 427.8 us)
Sparse Core Ops, SparseCore 0:
  12.2 143.3 all-gather.1

commit v8 on v7

--- a/solution.py
+++ b/solution.py
@@ -1128,7 +1128,7 @@
     vector = vector + vectors[0] + vectors[1] + vectors[2]
     vector = vector + after(exchange(vector, far_x=1), images_far, *last_line)
     vector = vector + after(exchange(vector, far_y=1), layer_far)
-    lower_z, up_z = after((tuple(lower_z), tuple(up_z)), *last_line, images_far)
+    lower_z, up_z = after((tuple(lower_z), tuple(up_z)), *last_line, layer_far)
     lower_owned = full_columns(scatter_last(lower_line[0], lower_z, core)).T
     upper_owned = full_columns(scatter_last(up_line[0], up_z, core))
 

time: 383 us -> 380 us (level)
  waiting for transfers between devices: 92.7 us -> 86.6 us
    ppermute x51, waiting for transfers between devices: 85 us -> 78.8 us  [exchange(): return lax.ppermute(value, BOTH, pairs)]
    unnamed x195 -> x197, local copies, waits for them, and re-layouts: 23.7 us -> 23.7 us
  transfers between devices with their start and end apart: 52 -> 52, of which waited for: 20 -> 20; matrix products, arithmetic and copies ran while one was open for 16% -> 17% of each run, Pallas kernels for 26% -> 26%
where the time goes in v8:
time: 380 us; the launch traced here: 374 us
  Pallas kernels  132 us (35%)
  waiting for transfers between devices  86.6 us (23%)
  starting transfers between devices  54.4 us (14%)
  local copies, waits for them, and re-layouts  38.8 us (10%)
  other arithmetic  30 us (8%)
  between operations  16.8 us (4%)
  matrix products  16 us (4%)
    ppermute x51, waiting for transfers between devices, exchange(): return lax.ppermute(value, BOTH, pairs)  78.8 us
    ppermute x51, starting transfers between devices, exchange(): return lax.ppermute(value, BOTH, pairs)  54.3 us
    pallas_call x2, Pallas kernels, attend_back_image(): pl.pallas_call(kernel, grid=(blocks,), in_specs=[pl.BlockSpec((rows, 3 *...  29.2 us
    pallas_call x6, Pallas kernels, weight_pieces(): pl.pallas_call(kernel, grid=(4,), in_specs=specs, out_specs=[pl.BlockSpec...  26.6 us
    unnamed x197, local copies, waits for them, and re-layouts  23.7 us
    pallas_call x2, Pallas kernels, down_call(): pl.pallas_call(down_kernel, grid_spec=pltpu.PrefetchScalarGridSpec(num_sc...  18.1 us
    pallas_call x2, Pallas kernels, attend_image(): pl.pallas_call(kernel, grid=(blocks,), in_specs=[pl.BlockSpec((rows, 3 *...  15.4 us
    pallas_call x1, Pallas kernels, up_call(): pl.pallas_call(up_kernel, grid_spec=pltpu.PrefetchScalarGridSpec(num_scal...  12.3 us
  transfers between devices with their start and end apart: 52, of which 20 were waited for; matrix products, arithmetic and copies ran while one was open for 17% of the time, Pallas kernels for 26%

profile of v8, /device:TPU:0, one launch (start us, length us, event | category | flops | bytes accessed | tf_op | source)
XLA Modules:
  0.0 374.1 jit_solution(2586554617234332867)
XLA Ops:
  13.9 3.0 collective-permute-start.3
  16.9 2.6 collective-permute-start.4
  20.4 2.9 copy.72
  24.7 1.8 collective-permute-start.1
  26.8 3.8 %collective-permute-done.3.refs_1_ = bf16[2,128,512]{2,1,0:T(8,128)(2,1)S(1)} collective-permute-done((bf16[2,128,512]{2,1,0:T(8,128)(2,1)S(1)}, bf16[2,128,512]{2,1,0:T(8,128)(2,1)S(1)}, u32[]{:S(2)}, u32[]{:S(2)}) %collective-permute-start.3) | collective-permute-done | bytes 262176 | tf_op jit(solution)/shard_map/ppermute | solution.py:304
  30.7 7.1 %collective-permute-done.4.refs_2_ = bf16[2,128,512]{2,1,0:T(8,128)(2,1)S(1)} collective-permute-done((bf16[2,128,512]{2,1,0:T(8,128)(2,1)S(1)}, bf16[2,128,512]{2,1,0:T(8,128)(2,1)S(1)}, u32[]{:S(2)}, u32[]{:S(2)}) %collective-permute-start.4) | collective-permute-done | bytes 262176 | tf_op jit(solution)/shard_map/ppermute | solution.py:304
  37.8 5.3 %collective-permute-done.5.refs_3_ = bf16[2,128,512]{2,1,0:T(8,128)(2,1)S(1)} collective-permute-done((bf16[2,128,512]{2,1,0:T(8,128)(2,1)S(1)}, bf16[2,128,512]{2,1,0:T(8,128)(2,1)S(1)}, u32[]{:S(2)}, u32[]{:S(2)}) %collective-permute-start.5) | collective-permute-done | bytes 262176 | tf_op jit(solution)/shard_map/ppermute | solution.py:304
  43.7 1.6 collective-permute-start.6
  45.3 1.5 collective-permute-start.7
  48.1 8.4 %collective-permute-done.6.refs_1_ = bf16[4,128,512]{2,1,0:T(8,128)(2,1)S(1)} collective-permute-done((bf16[4,128,512]{2,1,0:T(8,128)(2,1)S(1)}, bf16[4,128,512]{2,1,0:T(8,128)(2,1)S(1)}, u32[]{:S(2)}, u32[]{:S(2)}) %collective-permute-start.6) | collective-permute-done | bytes 524320 | tf_op jit(solution)/shard_map/ppermute | solution.py:304
  56.4 17.8 %collective-permute-done.7.refs_3_ = bf16[4,128,512]{2,1,0:T(8,128)(2,1)S(1)} collective-permute-done((bf16[4,128,512]{2,1,0:T(8,128)(2,1)S(1)}, bf16[4,128,512]{2,1,0:T(8,128)(2,1)S(1)}, u32[]{:S(2)}, u32[]{:S(2)}) %collective-permute-start.7) | collective-permute-done | bytes 524320 | tf_op jit(solution)/shard_map/ppermute | solution.py:304
  74.2 2.0 shard_map.306
  79.8 1.7 collective-permute-start.11
  85.4 2.2 shard_map.307.refs_0_
  87.6 3.3 shard_map.308.refs_0_
  90.9 1.5 copy-done.14
  92.4 18.7 %collective-permute-done.10.refs_1_ = bf16[2,4,128,512]{3,2,1,0:T(8,128)(2,1)} collective-permute-done((bf16[2,4,128,512]{3,2,1,0:T(8,128)(2,1)}, bf16[2,4,128,512]{3,2,1,0:T(8,128)(2,1)}, u32[]{:S(2)}, u32[]{:S(2)}) %collective-permute-start.10) | collective-permute-done | bytes 1048608 | tf_op jit(solution)/shard_map/ppermute | solution.py:304
  112.1 2.7 shard_map.309
  114.8 5.2 %fusion.refs_0_ = bf16[1184,1536]{1,0:T(8,128)(2,1)S(1)} fusion(bf16[1024,1536]{1,0:T(8,128)(2,1)S(1)} %bitcast.187, f32[1536]{0:T(1024)S(1)} %add.250, bf16[592,1024]{1,0:T(8,128)(2,1)S(1)} %copy-done.34, bf16[592,1024]{1,0:T(8,128)(2,1)S(1)} %copy-done.8), kind=kOutput, calls=%fused_computation.1 | convolution fusion | flops 3733028864 | bytes 9213952 | tf_op jit(solution)/shard_map/dot_general | solution.py:644
  120.1 7.7 %shard_map.310 = (bf16[1184,512]{1,0:T(8,128)(2,1)S(1)}, f32[8,8,592]{2,1,0:T(8,128)S(1)}) custom-call(bf16[1184,1536]{1,0:T(8,128)(2,1)S(1)} %fusion.refs_0_, bf16[592,128]{1,0:T(8,128)(2,1)S(1)} %broadcast_in_dim.56.refs_1_), custom_call_target="tpu_custom_call" | custom-call | flops 2871001088 | bytes 2424832 | tf_op jit(solution)/shard_map/pallas_call | solution.py:822
  128.9 7.7 %shard_map.311 = (bf16[1184,512]{1,0:T(8,128)(2,1)S(1)}, f32[8,8,592]{2,1,0:T(8,128)S(1)}) custom-call(bf16[1184,1536]{1,0:T(8,128)(2,1)S(1)} %fusion.refs_0_, bf16[592,128]{1,0:T(8,128)(2,1)S(1)} %broadcast_in_dim.56.refs_1_, bf16[1184,512]{1,0:T(8,128)(2,1)S(1)} %get-tuple-element.121.refs_2_, ...), custom_call_target="tpu_custom_call", output_to_operand_aliasing={{0}: (2, {}), {1}: (3, {})} | custom-call | flops 2871001088 | bytes 2424832 | tf_op jit(solution)/shard_map/pallas_call | solution.py:822
  140.3 2.8 collective-permute-done.13.far_ref
  143.1 3.3 shard_map.312.refs_0_
  146.4 1.5 copy-done.11
  147.9 7.7 %all-gather.2.cloned.1.call-done = bf16[2048,2048]{1,0:T(8,128)(2,1)} async-done(((bf16[128,2048]{1,0:T(8,128)(2,1)}), bf16[2048,2048]{1,0:T(8,128)(2,1)}) %all-gather.2.cloned.1.call-update) | async-done | bytes 8388624 | tf_op jit(solution)/shard_map/all_gather | solution.py:956
  155.6 12.3 %shard_map.313 = (bf16[1184,2048]{1,0:T(8,128)(2,1)S(1)}, bf16[1184,2048]{1,0:T(8,128)(2,1)S(1)}) custom-call(s32[4]{0:T(128)S(1)} %pad_add_fusion.places_ref, bf16[592,1024]{1,0:T(8,128)(2,1)} %add_convert_fusion.own_ref, bf16[592,1024]{1,0:T(8,128)(2,1)} %collective-permute-done.13.far_ref, bf16[8,2,128,2048]{3,2,1,0:T(8,128)(2,1)} %bitcast.194, ...), custom_call_target="tpu_custom_call" | custom-call | flops 4966055936 | bytes 16318464 | tf_op jit(solution)/shard_map/pallas_call | solution.py:539
  168.0 3.9 %shard_map.314 = (bf16[2,512,512]{2,1,0:T(8,128)(2,1)S(1)}, bf16[2,512,512]{2,1,0:T(8,128)(2,1)S(1)}) custom-call(bf16[2,512,1184]{2,1,0:T(8,128)(2,1)S(1)} %copy-done.15, bf16[1184,2048]{1,0:T(8,128)(2,1)S(1)} %get-tuple-element.168.refs_1_.left_ref), custom_call_target="tpu_custom_call" | custom-call | flops 2483027968 | bytes 11796480 | tf_op jit(solution)/shard_map/pallas_call | solution.py:723
  171.9 1.6 collective-permute-start.15
  175.0 3.9 %shard_map.315 = (bf16[2,512,512]{2,1,0:T(8,128)(2,1)S(1)}, bf16[2,512,512]{2,1,0:T(8,128)(2,1)S(1)}) custom-call(bf16[2,512,1184]{2,1,0:T(8,128)(2,1)S(1)} %copy-done.15, bf16[1184,2048]{1,0:T(8,128)(2,1)S(1)} %get-tuple-element.168.refs_1_.left_ref), custom_call_target="tpu_custom_call" | custom-call | flops 2483027968 | bytes 11796480 | tf_op jit(solution)/shard_map/pallas_call | solution.py:723
  180.9 9.9 %shard_map.316 = (bf16[1184,2048]{1,0:T(8,128)(2,1)S(1)}, f32[1,2048]{1,0:T(1,128)S(1)}) custom-call(s32[4]{0:T(128)S(1)} %pad_add_fusion.places_ref, bf16[592,1024]{1,0:T(8,128)(2,1)} %get-tuple-element.132.own_ref, bf16[592,1024]{1,0:T(8,128)(2,1)} %collective-permute-done.9.far_ref, bf16[8,2,128,2048]{3,2,1,0:T(8,128)(2,1)} %bitcast.195, ...), custom_call_target="tpu_custom_call" | custom-call | flops 4966055936 | bytes 16318464 | tf_op jit(solution)/shard_map/pallas_call | solution.py:579
  190.9 3.9 %shard_map.317 = (bf16[2,512,512]{2,1,0:T(8,128)(2,1)S(1)}, bf16[2,512,512]{2,1,0:T(8,128)(2,1)S(1)}) custom-call(bf16[2,512,1184]{2,1,0:T(8,128)(2,1)S(1)} %copy-done.12, bf16[1184,2048]{1,0:T(8,128)(2,1)S(1)} %get-tuple-element.144.refs_1_.left_ref), custom_call_target="tpu_custom_call" | custom-call | flops 2483027968 | bytes 11796480 | tf_op jit(solution)/shard_map/pallas_call | solution.py:723
  198.4 8.5 %shard_map.318 = (f32[592,1024]{1,0:T(8,128)S(1)}, bf16[592,1024]{1,0:T(8,128)(2,1)}) custom-call(s32[4]{0:T(128)S(1)} %pad_add_fusion.places_ref, bf16[1184,2048]{1,0:T(8,128)(2,1)S(1)} %get-tuple-element.144.refs_1_.left_ref, bf16[8,2,128,2048]{3,2,1,0:T(8,128)(2,1)} %bitcast.196), custom_call_target="tpu_custom_call" | custom-call | flops 1024 | bytes 1024 | tf_op jit(solution)/shard_map/pallas_call | solution.py:622
  211.6 1.5 fusion.39
  215.0 1.6 collective-permute-start.22
  216.7 3.3 multiply_reduce_fusion
  220.0 4.1 %convert_reduce_fusion.3 = (f32[1024]{0:T(1024)S(1)}, bf16[592,1024]{1,0:T(8,128)(2,1)S(1)}, f32[592,1024]{1,0:T(8,128)}) fusion(f32[592]{0:T(1024)S(1)} %broadcast_multiply_fusion.2, f32[592,1024]{1,0:T(8,128)S(1)} %copy-done.47, f32[592]{0:T(1024)S(1)} %broadcast_multiply_fusion.4, f32[592]{0:T(1024)S(1)} %broadcast_multiply_fusion.3, ...), kind=kLoop, calls=%fused_computation.27 | loop fusion | flops 11516928 | bytes 10931776 | tf_op jit(solution)/shard_map/reduce_sum | solution.py:897
  226.6 14.7 %shard_map.319.refs_5_ = bf16[1184,1536]{1,0:T(8,128)(2,1)S(1)} custom-call(bf16[1184,1536]{1,0:T(8,128)(2,1)S(1)} %copy-done.45, bf16[592,128]{1,0:T(8,128)(2,1)S(1)} %broadcast_in_dim.56.refs_1_, bf16[592,512]{1,0:T(8,128)(2,1)S(1)} %convolution_convert_fusion.1.refs_2_, bf16[1184,512]{1,0:T(8,128)(2,1)S(1)} %copy-done.10, ...), custom_call_target="tpu_custom_call" | custom-call | flops 7177502720 | bytes 4849664 | tf_op jit(solution)/shard_map/pallas_call | solution.py:856
  241.3 3.9 %shard_map.320 = (bf16[2,512,512]{2,1,0:T(8,128)(2,1)S(1)}, bf16[2,512,512]{2,1,0:T(8,128)(2,1)S(1)}) custom-call(bf16[2,512,1184]{2,1,0:T(8,128)(2,1)S(1)} %copy-done.13, bf16[1184,2048]{1,0:T(8,128)(2,1)S(1)} %bitcast.182), custom_call_target="tpu_custom_call" | custom-call | flops 2483027968 | bytes 11796480 | tf_op jit(solution)/shard_map/pallas_call | solution.py:723
  246.8 1.5 collective-permute-start.23
  251.6 1.8 collective-permute-start.26
  253.3 2.6 collective-permute-start.27
  256.7 1.6 shard_map.322.refs_2_
  258.4 14.5 %shard_map.323.refs_1_ = bf16[1184,1536]{1,0:T(8,128)(2,1)S(1)} custom-call(bf16[1184,1536]{1,0:T(8,128)(2,1)S(1)} %copy-done.45, bf16[592,128]{1,0:T(8,128)(2,1)S(1)} %broadcast_in_dim.56.refs_1_, bf16[592,512]{1,0:T(8,128)(2,1)S(1)} %convolution_convert_fusion.2.refs_2_, bf16[1184,512]{1,0:T(8,128)(2,1)S(1)} %copy-done.10, ...), custom_call_target="tpu_custom_call", output_to_operand_aliasing={{}: (5, {})} | custom-call | flops 7177502720 | bytes 4849664 | tf_op jit(solution)/shard_map/pallas_call | solution.py:856
  273.6 2.4 shard_map.324
  276.0 5.5 %shard_map.325 = (bf16[2,512,512]{2,1,0:T(8,128)(2,1)S(1)}, bf16[2,512,512]{2,1,0:T(8,128)(2,1)S(1)}) custom-call(bf16[2,512,1184]{2,1,0:T(8,128)(2,1)S(1)} %shard_map.307.refs_0_, bf16[1184,1536]{1,0:T(8,128)(2,1)S(1)} %shard_map.323.refs_1_, bf16[2,512,1184]{2,1,0:T(8,128)(2,1)S(1)} %shard_map.322.refs_2_, bf16[1184,512]{1,0:T(8,128)(2,1)S(1)} %copy-done.10), custom_call_target="tpu_custom_call" | custom-call | flops 1024 | bytes 1024 | tf_op jit(solution)/shard_map/pallas_call | solution.py:723
  282.7 2.9 collective-permute-start.31
  285.8 2.2 collective-permute-start.33
  288.0 5.5 %shard_map.326 = (bf16[2,512,512]{2,1,0:T(8,128)(2,1)S(1)}, bf16[2,512,512]{2,1,0:T(8,128)(2,1)S(1)}) custom-call(bf16[2,512,1184]{2,1,0:T(8,128)(2,1)S(1)} %shard_map.307.refs_0_, bf16[1184,1536]{1,0:T(8,128)(2,1)S(1)} %shard_map.323.refs_1_, bf16[2,512,1184]{2,1,0:T(8,128)(2,1)S(1)} %shard_map.322.refs_2_, bf16[1184,512]{1,0:T(8,128)(2,1)S(1)} %copy-done.10), custom_call_target="tpu_custom_call" | custom-call | flops 1024 | bytes 1024 | tf_op jit(solution)/shard_map/pallas_call | solution.py:723
  293.5 9.6 %shard_map.327 = (f32[592,1024]{1,0:T(8,128)S(1)}, bf16[592,1024]{1,0:T(8,128)(2,1)}) custom-call(s32[4]{0:T(128)S(1)} %pad_add_fusion.places_ref, bf16[1184,2048]{1,0:T(8,128)(2,1)S(1)} %bitcast.180, bf16[8,2,128,2048]{3,2,1,0:T(8,128)(2,1)} %bitcast.197), custom_call_target="tpu_custom_call" | custom-call | flops 1024 | bytes 1024 | tf_op jit(solution)/shard_map/pallas_call | solution.py:622
  303.2 2.4 collective-permute-done.32
  305.5 3.1 fusion.26
  311.9 1.5 collective-permute-start.36
  315.1 2.6 multiply_convert_fusion
  319.4 4.0 %fusion.13 = (f32[1024]{0:T(1024)S(1)}, f32[592]{0:T(1024)S(1)}, f32[592]{0:T(1024)S(1)}, f32[1024]{0:T(1024)S(1)}, f32[592,1024]{1,0:T(8,128)S(1)}) fusion(f32[592]{0:T(1024)S(1)} %add_rsqrt_fusion.1, f32[592]{0:T(1024)S(1)} %broadcast_multiply_fusion.5, bf16[296,1024]{1,0:T(8,128)(2,1)S(1)} %copy-done.54, bf16[296,1024]{1,0:T(8,128)(2,1)S(1)} %copy-done.50, ...), kind=kOutput, calls=%fused_computation.18 | convolution fusion | flops 1871360768 | bytes 9839232 | tf_op jit(solution)/shard_map/dot_general | solution.py:494
  324.7 1.9 collective-permute-start.42
  326.7 3.7 collective-permute-start.41
  330.5 1.5 fusion.12
  333.1 1.7 shard_map.328
  334.9 1.9 collective-permute-start.45
  337.0 2.4 collective-permute-start.47
  341.5 2.2 copy.92
  349.9 3.9 %collective-permute-done.38 = bf16[289,1024]{1,0:T(8,128)(2,1)} collective-permute-done((bf16[289,1024]{1,0:T(8,128)(2,1)}, bf16[289,1024]{1,0:T(8,128)(2,1)}, u32[]{:S(2)}, u32[]{:S(2)}) %collective-permute-start.38) | collective-permute-done | bytes 591904 | tf_op jit(solution)/shard_map/ppermute | solution.py:304
  355.0 1.8 fusion.29
  357.0 3.2 copy.93
  (393 shorter events, 72.5 us)
Async XLA Ops:
  7.2 148.4 %all-gather.2.cloned.1.call-start = ((), (), s32[]{:S(2)}) async-start(), calls=%async_computation | async-start | bytes 8912896 | tf_op jit(solution)/shard_map/all_gather | solution.py:956
  9.5 1.7 collective-permute-start.14
  12.3 1.4 collective-permute-start
  13.9 16.8 %collective-permute-start.3 = (bf16[2,128,512]{2,1,0:T(8,128)(2,1)S(1)}, bf16[2,128,512]{2,1,0:T(8,128)(2,1)S(1)}, u32[]{:S(2)}, u32[]{:S(2)}) collective-permute-start(bf16[2,128,512]{2,1,0:T(8,128)(2,1)S(1)} %bitcast.183), channel_id=1, source_target_pairs={{0,8},{1,9},{2,10},{3,11},{4,12},{5,13},{6,14},{7,15},{8,0},{9,1},... | collective-permute-start | bytes 786440 | tf_op jit(solution)/shard_map/ppermute | solution.py:304
  16.9 20.9 %collective-permute-start.4 = (bf16[2,128,512]{2,1,0:T(8,128)(2,1)S(1)}, bf16[2,128,512]{2,1,0:T(8,128)(2,1)S(1)}, u32[]{:S(2)}, u32[]{:S(2)}) collective-permute-start(bf16[2,128,512]{2,1,0:T(8,128)(2,1)S(1)} %bitcast.184), channel_id=1, source_target_pairs={{0,16},{1,17},{2,18},{3,19},{4,20},{5,21},{6,22},{7,23},{8,24},{9,... | collective-permute-start | bytes 786440 | tf_op jit(solution)/shard_map/ppermute | solution.py:304
  19.5 23.6 %collective-permute-start.5 = (bf16[2,128,512]{2,1,0:T(8,128)(2,1)S(1)}, bf16[2,128,512]{2,1,0:T(8,128)(2,1)S(1)}, u32[]{:S(2)}, u32[]{:S(2)}) collective-permute-start(bf16[2,128,512]{2,1,0:T(8,128)(2,1)S(1)} %bitcast.185), channel_id=1, source_target_pairs={{0,24},{1,25},{2,26},{3,27},{4,28},{5,29},{6,30},{7,31},{8,16},{9,... | collective-permute-start | bytes 786440 | tf_op jit(solution)/shard_map/ppermute | solution.py:304
  20.4 56.6 %copy-start.48 = (bf16[296,1024]{1,0:T(8,128)(2,1)}, bf16[296,1024]{1,0:T(8,128)(2,1)S(1)}, u32[]{:S(2)}) copy-start(bf16[296,1024]{1,0:T(8,128)(2,1)S(1)} %get-tuple-element.269) | copy-start | bytes 1818628
  20.4 26.4 %copy-start.79 = (bf16[1024]{0:T(1024)(128)(2,1)S(1)}, bf16[1024]{0:T(1024)(128)(2,1)}, u32[]{:S(2)}) copy-start(bf16[1024]{0:T(1024)(128)(2,1)} %param.22) | copy-start | bytes 6148
  20.4 26.4 %copy-start.80 = (bf16[1024]{0:T(1024)(128)(2,1)S(1)}, bf16[1024]{0:T(1024)(128)(2,1)}, u32[]{:S(2)}) copy-start(bf16[1024]{0:T(1024)(128)(2,1)} %param.21) | copy-start | bytes 6148
  20.4 26.4 %copy-start.87 = (s32[2]{0:T(128)S(1)}, s32[2]{0:T(128)}, u32[]{:S(2)}) copy-start(s32[2]{0:T(128)} %param.20) | copy-start | bytes 28
  24.6 53.0 %copy-start.56 = (bf16[296,1024]{1,0:T(8,128)(2,1)}, bf16[296,1024]{1,0:T(8,128)(2,1)S(1)}, u32[]{:S(2)}) copy-start(bf16[296,1024]{1,0:T(8,128)(2,1)S(1)} %get-tuple-element.267) | copy-start | bytes 1818628
  24.7 51.6 %collective-permute-start.1 = (bf16[296,1024]{1,0:T(8,128)(2,1)S(1)}, bf16[296,1024]{1,0:T(8,128)(2,1)S(1)}, u32[]{:S(2)}, u32[]{:S(2)}) collective-permute-start(bf16[296,1024]{1,0:T(8,128)(2,1)S(1)} %copy-done.61), channel_id=1, source_target_pairs={{0,1},{1,0},{2,3},{3,2},{4,5},{5,4},{6,7},{7,6},{8,9},{9,8},{10,11... | collective-permute-start | bytes 1818632 | tf_op jit(solution)/shard_map/ppermute | solution.py:304
  26.5 49.7 %collective-permute-start.2 = (bf16[296,1024]{1,0:T(8,128)(2,1)S(1)}, bf16[296,1024]{1,0:T(8,128)(2,1)S(1)}, u32[]{:S(2)}, u32[]{:S(2)}) collective-permute-start(bf16[296,1024]{1,0:T(8,128)(2,1)S(1)} %get-tuple-element.109), channel_id=1, source_target_pairs={{0,1},{1,0},{2,3},{3,2},{4,5},{5,4},{6,7},{7,6},{8,9},{9,8},{10,11... | collective-permute-start | bytes 1818632 | tf_op jit(solution)/shard_map/ppermute | solution.py:304
  43.7 12.7 %collective-permute-start.6 = (bf16[4,128,512]{2,1,0:T(8,128)(2,1)S(1)}, bf16[4,128,512]{2,1,0:T(8,128)(2,1)S(1)}, u32[]{:S(2)}, u32[]{:S(2)}) collective-permute-start(bf16[4,128,512]{2,1,0:T(8,128)(2,1)S(1)} %get-tuple-element.110.refs_0_), channel_id=1, source_target_pairs={{0,4},{1,5},{2,6},{3,7},{4,0},{5,1},{6,2},{7,3},{8,12},{9,13},{10,... | collective-permute-start | bytes 1572872 | tf_op jit(solution)/shard_map/ppermute | solution.py:304
  45.3 29.0 %collective-permute-start.7 = (bf16[4,128,512]{2,1,0:T(8,128)(2,1)S(1)}, bf16[4,128,512]{2,1,0:T(8,128)(2,1)S(1)}, u32[]{:S(2)}, u32[]{:S(2)}) collective-permute-start(bf16[4,128,512]{2,1,0:T(8,128)(2,1)S(1)} %get-tuple-element.111.refs_2_), channel_id=1, source_target_pairs={{0,1},{1,0},{2,3},{3,2},{4,5},{5,4},{6,7},{7,6},{8,9},{9,8},{10,11... | collective-permute-start | bytes 1572872 | tf_op jit(solution)/shard_map/ppermute | solution.py:304
  77.5 4.2 %collective-permute-start.8 = (bf16[592,1024]{1,0:T(8,128)(2,1)S(1)}, bf16[592,1024]{1,0:T(8,128)(2,1)S(1)}, u32[]{:S(2)}, u32[]{:S(2)}) collective-permute-start(bf16[592,1024]{1,0:T(8,128)(2,1)S(1)} %fusion.8.own_ref), channel_id=1, source_target_pairs={{0,2},{1,3},{2,0},{3,1},{4,6},{5,7},{6,4},{7,5},{8,10},{9,11},{10,... | collective-permute-start | bytes 3637256 | tf_op jit(solution)/shard_map/ppermute | solution.py:304
  79.0 8.6 %collective-permute-start.9 = (bf16[592,1024]{1,0:T(8,128)(2,1)}, bf16[592,1024]{1,0:T(8,128)(2,1)}, u32[]{:S(2)}, u32[]{:S(2)}) collective-permute-start(bf16[592,1024]{1,0:T(8,128)(2,1)} %get-tuple-element.132.own_ref), channel_id=1, source_target_pairs={{0,2},{1,3},{2,0},{3,1},{4,6},{5,7},{6,4},{7,5},{8,10},{9,11},{10,... | collective-permute-start | bytes 3637256 | tf_op jit(solution)/shard_map/ppermute | solution.py:304
  79.5 31.6 %collective-permute-start.10 = (bf16[2,4,128,512]{3,2,1,0:T(8,128)(2,1)}, bf16[2,4,128,512]{3,2,1,0:T(8,128)(2,1)}, u32[]{:S(2)}, u32[]{:S(2)}) collective-permute-start(bf16[2,4,128,512]{3,2,1,0:T(8,128)(2,1)} %get-tuple-element.112.refs_0_), channel_id=1, source_target_pairs={{0,1},{1,0},{2,3},{3,2},{4,5},{5,4},{6,7},{7,6},{8,9},{9,8},{10,11... | collective-permute-start | bytes 3145736 | tf_op jit(solution)/shard_map/ppermute | solution.py:304
  79.8 32.3 %collective-permute-start.11 = (bf16[2,4,128,512]{3,2,1,0:T(8,128)(2,1)}, bf16[2,4,128,512]{3,2,1,0:T(8,128)(2,1)}, u32[]{:S(2)}, u32[]{:S(2)}) collective-permute-start(bf16[2,4,128,512]{3,2,1,0:T(8,128)(2,1)} %get-tuple-element.113.refs_2_), channel_id=1, source_target_pairs={{0,4},{1,5},{2,6},{3,7},{4,0},{5,1},{6,2},{7,3},{8,12},{9,13},{10,... | collective-permute-start | bytes 3145736 | tf_op jit(solution)/shard_map/ppermute | solution.py:304
  92.4 22.4 %copy-start.8 = (bf16[592,1024]{1,0:T(8,128)(2,1)S(1)}, bf16[592,1024]{1,0:T(8,128)(2,1)}, u32[]{:S(2)}) copy-start(bf16[592,1024]{1,0:T(8,128)(2,1)} %copy-done.6) | copy-start | bytes 3637252
  92.4 22.4 %copy-start.34 = (bf16[592,1024]{1,0:T(8,128)(2,1)S(1)}, bf16[592,1024]{1,0:T(8,128)(2,1)}, u32[]{:S(2)}) copy-start(bf16[592,1024]{1,0:T(8,128)(2,1)} %copy-done.32) | copy-start | bytes 3637252
  114.7 21.9 %copy-start.40 = (bf16[4,2,128,512]{3,2,1,0:T(8,128)(2,1)}, bf16[4,2,128,512]{3,2,1,0:T(8,128)(2,1)S(1)}, u32[]{:S(2)}) copy-start(bf16[4,2,128,512]{3,2,1,0:T(8,128)(2,1)S(1)} %get-tuple-element.120) | copy-start | bytes 3145732
  128.7 7.9 %collective-permute-start.12 = (bf16[592,1024]{1,0:T(8,128)(2,1)S(1)}, bf16[592,1024]{1,0:T(8,128)(2,1)S(1)}, u32[]{:S(2)}, u32[]{:S(2)}) collective-permute-start(bf16[592,1024]{1,0:T(8,128)(2,1)S(1)} %convolution_convert_fusion), channel_id=1, source_target_pairs={{0,2},{1,3},{2,0},{3,1},{4,6},{5,7},{6,4},{7,5},{8,10},{9,11},{10,... | collective-permute-start | bytes 3637256 | tf_op jit(solution)/shard_map/ppermute | solution.py:304
  139.8 3.3 collective-permute-start.13
  171.9 25.2 %collective-permute-start.15 = (bf16[2,512,512]{2,1,0:T(8,128)(2,1)S(1)}, bf16[2,512,512]{2,1,0:T(8,128)(2,1)S(1)}, u32[]{:S(2)}, u32[]{:S(2)}) collective-permute-start(bf16[2,512,512]{2,1,0:T(8,128)(2,1)S(1)} %get-tuple-element.127), channel_id=1, source_target_pairs={{0,1},{1,0},{2,3},{3,2},{4,5},{5,4},{6,7},{7,6},{8,9},{9,8},{10,11... | collective-permute-start | bytes 3145736 | tf_op jit(solution)/shard_map/ppermute | solution.py:304
  173.5 24.8 %collective-permute-start.16 = (bf16[2,512,512]{2,1,0:T(8,128)(2,1)S(1)}, bf16[2,512,512]{2,1,0:T(8,128)(2,1)S(1)}, u32[]{:S(2)}, u32[]{:S(2)}) collective-permute-start(bf16[2,512,512]{2,1,0:T(8,128)(2,1)S(1)} %get-tuple-element.128), channel_id=1, source_target_pairs={{0,4},{1,5},{2,6},{3,7},{4,0},{5,1},{6,2},{7,3},{8,12},{9,13},{10,... | collective-permute-start | bytes 3145736 | tf_op jit(solution)/shard_map/ppermute | solution.py:304
  208.3 8.4 %collective-permute-start.17 = (bf16[592,1024]{1,0:T(8,128)(2,1)}, bf16[592,1024]{1,0:T(8,128)(2,1)}, u32[]{:S(2)}, u32[]{:S(2)}) collective-permute-start(bf16[592,1024]{1,0:T(8,128)(2,1)} %get-tuple-element.142), channel_id=1, source_target_pairs={{0,2},{1,3},{2,0},{3,1},{4,6},{5,7},{6,4},{7,5},{8,10},{9,11},{10,... | collective-permute-start | bytes 3637256 | tf_op jit(solution)/shard_map/ppermute | solution.py:304
  208.3 32.9 %collective-permute-start.19 = (bf16[2,512,512]{2,1,0:T(8,128)(2,1)}, bf16[2,512,512]{2,1,0:T(8,128)(2,1)}, u32[]{:S(2)}, u32[]{:S(2)}) collective-permute-start(bf16[2,512,512]{2,1,0:T(8,128)(2,1)} %copy-done.43), channel_id=1, source_target_pairs={{0,1},{1,0},{2,3},{3,2},{4,5},{5,4},{6,7},{7,6},{8,9},{9,8},{10,11... | collective-permute-start | bytes 3145736 | tf_op jit(solution)/shard_map/ppermute | solution.py:304
  208.8 32.4 %collective-permute-start.20 = (bf16[2,512,512]{2,1,0:T(8,128)(2,1)}, bf16[2,512,512]{2,1,0:T(8,128)(2,1)}, u32[]{:S(2)}, u32[]{:S(2)}) collective-permute-start(bf16[2,512,512]{2,1,0:T(8,128)(2,1)} %copy-done.42), channel_id=1, source_target_pairs={{0,4},{1,5},{2,6},{3,7},{4,0},{5,1},{6,2},{7,3},{8,12},{9,13},{10,... | collective-permute-start | bytes 3145736 | tf_op jit(solution)/shard_map/ppermute | solution.py:304
  213.1 32.4 %collective-permute-start.21 = (bf16[512,512]{1,0:T(8,128)(2,1)S(1)}, bf16[512,512]{1,0:T(8,128)(2,1)S(1)}, u32[]{:S(2)}, u32[]{:S(2)}) collective-permute-start(bf16[512,512]{1,0:T(8,128)(2,1)S(1)} %fusion.39), channel_id=1, source_target_pairs={{0,4},{1,5},{2,6},{3,7},{4,0},{5,1},{6,2},{7,3},{8,12},{9,13},{10,... | collective-permute-start | bytes 1572872 | tf_op jit(solution)/shard_map/ppermute | solution.py:304
  215.0 30.5 %collective-permute-start.22 = (bf16[512,512]{1,0:T(8,128)(2,1)S(1)}, bf16[512,512]{1,0:T(8,128)(2,1)S(1)}, u32[]{:S(2)}, u32[]{:S(2)}) collective-permute-start(bf16[512,512]{1,0:T(8,128)(2,1)S(1)} %fusion.40), channel_id=1, source_target_pairs={{0,1},{1,0},{2,3},{3,2},{4,5},{5,4},{6,7},{7,6},{8,9},{9,8},{10,11... | collective-permute-start | bytes 1572872 | tf_op jit(solution)/shard_map/ppermute | solution.py:304
  224.2 29.2 %collective-permute-start.18 = (bf16[592,1024]{1,0:T(8,128)(2,1)S(1)}, bf16[592,1024]{1,0:T(8,128)(2,1)S(1)}, u32[]{:S(2)}, u32[]{:S(2)}) collective-permute-start(bf16[592,1024]{1,0:T(8,128)(2,1)S(1)} %get-tuple-element.261.own_ref), channel_id=1, source_target_pairs={{0,2},{1,3},{2,0},{3,1},{4,6},{5,7},{6,4},{7,5},{8,10},{9,11},{10,... | collective-permute-start | bytes 3637256 | tf_op jit(solution)/shard_map/ppermute | solution.py:304
  224.2 17.1 %slice-start.2 = ((s8[4849664]{0:T(1024)(128)(4,1)}), s8[4194304]{0:T(1024)(128)(4,1)S(1)}, s32[]{:S(2)}) async-start(s8[4849664]{0:T(1024)(128)(4,1)} %bitcast.181), calls=%async_computation.3 | async-start | bytes 8388608
  246.8 26.1 %collective-permute-start.23 = (bf16[512,512]{1,0:T(8,128)(2,1)S(1)}, bf16[512,512]{1,0:T(8,128)(2,1)S(1)}, u32[]{:S(2)}, u32[]{:S(2)}) collective-permute-start(bf16[512,512]{1,0:T(8,128)(2,1)S(1)} %fusion.37), channel_id=1, source_target_pairs={{0,4},{1,5},{2,6},{3,7},{4,0},{5,1},{6,2},{7,3},{8,12},{9,13},{10,... | collective-permute-start | bytes 1572872 | tf_op jit(solution)/shard_map/ppermute | solution.py:304
  249.6 24.1 %collective-permute-start.24 = (bf16[512,512]{1,0:T(8,128)(2,1)S(1)}, bf16[512,512]{1,0:T(8,128)(2,1)S(1)}, u32[]{:S(2)}, u32[]{:S(2)}) collective-permute-start(bf16[512,512]{1,0:T(8,128)(2,1)S(1)} %fusion.38), channel_id=1, source_target_pairs={{0,1},{1,0},{2,3},{3,2},{4,5},{5,4},{6,7},{7,6},{8,9},{9,8},{10,11... | collective-permute-start | bytes 1572872 | tf_op jit(solution)/shard_map/ppermute | solution.py:304
  251.5 21.4 %collective-permute-start.25 = (bf16[2,128,512]{2,1,0:T(8,128)(2,1)S(1)}, bf16[2,128,512]{2,1,0:T(8,128)(2,1)S(1)}, u32[]{:S(2)}, u32[]{:S(2)}) collective-permute-start(bf16[2,128,512]{2,1,0:T(8,128)(2,1)S(1)} %get-tuple-element.152), channel_id=1, source_target_pairs={{0,8},{1,9},{2,10},{3,11},{4,12},{5,13},{6,14},{7,15},{8,0},{9,1},... | collective-permute-start | bytes 786440 | tf_op jit(solution)/shard_map/ppermute | solution.py:304
  251.6 21.4 %collective-permute-start.26 = (bf16[2,128,512]{2,1,0:T(8,128)(2,1)S(1)}, bf16[2,128,512]{2,1,0:T(8,128)(2,1)S(1)}, u32[]{:S(2)}, u32[]{:S(2)}) collective-permute-start(bf16[2,128,512]{2,1,0:T(8,128)(2,1)S(1)} %get-tuple-element.153), channel_id=1, source_target_pairs={{0,16},{1,17},{2,18},{3,19},{4,20},{5,21},{6,22},{7,23},{8,24},{9,... | collective-permute-start | bytes 786440 | tf_op jit(solution)/shard_map/ppermute | solution.py:304
  253.3 19.6 %collective-permute-start.27 = (bf16[2,128,512]{2,1,0:T(8,128)(2,1)S(1)}, bf16[2,128,512]{2,1,0:T(8,128)(2,1)S(1)}, u32[]{:S(2)}, u32[]{:S(2)}) collective-permute-start(bf16[2,128,512]{2,1,0:T(8,128)(2,1)S(1)} %get-tuple-element.154), channel_id=1, source_target_pairs={{0,24},{1,25},{2,26},{3,27},{4,28},{5,29},{6,30},{7,31},{8,16},{9,... | collective-permute-start | bytes 786440 | tf_op jit(solution)/shard_map/ppermute | solution.py:304
  272.9 41.5 %copy-start = (bf16[1184,1536]{1,0:T(8,128)(2,1)}, bf16[1184,1536]{1,0:T(8,128)(2,1)S(1)}, u32[]{:S(2)}) copy-start(bf16[1184,1536]{1,0:T(8,128)(2,1)S(1)} %shard_map.323.refs_1_) | copy-start | bytes 10911748
  281.5 27.2 %collective-permute-start.29 = (bf16[2,512,512]{2,1,0:T(8,128)(2,1)S(1)}, bf16[2,512,512]{2,1,0:T(8,128)(2,1)S(1)}, u32[]{:S(2)}, u32[]{:S(2)}) collective-permute-start(bf16[2,512,512]{2,1,0:T(8,128)(2,1)S(1)} %get-tuple-element.163), channel_id=1, source_target_pairs={{0,1},{1,0},{2,3},{3,2},{4,5},{5,4},{6,7},{7,6},{8,9},{9,8},{10,11... | collective-permute-start | bytes 3145736 | tf_op jit(solution)/shard_map/ppermute | solution.py:304
  282.2 26.6 %collective-permute-start.30 = (bf16[2,512,512]{2,1,0:T(8,128)(2,1)S(1)}, bf16[2,512,512]{2,1,0:T(8,128)(2,1)S(1)}, u32[]{:S(2)}, u32[]{:S(2)}) collective-permute-start(bf16[2,512,512]{2,1,0:T(8,128)(2,1)S(1)} %get-tuple-element.164), channel_id=1, source_target_pairs={{0,4},{1,5},{2,6},{3,7},{4,0},{5,1},{6,2},{7,3},{8,12},{9,13},{10,... | collective-permute-start | bytes 3145736 | tf_op jit(solution)/shard_map/ppermute | solution.py:304
  282.7 20.4 %collective-permute-start.31 = (bf16[2,128,512]{2,1,0:T(8,128)(2,1)S(1)}, bf16[2,128,512]{2,1,0:T(8,128)(2,1)S(1)}, u32[]{:S(2)}, u32[]{:S(2)}) collective-permute-start(bf16[2,128,512]{2,1,0:T(8,128)(2,1)S(1)} %get-tuple-element.159), channel_id=1, source_target_pairs={{0,8},{1,9},{2,10},{3,11},{4,12},{5,13},{6,14},{7,15},{8,0},{9,1},... | collective-permute-start | bytes 786440 | tf_op jit(solution)/shard_map/ppermute | solution.py:304
  285.6 19.9 %collective-permute-start.32 = (bf16[2,128,512]{2,1,0:T(8,128)(2,1)S(1)}, bf16[2,128,512]{2,1,0:T(8,128)(2,1)S(1)}, u32[]{:S(2)}, u32[]{:S(2)}) collective-permute-start(bf16[2,128,512]{2,1,0:T(8,128)(2,1)S(1)} %get-tuple-element.160), channel_id=1, source_target_pairs={{0,16},{1,17},{2,18},{3,19},{4,20},{5,21},{6,22},{7,23},{8,24},{9,... | collective-permute-start | bytes 786440 | tf_op jit(solution)/shard_map/ppermute | solution.py:304
  285.8 19.7 %collective-permute-start.33 = (bf16[2,128,512]{2,1,0:T(8,128)(2,1)S(1)}, bf16[2,128,512]{2,1,0:T(8,128)(2,1)S(1)}, u32[]{:S(2)}, u32[]{:S(2)}) collective-permute-start(bf16[2,128,512]{2,1,0:T(8,128)(2,1)S(1)} %get-tuple-element.161), channel_id=1, source_target_pairs={{0,24},{1,25},{2,26},{3,27},{4,28},{5,29},{6,30},{7,31},{8,16},{9,... | collective-permute-start | bytes 786440 | tf_op jit(solution)/shard_map/ppermute | solution.py:304
  293.5 15.3 %copy-start.20 = (bf16[2,512,512]{2,1,0:T(8,128)(2,1)}, bf16[2,512,512]{2,1,0:T(8,128)(2,1)S(1)}, u32[]{:S(2)}) copy-start(bf16[2,512,512]{2,1,0:T(8,128)(2,1)S(1)} %get-tuple-element.166.one_ref) | copy-start | bytes 3145732
  293.5 16.4 %copy-start.22 = (bf16[2,512,512]{2,1,0:T(8,128)(2,1)}, bf16[2,512,512]{2,1,0:T(8,128)(2,1)S(1)}, u32[]{:S(2)}) copy-start(bf16[2,512,512]{2,1,0:T(8,128)(2,1)S(1)} %get-tuple-element.167.two_ref) | copy-start | bytes 3145732
  303.2 11.9 %collective-permute-start.28 = (bf16[592,1024]{1,0:T(8,128)(2,1)}, bf16[592,1024]{1,0:T(8,128)(2,1)}, u32[]{:S(2)}, u32[]{:S(2)}) collective-permute-start(bf16[592,1024]{1,0:T(8,128)(2,1)} %get-tuple-element.170), channel_id=1, source_target_pairs={{0,2},{1,3},{2,0},{3,1},{4,6},{5,7},{6,4},{7,5},{8,10},{9,11},{10,... | collective-permute-start | bytes 3637256 | tf_op jit(solution)/shard_map/ppermute | solution.py:304
  308.7 10.3 %collective-permute-start.35 = (bf16[592,1024]{1,0:T(8,128)(2,1)}, bf16[592,1024]{1,0:T(8,128)(2,1)}, u32[]{:S(2)}, u32[]{:S(2)}) collective-permute-start(bf16[592,1024]{1,0:T(8,128)(2,1)} %fusion.26), channel_id=1, source_target_pairs={{0,2},{1,3},{2,0},{3,1},{4,6},{5,7},{6,4},{7,5},{8,10},{9,11},{10,... | collective-permute-start | bytes 3637256 | tf_op jit(solution)/shard_map/ppermute | solution.py:304
  311.9 18.4 %collective-permute-start.36 = (bf16[512,512]{1,0:T(8,128)(2,1)}, bf16[512,512]{1,0:T(8,128)(2,1)}, u32[]{:S(2)}, u32[]{:S(2)}) collective-permute-start(bf16[512,512]{1,0:T(8,128)(2,1)} %fusion.41), channel_id=1, source_target_pairs={{0,4},{1,5},{2,6},{3,7},{4,0},{5,1},{6,2},{7,3},{8,12},{9,13},{10,... | collective-permute-start | bytes 1572872 | tf_op jit(solution)/shard_map/ppermute | solution.py:304
  313.5 18.6 %collective-permute-start.37 = (bf16[512,512]{1,0:T(8,128)(2,1)}, bf16[512,512]{1,0:T(8,128)(2,1)}, u32[]{:S(2)}, u32[]{:S(2)}) collective-permute-start(bf16[512,512]{1,0:T(8,128)(2,1)} %fusion.42), channel_id=1, source_target_pairs={{0,1},{1,0},{2,3},{3,2},{4,5},{5,4},{6,7},{7,6},{8,9},{9,8},{10,11... | collective-permute-start | bytes 1572872 | tf_op jit(solution)/shard_map/ppermute | solution.py:304
  317.8 22.9 %collective-permute-start.34 = (bf16[289,1024]{1,0:T(8,128)(2,1)S(1)}, bf16[289,1024]{1,0:T(8,128)(2,1)S(1)}, u32[]{:S(2)}, u32[]{:S(2)}) collective-permute-start(bf16[289,1024]{1,0:T(8,128)(2,1)S(1)} %slice.197), channel_id=1, source_target_pairs={{0,1},{1,0},{2,3},{3,2},{4,5},{5,4},{6,7},{7,6},{8,9},{9,8},{10,11... | collective-permute-start | bytes 1775624 | tf_op jit(solution)/shard_map/ppermute | solution.py:304
  323.4 1.3 collective-permute-start.39
  324.7 12.1 %collective-permute-start.42 = (f32[12288]{0:T(1024)S(1)}, f32[12288]{0:T(1024)S(1)}, u32[]{:S(2)}, u32[]{:S(2)}) collective-permute-start(f32[12288]{0:T(1024)S(1)} %add.276), channel_id=1, source_target_pairs={{0,24},{1,25},{2,26},{3,27},{4,28},{5,29},{6,30},{7,31},{8,16},{9,... | collective-permute-start | bytes 147464 | tf_op jit(solution)/shard_map/ppermute | solution.py:304
  326.7 10.3 %collective-permute-start.41 = (f32[12288]{0:T(1024)S(1)}, f32[12288]{0:T(1024)S(1)}, u32[]{:S(2)}, u32[]{:S(2)}) collective-permute-start(f32[12288]{0:T(1024)S(1)} %add.276), channel_id=1, source_target_pairs={{0,16},{1,17},{2,18},{3,19},{4,20},{5,21},{6,22},{7,23},{8,24},{9,... | collective-permute-start | bytes 147464 | tf_op jit(solution)/shard_map/ppermute | solution.py:304
  330.3 9.0 %collective-permute-start.40 = (f32[12288]{0:T(1024)S(1)}, f32[12288]{0:T(1024)S(1)}, u32[]{:S(2)}, u32[]{:S(2)}) collective-permute-start(f32[12288]{0:T(1024)S(1)} %add.276), channel_id=1, source_target_pairs={{0,8},{1,9},{2,10},{3,11},{4,12},{5,13},{6,14},{7,15},{8,0},{9,1},... | collective-permute-start | bytes 147464 | tf_op jit(solution)/shard_map/ppermute | solution.py:304
  334.9 26.0 %collective-permute-start.45 = (bf16[2,128,512]{2,1,0:T(8,128)(2,1)S(1)}, bf16[2,128,512]{2,1,0:T(8,128)(2,1)S(1)}, u32[]{:S(2)}, u32[]{:S(2)}) collective-permute-start(bf16[2,128,512]{2,1,0:T(8,128)(2,1)S(1)} %get-tuple-element.179), channel_id=1, source_target_pairs={{0,8},{1,9},{2,10},{3,11},{4,12},{5,13},{6,14},{7,15},{8,0},{9,1},... | collective-permute-start | bytes 786440 | tf_op jit(solution)/shard_map/ppermute | solution.py:304
  336.8 24.1 %collective-permute-start.46 = (bf16[2,128,512]{2,1,0:T(8,128)(2,1)S(1)}, bf16[2,128,512]{2,1,0:T(8,128)(2,1)}, u32[]{:S(2)}, u32[]{:S(2)}) collective-permute-start(bf16[2,128,512]{2,1,0:T(8,128)(2,1)S(1)} %get-tuple-element.180), channel_id=1, source_target_pairs={{0,16},{1,17},{2,18},{3,19},{4,20},{5,21},{6,22},{7,23},{8,24},{9,... | collective-permute-start | bytes 786440 | tf_op jit(solution)/shard_map/ppermute | solution.py:304
  337.0 23.9 %collective-permute-start.47 = (bf16[2,128,512]{2,1,0:T(8,128)(2,1)S(1)}, bf16[2,128,512]{2,1,0:T(8,128)(2,1)}, u32[]{:S(2)}, u32[]{:S(2)}) collective-permute-start(bf16[2,128,512]{2,1,0:T(8,128)(2,1)S(1)} %get-tuple-element.181), channel_id=1, source_target_pairs={{0,24},{1,25},{2,26},{3,27},{4,28},{5,29},{6,30},{7,31},{8,16},{9,... | collective-permute-start | bytes 786440 | tf_op jit(solution)/shard_map/ppermute | solution.py:304
  339.3 14.5 %collective-permute-start.38 = (bf16[289,1024]{1,0:T(8,128)(2,1)}, bf16[289,1024]{1,0:T(8,128)(2,1)}, u32[]{:S(2)}, u32[]{:S(2)}) collective-permute-start(bf16[289,1024]{1,0:T(8,128)(2,1)} %slice.292), channel_id=1, source_target_pairs={{0,1},{1,0},{2,3},{3,2},{4,5},{5,4},{6,7},{7,6},{8,9},{9,8},{10,11... | collective-permute-start | bytes 1775624 | tf_op jit(solution)/shard_map/ppermute | solution.py:304
  340.9 2.8 collective-permute-start.48
  343.7 1.5 collective-permute-start.49
  345.3 4.7 %collective-permute-start.43 = (f32[12288]{0:T(1024)S(1)}, f32[12288]{0:T(1024)S(1)}, u32[]{:S(2)}, u32[]{:S(2)}) collective-permute-start(f32[12288]{0:T(1024)S(1)} %add_add_fusion), channel_id=1, source_target_pairs={{0,4},{1,5},{2,6},{3,7},{4,0},{5,1},{6,2},{7,3},{8,12},{9,13},{10,... | collective-permute-start | bytes 147464 | tf_op jit(solution)/shard_map/ppermute | solution.py:304
  353.9 6.4 %collective-permute-start.44 = (f32[12288]{0:T(1024)S(1)}, f32[12288]{0:T(1024)S(1)}, u32[]{:S(2)}, u32[]{:S(2)}) collective-permute-start(f32[12288]{0:T(1024)S(1)} %add.280), channel_id=1, source_target_pairs={{0,1},{1,0},{2,3},{3,2},{4,5},{5,4},{6,7},{7,6},{8,9},{9,8},{10,11... | collective-permute-start | bytes 147464 | tf_op jit(solution)/shard_map/ppermute | solution.py:304
  362.1 1.4 collective-permute-start.50
  (80 other events, 388.0 us)
Sparse Core Ops, SparseCore 0:
  12.2 143.3 all-gather.1

commit v9 on v8

--- a/solution.py
+++ b/solution.py
@@ -781,6 +781,16 @@
     bias = bias_ref[...]
     grad = grad_ref[...]
     product = grad.astype(jnp.float32) * mixed_ref[...].astype(jnp.float32)
+    shape = (8, LANES)
+    head_of = lane_of(shape) // HDIM
+    ones = jnp.where(head_of == lax.broadcasted_iota(jnp.int32, shape, 0), 1.0, 0.0)
+    inner = lax.dot_general(
+        ones,
+        product,
+        (((1,), (1,)), ((), ())),
+        precision=lax.Precision.HIGHEST,
+        preferred_element_type=jnp.float32,
+    )
     grad_query = grad_key = grad_value = None
     for head in range(2):
         mine, query_view, key_view = head_views(query, key, bias, head)
@@ -789,15 +799,7 @@
         probs = jnp.exp(scores - total_ref[0, head : head + 1, :])
         grad_view = jnp.where(mine, grad, zero)
         grad_probs = mat_far(value, grad_view)
-        ones = jnp.where(mine[0:8], 1.0, 0.0)
-        inner = lax.dot_general(
-            ones,
-            product,
-            (((1,), (1,)), ((), ())),
-            precision=lax.Precision.HIGHEST,
-            preferred_element_type=jnp.float32,
-        )
-        grad_scores = (probs * (grad_probs - inner[0:1])).astype(LOW)
+        grad_scores = (probs * (grad_probs - inner[head : head + 1])).astype(LOW)
         one_value = jnp.dot(probs.astype(LOW), grad_view, preferred_element_type=jnp.float32)
         one_key = jnp.dot(
             grad_scores, jnp.where(mine, query, zero), preferred_element_type=jnp.float32

time: 380 us -> 380 us (level)
  transfers between devices with their start and end apart: 52 -> 52, of which waited for: 20 -> 21; matrix products, arithmetic and copies ran while one was open for 17% -> 16% of each run, Pallas kernels for 26% -> 26%
where the time goes in v9:
time: 380 us; the launch traced here: 374 us
  Pallas kernels  130 us (34%)
  waiting for transfers between devices  88.4 us (23%)
  starting transfers between devices  55.3 us (15%)
  local copies, waits for them, and re-layouts  38.2 us (10%)
  other arithmetic  29.8 us (8%)
  between operations  16.9 us (4%)
  matrix products  16 us (4%)
    ppermute x51, waiting for transfers between devices, exchange(): return lax.ppermute(value, BOTH, pairs)  80.7 us
    ppermute x51, starting transfers between devices, exchange(): return lax.ppermute(value, BOTH, pairs)  55.2 us
    pallas_call x2, Pallas kernels, attend_back_image(): pl.pallas_call(kernel, grid=(blocks,), in_specs=[pl.BlockSpec((rows, 3 *...  27.3 us
    pallas_call x6, Pallas kernels, weight_pieces(): pl.pallas_call(kernel, grid=(4,), in_specs=specs, out_specs=[pl.BlockSpec...  26.6 us
    unnamed x197, local copies, waits for them, and re-layouts  23.2 us
    pallas_call x2, Pallas kernels, down_call(): pl.pallas_call(down_kernel, grid_spec=pltpu.PrefetchScalarGridSpec(num_sc...  18.1 us
    pallas_call x2, Pallas kernels, attend_image(): pl.pallas_call(kernel, grid=(blocks,), in_specs=[pl.BlockSpec((rows, 3 *...  15.4 us
    pallas_call x1, Pallas kernels, up_call(): pl.pallas_call(up_kernel, grid_spec=pltpu.PrefetchScalarGridSpec(num_scal...  12.3 us
  transfers between devices with their start and end apart: 52, of which 21 were waited for; matrix products, arithmetic and copies ran while one was open for 16% of the time, Pallas kernels for 26%

profile of v9, /device:TPU:0, one launch (start us, length us, event | category | flops | bytes accessed | tf_op | source)
XLA Modules:
  0.0 374.1 jit_solution(11771278371558994264)
XLA Ops:
  13.9 3.0 collective-permute-start.3
  16.9 2.6 collective-permute-start.4
  20.4 2.9 copy.72
  24.7 1.8 collective-permute-start.1
  26.8 3.8 %collective-permute-done.3.refs_1_ = bf16[2,128,512]{2,1,0:T(8,128)(2,1)S(1)} collective-permute-done((bf16[2,128,512]{2,1,0:T(8,128)(2,1)S(1)}, bf16[2,128,512]{2,1,0:T(8,128)(2,1)S(1)}, u32[]{:S(2)}, u32[]{:S(2)}) %collective-permute-start.3) | collective-permute-done | bytes 262176 | tf_op jit(solution)/shard_map/ppermute | solution.py:304
  30.7 7.1 %collective-permute-done.4.refs_2_ = bf16[2,128,512]{2,1,0:T(8,128)(2,1)S(1)} collective-permute-done((bf16[2,128,512]{2,1,0:T(8,128)(2,1)S(1)}, bf16[2,128,512]{2,1,0:T(8,128)(2,1)S(1)}, u32[]{:S(2)}, u32[]{:S(2)}) %collective-permute-start.4) | collective-permute-done | bytes 262176 | tf_op jit(solution)/shard_map/ppermute | solution.py:304
  37.8 5.3 %collective-permute-done.5.refs_3_ = bf16[2,128,512]{2,1,0:T(8,128)(2,1)S(1)} collective-permute-done((bf16[2,128,512]{2,1,0:T(8,128)(2,1)S(1)}, bf16[2,128,512]{2,1,0:T(8,128)(2,1)S(1)}, u32[]{:S(2)}, u32[]{:S(2)}) %collective-permute-start.5) | collective-permute-done | bytes 262176 | tf_op jit(solution)/shard_map/ppermute | solution.py:304
  43.7 1.6 collective-permute-start.6
  45.3 1.5 collective-permute-start.7
  48.1 8.4 %collective-permute-done.6.refs_1_ = bf16[4,128,512]{2,1,0:T(8,128)(2,1)S(1)} collective-permute-done((bf16[4,128,512]{2,1,0:T(8,128)(2,1)S(1)}, bf16[4,128,512]{2,1,0:T(8,128)(2,1)S(1)}, u32[]{:S(2)}, u32[]{:S(2)}) %collective-permute-start.6) | collective-permute-done | bytes 524320 | tf_op jit(solution)/shard_map/ppermute | solution.py:304
  56.4 17.8 %collective-permute-done.7.refs_3_ = bf16[4,128,512]{2,1,0:T(8,128)(2,1)S(1)} collective-permute-done((bf16[4,128,512]{2,1,0:T(8,128)(2,1)S(1)}, bf16[4,128,512]{2,1,0:T(8,128)(2,1)S(1)}, u32[]{:S(2)}, u32[]{:S(2)}) %collective-permute-start.7) | collective-permute-done | bytes 524320 | tf_op jit(solution)/shard_map/ppermute | solution.py:304
  74.2 2.0 shard_map.306
  79.8 1.7 collective-permute-start.11
  85.4 2.2 shard_map.307.refs_0_
  87.6 3.3 shard_map.308.refs_0_
  92.4 18.7 %collective-permute-done.10.refs_1_ = bf16[2,4,128,512]{3,2,1,0:T(8,128)(2,1)} collective-permute-done((bf16[2,4,128,512]{3,2,1,0:T(8,128)(2,1)}, bf16[2,4,128,512]{3,2,1,0:T(8,128)(2,1)}, u32[]{:S(2)}, u32[]{:S(2)}) %collective-permute-start.10) | collective-permute-done | bytes 1048608 | tf_op jit(solution)/shard_map/ppermute | solution.py:304
  112.1 2.7 shard_map.309
  114.8 5.2 %fusion.refs_0_ = bf16[1184,1536]{1,0:T(8,128)(2,1)S(1)} fusion(bf16[1024,1536]{1,0:T(8,128)(2,1)S(1)} %bitcast.187, f32[1536]{0:T(1024)S(1)} %add.250, bf16[592,1024]{1,0:T(8,128)(2,1)S(1)} %copy-done.34, bf16[592,1024]{1,0:T(8,128)(2,1)S(1)} %copy-done.8), kind=kOutput, calls=%fused_computation.1 | convolution fusion | flops 3733028864 | bytes 9213952 | tf_op jit(solution)/shard_map/dot_general | solution.py:644
  120.1 7.7 %shard_map.310 = (bf16[1184,512]{1,0:T(8,128)(2,1)S(1)}, f32[8,8,592]{2,1,0:T(8,128)S(1)}) custom-call(bf16[1184,1536]{1,0:T(8,128)(2,1)S(1)} %fusion.refs_0_, bf16[592,128]{1,0:T(8,128)(2,1)S(1)} %broadcast_in_dim.56.refs_1_), custom_call_target="tpu_custom_call" | custom-call | flops 2871001088 | bytes 2424832 | tf_op jit(solution)/shard_map/pallas_call | solution.py:824
  128.9 7.7 %shard_map.311 = (bf16[1184,512]{1,0:T(8,128)(2,1)S(1)}, f32[8,8,592]{2,1,0:T(8,128)S(1)}) custom-call(bf16[1184,1536]{1,0:T(8,128)(2,1)S(1)} %fusion.refs_0_, bf16[592,128]{1,0:T(8,128)(2,1)S(1)} %broadcast_in_dim.56.refs_1_, bf16[1184,512]{1,0:T(8,128)(2,1)S(1)} %get-tuple-element.121.refs_2_, ...), custom_call_target="tpu_custom_call", output_to_operand_aliasing={{0}: (2, {}), {1}: (3, {})} | custom-call | flops 2871001088 | bytes 2424832 | tf_op jit(solution)/shard_map/pallas_call | solution.py:824
  140.3 2.8 collective-permute-done.13.far_ref
  143.1 3.3 shard_map.312.refs_0_
  146.4 1.5 copy-done.11
  147.9 7.7 %all-gather.2.cloned.1.call-done = bf16[2048,2048]{1,0:T(8,128)(2,1)} async-done(((bf16[128,2048]{1,0:T(8,128)(2,1)}), bf16[2048,2048]{1,0:T(8,128)(2,1)}) %all-gather.2.cloned.1.call-update) | async-done | bytes 8388624 | tf_op jit(solution)/shard_map/all_gather | solution.py:958
  155.6 12.3 %shard_map.313 = (bf16[1184,2048]{1,0:T(8,128)(2,1)S(1)}, bf16[1184,2048]{1,0:T(8,128)(2,1)S(1)}) custom-call(s32[4]{0:T(128)S(1)} %pad_add_fusion.places_ref, bf16[592,1024]{1,0:T(8,128)(2,1)} %add_convert_fusion.own_ref, bf16[592,1024]{1,0:T(8,128)(2,1)} %collective-permute-done.13.far_ref, bf16[8,2,128,2048]{3,2,1,0:T(8,128)(2,1)} %bitcast.194, ...), custom_call_target="tpu_custom_call" | custom-call | flops 4966055936 | bytes 16318464 | tf_op jit(solution)/shard_map/pallas_call | solution.py:539
  168.0 3.9 %shard_map.314 = (bf16[2,512,512]{2,1,0:T(8,128)(2,1)S(1)}, bf16[2,512,512]{2,1,0:T(8,128)(2,1)S(1)}) custom-call(bf16[2,512,1184]{2,1,0:T(8,128)(2,1)S(1)} %copy-done.15, bf16[1184,2048]{1,0:T(8,128)(2,1)S(1)} %get-tuple-element.168.refs_1_.left_ref), custom_call_target="tpu_custom_call" | custom-call | flops 2483027968 | bytes 11796480 | tf_op jit(solution)/shard_map/pallas_call | solution.py:723
  171.9 1.6 collective-permute-start.15
  175.0 3.9 %shard_map.315 = (bf16[2,512,512]{2,1,0:T(8,128)(2,1)S(1)}, bf16[2,512,512]{2,1,0:T(8,128)(2,1)S(1)}) custom-call(bf16[2,512,1184]{2,1,0:T(8,128)(2,1)S(1)} %copy-done.15, bf16[1184,2048]{1,0:T(8,128)(2,1)S(1)} %get-tuple-element.168.refs_1_.left_ref), custom_call_target="tpu_custom_call" | custom-call | flops 2483027968 | bytes 11796480 | tf_op jit(solution)/shard_map/pallas_call | solution.py:723
  180.9 9.9 %shard_map.316 = (bf16[1184,2048]{1,0:T(8,128)(2,1)S(1)}, f32[1,2048]{1,0:T(1,128)S(1)}) custom-call(s32[4]{0:T(128)S(1)} %pad_add_fusion.places_ref, bf16[592,1024]{1,0:T(8,128)(2,1)} %get-tuple-element.132.own_ref, bf16[592,1024]{1,0:T(8,128)(2,1)} %collective-permute-done.9.far_ref, bf16[8,2,128,2048]{3,2,1,0:T(8,128)(2,1)} %bitcast.195, ...), custom_call_target="tpu_custom_call" | custom-call | flops 4966055936 | bytes 16318464 | tf_op jit(solution)/shard_map/pallas_call | solution.py:579
  190.9 3.9 %shard_map.317 = (bf16[2,512,512]{2,1,0:T(8,128)(2,1)S(1)}, bf16[2,512,512]{2,1,0:T(8,128)(2,1)S(1)}) custom-call(bf16[2,512,1184]{2,1,0:T(8,128)(2,1)S(1)} %copy-done.12, bf16[1184,2048]{1,0:T(8,128)(2,1)S(1)} %get-tuple-element.144.refs_1_.left_ref), custom_call_target="tpu_custom_call" | custom-call | flops 2483027968 | bytes 11796480 | tf_op jit(solution)/shard_map/pallas_call | solution.py:723
  198.4 8.5 %shard_map.318 = (f32[592,1024]{1,0:T(8,128)S(1)}, bf16[592,1024]{1,0:T(8,128)(2,1)}) custom-call(s32[4]{0:T(128)S(1)} %pad_add_fusion.places_ref, bf16[1184,2048]{1,0:T(8,128)(2,1)S(1)} %get-tuple-element.144.refs_1_.left_ref, bf16[8,2,128,2048]{3,2,1,0:T(8,128)(2,1)} %bitcast.196), custom_call_target="tpu_custom_call" | custom-call | flops 1024 | bytes 1024 | tf_op jit(solution)/shard_map/pallas_call | solution.py:622
  211.6 1.5 fusion.39
  215.0 1.6 collective-permute-start.22
  216.7 3.3 multiply_reduce_fusion
  220.0 4.1 %convert_reduce_fusion.3 = (f32[1024]{0:T(1024)S(1)}, bf16[592,1024]{1,0:T(8,128)(2,1)S(1)}, f32[592,1024]{1,0:T(8,128)}) fusion(f32[592]{0:T(1024)S(1)} %broadcast_multiply_fusion.2, f32[592,1024]{1,0:T(8,128)S(1)} %copy-done.47, f32[592]{0:T(1024)S(1)} %broadcast_multiply_fusion.4, f32[592]{0:T(1024)S(1)} %broadcast_multiply_fusion.3, ...), kind=kLoop, calls=%fused_computation.27 | loop fusion | flops 11516928 | bytes 10931776 | tf_op jit(solution)/shard_map/reduce_sum | solution.py:899
  226.6 13.7 %shard_map.319.refs_5_ = bf16[1184,1536]{1,0:T(8,128)(2,1)S(1)} custom-call(bf16[1184,1536]{1,0:T(8,128)(2,1)S(1)} %copy-done.45, bf16[592,128]{1,0:T(8,128)(2,1)S(1)} %broadcast_in_dim.56.refs_1_, bf16[592,512]{1,0:T(8,128)(2,1)S(1)} %convolution_convert_fusion.1.refs_2_, bf16[1184,512]{1,0:T(8,128)(2,1)S(1)} %copy-done.10, ...), custom_call_target="tpu_custom_call" | custom-call | flops 7177502720 | bytes 4849664 | tf_op jit(solution)/shard_map/pallas_call | solution.py:858
  240.4 3.9 %shard_map.320 = (bf16[2,512,512]{2,1,0:T(8,128)(2,1)S(1)}, bf16[2,512,512]{2,1,0:T(8,128)(2,1)S(1)}) custom-call(bf16[2,512,1184]{2,1,0:T(8,128)(2,1)S(1)} %copy-done.13, bf16[1184,2048]{1,0:T(8,128)(2,1)S(1)} %bitcast.182), custom_call_target="tpu_custom_call" | custom-call | flops 2483027968 | bytes 11796480 | tf_op jit(solution)/shard_map/pallas_call | solution.py:723
  246.7 1.5 collective-permute-start.23
  249.4 1.6 collective-permute-start.24
  251.6 1.6 collective-permute-start.26
  253.2 2.8 collective-permute-start.27
  256.7 1.6 shard_map.322.refs_2_
  258.4 13.6 %shard_map.323.refs_1_ = bf16[1184,1536]{1,0:T(8,128)(2,1)S(1)} custom-call(bf16[1184,1536]{1,0:T(8,128)(2,1)S(1)} %copy-done.45, bf16[592,128]{1,0:T(8,128)(2,1)S(1)} %broadcast_in_dim.56.refs_1_, bf16[592,512]{1,0:T(8,128)(2,1)S(1)} %convolution_convert_fusion.2.refs_2_, bf16[1184,512]{1,0:T(8,128)(2,1)S(1)} %copy-done.10, ...), custom_call_target="tpu_custom_call", output_to_operand_aliasing={{}: (5, {})} | custom-call | flops 7177502720 | bytes 4849664 | tf_op jit(solution)/shard_map/pallas_call | solution.py:858
  272.9 2.1 shard_map.324
  275.1 5.5 %shard_map.325 = (bf16[2,512,512]{2,1,0:T(8,128)(2,1)S(1)}, bf16[2,512,512]{2,1,0:T(8,128)(2,1)S(1)}) custom-call(bf16[2,512,1184]{2,1,0:T(8,128)(2,1)S(1)} %shard_map.307.refs_0_, bf16[1184,1536]{1,0:T(8,128)(2,1)S(1)} %shard_map.323.refs_1_, bf16[2,512,1184]{2,1,0:T(8,128)(2,1)S(1)} %shard_map.322.refs_2_, bf16[1184,512]{1,0:T(8,128)(2,1)S(1)} %copy-done.10), custom_call_target="tpu_custom_call" | custom-call | flops 1024 | bytes 1024 | tf_op jit(solution)/shard_map/pallas_call | solution.py:723
  281.6 3.8 %collective-permute-start.31 = (bf16[2,128,512]{2,1,0:T(8,128)(2,1)S(1)}, bf16[2,128,512]{2,1,0:T(8,128)(2,1)S(1)}, u32[]{:S(2)}, u32[]{:S(2)}) collective-permute-start(bf16[2,128,512]{2,1,0:T(8,128)(2,1)S(1)} %get-tuple-element.159), channel_id=1, source_target_pairs={{0,8},{1,9},{2,10},{3,11},{4,12},{5,13},{6,14},{7,15},{8,0},{9,1},... | collective-permute-start | bytes 786440 | tf_op jit(solution)/shard_map/ppermute | solution.py:304
  285.8 2.0 collective-permute-start.33
  287.8 5.5 %shard_map.326 = (bf16[2,512,512]{2,1,0:T(8,128)(2,1)S(1)}, bf16[2,512,512]{2,1,0:T(8,128)(2,1)S(1)}) custom-call(bf16[2,512,1184]{2,1,0:T(8,128)(2,1)S(1)} %shard_map.307.refs_0_, bf16[1184,1536]{1,0:T(8,128)(2,1)S(1)} %shard_map.323.refs_1_, bf16[2,512,1184]{2,1,0:T(8,128)(2,1)S(1)} %shard_map.322.refs_2_, bf16[1184,512]{1,0:T(8,128)(2,1)S(1)} %copy-done.10), custom_call_target="tpu_custom_call" | custom-call | flops 1024 | bytes 1024 | tf_op jit(solution)/shard_map/pallas_call | solution.py:723
  293.3 9.6 %shard_map.327 = (f32[592,1024]{1,0:T(8,128)S(1)}, bf16[592,1024]{1,0:T(8,128)(2,1)}) custom-call(s32[4]{0:T(128)S(1)} %pad_add_fusion.places_ref, bf16[1184,2048]{1,0:T(8,128)(2,1)S(1)} %bitcast.180, bf16[8,2,128,2048]{3,2,1,0:T(8,128)(2,1)} %bitcast.197), custom_call_target="tpu_custom_call" | custom-call | flops 1024 | bytes 1024 | tf_op jit(solution)/shard_map/pallas_call | solution.py:622
  303.0 2.5 collective-permute-done.32
  305.4 3.1 fusion.26
  311.8 1.5 collective-permute-start.36
  315.1 2.6 multiply_convert_fusion
  319.4 4.0 %fusion.13 = (f32[1024]{0:T(1024)S(1)}, f32[592]{0:T(1024)S(1)}, f32[592]{0:T(1024)S(1)}, f32[1024]{0:T(1024)S(1)}, f32[592,1024]{1,0:T(8,128)S(1)}) fusion(f32[592]{0:T(1024)S(1)} %add_rsqrt_fusion.1, f32[592]{0:T(1024)S(1)} %broadcast_multiply_fusion.5, bf16[296,1024]{1,0:T(8,128)(2,1)S(1)} %copy-done.54, bf16[296,1024]{1,0:T(8,128)(2,1)S(1)} %copy-done.50, ...), kind=kOutput, calls=%fused_computation.18 | convolution fusion | flops 1871360768 | bytes 9839232 | tf_op jit(solution)/shard_map/dot_general | solution.py:494
  324.8 1.9 collective-permute-start.42
  326.6 3.8 %collective-permute-start.41 = (f32[12288]{0:T(1024)S(1)}, f32[12288]{0:T(1024)S(1)}, u32[]{:S(2)}, u32[]{:S(2)}) collective-permute-start(f32[12288]{0:T(1024)S(1)} %add.276), channel_id=1, source_target_pairs={{0,16},{1,17},{2,18},{3,19},{4,20},{5,21},{6,22},{7,23},{8,24},{9,... | collective-permute-start | bytes 147464 | tf_op jit(solution)/shard_map/ppermute | solution.py:304
  330.4 1.5 fusion.12
  333.1 1.7 shard_map.328
  334.8 2.1 collective-permute-start.45
  337.0 2.4 collective-permute-start.47
  341.4 2.2 copy.92
  350.0 3.9 %collective-permute-done.38 = bf16[289,1024]{1,0:T(8,128)(2,1)} collective-permute-done((bf16[289,1024]{1,0:T(8,128)(2,1)}, bf16[289,1024]{1,0:T(8,128)(2,1)}, u32[]{:S(2)}, u32[]{:S(2)}) %collective-permute-start.38) | collective-permute-done | bytes 591904 | tf_op jit(solution)/shard_map/ppermute | solution.py:304
  355.0 1.8 fusion.29
  357.0 3.2 copy.93
  (393 shorter events, 73.4 us)
Async XLA Ops:
  7.2 148.4 %all-gather.2.cloned.1.call-start = ((), (), s32[]{:S(2)}) async-start(), calls=%async_computation | async-start | bytes 8912896 | tf_op jit(solution)/shard_map/all_gather | solution.py:958
  9.5 1.7 collective-permute-start.14
  12.3 1.4 collective-permute-start
  13.9 16.8 %collective-permute-start.3 = (bf16[2,128,512]{2,1,0:T(8,128)(2,1)S(1)}, bf16[2,128,512]{2,1,0:T(8,128)(2,1)S(1)}, u32[]{:S(2)}, u32[]{:S(2)}) collective-permute-start(bf16[2,128,512]{2,1,0:T(8,128)(2,1)S(1)} %bitcast.183), channel_id=1, source_target_pairs={{0,8},{1,9},{2,10},{3,11},{4,12},{5,13},{6,14},{7,15},{8,0},{9,1},... | collective-permute-start | bytes 786440 | tf_op jit(solution)/shard_map/ppermute | solution.py:304
  16.9 20.9 %collective-permute-start.4 = (bf16[2,128,512]{2,1,0:T(8,128)(2,1)S(1)}, bf16[2,128,512]{2,1,0:T(8,128)(2,1)S(1)}, u32[]{:S(2)}, u32[]{:S(2)}) collective-permute-start(bf16[2,128,512]{2,1,0:T(8,128)(2,1)S(1)} %bitcast.184), channel_id=1, source_target_pairs={{0,16},{1,17},{2,18},{3,19},{4,20},{5,21},{6,22},{7,23},{8,24},{9,... | collective-permute-start | bytes 786440 | tf_op jit(solution)/shard_map/ppermute | solution.py:304
  19.5 23.6 %collective-permute-start.5 = (bf16[2,128,512]{2,1,0:T(8,128)(2,1)S(1)}, bf16[2,128,512]{2,1,0:T(8,128)(2,1)S(1)}, u32[]{:S(2)}, u32[]{:S(2)}) collective-permute-start(bf16[2,128,512]{2,1,0:T(8,128)(2,1)S(1)} %bitcast.185), channel_id=1, source_target_pairs={{0,24},{1,25},{2,26},{3,27},{4,28},{5,29},{6,30},{7,31},{8,16},{9,... | collective-permute-start | bytes 786440 | tf_op jit(solution)/shard_map/ppermute | solution.py:304
  20.4 56.6 %copy-start.48 = (bf16[296,1024]{1,0:T(8,128)(2,1)}, bf16[296,1024]{1,0:T(8,128)(2,1)S(1)}, u32[]{:S(2)}) copy-start(bf16[296,1024]{1,0:T(8,128)(2,1)S(1)} %get-tuple-element.269) | copy-start | bytes 1818628
  20.4 26.4 %copy-start.79 = (bf16[1024]{0:T(1024)(128)(2,1)S(1)}, bf16[1024]{0:T(1024)(128)(2,1)}, u32[]{:S(2)}) copy-start(bf16[1024]{0:T(1024)(128)(2,1)} %param.22) | copy-start | bytes 6148
  20.4 26.4 %copy-start.80 = (bf16[1024]{0:T(1024)(128)(2,1)S(1)}, bf16[1024]{0:T(1024)(128)(2,1)}, u32[]{:S(2)}) copy-start(bf16[1024]{0:T(1024)(128)(2,1)} %param.21) | copy-start | bytes 6148
  20.4 26.4 %copy-start.87 = (s32[2]{0:T(128)S(1)}, s32[2]{0:T(128)}, u32[]{:S(2)}) copy-start(s32[2]{0:T(128)} %param.20) | copy-start | bytes 28
  24.6 53.0 %copy-start.56 = (bf16[296,1024]{1,0:T(8,128)(2,1)}, bf16[296,1024]{1,0:T(8,128)(2,1)S(1)}, u32[]{:S(2)}) copy-start(bf16[296,1024]{1,0:T(8,128)(2,1)S(1)} %get-tuple-element.267) | copy-start | bytes 1818628
  24.7 51.6 %collective-permute-start.1 = (bf16[296,1024]{1,0:T(8,128)(2,1)S(1)}, bf16[296,1024]{1,0:T(8,128)(2,1)S(1)}, u32[]{:S(2)}, u32[]{:S(2)}) collective-permute-start(bf16[296,1024]{1,0:T(8,128)(2,1)S(1)} %copy-done.61), channel_id=1, source_target_pairs={{0,1},{1,0},{2,3},{3,2},{4,5},{5,4},{6,7},{7,6},{8,9},{9,8},{10,11... | collective-permute-start | bytes 1818632 | tf_op jit(solution)/shard_map/ppermute | solution.py:304
  26.5 49.7 %collective-permute-start.2 = (bf16[296,1024]{1,0:T(8,128)(2,1)S(1)}, bf16[296,1024]{1,0:T(8,128)(2,1)S(1)}, u32[]{:S(2)}, u32[]{:S(2)}) collective-permute-start(bf16[296,1024]{1,0:T(8,128)(2,1)S(1)} %get-tuple-element.109), channel_id=1, source_target_pairs={{0,1},{1,0},{2,3},{3,2},{4,5},{5,4},{6,7},{7,6},{8,9},{9,8},{10,11... | collective-permute-start | bytes 1818632 | tf_op jit(solution)/shard_map/ppermute | solution.py:304
  43.7 12.7 %collective-permute-start.6 = (bf16[4,128,512]{2,1,0:T(8,128)(2,1)S(1)}, bf16[4,128,512]{2,1,0:T(8,128)(2,1)S(1)}, u32[]{:S(2)}, u32[]{:S(2)}) collective-permute-start(bf16[4,128,512]{2,1,0:T(8,128)(2,1)S(1)} %get-tuple-element.110.refs_0_), channel_id=1, source_target_pairs={{0,4},{1,5},{2,6},{3,7},{4,0},{5,1},{6,2},{7,3},{8,12},{9,13},{10,... | collective-permute-start | bytes 1572872 | tf_op jit(solution)/shard_map/ppermute | solution.py:304
  45.3 29.0 %collective-permute-start.7 = (bf16[4,128,512]{2,1,0:T(8,128)(2,1)S(1)}, bf16[4,128,512]{2,1,0:T(8,128)(2,1)S(1)}, u32[]{:S(2)}, u32[]{:S(2)}) collective-permute-start(bf16[4,128,512]{2,1,0:T(8,128)(2,1)S(1)} %get-tuple-element.111.refs_2_), channel_id=1, source_target_pairs={{0,1},{1,0},{2,3},{3,2},{4,5},{5,4},{6,7},{7,6},{8,9},{9,8},{10,11... | collective-permute-start | bytes 1572872 | tf_op jit(solution)/shard_map/ppermute | solution.py:304
  77.5 4.2 %collective-permute-start.8 = (bf16[592,1024]{1,0:T(8,128)(2,1)S(1)}, bf16[592,1024]{1,0:T(8,128)(2,1)S(1)}, u32[]{:S(2)}, u32[]{:S(2)}) collective-permute-start(bf16[592,1024]{1,0:T(8,128)(2,1)S(1)} %fusion.8.own_ref), channel_id=1, source_target_pairs={{0,2},{1,3},{2,0},{3,1},{4,6},{5,7},{6,4},{7,5},{8,10},{9,11},{10,... | collective-permute-start | bytes 3637256 | tf_op jit(solution)/shard_map/ppermute | solution.py:304
  79.0 8.6 %collective-permute-start.9 = (bf16[592,1024]{1,0:T(8,128)(2,1)}, bf16[592,1024]{1,0:T(8,128)(2,1)}, u32[]{:S(2)}, u32[]{:S(2)}) collective-permute-start(bf16[592,1024]{1,0:T(8,128)(2,1)} %get-tuple-element.132.own_ref), channel_id=1, source_target_pairs={{0,2},{1,3},{2,0},{3,1},{4,6},{5,7},{6,4},{7,5},{8,10},{9,11},{10,... | collective-permute-start | bytes 3637256 | tf_op jit(solution)/shard_map/ppermute | solution.py:304
  79.5 31.6 %collective-permute-start.10 = (bf16[2,4,128,512]{3,2,1,0:T(8,128)(2,1)}, bf16[2,4,128,512]{3,2,1,0:T(8,128)(2,1)}, u32[]{:S(2)}, u32[]{:S(2)}) collective-permute-start(bf16[2,4,128,512]{3,2,1,0:T(8,128)(2,1)} %get-tuple-element.112.refs_0_), channel_id=1, source_target_pairs={{0,1},{1,0},{2,3},{3,2},{4,5},{5,4},{6,7},{7,6},{8,9},{9,8},{10,11... | collective-permute-start | bytes 3145736 | tf_op jit(solution)/shard_map/ppermute | solution.py:304
  79.8 32.3 %collective-permute-start.11 = (bf16[2,4,128,512]{3,2,1,0:T(8,128)(2,1)}, bf16[2,4,128,512]{3,2,1,0:T(8,128)(2,1)}, u32[]{:S(2)}, u32[]{:S(2)}) collective-permute-start(bf16[2,4,128,512]{3,2,1,0:T(8,128)(2,1)} %get-tuple-element.113.refs_2_), channel_id=1, source_target_pairs={{0,4},{1,5},{2,6},{3,7},{4,0},{5,1},{6,2},{7,3},{8,12},{9,13},{10,... | collective-permute-start | bytes 3145736 | tf_op jit(solution)/shard_map/ppermute | solution.py:304
  92.4 22.4 %copy-start.8 = (bf16[592,1024]{1,0:T(8,128)(2,1)S(1)}, bf16[592,1024]{1,0:T(8,128)(2,1)}, u32[]{:S(2)}) copy-start(bf16[592,1024]{1,0:T(8,128)(2,1)} %copy-done.6) | copy-start | bytes 3637252
  92.4 22.4 %copy-start.34 = (bf16[592,1024]{1,0:T(8,128)(2,1)S(1)}, bf16[592,1024]{1,0:T(8,128)(2,1)}, u32[]{:S(2)}) copy-start(bf16[592,1024]{1,0:T(8,128)(2,1)} %copy-done.32) | copy-start | bytes 3637252
  114.7 21.9 %copy-start.40 = (bf16[4,2,128,512]{3,2,1,0:T(8,128)(2,1)}, bf16[4,2,128,512]{3,2,1,0:T(8,128)(2,1)S(1)}, u32[]{:S(2)}) copy-start(bf16[4,2,128,512]{3,2,1,0:T(8,128)(2,1)S(1)} %get-tuple-element.120) | copy-start | bytes 3145732
  128.7 7.9 %collective-permute-start.12 = (bf16[592,1024]{1,0:T(8,128)(2,1)S(1)}, bf16[592,1024]{1,0:T(8,128)(2,1)S(1)}, u32[]{:S(2)}, u32[]{:S(2)}) collective-permute-start(bf16[592,1024]{1,0:T(8,128)(2,1)S(1)} %convolution_convert_fusion), channel_id=1, source_target_pairs={{0,2},{1,3},{2,0},{3,1},{4,6},{5,7},{6,4},{7,5},{8,10},{9,11},{10,... | collective-permute-start | bytes 3637256 | tf_op jit(solution)/shard_map/ppermute | solution.py:304
  139.8 3.3 collective-permute-start.13
  171.9 25.2 %collective-permute-start.15 = (bf16[2,512,512]{2,1,0:T(8,128)(2,1)S(1)}, bf16[2,512,512]{2,1,0:T(8,128)(2,1)S(1)}, u32[]{:S(2)}, u32[]{:S(2)}) collective-permute-start(bf16[2,512,512]{2,1,0:T(8,128)(2,1)S(1)} %get-tuple-element.127), channel_id=1, source_target_pairs={{0,1},{1,0},{2,3},{3,2},{4,5},{5,4},{6,7},{7,6},{8,9},{9,8},{10,11... | collective-permute-start | bytes 3145736 | tf_op jit(solution)/shard_map/ppermute | solution.py:304
  173.5 24.8 %collective-permute-start.16 = (bf16[2,512,512]{2,1,0:T(8,128)(2,1)S(1)}, bf16[2,512,512]{2,1,0:T(8,128)(2,1)S(1)}, u32[]{:S(2)}, u32[]{:S(2)}) collective-permute-start(bf16[2,512,512]{2,1,0:T(8,128)(2,1)S(1)} %get-tuple-element.128), channel_id=1, source_target_pairs={{0,4},{1,5},{2,6},{3,7},{4,0},{5,1},{6,2},{7,3},{8,12},{9,13},{10,... | collective-permute-start | bytes 3145736 | tf_op jit(solution)/shard_map/ppermute | solution.py:304
  208.3 8.4 %collective-permute-start.17 = (bf16[592,1024]{1,0:T(8,128)(2,1)}, bf16[592,1024]{1,0:T(8,128)(2,1)}, u32[]{:S(2)}, u32[]{:S(2)}) collective-permute-start(bf16[592,1024]{1,0:T(8,128)(2,1)} %get-tuple-element.142), channel_id=1, source_target_pairs={{0,2},{1,3},{2,0},{3,1},{4,6},{5,7},{6,4},{7,5},{8,10},{9,11},{10,... | collective-permute-start | bytes 3637256 | tf_op jit(solution)/shard_map/ppermute | solution.py:304
  208.3 32.0 %collective-permute-start.19 = (bf16[2,512,512]{2,1,0:T(8,128)(2,1)}, bf16[2,512,512]{2,1,0:T(8,128)(2,1)}, u32[]{:S(2)}, u32[]{:S(2)}) collective-permute-start(bf16[2,512,512]{2,1,0:T(8,128)(2,1)} %copy-done.43), channel_id=1, source_target_pairs={{0,1},{1,0},{2,3},{3,2},{4,5},{5,4},{6,7},{7,6},{8,9},{9,8},{10,11... | collective-permute-start | bytes 3145736 | tf_op jit(solution)/shard_map/ppermute | solution.py:304
  208.8 31.5 %collective-permute-start.20 = (bf16[2,512,512]{2,1,0:T(8,128)(2,1)}, bf16[2,512,512]{2,1,0:T(8,128)(2,1)}, u32[]{:S(2)}, u32[]{:S(2)}) collective-permute-start(bf16[2,512,512]{2,1,0:T(8,128)(2,1)} %copy-done.42), channel_id=1, source_target_pairs={{0,4},{1,5},{2,6},{3,7},{4,0},{5,1},{6,2},{7,3},{8,12},{9,13},{10,... | collective-permute-start | bytes 3145736 | tf_op jit(solution)/shard_map/ppermute | solution.py:304
  213.1 32.4 %collective-permute-start.21 = (bf16[512,512]{1,0:T(8,128)(2,1)S(1)}, bf16[512,512]{1,0:T(8,128)(2,1)S(1)}, u32[]{:S(2)}, u32[]{:S(2)}) collective-permute-start(bf16[512,512]{1,0:T(8,128)(2,1)S(1)} %fusion.39), channel_id=1, source_target_pairs={{0,4},{1,5},{2,6},{3,7},{4,0},{5,1},{6,2},{7,3},{8,12},{9,13},{10,... | collective-permute-start | bytes 1572872 | tf_op jit(solution)/shard_map/ppermute | solution.py:304
  215.0 30.5 %collective-permute-start.22 = (bf16[512,512]{1,0:T(8,128)(2,1)S(1)}, bf16[512,512]{1,0:T(8,128)(2,1)S(1)}, u32[]{:S(2)}, u32[]{:S(2)}) collective-permute-start(bf16[512,512]{1,0:T(8,128)(2,1)S(1)} %fusion.40), channel_id=1, source_target_pairs={{0,1},{1,0},{2,3},{3,2},{4,5},{5,4},{6,7},{7,6},{8,9},{9,8},{10,11... | collective-permute-start | bytes 1572872 | tf_op jit(solution)/shard_map/ppermute | solution.py:304
  224.2 29.0 %collective-permute-start.18 = (bf16[592,1024]{1,0:T(8,128)(2,1)S(1)}, bf16[592,1024]{1,0:T(8,128)(2,1)S(1)}, u32[]{:S(2)}, u32[]{:S(2)}) collective-permute-start(bf16[592,1024]{1,0:T(8,128)(2,1)S(1)} %get-tuple-element.261.own_ref), channel_id=1, source_target_pairs={{0,2},{1,3},{2,0},{3,1},{4,6},{5,7},{6,4},{7,5},{8,10},{9,11},{10,... | collective-permute-start | bytes 3637256 | tf_op jit(solution)/shard_map/ppermute | solution.py:304
  224.2 16.2 %slice-start.2 = ((s8[4849664]{0:T(1024)(128)(4,1)}), s8[4194304]{0:T(1024)(128)(4,1)S(1)}, s32[]{:S(2)}) async-start(s8[4849664]{0:T(1024)(128)(4,1)} %bitcast.181), calls=%async_computation.3 | async-start | bytes 8388608
  246.7 26.2 %collective-permute-start.23 = (bf16[512,512]{1,0:T(8,128)(2,1)S(1)}, bf16[512,512]{1,0:T(8,128)(2,1)S(1)}, u32[]{:S(2)}, u32[]{:S(2)}) collective-permute-start(bf16[512,512]{1,0:T(8,128)(2,1)S(1)} %fusion.37), channel_id=1, source_target_pairs={{0,4},{1,5},{2,6},{3,7},{4,0},{5,1},{6,2},{7,3},{8,12},{9,13},{10,... | collective-permute-start | bytes 1572872 | tf_op jit(solution)/shard_map/ppermute | solution.py:304
  249.4 23.5 %collective-permute-start.24 = (bf16[512,512]{1,0:T(8,128)(2,1)S(1)}, bf16[512,512]{1,0:T(8,128)(2,1)S(1)}, u32[]{:S(2)}, u32[]{:S(2)}) collective-permute-start(bf16[512,512]{1,0:T(8,128)(2,1)S(1)} %fusion.38), channel_id=1, source_target_pairs={{0,1},{1,0},{2,3},{3,2},{4,5},{5,4},{6,7},{7,6},{8,9},{9,8},{10,11... | collective-permute-start | bytes 1572872 | tf_op jit(solution)/shard_map/ppermute | solution.py:304
  251.5 20.5 %collective-permute-start.25 = (bf16[2,128,512]{2,1,0:T(8,128)(2,1)S(1)}, bf16[2,128,512]{2,1,0:T(8,128)(2,1)S(1)}, u32[]{:S(2)}, u32[]{:S(2)}) collective-permute-start(bf16[2,128,512]{2,1,0:T(8,128)(2,1)S(1)} %get-tuple-element.152), channel_id=1, source_target_pairs={{0,8},{1,9},{2,10},{3,11},{4,12},{5,13},{6,14},{7,15},{8,0},{9,1},... | collective-permute-start | bytes 786440 | tf_op jit(solution)/shard_map/ppermute | solution.py:304
  251.6 21.3 %collective-permute-start.26 = (bf16[2,128,512]{2,1,0:T(8,128)(2,1)S(1)}, bf16[2,128,512]{2,1,0:T(8,128)(2,1)S(1)}, u32[]{:S(2)}, u32[]{:S(2)}) collective-permute-start(bf16[2,128,512]{2,1,0:T(8,128)(2,1)S(1)} %get-tuple-element.153), channel_id=1, source_target_pairs={{0,16},{1,17},{2,18},{3,19},{4,20},{5,21},{6,22},{7,23},{8,24},{9,... | collective-permute-start | bytes 786440 | tf_op jit(solution)/shard_map/ppermute | solution.py:304
  253.2 19.7 %collective-permute-start.27 = (bf16[2,128,512]{2,1,0:T(8,128)(2,1)S(1)}, bf16[2,128,512]{2,1,0:T(8,128)(2,1)S(1)}, u32[]{:S(2)}, u32[]{:S(2)}) collective-permute-start(bf16[2,128,512]{2,1,0:T(8,128)(2,1)S(1)} %get-tuple-element.154), channel_id=1, source_target_pairs={{0,24},{1,25},{2,26},{3,27},{4,28},{5,29},{6,30},{7,31},{8,16},{9,... | collective-permute-start | bytes 786440 | tf_op jit(solution)/shard_map/ppermute | solution.py:304
  271.9 42.4 %copy-start = (bf16[1184,1536]{1,0:T(8,128)(2,1)}, bf16[1184,1536]{1,0:T(8,128)(2,1)S(1)}, u32[]{:S(2)}) copy-start(bf16[1184,1536]{1,0:T(8,128)(2,1)S(1)} %shard_map.323.refs_1_) | copy-start | bytes 10911748
  280.6 28.1 %collective-permute-start.29 = (bf16[2,512,512]{2,1,0:T(8,128)(2,1)S(1)}, bf16[2,512,512]{2,1,0:T(8,128)(2,1)S(1)}, u32[]{:S(2)}, u32[]{:S(2)}) collective-permute-start(bf16[2,512,512]{2,1,0:T(8,128)(2,1)S(1)} %get-tuple-element.163), channel_id=1, source_target_pairs={{0,1},{1,0},{2,3},{3,2},{4,5},{5,4},{6,7},{7,6},{8,9},{9,8},{10,11... | collective-permute-start | bytes 3145736 | tf_op jit(solution)/shard_map/ppermute | solution.py:304
  281.1 27.6 %collective-permute-start.30 = (bf16[2,512,512]{2,1,0:T(8,128)(2,1)S(1)}, bf16[2,512,512]{2,1,0:T(8,128)(2,1)S(1)}, u32[]{:S(2)}, u32[]{:S(2)}) collective-permute-start(bf16[2,512,512]{2,1,0:T(8,128)(2,1)S(1)} %get-tuple-element.164), channel_id=1, source_target_pairs={{0,4},{1,5},{2,6},{3,7},{4,0},{5,1},{6,2},{7,3},{8,12},{9,13},{10,... | collective-permute-start | bytes 3145736 | tf_op jit(solution)/shard_map/ppermute | solution.py:304
  281.6 21.3 %collective-permute-start.31 = (bf16[2,128,512]{2,1,0:T(8,128)(2,1)S(1)}, bf16[2,128,512]{2,1,0:T(8,128)(2,1)S(1)}, u32[]{:S(2)}, u32[]{:S(2)}) collective-permute-start(bf16[2,128,512]{2,1,0:T(8,128)(2,1)S(1)} %get-tuple-element.159), channel_id=1, source_target_pairs={{0,8},{1,9},{2,10},{3,11},{4,12},{5,13},{6,14},{7,15},{8,0},{9,1},... | collective-permute-start | bytes 786440 | tf_op jit(solution)/shard_map/ppermute | solution.py:304
  285.4 20.0 %collective-permute-start.32 = (bf16[2,128,512]{2,1,0:T(8,128)(2,1)S(1)}, bf16[2,128,512]{2,1,0:T(8,128)(2,1)S(1)}, u32[]{:S(2)}, u32[]{:S(2)}) collective-permute-start(bf16[2,128,512]{2,1,0:T(8,128)(2,1)S(1)} %get-tuple-element.160), channel_id=1, source_target_pairs={{0,16},{1,17},{2,18},{3,19},{4,20},{5,21},{6,22},{7,23},{8,24},{9,... | collective-permute-start | bytes 786440 | tf_op jit(solution)/shard_map/ppermute | solution.py:304
  285.8 19.6 %collective-permute-start.33 = (bf16[2,128,512]{2,1,0:T(8,128)(2,1)S(1)}, bf16[2,128,512]{2,1,0:T(8,128)(2,1)S(1)}, u32[]{:S(2)}, u32[]{:S(2)}) collective-permute-start(bf16[2,128,512]{2,1,0:T(8,128)(2,1)S(1)} %get-tuple-element.161), channel_id=1, source_target_pairs={{0,24},{1,25},{2,26},{3,27},{4,28},{5,29},{6,30},{7,31},{8,16},{9,... | collective-permute-start | bytes 786440 | tf_op jit(solution)/shard_map/ppermute | solution.py:304
  293.3 15.4 %copy-start.20 = (bf16[2,512,512]{2,1,0:T(8,128)(2,1)}, bf16[2,512,512]{2,1,0:T(8,128)(2,1)S(1)}, u32[]{:S(2)}) copy-start(bf16[2,512,512]{2,1,0:T(8,128)(2,1)S(1)} %get-tuple-element.166.one_ref) | copy-start | bytes 3145732
  293.3 16.5 %copy-start.22 = (bf16[2,512,512]{2,1,0:T(8,128)(2,1)}, bf16[2,512,512]{2,1,0:T(8,128)(2,1)S(1)}, u32[]{:S(2)}) copy-start(bf16[2,512,512]{2,1,0:T(8,128)(2,1)S(1)} %get-tuple-element.167.two_ref) | copy-start | bytes 3145732
  302.9 12.2 %collective-permute-start.28 = (bf16[592,1024]{1,0:T(8,128)(2,1)}, bf16[592,1024]{1,0:T(8,128)(2,1)}, u32[]{:S(2)}, u32[]{:S(2)}) collective-permute-start(bf16[592,1024]{1,0:T(8,128)(2,1)} %get-tuple-element.170), channel_id=1, source_target_pairs={{0,2},{1,3},{2,0},{3,1},{4,6},{5,7},{6,4},{7,5},{8,10},{9,11},{10,... | collective-permute-start | bytes 3637256 | tf_op jit(solution)/shard_map/ppermute | solution.py:304
  308.6 10.3 %collective-permute-start.35 = (bf16[592,1024]{1,0:T(8,128)(2,1)}, bf16[592,1024]{1,0:T(8,128)(2,1)}, u32[]{:S(2)}, u32[]{:S(2)}) collective-permute-start(bf16[592,1024]{1,0:T(8,128)(2,1)} %fusion.26), channel_id=1, source_target_pairs={{0,2},{1,3},{2,0},{3,1},{4,6},{5,7},{6,4},{7,5},{8,10},{9,11},{10,... | collective-permute-start | bytes 3637256 | tf_op jit(solution)/shard_map/ppermute | solution.py:304
  311.8 18.6 %collective-permute-start.36 = (bf16[512,512]{1,0:T(8,128)(2,1)}, bf16[512,512]{1,0:T(8,128)(2,1)}, u32[]{:S(2)}, u32[]{:S(2)}) collective-permute-start(bf16[512,512]{1,0:T(8,128)(2,1)} %fusion.41), channel_id=1, source_target_pairs={{0,4},{1,5},{2,6},{3,7},{4,0},{5,1},{6,2},{7,3},{8,12},{9,13},{10,... | collective-permute-start | bytes 1572872 | tf_op jit(solution)/shard_map/ppermute | solution.py:304
  313.4 18.6 %collective-permute-start.37 = (bf16[512,512]{1,0:T(8,128)(2,1)}, bf16[512,512]{1,0:T(8,128)(2,1)}, u32[]{:S(2)}, u32[]{:S(2)}) collective-permute-start(bf16[512,512]{1,0:T(8,128)(2,1)} %fusion.42), channel_id=1, source_target_pairs={{0,1},{1,0},{2,3},{3,2},{4,5},{5,4},{6,7},{7,6},{8,9},{9,8},{10,11... | collective-permute-start | bytes 1572872 | tf_op jit(solution)/shard_map/ppermute | solution.py:304
  317.8 22.8 %collective-permute-start.34 = (bf16[289,1024]{1,0:T(8,128)(2,1)S(1)}, bf16[289,1024]{1,0:T(8,128)(2,1)S(1)}, u32[]{:S(2)}, u32[]{:S(2)}) collective-permute-start(bf16[289,1024]{1,0:T(8,128)(2,1)S(1)} %slice.197), channel_id=1, source_target_pairs={{0,1},{1,0},{2,3},{3,2},{4,5},{5,4},{6,7},{7,6},{8,9},{9,8},{10,11... | collective-permute-start | bytes 1775624 | tf_op jit(solution)/shard_map/ppermute | solution.py:304
  323.5 1.3 collective-permute-start.39
  324.8 12.1 %collective-permute-start.42 = (f32[12288]{0:T(1024)S(1)}, f32[12288]{0:T(1024)S(1)}, u32[]{:S(2)}, u32[]{:S(2)}) collective-permute-start(f32[12288]{0:T(1024)S(1)} %add.276), channel_id=1, source_target_pairs={{0,24},{1,25},{2,26},{3,27},{4,28},{5,29},{6,30},{7,31},{8,16},{9,... | collective-permute-start | bytes 147464 | tf_op jit(solution)/shard_map/ppermute | solution.py:304
  326.6 10.3 %collective-permute-start.41 = (f32[12288]{0:T(1024)S(1)}, f32[12288]{0:T(1024)S(1)}, u32[]{:S(2)}, u32[]{:S(2)}) collective-permute-start(f32[12288]{0:T(1024)S(1)} %add.276), channel_id=1, source_target_pairs={{0,16},{1,17},{2,18},{3,19},{4,20},{5,21},{6,22},{7,23},{8,24},{9,... | collective-permute-start | bytes 147464 | tf_op jit(solution)/shard_map/ppermute | solution.py:304
  330.4 8.9 %collective-permute-start.40 = (f32[12288]{0:T(1024)S(1)}, f32[12288]{0:T(1024)S(1)}, u32[]{:S(2)}, u32[]{:S(2)}) collective-permute-start(f32[12288]{0:T(1024)S(1)} %add.276), channel_id=1, source_target_pairs={{0,8},{1,9},{2,10},{3,11},{4,12},{5,13},{6,14},{7,15},{8,0},{9,1},... | collective-permute-start | bytes 147464 | tf_op jit(solution)/shard_map/ppermute | solution.py:304
  334.8 26.0 %collective-permute-start.45 = (bf16[2,128,512]{2,1,0:T(8,128)(2,1)S(1)}, bf16[2,128,512]{2,1,0:T(8,128)(2,1)S(1)}, u32[]{:S(2)}, u32[]{:S(2)}) collective-permute-start(bf16[2,128,512]{2,1,0:T(8,128)(2,1)S(1)} %get-tuple-element.179), channel_id=1, source_target_pairs={{0,8},{1,9},{2,10},{3,11},{4,12},{5,13},{6,14},{7,15},{8,0},{9,1},... | collective-permute-start | bytes 786440 | tf_op jit(solution)/shard_map/ppermute | solution.py:304
  336.9 24.0 %collective-permute-start.46 = (bf16[2,128,512]{2,1,0:T(8,128)(2,1)S(1)}, bf16[2,128,512]{2,1,0:T(8,128)(2,1)}, u32[]{:S(2)}, u32[]{:S(2)}) collective-permute-start(bf16[2,128,512]{2,1,0:T(8,128)(2,1)S(1)} %get-tuple-element.180), channel_id=1, source_target_pairs={{0,16},{1,17},{2,18},{3,19},{4,20},{5,21},{6,22},{7,23},{8,24},{9,... | collective-permute-start | bytes 786440 | tf_op jit(solution)/shard_map/ppermute | solution.py:304
  337.0 23.9 %collective-permute-start.47 = (bf16[2,128,512]{2,1,0:T(8,128)(2,1)S(1)}, bf16[2,128,512]{2,1,0:T(8,128)(2,1)}, u32[]{:S(2)}, u32[]{:S(2)}) collective-permute-start(bf16[2,128,512]{2,1,0:T(8,128)(2,1)S(1)} %get-tuple-element.181), channel_id=1, source_target_pairs={{0,24},{1,25},{2,26},{3,27},{4,28},{5,29},{6,30},{7,31},{8,16},{9,... | collective-permute-start | bytes 786440 | tf_op jit(solution)/shard_map/ppermute | solution.py:304
  339.3 14.6 %collective-permute-start.38 = (bf16[289,1024]{1,0:T(8,128)(2,1)}, bf16[289,1024]{1,0:T(8,128)(2,1)}, u32[]{:S(2)}, u32[]{:S(2)}) collective-permute-start(bf16[289,1024]{1,0:T(8,128)(2,1)} %slice.292), channel_id=1, source_target_pairs={{0,1},{1,0},{2,3},{3,2},{4,5},{5,4},{6,7},{7,6},{8,9},{9,8},{10,11... | collective-permute-start | bytes 1775624 | tf_op jit(solution)/shard_map/ppermute | solution.py:304
  340.8 2.8 collective-permute-start.48
  343.6 1.5 collective-permute-start.49
  345.2 4.8 %collective-permute-start.43 = (f32[12288]{0:T(1024)S(1)}, f32[12288]{0:T(1024)S(1)}, u32[]{:S(2)}, u32[]{:S(2)}) collective-permute-start(f32[12288]{0:T(1024)S(1)} %add_add_fusion), channel_id=1, source_target_pairs={{0,4},{1,5},{2,6},{3,7},{4,0},{5,1},{6,2},{7,3},{8,12},{9,13},{10,... | collective-permute-start | bytes 147464 | tf_op jit(solution)/shard_map/ppermute | solution.py:304
  353.9 6.3 %collective-permute-start.44 = (f32[12288]{0:T(1024)S(1)}, f32[12288]{0:T(1024)S(1)}, u32[]{:S(2)}, u32[]{:S(2)}) collective-permute-start(f32[12288]{0:T(1024)S(1)} %add.280), channel_id=1, source_target_pairs={{0,1},{1,0},{2,3},{3,2},{4,5},{5,4},{6,7},{7,6},{8,9},{9,8},{10,11... | collective-permute-start | bytes 147464 | tf_op jit(solution)/shard_map/ppermute | solution.py:304
  362.1 1.4 collective-permute-start.50
  (80 other events, 388.1 us)
Sparse Core Ops, SparseCore 0:
  12.2 143.3 all-gather.1
